TPU v7x, 512 devices: a whole 4x8x8 slice. The times are simulated.
512 devices in a mesh: pts: 32 (over z, x_hi, core), orb: 16 (over x_lo, y).
Axes of the slice: x: 4 (x_hi: 2, x_lo: 2; x = x_hi * 2 + x_lo), y: 8, z: 8, core: 2. Of those that a mesh axis runs over, the one named last changes fastest.
Arguments:
- phi_occ: bfloat16 [3072, 2048], P('pts', 'orb'), may hold values from -0.75 to 0.75
- phi_vir: bfloat16 [3072, 20480], P('pts', 'orb'), may hold values from -0.5 to 0.5
- eps_occ: float32 [2048], P('orb'), may hold values from -1 to -0.2
- eps_vir: float32 [20480], P('orb'), may hold values from 0.02 to 1.5
- taus: float32 [2], replicated, may hold values from 0.5 to 3
- pair_mask: int32 [32, 8], P('pts'), may hold values 0 or 1
- basis: bfloat16 [3072, 4096], P('pts', 'orb'), may hold values from -0.375 to 0.375
Outputs:
- aux_response: float32 [4096, 2, 4096], P('pts', None, 'orb')
All inputs are finite; a program needn't handle non-finite values. No bound on the sum of `pair_mask` on one device may be relied on, other than what follows from the above.
Results may differ from a plain program's by a relative error of at most 0.0057.
Values may be sent and summed in bfloat16 or wider, within the bound.
No kernel may reach another device: no remote copies, remote signals or barrier semaphores. Data moves between devices by JAX's collectives and lax.ppermute only.
A program may use at most 64 MiB of HBM per device.

v0:
```python
import jax
import jax.numpy as jnp
from jax import lax
from jax.sharding import PartitionSpec as P

NOFF = 8


def from_behind(value, axis, steps):
    count = lax.axis_size(axis)
    pairs = [(source, (source + steps) % count) for source in range(count)]
    return lax.ppermute(value, axis, pairs)


def on_device(phi_occ, phi_vir, eps_occ, eps_vir, taus, pair_mask, basis):
    half = NOFF // 2
    expo_occ = jnp.exp(taus[:, None] * eps_occ[None, :])
    expo_vir = jnp.exp(-taus[:, None] * eps_vir[None, :])
    weighted_occ = (phi_occ.astype(jnp.float32)[None] * expo_occ[:, None, :]).astype(jnp.bfloat16)
    weighted_vir = (phi_vir.astype(jnp.float32)[None] * expo_vir[:, None, :]).astype(jnp.bfloat16)
    factors = pair_mask[0].astype(jnp.float32)
    totals = jnp.zeros((taus.shape[0], phi_occ.shape[0], basis.shape[1]), jnp.float32)
    for slot in range(NOFF):
        distance = slot - half if slot < half else slot - half + 1
        panels = from_behind((phi_occ, phi_vir, basis), "pts", -distance)
        occ_part, vir_part, basis_part = panels
        g_occ = jnp.einsum(
            "tro,co->trc", weighted_occ, occ_part, preferred_element_type=jnp.float32
        )
        g_vir = jnp.einsum(
            "tra,ca->trc", weighted_vir, vir_part, preferred_element_type=jnp.float32
        )
        g_occ, g_vir = lax.psum((g_occ, g_vir), "orb")
        chi = (g_occ * g_vir * factors[slot]).astype(jnp.bfloat16)
        totals = totals + jnp.einsum(
            "trc,cq->trq", chi, basis_part, preferred_element_type=jnp.float32
        )
    projected = totals.astype(jnp.bfloat16)
    full_basis = lax.all_gather(basis, "orb", axis=1, tiled=True)
    basis_cols = lax.all_to_all(full_basis, "pts", split_axis=1, concat_axis=0, tiled=True)
    return jnp.einsum(
        "rp,trq->ptq",
        basis_cols,
        lax.all_gather(projected, "pts", axis=1, tiled=True),
        preferred_element_type=jnp.float32,
    )


def solution(mesh):
    placed = (
        P("pts", "orb"),
        P("pts", "orb"),
        P("orb"),
        P("orb"),
        P(),
        P("pts", None),
        P("pts", "orb"),
    )
    return jax.shard_map(
        on_device, mesh=mesh, in_specs=placed, out_specs=P("pts", None, "orb"), check_vma=False
    )
```

profile of v0, /device:TPU:1, one launch (start us, length us, event | category | flops | bytes accessed | tf_op | source)
XLA Modules:
  0.0 362.3 jit_solution(7681334299482809656)
XLA Ops:
  6.5 14.1 %collective-permute-start.15 = (bf16[96,128]{1,0:T(8,128)(2,1)}, bf16[96,128]{1,0:T(8,128)(2,1)S(1)}, u32[]{:S(2)}, u32[]{:S(2)}) collective-permute-start(bf16[96,128]{1,0:T(8,128)(2,1)} %param.7), channel_id=1, source_target_pairs={{0,480},{16,496},{32,0},{48,16},{64,32},{80,48},{96,64},{112,80},{... | collective-permute-start | bytes 73736 | tf_op jit(solution)/shard_map/ppermute | solution.py:12
  20.6 2.9 collective-permute-start.12
  23.5 4.2 %collective-permute-start.9 = (bf16[96,128]{1,0:T(8,128)(2,1)}, bf16[96,128]{1,0:T(8,128)(2,1)S(1)}, u32[]{:S(2)}, u32[]{:S(2)}) collective-permute-start(bf16[96,128]{1,0:T(8,128)(2,1)} %param.7), channel_id=1, source_target_pairs={{0,16},{16,32},{32,48},{48,64},{64,80},{80,96},{96,112},{112,128},... | collective-permute-start | bytes 73736 | tf_op jit(solution)/shard_map/ppermute | solution.py:12
  29.6 4.9 %collective-permute-start.21 = (bf16[96,128]{1,0:T(8,128)(2,1)}, bf16[96,128]{1,0:T(8,128)(2,1)S(1)}, u32[]{:S(2)}, u32[]{:S(2)}) collective-permute-start(bf16[96,128]{1,0:T(8,128)(2,1)} %param.7), channel_id=1, source_target_pairs={{0,448},{16,464},{32,480},{48,496},{64,0},{80,16},{96,32},{112,48}... | collective-permute-start | bytes 73736 | tf_op jit(solution)/shard_map/ppermute | solution.py:12
  38.4 3.7 %collective-permute-start.18 = (bf16[96,128]{1,0:T(8,128)(2,1)}, bf16[96,128]{1,0:T(8,128)(2,1)S(1)}, u32[]{:S(2)}, u32[]{:S(2)}) collective-permute-start(bf16[96,128]{1,0:T(8,128)(2,1)} %param.7), channel_id=1, source_target_pairs={{0,464},{16,480},{32,496},{48,0},{64,16},{80,32},{96,48},{112,64},... | collective-permute-start | bytes 73736 | tf_op jit(solution)/shard_map/ppermute | solution.py:12
  49.8 7.2 %collective-permute-start.16 = (bf16[96,1280]{1,0:T(8,128)(2,1)}, bf16[96,1280]{1,0:T(8,128)(2,1)S(1)}, u32[]{:S(2)}, u32[]{:S(2)}) collective-permute-start(bf16[96,1280]{1,0:T(8,128)(2,1)} %param.8), channel_id=1, source_target_pairs={{0,480},{16,496},{32,0},{48,16},{64,32},{80,48},{96,64},{112,80},{... | collective-permute-start | bytes 737288 | tf_op jit(solution)/shard_map/ppermute | solution.py:12
  57.8 2.6 collective-permute-start.13
  61.2 4.5 %collective-permute-start.10 = (bf16[96,1280]{1,0:T(8,128)(2,1)}, bf16[96,1280]{1,0:T(8,128)(2,1)S(1)}, u32[]{:S(2)}, u32[]{:S(2)}) collective-permute-start(bf16[96,1280]{1,0:T(8,128)(2,1)} %param.8), channel_id=1, source_target_pairs={{0,16},{16,32},{32,48},{48,64},{64,80},{80,96},{96,112},{112,128},... | collective-permute-start | bytes 737288 | tf_op jit(solution)/shard_map/ppermute | solution.py:12
  66.4 3.4 collective-permute-start.22
  70.6 2.9 collective-permute-start.19
  74.6 4.5 %collective-permute-start.7 = (bf16[96,1280]{1,0:T(8,128)(2,1)}, bf16[96,1280]{1,0:T(8,128)(2,1)S(1)}, u32[]{:S(2)}, u32[]{:S(2)}) collective-permute-start(bf16[96,1280]{1,0:T(8,128)(2,1)} %param.8), channel_id=1, source_target_pairs={{0,32},{16,48},{32,64},{48,80},{64,96},{80,112},{96,128},{112,144}... | collective-permute-start | bytes 737288 | tf_op jit(solution)/shard_map/ppermute | solution.py:12
  89.6 4.7 %collective-permute-done.4 = bf16[96,1280]{1,0:T(8,128)(2,1)S(1)} collective-permute-done((bf16[96,1280]{1,0:T(8,128)(2,1)}, bf16[96,1280]{1,0:T(8,128)(2,1)S(1)}, u32[]{:S(2)}, u32[]{:S(2)}) %collective-permute-start.4) | collective-permute-done | bytes 245792 | tf_op jit(solution)/shard_map/ppermute | solution.py:12
  96.3 7.2 %collective-permute-start.20 = (bf16[96,256]{1,0:T(8,128)(2,1)S(1)}, bf16[96,256]{1,0:T(8,128)(2,1)S(1)}, u32[]{:S(2)}, u32[]{:S(2)}) collective-permute-start(bf16[96,256]{1,0:T(8,128)(2,1)S(1)} %copy-done.3), channel_id=1, source_target_pairs={{0,464},{16,480},{32,496},{48,0},{64,16},{80,32},{96,48},{112,64},... | collective-permute-start | bytes 147464 | tf_op jit(solution)/shard_map/ppermute | solution.py:12
  105.4 2.3 collective-permute-start.14
  107.7 4.8 %collective-permute-start.11 = (bf16[96,256]{1,0:T(8,128)(2,1)S(1)}, bf16[96,256]{1,0:T(8,128)(2,1)S(1)}, u32[]{:S(2)}, u32[]{:S(2)}) collective-permute-start(bf16[96,256]{1,0:T(8,128)(2,1)S(1)} %copy-done.3), channel_id=1, source_target_pairs={{0,16},{16,32},{32,48},{48,64},{64,80},{80,96},{96,112},{112,128},... | collective-permute-start | bytes 147464 | tf_op jit(solution)/shard_map/ppermute | solution.py:12
  115.1 3.0 collective-permute-done.23
  118.1 4.9 %collective-permute-start.8 = (bf16[96,256]{1,0:T(8,128)(2,1)S(1)}, bf16[96,256]{1,0:T(8,128)(2,1)S(1)}, u32[]{:S(2)}, u32[]{:S(2)}) collective-permute-start(bf16[96,256]{1,0:T(8,128)(2,1)S(1)} %copy-done.3), channel_id=1, source_target_pairs={{0,32},{16,48},{32,64},{48,80},{64,96},{80,112},{96,128},{112,144}... | collective-permute-start | bytes 147464 | tf_op jit(solution)/shard_map/ppermute | solution.py:12
  123.1 108.3 %all-reduce.3.cloned.1.call-done = (f32[2,96,96]{2,1,0:T(8,128)}, f32[2,96,96]{2,1,0:T(8,128)}, f32[2,96,96]{2,1,0:T(8,128)}, f32[2,96,96]{2,1,0:T(8,128)}, f32[...) async-done(((f32[2,96,96]{2,1,0:T(8,128)}, ...) | async-done | bytes 1179664 | tf_op jit(solution)/shard_map/psum | solution.py:33
  233.2 13.7 %collective-permute-start.5 = (bf16[96,256]{1,0:T(8,128)(2,1)S(1)}, bf16[96,256]{1,0:T(8,128)(2,1)S(1)}, u32[]{:S(2)}, u32[]{:S(2)}) collective-permute-start(bf16[96,256]{1,0:T(8,128)(2,1)S(1)} %copy-done.3), channel_id=1, source_target_pairs={{0,48},{16,64},{32,80},{48,96},{64,112},{80,128},{96,144},{112,160... | collective-permute-start | bytes 147464 | tf_op jit(solution)/shard_map/ppermute | solution.py:12
  248.6 3.3 collective-permute-start.2
  262.1 30.2 %all_gather.7 = bf16[96,4096]{1,0:T(8,128)(2,1)S(1)} all-gather(bf16[96,256]{1,0:T(8,128)(2,1)S(1)} %copy-done.3), channel_id=1, replica_groups=mesh['pts'=32,'orb'=16] {'orb'}, dimensions={1}, use_global_device_ids=true | all-gather | bytes 835584 | tf_op jit(solution)/shard_map/all_gather | solution.py:39
  292.4 39.0 %all_to_all.19 = bf16[96,32,128]{2,0,1:T(8,128)(2,1)S(1)} all-to-all(bf16[96,32,128]{2,0,1:T(8,128)(2,1)S(1)} %copy_bitcast_fusion), channel_id=1, replica_groups=mesh['pts'=32,'orb'=16] {'pts'}, dimensions={1} | all-to-all | bytes 1572864 | tf_op jit(solution)/shard_map/all_to_all | solution.py:40
  331.4 20.3 %all-gather.2.cloned.1.call-done = bf16[2,3072,256]{2,1,0:T(8,128)(2,1)} async-done(((bf16[2,96,256]{2,1,0:T(8,128)(2,1)}), bf16[2,3072,256]{2,1,0:T(8,128)(2,1)}) %all-gather.2.cloned.1.call-update) | async-done | bytes 3145744 | tf_op jit(solution)/shard_map/all_gather | solution.py:44
  351.7 2.9 convolution_bitcast_fusion
  (76 shorter events, 49.3 us)
Async XLA Ops:
  6.5 224.8 %all-reduce.3.cloned.1.call-start = ((), (), s32[]{:S(2)}) async-start(), calls=%async_computation.2 | async-start | bytes 3145728 | tf_op jit(solution)/shard_map/psum | solution.py:33
  6.5 40.5 %collective-permute-start.15 = (bf16[96,128]{1,0:T(8,128)(2,1)}, bf16[96,128]{1,0:T(8,128)(2,1)S(1)}, u32[]{:S(2)}, u32[]{:S(2)}) collective-permute-start(bf16[96,128]{1,0:T(8,128)(2,1)} %param.7), channel_id=1, source_target_pairs={{0,480},{16,496},{32,0},{48,16},{64,32},{80,48},{96,64},{112,80},{... | collective-permute-start | bytes 73736 | tf_op jit(solution)/shard_map/ppermute | solution.py:12
  20.6 29.1 %collective-permute-start.12 = (bf16[96,128]{1,0:T(8,128)(2,1)}, bf16[96,128]{1,0:T(8,128)(2,1)S(1)}, u32[]{:S(2)}, u32[]{:S(2)}) collective-permute-start(bf16[96,128]{1,0:T(8,128)(2,1)} %param.7), channel_id=1, source_target_pairs={{0,496},{16,0},{32,16},{48,32},{64,48},{80,64},{96,80},{112,96},{1... | collective-permute-start | bytes 73736 | tf_op jit(solution)/shard_map/ppermute | solution.py:12
  23.5 34.3 %collective-permute-start.9 = (bf16[96,128]{1,0:T(8,128)(2,1)}, bf16[96,128]{1,0:T(8,128)(2,1)S(1)}, u32[]{:S(2)}, u32[]{:S(2)}) collective-permute-start(bf16[96,128]{1,0:T(8,128)(2,1)} %param.7), channel_id=1, source_target_pairs={{0,16},{16,32},{32,48},{48,64},{64,80},{80,96},{96,112},{112,128},... | collective-permute-start | bytes 73736 | tf_op jit(solution)/shard_map/ppermute | solution.py:12
  27.7 33.5 %collective-permute-start.6 = (bf16[96,128]{1,0:T(8,128)(2,1)}, bf16[96,128]{1,0:T(8,128)(2,1)S(1)}, u32[]{:S(2)}, u32[]{:S(2)}) collective-permute-start(bf16[96,128]{1,0:T(8,128)(2,1)} %param.7), channel_id=1, source_target_pairs={{0,32},{16,48},{32,64},{48,80},{64,96},{80,112},{96,128},{112,144}... | collective-permute-start | bytes 73736 | tf_op jit(solution)/shard_map/ppermute | solution.py:12
  29.6 8.8 %collective-permute-start.21 = (bf16[96,128]{1,0:T(8,128)(2,1)}, bf16[96,128]{1,0:T(8,128)(2,1)S(1)}, u32[]{:S(2)}, u32[]{:S(2)}) collective-permute-start(bf16[96,128]{1,0:T(8,128)(2,1)} %param.7), channel_id=1, source_target_pairs={{0,448},{16,464},{32,480},{48,496},{64,0},{80,16},{96,32},{112,48}... | collective-permute-start | bytes 73736 | tf_op jit(solution)/shard_map/ppermute | solution.py:12
  44.1 22.3 %collective-permute-start.3 = (bf16[96,128]{1,0:T(8,128)(2,1)}, bf16[96,128]{1,0:T(8,128)(2,1)S(1)}, u32[]{:S(2)}, u32[]{:S(2)}) collective-permute-start(bf16[96,128]{1,0:T(8,128)(2,1)} %param.7), channel_id=1, source_target_pairs={{0,48},{16,64},{32,80},{48,96},{64,112},{80,128},{96,144},{112,160... | collective-permute-start | bytes 73736 | tf_op jit(solution)/shard_map/ppermute | solution.py:12
  47.1 23.5 %collective-permute-start = (bf16[96,128]{1,0:T(8,128)(2,1)}, bf16[96,128]{1,0:T(8,128)(2,1)S(1)}, u32[]{:S(2)}, u32[]{:S(2)}) collective-permute-start(bf16[96,128]{1,0:T(8,128)(2,1)} %param.7), channel_id=1, source_target_pairs={{0,64},{16,80},{32,96},{48,112},{64,128},{80,144},{96,160},{112,17... | collective-permute-start | bytes 73736 | tf_op jit(solution)/shard_map/ppermute | solution.py:12
  49.8 33.5 %collective-permute-start.16 = (bf16[96,1280]{1,0:T(8,128)(2,1)}, bf16[96,1280]{1,0:T(8,128)(2,1)S(1)}, u32[]{:S(2)}, u32[]{:S(2)}) collective-permute-start(bf16[96,1280]{1,0:T(8,128)(2,1)} %param.8), channel_id=1, source_target_pairs={{0,480},{16,496},{32,0},{48,16},{64,32},{80,48},{96,64},{112,80},{... | collective-permute-start | bytes 737288 | tf_op jit(solution)/shard_map/ppermute | solution.py:12
  57.8 28.4 %collective-permute-start.13 = (bf16[96,1280]{1,0:T(8,128)(2,1)}, bf16[96,1280]{1,0:T(8,128)(2,1)S(1)}, u32[]{:S(2)}, u32[]{:S(2)}) collective-permute-start(bf16[96,1280]{1,0:T(8,128)(2,1)} %param.8), channel_id=1, source_target_pairs={{0,496},{16,0},{32,16},{48,32},{64,48},{80,64},{96,80},{112,96},{1... | collective-permute-start | bytes 737288 | tf_op jit(solution)/shard_map/ppermute | solution.py:12
  61.2 26.0 %collective-permute-start.10 = (bf16[96,1280]{1,0:T(8,128)(2,1)}, bf16[96,1280]{1,0:T(8,128)(2,1)S(1)}, u32[]{:S(2)}, u32[]{:S(2)}) collective-permute-start(bf16[96,1280]{1,0:T(8,128)(2,1)} %param.8), channel_id=1, source_target_pairs={{0,16},{16,32},{32,48},{48,64},{64,80},{80,96},{96,112},{112,128},... | collective-permute-start | bytes 737288 | tf_op jit(solution)/shard_map/ppermute | solution.py:12
  66.4 8.2 %collective-permute-start.22 = (bf16[96,1280]{1,0:T(8,128)(2,1)}, bf16[96,1280]{1,0:T(8,128)(2,1)S(1)}, u32[]{:S(2)}, u32[]{:S(2)}) collective-permute-start(bf16[96,1280]{1,0:T(8,128)(2,1)} %param.8), channel_id=1, source_target_pairs={{0,448},{16,464},{32,480},{48,496},{64,0},{80,16},{96,32},{112,48}... | collective-permute-start | bytes 737288 | tf_op jit(solution)/shard_map/ppermute | solution.py:12
  70.6 9.8 %collective-permute-start.19 = (bf16[96,1280]{1,0:T(8,128)(2,1)}, bf16[96,1280]{1,0:T(8,128)(2,1)S(1)}, u32[]{:S(2)}, u32[]{:S(2)}) collective-permute-start(bf16[96,1280]{1,0:T(8,128)(2,1)} %param.8), channel_id=1, source_target_pairs={{0,464},{16,480},{32,496},{48,0},{64,16},{80,32},{96,48},{112,64},... | collective-permute-start | bytes 737288 | tf_op jit(solution)/shard_map/ppermute | solution.py:12
  74.6 14.1 %collective-permute-start.7 = (bf16[96,1280]{1,0:T(8,128)(2,1)}, bf16[96,1280]{1,0:T(8,128)(2,1)S(1)}, u32[]{:S(2)}, u32[]{:S(2)}) collective-permute-start(bf16[96,1280]{1,0:T(8,128)(2,1)} %param.8), channel_id=1, source_target_pairs={{0,32},{16,48},{32,64},{48,80},{64,96},{80,112},{96,128},{112,144}... | collective-permute-start | bytes 737288 | tf_op jit(solution)/shard_map/ppermute | solution.py:12
  80.4 14.0 %collective-permute-start.4 = (bf16[96,1280]{1,0:T(8,128)(2,1)}, bf16[96,1280]{1,0:T(8,128)(2,1)S(1)}, u32[]{:S(2)}, u32[]{:S(2)}) collective-permute-start(bf16[96,1280]{1,0:T(8,128)(2,1)} %param.8), channel_id=1, source_target_pairs={{0,48},{16,64},{32,80},{48,96},{64,112},{80,128},{96,144},{112,160... | collective-permute-start | bytes 737288 | tf_op jit(solution)/shard_map/ppermute | solution.py:12
  83.2 12.0 %collective-permute-start.1 = (bf16[96,1280]{1,0:T(8,128)(2,1)S(1)}, bf16[96,1280]{1,0:T(8,128)(2,1)S(1)}, u32[]{:S(2)}, u32[]{:S(2)}) collective-permute-start(bf16[96,1280]{1,0:T(8,128)(2,1)S(1)} %copy-done), channel_id=1, source_target_pairs={{0,64},{16,80},{32,96},{48,112},{64,128},{80,144},{96,160},{112,17... | collective-permute-start | bytes 737288 | tf_op jit(solution)/shard_map/ppermute | solution.py:12
  96.2 255.5 %all-gather.2.cloned.1.call-start = ((), (), s32[]{:S(2)}) async-start(), calls=%async_computation.1 | async-start | bytes 3244032 | tf_op jit(solution)/shard_map/all_gather | solution.py:44
  96.3 137.0 %collective-permute-start.20 = (bf16[96,256]{1,0:T(8,128)(2,1)S(1)}, bf16[96,256]{1,0:T(8,128)(2,1)S(1)}, u32[]{:S(2)}, u32[]{:S(2)}) collective-permute-start(bf16[96,256]{1,0:T(8,128)(2,1)S(1)} %copy-done.3), channel_id=1, source_target_pairs={{0,464},{16,480},{32,496},{48,0},{64,16},{80,32},{96,48},{112,64},... | collective-permute-start | bytes 147464 | tf_op jit(solution)/shard_map/ppermute | solution.py:12
  103.5 145.2 %collective-permute-start.17 = (bf16[96,256]{1,0:T(8,128)(2,1)S(1)}, bf16[96,256]{1,0:T(8,128)(2,1)S(1)}, u32[]{:S(2)}, u32[]{:S(2)}) collective-permute-start(bf16[96,256]{1,0:T(8,128)(2,1)S(1)} %copy-done.3), channel_id=1, source_target_pairs={{0,480},{16,496},{32,0},{48,16},{64,32},{80,48},{96,64},{112,80},{... | collective-permute-start | bytes 147464 | tf_op jit(solution)/shard_map/ppermute | solution.py:12
  105.4 148.2 %collective-permute-start.14 = (bf16[96,256]{1,0:T(8,128)(2,1)S(1)}, bf16[96,256]{1,0:T(8,128)(2,1)S(1)}, u32[]{:S(2)}, u32[]{:S(2)}) collective-permute-start(bf16[96,256]{1,0:T(8,128)(2,1)S(1)} %copy-done.3), channel_id=1, source_target_pairs={{0,496},{16,0},{32,16},{48,32},{64,48},{80,64},{96,80},{112,96},{1... | collective-permute-start | bytes 147464 | tf_op jit(solution)/shard_map/ppermute | solution.py:12
  107.7 147.7 %collective-permute-start.11 = (bf16[96,256]{1,0:T(8,128)(2,1)S(1)}, bf16[96,256]{1,0:T(8,128)(2,1)S(1)}, u32[]{:S(2)}, u32[]{:S(2)}) collective-permute-start(bf16[96,256]{1,0:T(8,128)(2,1)S(1)} %copy-done.3), channel_id=1, source_target_pairs={{0,16},{16,32},{32,48},{48,64},{64,80},{80,96},{96,112},{112,128},... | collective-permute-start | bytes 147464 | tf_op jit(solution)/shard_map/ppermute | solution.py:12
  118.1 139.0 %collective-permute-start.8 = (bf16[96,256]{1,0:T(8,128)(2,1)S(1)}, bf16[96,256]{1,0:T(8,128)(2,1)S(1)}, u32[]{:S(2)}, u32[]{:S(2)}) collective-permute-start(bf16[96,256]{1,0:T(8,128)(2,1)S(1)} %copy-done.3), channel_id=1, source_target_pairs={{0,32},{16,48},{32,64},{48,80},{64,96},{80,112},{96,128},{112,144}... | collective-permute-start | bytes 147464 | tf_op jit(solution)/shard_map/ppermute | solution.py:12
  233.2 25.6 %collective-permute-start.5 = (bf16[96,256]{1,0:T(8,128)(2,1)S(1)}, bf16[96,256]{1,0:T(8,128)(2,1)S(1)}, u32[]{:S(2)}, u32[]{:S(2)}) collective-permute-start(bf16[96,256]{1,0:T(8,128)(2,1)S(1)} %copy-done.3), channel_id=1, source_target_pairs={{0,48},{16,64},{32,80},{48,96},{64,112},{80,128},{96,144},{112,160... | collective-permute-start | bytes 147464 | tf_op jit(solution)/shard_map/ppermute | solution.py:12
  248.6 12.0 %collective-permute-start.2 = (bf16[96,256]{1,0:T(8,128)(2,1)S(1)}, bf16[96,256]{1,0:T(8,128)(2,1)S(1)}, u32[]{:S(2)}, u32[]{:S(2)}) collective-permute-start(bf16[96,256]{1,0:T(8,128)(2,1)S(1)} %copy-done.3), channel_id=1, source_target_pairs={{0,64},{16,80},{32,96},{48,112},{64,128},{80,144},{96,160},{112,17... | collective-permute-start | bytes 147464 | tf_op jit(solution)/shard_map/ppermute | solution.py:12
  (7 other events, 190.7 us)
Sparse Core Ops, SparseCore 0:
  96.3 135.0 all-reduce.2
  262.2 89.4 all-gather.1
where the time goes:
time: 364 us; the launch traced here: 362 us
  waiting for transfers between devices  139 us (38%)
  starting transfers between devices  105 us (29%)
  blocking collectives  69.2 us (19%)
  matrix products  30.2 us (8%)
  between operations  13.8 us (4%)
  other arithmetic  3.91 us (1%)
    psum x1, waiting for transfers between devices, on_device(): g_occ, g_vir = lax.psum((g_occ, g_vir), 'orb')  108 us
    ppermute x24, starting transfers between devices, from_behind(): return lax.ppermute(value, axis, pairs)  105 us
    all_to_all x1, blocking collectives, on_device(): lax.all_to_all(full_basis, 'pts', split_axis=1, concat_axis=0, tiled=True)  39 us
    all_gather x1, blocking collectives, on_device(): full_basis = lax.all_gather(basis, 'orb', axis=1, tiled=True)  30.2 us
    all_gather x1, waiting for transfers between devices, on_device(): lax.all_gather(projected, 'pts', axis=1, tiled=True)  20.3 us
    dot_general x8, matrix products, on_device(): jnp.einsum('trc,cq->trq', chi, basis_part, preferred_element_type=jnp.flo...  13.6 us
    ppermute x24, waiting for transfers between devices, from_behind(): return lax.ppermute(value, axis, pairs)  10.3 us
    dot_general x8, matrix products, on_device(): jnp.einsum('tra,ca->trc', weighted_vir, vir_part, preferred_element_type=...  7.43 us
  transfers between devices with their start and end apart: 26, of which 8 were waited for; matrix products, arithmetic and copies ran while one was open for 8% of the time, Pallas kernels for 0%

commit v1 on v0

v1 whole, which is shorter than its diff:
```python
import jax
import jax.numpy as jnp
from jax import lax
from jax.sharding import Mesh, PartitionSpec as P

ORB = ("xl", "y")
PTS = ("z", "xh", "core")
BF = jnp.bfloat16
F32 = jnp.float32


def shift_tiles(value, steps):
    pairs = [((i + steps) % 32, i) for i in range(32)]
    return lax.ppermute(value, PTS, pairs)


def swap_core(value):
    return lax.ppermute(value, "core", [(0, 1), (1, 0)])


def to_all(value, axes, count):
    copies = jnp.broadcast_to(value[None], (count,) + value.shape)
    return lax.all_to_all(copies, axes, 0, 0, tiled=True)


def on_device(phi_occ, phi_vir, eps_occ, eps_vir, taus, pair_mask, basis):
    core = lax.axis_index("core")
    nocc, nvir, naux = phi_occ.shape[1], phi_vir.shape[1], basis.shape[1]
    rows = phi_occ.shape[0]
    mask = jnp.pad(pair_mask.astype(BF), ((0, 0), (0, 120)))
    mask = jnp.broadcast_to(mask, (rows, 128))
    packed = jnp.concatenate([phi_occ, phi_vir, basis], axis=1)
    moves = []
    for z in range(8):
        for o in range(16):
            moves.append((z * 16 + o, (o // 2) * 16 + z * 2 + o % 2))
    basis_part = lax.ppermute(basis, ("z", "xl", "y"), moves)
    other = swap_core(jnp.concatenate([packed, mask], axis=1))
    got = [shift_tiles(packed, d) for d in (-4, -2, 2, 4)]
    basis_cols = to_all(basis_part, ORB, 16)
    tiles = [got[0], got[1], packed, got[2], got[3]]
    own_panel = jnp.concatenate([got[0], got[1], got[2], got[3]], axis=0)
    low = jnp.concatenate([got[0], got[1], packed, got[2]], axis=0)
    high = jnp.concatenate([got[1], packed, got[2], got[3]], axis=0)
    other_panel = jnp.where(core == 0, high, low)
    mask_own = mask[0, :8].astype(F32)
    mask_other = other[0, nocc + nvir + naux : nocc + nvir + naux + 8].astype(F32)
    expo_occ = jnp.exp(taus[:, None] * eps_occ[None, :])
    expo_vir = jnp.exp(-taus[:, None] * eps_vir[None, :])
    left = jnp.stack([packed, other[:, : nocc + nvir + naux]]).astype(F32)
    w_occ = (left[None, :, :, :nocc] * expo_occ[:, None, None, :]).astype(BF)
    w_vir = (left[None, :, :, nocc : nocc + nvir] * expo_vir[:, None, None, :]).astype(BF)
    panels = jnp.stack([own_panel, other_panel])
    g_occ = jnp.einsum("tsra,sca->tsrc", w_occ, panels[:, :, :nocc], preferred_element_type=F32)
    g_vir = jnp.einsum(
        "tsra,sca->tsrc", w_vir, panels[:, :, nocc : nocc + nvir], preferred_element_type=F32
    )
    part = jnp.stack([g_occ.astype(BF), g_vir.astype(BF)], axis=3)
    part = part.reshape(16, 24, 2, 384).transpose(0, 2, 1, 3)
    recv = lax.all_to_all(part, ORB, 0, 0, tiled=True).astype(F32)
    total = recv.sum(axis=0)
    me = lax.axis_index(ORB)
    s = (me // 4) % 2
    m_own = jnp.stack([mask_own[i] for i in (0, 2, 5, 7)])
    m_other = jnp.stack([mask_other[i] for i in (1, 3, 4, 6)])
    factor = jnp.repeat(jnp.where(s == 0, m_own, m_other), 96)
    chi = (total[0] * total[1] * factor[None, :]).astype(BF)
    chi = to_all(chi, ORB, 16).reshape(2, 2, 96, 384)
    proj = jnp.einsum(
        "tsrc,scq->strq".replace(" ", ""), chi, panels[:, :, nocc + nvir :], preferred_element_type=F32
    )
    projected = (proj[0] + swap_core(proj[1])).astype(BF)
    gathered = to_all(projected, "z", 8)
    cols = basis_cols.reshape(8, 2, rows, naux)
    resp = jnp.einsum("zhrp,ztrq->hptq", cols, gathered, preferred_element_type=F32)
    resp = resp.reshape(4, 128, 2, naux).astype(BF)
    resp = lax.all_to_all(resp, ("xh", "core"), 0, 0, tiled=True)
    return resp.astype(F32).sum(axis=0)


def solution(mesh):
    names = ("z", "xh", "core", "xl", "y")
    fine = Mesh(mesh.devices.reshape(8, 2, 2, 2, 8), names)
    placed = (P(PTS, ORB), P(PTS, ORB), P(ORB), P(ORB), P(), P(PTS, None), P(PTS, ORB))
    return jax.shard_map(
        on_device, mesh=fine, in_specs=placed, out_specs=P(PTS, None, ORB), check_vma=False
    )
```

time: 364 us -> 149 us (0.41)
  waiting for transfers between devices: 139 us -> 27.8 us
  starting transfers between devices: 105 us -> 58.2 us
  blocking collectives: 69.2 us -> 38.7 us
  matrix products: 30.2 us -> 3.05 us
  between operations: 13.8 us -> 0.32 us
  local copies, waits for them, and re-layouts: 1.68 us -> 9.37 us
  other arithmetic: 3.91 us -> 8.73 us
    psum x1 -> x0, waiting for transfers between devices: 108 us -> none  [on_device(): g_occ, g_vir = lax.psum((g_occ, g_vir), 'orb')]
    ppermute x24 -> x7, starting transfers between devices: 105 us -> 31.2 us  [the longest x4 21.1 us: shift_tiles(): return lax.ppermute(value, PTS, pairs)]
    all_gather x1 -> x0, blocking collectives: 30.2 us -> none  [on_device(): full_basis = lax.all_gather(basis, 'orb', axis=1, tiled=True)]
    dot_general x25 -> x4, matrix products: 30.2 us -> 3.05 us  [the longest x1 1.75 us: on_device(): jnp.einsum('zhrp,ztrq->hptq', cols, gathered, preferred_element_type=F32)]
    all_to_all x0 -> x3, starting transfers between devices: none -> 27 us  [the longest x2 19 us: to_all(): return lax.all_to_all(copies, axes, 0, 0, tiled=True)]
    all_to_all x0 -> x3, waiting for transfers between devices: none -> 24.1 us  [the longest x2 16.5 us: to_all(): return lax.all_to_all(copies, axes, 0, 0, tiled=True)]
    all_gather x1 -> x0, waiting for transfers between devices: 20.3 us -> none  [on_device(): lax.all_gather(projected, 'pts', axis=1, tiled=True)]
    ppermute x24 -> x7, waiting for transfers between devices: 10.3 us -> 3.68 us  [the longest x4 2.62 us: shift_tiles(): return lax.ppermute(value, PTS, pairs)]
  transfers between devices with their start and end apart: 26 -> 10, of which waited for: 8 -> 6; matrix products, arithmetic and copies ran while one was open for 8% -> 7% of each run, Pallas kernels for 0% -> 0%
where the time goes in v1:
time: 149 us; the launch traced here: 146 us
  starting transfers between devices  58.2 us (39%)
  blocking collectives  38.7 us (26%)
  waiting for transfers between devices  27.8 us (19%)
  local copies, waits for them, and re-layouts  9.37 us (6%)
  other arithmetic  8.73 us (6%)
  matrix products  3.05 us (2%)
    ppermute x4, starting transfers between devices, shift_tiles(): return lax.ppermute(value, PTS, pairs)  21.1 us
    all_to_all x1, blocking collectives, to_all(): return lax.all_to_all(copies, axes, 0, 0, tiled=True)  19.6 us
    all_to_all x1, blocking collectives, on_device(): resp = lax.all_to_all(resp, ('xh', 'core'), 0, 0, tiled=True)  19.1 us
    all_to_all x2, starting transfers between devices, to_all(): return lax.all_to_all(copies, axes, 0, 0, tiled=True)  19 us
    all_to_all x2, waiting for transfers between devices, to_all(): return lax.all_to_all(copies, axes, 0, 0, tiled=True)  16.5 us
    ppermute x2, starting transfers between devices, swap_core(): return lax.ppermute(value, 'core', [(0, 1), (1, 0)])  9.43 us
    all_to_all x1, starting transfers between devices, on_device(): recv = lax.all_to_all(part, ORB, 0, 0, tiled=True).astype(F32)  7.98 us
    all_to_all x1, waiting for transfers between devices, on_device(): recv = lax.all_to_all(part, ORB, 0, 0, tiled=True).astype(F32)  7.66 us
  transfers between devices with their start and end apart: 10, of which 6 were waited for; matrix products, arithmetic and copies ran while one was open for 7% of the time, Pallas kernels for 0%

profile of v1, /device:TPU:1, one launch (start us, length us, event | category | flops | bytes accessed | tf_op | source)
XLA Modules:
  0.0 146.2 jit_solution(7213854345538399990)
XLA Ops:
  0.8 1.0 constant_dynamic-update-slice_fusion.1
  2.6 5.5 %collective-permute-start.1 = (bf16[96,1664]{1,0:T(8,128)(2,1)S(1)}, bf16[96,1664]{1,0:T(8,128)(2,1)S(1)}, u32[]{:S(2)}, u32[]{:S(2)}) collective-permute-start(bf16[96,1664]{1,0:T(8,128)(2,1)S(1)} %constant_dynamic-update-slice_fusion), channel_id=1, source_target_pairs={{480,0},{496,16},{0,32},{16,48},{32,64},{48,80},{64,96},{80,112},{... | collective-permute-start | bytes 958472 | tf_op jit(solution)/shard_map/ppermute | solution.py:14
  8.0 10.4 %collective-permute-start.2 = (bf16[96,1664]{1,0:T(8,128)(2,1)S(1)}, bf16[96,1664]{1,0:T(8,128)(2,1)S(1)}, u32[]{:S(2)}, u32[]{:S(2)}) collective-permute-start(bf16[96,1664]{1,0:T(8,128)(2,1)S(1)} %constant_dynamic-update-slice_fusion), channel_id=1, source_target_pairs={{32,0},{48,16},{64,32},{80,48},{96,64},{112,80},{128,96},{144,112}... | collective-permute-start | bytes 958472 | tf_op jit(solution)/shard_map/ppermute | solution.py:14
  18.4 3.3 %collective-permute-start.3 = (bf16[96,1664]{1,0:T(8,128)(2,1)S(1)}, bf16[96,1664]{1,0:T(8,128)(2,1)S(1)}, u32[]{:S(2)}, u32[]{:S(2)}) collective-permute-start(bf16[96,1664]{1,0:T(8,128)(2,1)S(1)} %constant_dynamic-update-slice_fusion), channel_id=1, source_target_pairs={{64,0},{80,16},{96,32},{112,48},{128,64},{144,80},{160,96},{176,11... | collective-permute-start | bytes 958472 | tf_op jit(solution)/shard_map/ppermute | solution.py:14
  21.7 2.0 %collective-permute-start = (bf16[96,1664]{1,0:T(8,128)(2,1)S(1)}, bf16[96,1664]{1,0:T(8,128)(2,1)S(1)}, u32[]{:S(2)}, u32[]{:S(2)}) collective-permute-start(bf16[96,1664]{1,0:T(8,128)(2,1)S(1)} %constant_dynamic-update-slice_fusion), channel_id=1, source_target_pairs={{448,0},{464,16},{480,32},{496,48},{0,64},{16,80},{32,96},{48,112}... | collective-permute-start | bytes 958472 | tf_op jit(solution)/shard_map/ppermute | solution.py:14
  24.4 1.8 %maximum_maximum_fusion = bf16[96,1792]{1,0:T(8,128)(2,1)} fusion(bf16[96,256]{1,0:T(8,128)(2,1)} %param.13, bf16[96,1280]{1,0:T(8,128)(2,1)} %param.8, bf16[96,128]{1,0:T(8,128)(2,1)} %param.7, bf16[1792]{0:T(1024)(128)(2,1)S(1)} %pad.19.clone), kind=kLoop, calls=%fused_computation.28 | loop fusion | flops 1376256 | bytes 667136 | tf_op jit(solution)/shard_map/concatenate | solution.py:38
  26.2 3.4 %collective-permute-start.4 = (bf16[96,1792]{1,0:T(8,128)(2,1)}, bf16[96,1792]{1,0:T(8,128)(2,1)}, u32[]{:S(2)}, u32[]{:S(2)}) collective-permute-start(bf16[96,1792]{1,0:T(8,128)(2,1)} %maximum_maximum_fusion), channel_id=1, source_target_pairs={{0,16},{16,0},{1,17},{17,1},{2,18},{18,2},{3,19},{19,3},{4,20},{20... | collective-permute-start | bytes 1032200 | tf_op jit(solution)/shard_map/ppermute | solution.py:18
  29.8 1.7 %collective-permute-done.3 = bf16[96,1664]{1,0:T(8,128)(2,1)S(1)} collective-permute-done((bf16[96,1664]{1,0:T(8,128)(2,1)S(1)}, bf16[96,1664]{1,0:T(8,128)(2,1)S(1)}, u32[]{:S(2)}, u32[]{:S(2)}) %collective-permute-start.3) | collective-permute-done | bytes 319520 | tf_op jit(solution)/shard_map/ppermute | solution.py:14
  33.1 1.3 maximum_select_fusion
  34.5 1.0 slice_bitcast_fusion
  37.7 8.0 %all-to-all-start = ((bf16[16,2,24,384]{3,2,1,0:T(8,128)(2,1)}), bf16[16,2,24,384]{3,2,1,0:T(8,128)(2,1)S(1)}, u32[]{:S(2)}, u32[]{:S(2)}) async-start(bf16[16,2,24,384]{3,2,1,0:T(8,128)(2,1)} %copy.14), calls=%async_computation | async-start | bytes 1179648 | tf_op jit(solution)/shard_map/all_to_all | solution.py:60
  47.7 3.7 %broadcast_select_fusion = f32[4]{0:T(128)S(1)} fusion(pred[]{:T(512)S(6)} %eq.9, f32[1]{0:T(128)} %bitcast.20, f32[1]{0:T(128)} %bitcast.19, f32[1]{0:T(128)} %bitcast.18, f32[1]{0:T(128)} %bitcast.17, f32[1]{0:T(128)} %bitcast.23, f32[2]{0:T(128)S(1)} %slice_bitcast_fusion.3, f32[1]{0:T(128)} %bitcast.21), kind=kLoop, calls=%fused_computation.51 | loop fusion | flops 24 | bytes 49 | tf_op jit(solution)/shard_map/jit(_where)/select_n | solution.py:66
  51.6 7.7 %all-to-all-done = bf16[16,2,24,384]{3,2,1,0:T(8,128)(2,1)S(1)} async-done(((bf16[16,2,24,384]{3,2,1,0:T(8,128)(2,1)}), bf16[16,2,24,384]{3,2,1,0:T(8,128)(2,1)S(1)}, u32[]{:S(2)}, u32[]{:S(2)}) %all-to-all-start) | async-done | bytes 589856 | tf_op jit(solution)/shard_map/all_to_all | solution.py:60
  60.1 6.6 %all-to-all-start.1 = ((bf16[16,24,384]{2,1,0:T(8,128)(2,1)}), bf16[16,24,384]{2,1,0:T(8,128)(2,1)S(1)}, u32[]{:S(2)}, u32[]{:S(2)}) async-start(bf16[16,24,384]{2,1,0:T(8,128)(2,1)} %broadcast_in_dim.18), calls=%async_computation.1 | async-start | bytes 589824 | tf_op jit(solution)/shard_map/all_to_all | solution.py:23
  67.4 7.2 %all-to-all-done.1 = bf16[16,24,384]{2,1,0:T(8,128)(2,1)S(1)} async-done(((bf16[16,24,384]{2,1,0:T(8,128)(2,1)}), bf16[16,24,384]{2,1,0:T(8,128)(2,1)S(1)}, u32[]{:S(2)}, u32[]{:S(2)}) %all-to-all-start.1) | async-done | bytes 294944 | tf_op jit(solution)/shard_map/all_to_all | solution.py:23
  74.6 1.0 broadcast_in_dim.20
  75.6 12.4 %all-to-all-start.3 = ((bf16[16,96,256]{2,1,0:T(8,128)(2,1)}), bf16[16,96,256]{2,1,0:T(8,128)(2,1)}, u32[]{:S(2)}, u32[]{:S(2)}) async-start(bf16[16,96,256]{2,1,0:T(8,128)(2,1)} %broadcast_in_dim.20), calls=%async_computation.3 | async-start | bytes 1572864 | tf_op jit(solution)/shard_map/all_to_all | solution.py:23
  88.3 6.0 %collective-permute-start.5 = (f32[2,96,256]{2,1,0:T(8,128)S(1)}, f32[2,96,256]{2,1,0:T(8,128)S(1)}, u32[]{:S(2)}, u32[]{:S(2)}) collective-permute-start(f32[2,96,256]{2,1,0:T(8,128)S(1)} %slice_bitcast_fusion.1), channel_id=1, source_target_pairs={{0,16},{16,0},{1,17},{17,1},{2,18},{18,2},{3,19},{19,3},{4,20},{20... | collective-permute-start | bytes 589832 | tf_op jit(solution)/shard_map/ppermute | solution.py:18
  94.3 1.0 collective-permute-done.5
  95.4 9.3 %all-to-all-done.3 = bf16[16,96,256]{2,1,0:T(8,128)(2,1)} async-done(((bf16[16,96,256]{2,1,0:T(8,128)(2,1)}), bf16[16,96,256]{2,1,0:T(8,128)(2,1)}, u32[]{:S(2)}, u32[]{:S(2)}) %all-to-all-start.3) | async-done | bytes 786464 | tf_op jit(solution)/shard_map/all_to_all | solution.py:23
  104.7 19.6 %all_to_all.25 = bf16[8,2,96,256]{3,2,1,0:T(8,128)(2,1)S(1)} all-to-all(bf16[8,2,96,256]{3,2,1,0:T(8,128)(2,1)S(1)} %broadcast_in_dim.19), channel_id=1, replica_groups=mesh['z'=8,'xh'=2,'core'=2,'xl'=2,'y'=8] {'z'}, dimensions={0} | all-to-all | bytes 1572864 | tf_op jit(solution)/shard_map/all_to_all | solution.py:23
  124.3 1.8 %fusion.4 = bf16[2,256,2,256]{1,3,2,0:T(8,128)(2,1)S(1)} fusion(bf16[8,2,96,256]{3,2,1,0:T(8,128)(2,1)} %bitcast.31, bf16[8,2,96,256]{3,2,1,0:T(8,128)(2,1)S(1)} %all_to_all.25), kind=kOutput, calls=%fused_computation.7 | convolution fusion | flops 402915328 | bytes 2097152 | tf_op jit(solution)/shard_map/zhrp,ztrq->hptq/dot_general | solution.py:75
  126.1 19.1 %all_to_all.26 = bf16[4,128,2,256]{3,1,2,0:T(8,128)(2,1)S(1)} all-to-all(bf16[4,128,2,256]{3,1,2,0:T(8,128)(2,1)S(1)} %copy.18), channel_id=1, replica_groups=mesh['z'=8,'xh'=2,'core'=2,'xl'=2,'y'=8] {'xh','core'}, dimensions={0} | all-to-all | bytes 1048576 | tf_op jit(solution)/shard_map/all_to_all | solution.py:77
  145.3 0.9 copy.20
  (50 shorter events, 10.3 us)
Async XLA Ops:
  0.0 29.6 %copy-start.4 = (f32[2]{0:T(128)S(1)}, f32[2]{0:T(128)}, u32[]{:S(2)}) copy-start(f32[2]{0:T(128)} %param.11) | copy-start | bytes 28
  0.0 29.6 %copy-start.3 = (f32[1280]{0:T(1024)S(1)}, f32[1280]{0:T(1024)}, u32[]{:S(2)}) copy-start(f32[1280]{0:T(1024)} %param.10) | copy-start | bytes 15364
  0.0 29.7 %copy-start.5 = (f32[128]{0:T(128)S(1)}, f32[128]{0:T(128)}, u32[]{:S(2)}) copy-start(f32[128]{0:T(128)} %param.9) | copy-start | bytes 1540
  2.6 27.2 %collective-permute-start.1 = (bf16[96,1664]{1,0:T(8,128)(2,1)S(1)}, bf16[96,1664]{1,0:T(8,128)(2,1)S(1)}, u32[]{:S(2)}, u32[]{:S(2)}) collective-permute-start(bf16[96,1664]{1,0:T(8,128)(2,1)S(1)} %constant_dynamic-update-slice_fusion), channel_id=1, source_target_pairs={{480,0},{496,16},{0,32},{16,48},{32,64},{48,80},{64,96},{80,112},{... | collective-permute-start | bytes 958472 | tf_op jit(solution)/shard_map/ppermute | solution.py:14
  8.0 21.8 %collective-permute-start.2 = (bf16[96,1664]{1,0:T(8,128)(2,1)S(1)}, bf16[96,1664]{1,0:T(8,128)(2,1)S(1)}, u32[]{:S(2)}, u32[]{:S(2)}) collective-permute-start(bf16[96,1664]{1,0:T(8,128)(2,1)S(1)} %constant_dynamic-update-slice_fusion), channel_id=1, source_target_pairs={{32,0},{48,16},{64,32},{80,48},{96,64},{112,80},{128,96},{144,112}... | collective-permute-start | bytes 958472 | tf_op jit(solution)/shard_map/ppermute | solution.py:14
  18.4 13.1 %collective-permute-start.3 = (bf16[96,1664]{1,0:T(8,128)(2,1)S(1)}, bf16[96,1664]{1,0:T(8,128)(2,1)S(1)}, u32[]{:S(2)}, u32[]{:S(2)}) collective-permute-start(bf16[96,1664]{1,0:T(8,128)(2,1)S(1)} %constant_dynamic-update-slice_fusion), channel_id=1, source_target_pairs={{64,0},{80,16},{96,32},{112,48},{128,64},{144,80},{160,96},{176,11... | collective-permute-start | bytes 958472 | tf_op jit(solution)/shard_map/ppermute | solution.py:14
  21.7 10.7 %collective-permute-start = (bf16[96,1664]{1,0:T(8,128)(2,1)S(1)}, bf16[96,1664]{1,0:T(8,128)(2,1)S(1)}, u32[]{:S(2)}, u32[]{:S(2)}) collective-permute-start(bf16[96,1664]{1,0:T(8,128)(2,1)S(1)} %constant_dynamic-update-slice_fusion), channel_id=1, source_target_pairs={{448,0},{464,16},{480,32},{496,48},{0,64},{16,80},{32,96},{48,112}... | collective-permute-start | bytes 958472 | tf_op jit(solution)/shard_map/ppermute | solution.py:14
  26.2 8.3 %collective-permute-start.4 = (bf16[96,1792]{1,0:T(8,128)(2,1)}, bf16[96,1792]{1,0:T(8,128)(2,1)}, u32[]{:S(2)}, u32[]{:S(2)}) collective-permute-start(bf16[96,1792]{1,0:T(8,128)(2,1)} %maximum_maximum_fusion), channel_id=1, source_target_pairs={{0,16},{16,0},{1,17},{17,1},{2,18},{18,2},{3,19},{19,3},{4,20},{20... | collective-permute-start | bytes 1032200 | tf_op jit(solution)/shard_map/ppermute | solution.py:18
  31.5 1.0 copy-start
  32.4 0.7 copy-start.1
  37.7 29.0 %copy-start.2 = (bf16[96,256]{1,0:T(8,128)(2,1)S(1)}, bf16[96,256]{1,0:T(8,128)(2,1)}, u32[]{:S(2)}) copy-start(bf16[96,256]{1,0:T(8,128)(2,1)} %param.13) | copy-start | bytes 147460
  37.7 21.6 %all-to-all-start = ((bf16[16,2,24,384]{3,2,1,0:T(8,128)(2,1)}), bf16[16,2,24,384]{3,2,1,0:T(8,128)(2,1)S(1)}, u32[]{:S(2)}, u32[]{:S(2)}) async-start(bf16[16,2,24,384]{3,2,1,0:T(8,128)(2,1)} %copy.14), calls=%async_computation | async-start | bytes 1179648 | tf_op jit(solution)/shard_map/all_to_all | solution.py:60
  60.1 14.5 %all-to-all-start.1 = ((bf16[16,24,384]{2,1,0:T(8,128)(2,1)}), bf16[16,24,384]{2,1,0:T(8,128)(2,1)S(1)}, u32[]{:S(2)}, u32[]{:S(2)}) async-start(bf16[16,24,384]{2,1,0:T(8,128)(2,1)} %broadcast_in_dim.18), calls=%async_computation.1 | async-start | bytes 589824 | tf_op jit(solution)/shard_map/all_to_all | solution.py:23
  66.7 0.7 collective-permute-start.6
  75.6 29.0 %all-to-all-start.3 = ((bf16[16,96,256]{2,1,0:T(8,128)(2,1)}), bf16[16,96,256]{2,1,0:T(8,128)(2,1)}, u32[]{:S(2)}, u32[]{:S(2)}) async-start(bf16[16,96,256]{2,1,0:T(8,128)(2,1)} %broadcast_in_dim.20), calls=%async_computation.3 | async-start | bytes 1572864 | tf_op jit(solution)/shard_map/all_to_all | solution.py:23
  88.3 7.1 %collective-permute-start.5 = (f32[2,96,256]{2,1,0:T(8,128)S(1)}, f32[2,96,256]{2,1,0:T(8,128)S(1)}, u32[]{:S(2)}, u32[]{:S(2)}) collective-permute-start(f32[2,96,256]{2,1,0:T(8,128)S(1)} %slice_bitcast_fusion.1), channel_id=1, source_target_pairs={{0,16},{16,0},{1,17},{17,1},{2,18},{18,2},{3,19},{19,3},{4,20},{20... | collective-permute-start | bytes 589832 | tf_op jit(solution)/shard_map/ppermute | solution.py:18

commit v2 on v1

v2 whole, which is shorter than its diff:
```python
import jax
import jax.numpy as jnp
from jax import lax
from jax.sharding import Mesh, PartitionSpec as P

ORB = ("xl", "y")
PTS = ("z", "xh", "core")
BF = jnp.bfloat16
F32 = jnp.float32
SWAP = [(0, 1), (1, 0)]


def from_tile(value, steps):
    return lax.ppermute(value, PTS, [((i + steps) % 32, i) for i in range(32)])


def to_all(value, axes, count):
    copies = jnp.broadcast_to(value[None], (count,) + value.shape)
    return lax.all_to_all(copies, axes, 0, 0, tiled=True)


def on_device(phi_occ, phi_vir, eps_occ, eps_vir, taus, pair_mask, basis):
    core, xl, xh = lax.axis_index("core"), lax.axis_index("xl"), lax.axis_index("xh")
    nocc, nvir, naux = phi_occ.shape[1], phi_vir.shape[1], basis.shape[1]
    rows = phi_occ.shape[0]
    ends = (nocc, nocc + nvir, nocc + nvir + naux)
    first = core == 0
    mask = jnp.pad(pair_mask.astype(BF), ((0, 0), (0, 120)))
    mine = jnp.concatenate(
        [phi_occ, phi_vir, basis, jnp.broadcast_to(mask, (rows, 128))], axis=1
    )
    up = from_tile(mine, 2)
    down = from_tile(mine, -4)
    mate = lax.ppermute(mine, "core", SWAP)
    moves = [(z * 16 + o, (o // 2) * 16 + z * 2 + o % 2) for z in range(8) for o in range(16)]
    part = lax.ppermute(basis, ("z", "xl", "y"), moves)
    near = to_all(part, "y", 8)

    fourth = jnp.where(first, mine, down)

    def masks(slab):
        return slab[0, ends[2] : ends[2] + 8].astype(F32)

    m_own, m_mate, m_up, m_down = masks(mine), masks(mate), masks(up), masks(down)
    row_mask = jnp.stack(
        [m_own[5], m_own[0], jnp.where(first, m_mate[4], m_mate[6]), jnp.where(first, m_mate[3], m_mate[1])]
    )
    col_mask = jnp.stack(
        [m_up[2], m_down[7], jnp.where(first, m_up[3], m_up[1]), jnp.where(first, m_own[4], m_down[6])]
    )
    row_mask = jnp.repeat(row_mask, rows)
    col_mask = jnp.repeat(col_mask, rows)

    expo_occ = jnp.exp(taus[:, None] * eps_occ[None, :])
    expo_vir = jnp.exp(-taus[:, None] * eps_vir[None, :])

    def weighted(slab, lo, hi, expo):
        return (slab[None, :, lo:hi].astype(F32) * expo[:, None, :]).astype(BF)

    def green(lo, hi, expo):
        a = jnp.einsum(
            "tra,ca->trc",
            weighted(mine, lo, hi, expo),
            jnp.concatenate([up[:, lo:hi], down[:, lo:hi]]),
            preferred_element_type=F32,
        )
        b = jnp.einsum(
            "tra,ca->trc",
            weighted(mate, lo, hi, expo),
            jnp.concatenate([up[:, lo:hi], fourth[:, lo:hi]]),
            preferred_element_type=F32,
        )
        return jnp.concatenate([a, b], axis=2).astype(BF).reshape(16, 12, 4 * rows)

    part_sums = jnp.concatenate(
        [green(0, ends[0], expo_occ), green(ends[0], ends[1], expo_vir)], axis=1
    )
    part_sums, near = lax.optimization_barrier((part_sums, near))
    sums = lax.all_to_all(part_sums, ORB, 0, 0, tiled=True).astype(F32).sum(axis=0)
    both = (sums[:12] * sums[12:]).astype(BF)
    far = lax.ppermute(near, "xl", SWAP)
    low = jnp.where(xl == 0, near, far)
    high = jnp.where(xl == 0, far, near)
    cols = jnp.concatenate([low, high]).reshape(8, 2, rows, naux)
    both = to_all(both, ORB, 16).reshape(2, rows, 4 * rows)
    by_row = (both.astype(F32) * row_mask).astype(BF)
    by_col = (both.astype(F32) * col_mask).astype(BF)

    def aux(slab):
        return slab[:, ends[1] : ends[2]]

    def rows_of(block, *panels):
        return jnp.einsum("trc,cq->trq", block, jnp.concatenate(panels), preferred_element_type=F32)

    def cols_of(block, panel):
        return jnp.einsum("trc,rq->tcq", block, panel, preferred_element_type=F32)

    r2, r3 = 2 * rows, 3 * rows
    to_mate = rows_of(by_row[:, :, r2:], aux(up), aux(fourth))
    to_up = cols_of(by_col[:, :, :rows], aux(mine)) + cols_of(by_col[:, :, r2:r3], aux(mate))
    last = cols_of(by_col[:, :, r3:], aux(mate))
    zero = jnp.zeros_like(last)
    to_down = cols_of(by_col[:, :, rows:r2], aux(mine)) + jnp.where(first, zero, last)
    own = rows_of(by_row[:, :, :r2], aux(up), aux(down)) + jnp.where(first, last, zero)
    got_up = from_tile(to_up.astype(BF), -2)
    got_down = from_tile(to_down.astype(BF), 4)
    got_mate = lax.ppermute(to_mate, "core", SWAP)
    projected = (own + got_mate + got_up.astype(F32) + got_down.astype(F32)).astype(BF)

    gathered = to_all(projected, "z", 8)
    at = xh * 2 + core
    blocks = cols.reshape(8, 2, rows, 2, naux // 2)

    def response(flip):
        j = at ^ flip
        chosen = lax.dynamic_slice(
            blocks, (0, j // 2, 0, j % 2, 0), (8, 1, rows, 1, naux // 2)
        ).reshape(8, rows, naux // 2)
        return jnp.einsum("zrp,ztrq->ptq", chosen, gathered, preferred_element_type=F32)

    both_way = lax.ppermute(
        response(3).astype(BF), ("xh", "core"), [(0, 3), (3, 0), (1, 2), (2, 1)]
    )
    across = lax.ppermute(response(2).astype(BF), "xh", SWAP)
    beside = lax.ppermute(response(1), "core", SWAP)
    return response(0) + beside + across.astype(F32) + both_way.astype(F32)


def solution(mesh):
    names = ("z", "xh", "core", "xl", "y")
    fine = Mesh(mesh.devices.reshape(8, 2, 2, 2, 8), names)
    placed = (P(PTS, ORB), P(PTS, ORB), P(ORB), P(ORB), P(), P(PTS, None), P(PTS, ORB))
    return jax.shard_map(
        on_device, mesh=fine, in_specs=placed, out_specs=P(PTS, None, ORB), check_vma=False
    )
```

time: 149 us -> 138 us (0.926); the launches traced: 146 us -> 137 us
  blocking collectives: 38.7 us -> 0 us
  waiting for transfers between devices: 27.8 us -> 44.6 us
  starting transfers between devices: 58.2 us -> 65.5 us
  between operations: 0.32 us -> 5.64 us
  local copies, waits for them, and re-layouts: 9.37 us -> 12.2 us
  other arithmetic: 8.73 us -> 5.91 us
    all_to_all x2 -> x0, blocking collectives: 38.7 us -> none  [the longest x1 19.6 us: to_all(): return lax.all_to_all(copies, axes, 0, 0, tiled=True)]
    ppermute x7 -> x11, waiting for transfers between devices: 3.68 us -> 18 us  [the longest x1 8.78 us: on_device(): far = lax.ppermute(near, 'xl', SWAP)]
    ppermute x7 -> x11, starting transfers between devices: 31.2 us -> 44.2 us  [the longest x4 17.2 us: from_tile(): return lax.ppermute(value, PTS, [((i + steps) % 32, i) for i in range(32)])]
    select_n x2, other arithmetic: 5.03 us -> 0.16 us  [the longest x1 0.11 us: on_device(): fourth = jnp.where(first, mine, down)]
    slice x3 -> x18, local copies, waits for them, and re-layouts: 1.33 us -> 5.16 us  [the longest x4 1.67 us: green(): down[:, lo:hi]]
    all_to_all x1, starting transfers between devices: 7.98 us -> 4.38 us  [on_device(): lax.all_to_all(part_sums, ORB, 0, 0, tiled=True).astype(F32).sum(axis=0)]
    another operation x1 -> x2, other arithmetic: 0.1 us -> 2.58 us  [the longest x1 1.3 us: on_device(): jnp.stack([m_own[5], m_own[0], jnp.where(first, m_mate[4], m_mate[6]), jn...]
    dynamic_slice x0 -> x1, local copies, waits for them, and re-layouts: none -> 2.09 us  [response(): lax.dynamic_slice(blocks, (0, j // 2, 0, j % 2, 0), (8, 1, rows, 1, naux...]
  transfers between devices with their start and end apart: 10 -> 15, of which waited for: 6 -> 7; matrix products, arithmetic and copies ran while one was open for 7% -> 10% of each run, Pallas kernels for 0% -> 0%
where the time goes in v2:
time: 138 us; the launch traced here: 137 us
  starting transfers between devices  65.5 us (47%)
  waiting for transfers between devices  44.6 us (32%)
  local copies, waits for them, and re-layouts  12.2 us (9%)
  other arithmetic  5.91 us (4%)
  between operations  5.64 us (4%)
  matrix products  3.19 us (2%)
    all_to_all x3, waiting for transfers between devices, to_all(): return lax.all_to_all(copies, axes, 0, 0, tiled=True)  17.5 us
    ppermute x4, starting transfers between devices, from_tile(): return lax.ppermute(value, PTS, [((i + steps) % 32, i) for i in range(32)])  17.2 us
    all_to_all x3, starting transfers between devices, to_all(): return lax.all_to_all(copies, axes, 0, 0, tiled=True)  17 us
    all_to_all x1, waiting for transfers between devices, on_device(): lax.all_to_all(part_sums, ORB, 0, 0, tiled=True).astype(F32).sum(axis=0)  9.02 us
    ppermute x1, waiting for transfers between devices, on_device(): far = lax.ppermute(near, 'xl', SWAP)  8.78 us
    ppermute x1, starting transfers between devices, on_device(): mate = lax.ppermute(mine, 'core', SWAP)  8.75 us
    ppermute x4, waiting for transfers between devices, from_tile(): return lax.ppermute(value, PTS, [((i + steps) % 32, i) for i in range(32)])  5.42 us
    ppermute x1, starting transfers between devices, on_device(): lax.ppermute(response(3).astype(BF), ('xh', 'core'), [(0, 3), (3, 0), (1,...  5.04 us
  transfers between devices with their start and end apart: 15, of which 7 were waited for; matrix products, arithmetic and copies ran while one was open for 10% of the time, Pallas kernels for 0%

profile of v2, /device:TPU:1, one launch (start us, length us, event | category | flops | bytes accessed | tf_op | source)
XLA Modules:
  0.0 137.0 jit_solution(15744759067580472850)
XLA Ops:
  0.0 1.4 %collective-permute-start.3 = (bf16[96,256]{1,0:T(8,128)(2,1)}, bf16[96,256]{1,0:T(8,128)(2,1)S(1)}, u32[]{:S(2)}, u32[]{:S(2)}) collective-permute-start(bf16[96,256]{1,0:T(8,128)(2,1)} %param.13), channel_id=1, source_target_pairs={{0,0},{1,1},{2,64},{3,65},{4,128},{5,129},{6,192},{7,193},{8,256},... | collective-permute-start | bytes 147464 | tf_op jit(solution)/shard_map/ppermute | solution.py:36
  3.3 8.7 %collective-permute-start.2 = (bf16[96,1792]{1,0:T(8,128)(2,1)S(1)}, bf16[96,1792]{1,0:T(8,128)(2,1)S(1)}, u32[]{:S(2)}, u32[]{:S(2)}) collective-permute-start(bf16[96,1792]{1,0:T(8,128)(2,1)S(1)} %maximum_maximum_fusion), channel_id=1, source_target_pairs={{0,16},{16,0},{1,17},{17,1},{2,18},{18,2},{3,19},{19,3},{4,20},{20... | collective-permute-start | bytes 1032200 | tf_op jit(solution)/shard_map/ppermute | solution.py:34
  12.0 1.9 %collective-permute-start.1 = (bf16[96,1792]{1,0:T(8,128)(2,1)S(1)}, bf16[96,1792]{1,0:T(8,128)(2,1)S(1)}, u32[]{:S(2)}, u32[]{:S(2)}) collective-permute-start(bf16[96,1792]{1,0:T(8,128)(2,1)S(1)} %maximum_maximum_fusion), channel_id=1, source_target_pairs={{448,0},{464,16},{480,32},{496,48},{0,64},{16,80},{32,96},{48,112}... | collective-permute-start | bytes 1032200 | tf_op jit(solution)/shard_map/ppermute | solution.py:14
  13.9 8.3 %collective-permute-start = (bf16[96,1792]{1,0:T(8,128)(2,1)S(1)}, bf16[96,1792]{1,0:T(8,128)(2,1)S(1)}, u32[]{:S(2)}, u32[]{:S(2)}) collective-permute-start(bf16[96,1792]{1,0:T(8,128)(2,1)S(1)} %maximum_maximum_fusion), channel_id=1, source_target_pairs={{32,0},{48,16},{64,32},{80,48},{96,64},{112,80},{128,96},{144,112}... | collective-permute-start | bytes 1032200 | tf_op jit(solution)/shard_map/ppermute | solution.py:14
  23.9 7.0 %all-to-all-start = ((bf16[8,96,256]{2,1,0:T(8,128)(2,1)}), bf16[8,96,256]{2,1,0:T(8,128)(2,1)S(1)}, u32[]{:S(2)}, u32[]{:S(2)}) async-start(bf16[8,96,256]{2,1,0:T(8,128)(2,1)} %broadcast_in_dim.18), calls=%async_computation | async-start | bytes 786432 | tf_op jit(solution)/shard_map/all_to_all | solution.py:19
  39.7 6.3 %all-to-all-done = bf16[8,96,256]{2,1,0:T(8,128)(2,1)S(1)} async-done(((bf16[8,96,256]{2,1,0:T(8,128)(2,1)}), bf16[8,96,256]{2,1,0:T(8,128)(2,1)S(1)}, u32[]{:S(2)}, u32[]{:S(2)}) %all-to-all-start) | async-done | bytes 393248 | tf_op jit(solution)/shard_map/all_to_all | solution.py:19
  46.0 4.4 %all-to-all-start.1 = ((bf16[16,24,384]{2,1,0:T(8,128)(2,1)}), bf16[16,24,384]{2,1,0:T(8,128)(2,1)S(1)}, u32[]{:S(2)}, u32[]{:S(2)}) async-start(bf16[16,24,384]{2,1,0:T(8,128)(2,1)} %maximum_maximum_fusion.1), calls=%async_computation.1 | async-start | bytes 589824 | tf_op jit(solution)/shard_map/all_to_all | solution.py:79
  51.0 9.0 %all-to-all-done.1 = bf16[16,24,384]{2,1,0:T(8,128)(2,1)S(1)} async-done(((bf16[16,24,384]{2,1,0:T(8,128)(2,1)}), bf16[16,24,384]{2,1,0:T(8,128)(2,1)S(1)}, u32[]{:S(2)}, u32[]{:S(2)}) %all-to-all-start.1) | async-done | bytes 294944 | tf_op jit(solution)/shard_map/all_to_all | solution.py:79
  60.8 5.2 %all-to-all-start.2 = ((bf16[16,12,384]{2,1,0:T(8,128)(2,1)}), bf16[16,12,384]{2,1,0:T(8,128)(2,1)S(1)}, u32[]{:S(2)}, u32[]{:S(2)}) async-start(bf16[16,12,384]{2,1,0:T(8,128)(2,1)} %broadcast_in_dim.19), calls=%async_computation.2 | async-start | bytes 393216 | tf_op jit(solution)/shard_map/all_to_all | solution.py:19
  66.0 1.3 pad_maximum_fusion.7
  72.0 1.5 %all-to-all-done.2 = bf16[16,12,384]{2,1,0:T(8,128)(2,1)S(1)} async-done(((bf16[16,12,384]{2,1,0:T(8,128)(2,1)}), bf16[16,12,384]{2,1,0:T(8,128)(2,1)S(1)}, u32[]{:S(2)}, u32[]{:S(2)}) %all-to-all-start.2) | async-done | bytes 147488 | tf_op jit(solution)/shard_map/all_to_all | solution.py:19
  74.3 2.5 %collective-permute-start.7 = (bf16[2,96,256]{2,1,0:T(8,128)(2,1)S(1)}, bf16[2,96,256]{2,1,0:T(8,128)(2,1)S(1)}, u32[]{:S(2)}, u32[]{:S(2)}) collective-permute-start(bf16[2,96,256]{2,1,0:T(8,128)(2,1)S(1)} %add_convert_fusion), channel_id=1, source_target_pairs={{64,0},{80,16},{96,32},{112,48},{128,64},{144,80},{160,96},{176,11... | collective-permute-start | bytes 294920 | tf_op jit(solution)/shard_map/ppermute | solution.py:14
  77.0 4.9 %collective-permute-start.5 = (f32[2,96,256]{2,1,0:T(8,128)S(1)}, f32[2,96,256]{2,1,0:T(8,128)S(1)}, u32[]{:S(2)}, u32[]{:S(2)}) collective-permute-start(f32[2,96,256]{2,1,0:T(8,128)S(1)} %fusion.31), channel_id=1, source_target_pairs={{0,16},{16,0},{1,17},{17,1},{2,18},{18,2},{3,19},{19,3},{4,20},{20... | collective-permute-start | bytes 589832 | tf_op jit(solution)/shard_map/ppermute | solution.py:107
  82.1 4.6 %collective-permute-start.6 = (bf16[2,96,256]{2,1,0:T(8,128)(2,1)S(1)}, bf16[2,96,256]{2,1,0:T(8,128)(2,1)S(1)}, u32[]{:S(2)}, u32[]{:S(2)}) collective-permute-start(bf16[2,96,256]{2,1,0:T(8,128)(2,1)S(1)} %fusion.9), channel_id=1, source_target_pairs={{480,0},{496,16},{0,32},{16,48},{32,64},{48,80},{64,96},{80,112},{... | collective-permute-start | bytes 294920 | tf_op jit(solution)/shard_map/ppermute | solution.py:14
  86.7 5.4 %collective-permute-done.6 = bf16[2,96,256]{2,1,0:T(8,128)(2,1)S(1)} collective-permute-done((bf16[2,96,256]{2,1,0:T(8,128)(2,1)S(1)}, bf16[2,96,256]{2,1,0:T(8,128)(2,1)S(1)}, u32[]{:S(2)}, u32[]{:S(2)}) %collective-permute-start.6) | collective-permute-done | bytes 98336 | tf_op jit(solution)/shard_map/ppermute | solution.py:14
  93.3 4.8 %all-to-all-start.3 = ((bf16[8,2,96,256]{3,2,1,0:T(8,128)(2,1)}), bf16[8,2,96,256]{3,2,1,0:T(8,128)(2,1)S(1)}, u32[]{:S(2)}, u32[]{:S(2)}) async-start(bf16[8,2,96,256]{3,2,1,0:T(8,128)(2,1)} %broadcast_in_dim.23), calls=%async_computation.3 | async-start | bytes 1572864 | tf_op jit(solution)/shard_map/all_to_all | solution.py:19
  98.1 2.5 %collective-permute-start.4 = (bf16[8,96,256]{2,1,0:T(8,128)(2,1)S(1)}, bf16[8,96,256]{2,1,0:T(8,128)(2,1)S(1)}, u32[]{:S(2)}, u32[]{:S(2)}) collective-permute-start(bf16[8,96,256]{2,1,0:T(8,128)(2,1)S(1)} %all-to-all-done), channel_id=1, source_target_pairs={{0,8},{8,0},{1,9},{9,1},{2,10},{10,2},{3,11},{11,3},{4,12},{12,4},... | collective-permute-start | bytes 1179656 | tf_op jit(solution)/shard_map/ppermute | solution.py:81
  100.7 8.8 %collective-permute-done.4 = bf16[8,96,256]{2,1,0:T(8,128)(2,1)S(1)} collective-permute-done((bf16[8,96,256]{2,1,0:T(8,128)(2,1)S(1)}, bf16[8,96,256]{2,1,0:T(8,128)(2,1)S(1)}, u32[]{:S(2)}, u32[]{:S(2)}) %collective-permute-start.4) | collective-permute-done | bytes 393248 | tf_op jit(solution)/shard_map/ppermute | solution.py:81
  109.8 2.1 %constant_dynamic-slice_fusion.3 = (bf16[8,1,96,1,128]{4,3,2,1,0:T(2,128)(2,1)S(1)}, bf16[8,1,96,1,128]{4,3,2,1,0:T(2,128)(2,1)S(1)}, bf16[8,1,96,1,128]{4,3,2,1,0:T(2,128)(2,1)S(1)}, bf16[8,1,96,1,128]{4,3,2,1,0:T(2,128)(2,1)S(1)}) fusion(bf16[8,2,96,2,128]{4,3,2,1,0:T(2,128)(2,1)S(1)} %reshape_reshape.3, s32[]{:T(128)S(6)} %select_n.107, ...), kind=kLoop, calls=%fused_computation.90 | loop fusion | bytes 1572896 | tf_op jit(solution)/shard_map/dynamic_slice | solution.py:116
  111.9 9.7 %all-to-all-done.3 = bf16[8,2,96,256]{3,2,1,0:T(8,128)(2,1)S(1)} async-done(((bf16[8,2,96,256]{3,2,1,0:T(8,128)(2,1)}), bf16[8,2,96,256]{3,2,1,0:T(8,128)(2,1)S(1)}, u32[]{:S(2)}, u32[]{:S(2)}) %all-to-all-start.3) | async-done | bytes 786464 | tf_op jit(solution)/shard_map/all_to_all | solution.py:19
  122.0 1.9 %collective-permute-start.9 = (bf16[128,2,256]{2,0,1:T(8,128)(2,1)S(1)}, bf16[128,2,256]{2,0,1:T(8,128)(2,1)S(1)}, u32[]{:S(2)}, u32[]{:S(2)}) collective-permute-start(bf16[128,2,256]{2,0,1:T(8,128)(2,1)S(1)} %fusion.6), channel_id=1, source_target_pairs={{0,32},{32,0},{1,33},{33,1},{2,34},{34,2},{3,35},{35,3},{4,36},{36... | collective-permute-start | bytes 393224 | tf_op jit(solution)/shard_map/ppermute | solution.py:124
  124.2 2.4 %collective-permute-start.8 = (f32[128,2,256]{2,0,1:T(8,128)S(1)}, f32[128,2,256]{2,0,1:T(8,128)S(1)}, u32[]{:S(2)}, u32[]{:S(2)}) collective-permute-start(f32[128,2,256]{2,0,1:T(8,128)S(1)} %convolution_bitcast_fusion.2), channel_id=1, source_target_pairs={{0,16},{16,0},{1,17},{17,1},{2,18},{18,2},{3,19},{19,3},{4,20},{20... | collective-permute-start | bytes 786440 | tf_op jit(solution)/shard_map/ppermute | solution.py:125
  126.9 5.0 %collective-permute-start.10 = (bf16[128,2,256]{2,0,1:T(8,128)(2,1)S(1)}, bf16[128,2,256]{2,0,1:T(8,128)(2,1)S(1)}, u32[]{:S(2)}, u32[]{:S(2)}) collective-permute-start(bf16[128,2,256]{2,0,1:T(8,128)(2,1)S(1)} %fusion.7), channel_id=1, source_target_pairs={{0,48},{48,0},{16,32},{32,16},{1,49},{49,1},{17,33},{33,17},{2,50}... | collective-permute-start | bytes 393224 | tf_op jit(solution)/shard_map/ppermute | solution.py:121
  132.0 3.8 %collective-permute-done.10 = bf16[128,2,256]{2,0,1:T(8,128)(2,1)S(1)} collective-permute-done((bf16[128,2,256]{2,0,1:T(8,128)(2,1)S(1)}, bf16[128,2,256]{2,0,1:T(8,128)(2,1)S(1)}, u32[]{:S(2)}, u32[]{:S(2)}) %collective-permute-start.10) | collective-permute-done | bytes 131104 | tf_op jit(solution)/shard_map/ppermute | solution.py:121
  (96 shorter events, 18.0 us)
Async XLA Ops:
  0.0 23.1 %collective-permute-start.3 = (bf16[96,256]{1,0:T(8,128)(2,1)}, bf16[96,256]{1,0:T(8,128)(2,1)S(1)}, u32[]{:S(2)}, u32[]{:S(2)}) collective-permute-start(bf16[96,256]{1,0:T(8,128)(2,1)} %param.13), channel_id=1, source_target_pairs={{0,0},{1,1},{2,64},{3,65},{4,128},{5,129},{6,192},{7,193},{8,256},... | collective-permute-start | bytes 147464 | tf_op jit(solution)/shard_map/ppermute | solution.py:36
  2.1 20.1 %copy-start.7 = (f32[2]{0:T(128)S(1)}, f32[2]{0:T(128)}, u32[]{:S(2)}) copy-start(f32[2]{0:T(128)} %param.11) | copy-start | bytes 28
  2.1 20.1 %copy-start.6 = (f32[1280]{0:T(1024)S(1)}, f32[1280]{0:T(1024)}, u32[]{:S(2)}) copy-start(f32[1280]{0:T(1024)} %param.10) | copy-start | bytes 15364
  2.1 20.2 %copy-start.8 = (f32[128]{0:T(128)S(1)}, f32[128]{0:T(128)}, u32[]{:S(2)}) copy-start(f32[128]{0:T(128)} %param.9) | copy-start | bytes 1540
  2.2 20.9 %copy-start = (bf16[96,1280]{1,0:T(8,128)(2,1)S(1)}, bf16[96,1280]{1,0:T(8,128)(2,1)}, u32[]{:S(2)}) copy-start(bf16[96,1280]{1,0:T(8,128)(2,1)} %param.8) | copy-start | bytes 737284
  3.2 19.8 %copy-start.5 = (bf16[96,128]{1,0:T(8,128)(2,1)S(1)}, bf16[96,128]{1,0:T(8,128)(2,1)}, u32[]{:S(2)}) copy-start(bf16[96,128]{1,0:T(8,128)(2,1)} %param.7) | copy-start | bytes 73732
  3.3 29.4 %collective-permute-start.2 = (bf16[96,1792]{1,0:T(8,128)(2,1)S(1)}, bf16[96,1792]{1,0:T(8,128)(2,1)S(1)}, u32[]{:S(2)}, u32[]{:S(2)}) collective-permute-start(bf16[96,1792]{1,0:T(8,128)(2,1)S(1)} %maximum_maximum_fusion), channel_id=1, source_target_pairs={{0,16},{16,0},{1,17},{17,1},{2,18},{18,2},{3,19},{19,3},{4,20},{20... | collective-permute-start | bytes 1032200 | tf_op jit(solution)/shard_map/ppermute | solution.py:34
  12.0 18.8 %collective-permute-start.1 = (bf16[96,1792]{1,0:T(8,128)(2,1)S(1)}, bf16[96,1792]{1,0:T(8,128)(2,1)S(1)}, u32[]{:S(2)}, u32[]{:S(2)}) collective-permute-start(bf16[96,1792]{1,0:T(8,128)(2,1)S(1)} %maximum_maximum_fusion), channel_id=1, source_target_pairs={{448,0},{464,16},{480,32},{496,48},{0,64},{16,80},{32,96},{48,112}... | collective-permute-start | bytes 1032200 | tf_op jit(solution)/shard_map/ppermute | solution.py:14
  13.9 17.8 %collective-permute-start = (bf16[96,1792]{1,0:T(8,128)(2,1)S(1)}, bf16[96,1792]{1,0:T(8,128)(2,1)S(1)}, u32[]{:S(2)}, u32[]{:S(2)}) collective-permute-start(bf16[96,1792]{1,0:T(8,128)(2,1)S(1)} %maximum_maximum_fusion), channel_id=1, source_target_pairs={{32,0},{48,16},{64,32},{80,48},{96,64},{112,80},{128,96},{144,112}... | collective-permute-start | bytes 1032200 | tf_op jit(solution)/shard_map/ppermute | solution.py:14
  23.9 7.0 %copy-start.4 = (bf16[96,256]{1,0:T(8,128)(2,1)S(1)}, bf16[96,256]{1,0:T(8,128)(2,1)}, u32[]{:S(2)}) copy-start(bf16[96,256]{1,0:T(8,128)(2,1)} %param.13) | copy-start | bytes 147460
  23.9 22.1 %all-to-all-start = ((bf16[8,96,256]{2,1,0:T(8,128)(2,1)}), bf16[8,96,256]{2,1,0:T(8,128)(2,1)S(1)}, u32[]{:S(2)}, u32[]{:S(2)}) async-start(bf16[8,96,256]{2,1,0:T(8,128)(2,1)} %broadcast_in_dim.18), calls=%async_computation | async-start | bytes 786432 | tf_op jit(solution)/shard_map/all_to_all | solution.py:19
  39.7 10.7 %copy-start.2 = (bf16[96,1792]{1,0:T(8,128)(2,1)S(1)}, bf16[96,1792]{1,0:T(8,128)(2,1)}, u32[]{:S(2)}) copy-start(bf16[96,1792]{1,0:T(8,128)(2,1)} %copy-done.1) | copy-start | bytes 1032196
  46.0 14.0 %all-to-all-start.1 = ((bf16[16,24,384]{2,1,0:T(8,128)(2,1)}), bf16[16,24,384]{2,1,0:T(8,128)(2,1)S(1)}, u32[]{:S(2)}, u32[]{:S(2)}) async-start(bf16[16,24,384]{2,1,0:T(8,128)(2,1)} %maximum_maximum_fusion.1), calls=%async_computation.1 | async-start | bytes 589824 | tf_op jit(solution)/shard_map/all_to_all | solution.py:79
  60.8 12.7 %all-to-all-start.2 = ((bf16[16,12,384]{2,1,0:T(8,128)(2,1)}), bf16[16,12,384]{2,1,0:T(8,128)(2,1)S(1)}, u32[]{:S(2)}, u32[]{:S(2)}) async-start(bf16[16,12,384]{2,1,0:T(8,128)(2,1)} %broadcast_in_dim.19), calls=%async_computation.2 | async-start | bytes 393216 | tf_op jit(solution)/shard_map/all_to_all | solution.py:19
  74.1 2.7 %slice-start.4 = ((bf16[96,1792]{1,0:T(8,128)(2,1)}), bf16[96,256]{1,0:T(8,128)(2,1)S(1)}, s32[]{:S(2)}) async-start(bf16[96,1792]{1,0:T(8,128)(2,1)} %copy-done.3), calls=%async_computation.8 | async-start | bytes 98304 | tf_op jit(solution)/shard_map/slice | solution.py:90
  74.3 12.4 %collective-permute-start.7 = (bf16[2,96,256]{2,1,0:T(8,128)(2,1)S(1)}, bf16[2,96,256]{2,1,0:T(8,128)(2,1)S(1)}, u32[]{:S(2)}, u32[]{:S(2)}) collective-permute-start(bf16[2,96,256]{2,1,0:T(8,128)(2,1)S(1)} %add_convert_fusion), channel_id=1, source_target_pairs={{64,0},{80,16},{96,32},{112,48},{128,64},{144,80},{160,96},{176,11... | collective-permute-start | bytes 294920 | tf_op jit(solution)/shard_map/ppermute | solution.py:14
  77.0 15.1 %collective-permute-start.5 = (f32[2,96,256]{2,1,0:T(8,128)S(1)}, f32[2,96,256]{2,1,0:T(8,128)S(1)}, u32[]{:S(2)}, u32[]{:S(2)}) collective-permute-start(f32[2,96,256]{2,1,0:T(8,128)S(1)} %fusion.31), channel_id=1, source_target_pairs={{0,16},{16,0},{1,17},{17,1},{2,18},{18,2},{3,19},{19,3},{4,20},{20... | collective-permute-start | bytes 589832 | tf_op jit(solution)/shard_map/ppermute | solution.py:107
  82.1 10.0 %slice-start.2 = ((bf16[96,1792]{1,0:T(8,128)(2,1)}), bf16[96,256]{1,0:T(8,128)(2,1)S(1)}, s32[]{:S(2)}) async-start(bf16[96,1792]{1,0:T(8,128)(2,1)} %copy-done.1), calls=%async_computation.6 | async-start | bytes 98304 | tf_op jit(solution)/shard_map/slice | solution.py:90
  82.1 10.0 %collective-permute-start.6 = (bf16[2,96,256]{2,1,0:T(8,128)(2,1)S(1)}, bf16[2,96,256]{2,1,0:T(8,128)(2,1)S(1)}, u32[]{:S(2)}, u32[]{:S(2)}) collective-permute-start(bf16[2,96,256]{2,1,0:T(8,128)(2,1)S(1)} %fusion.9), channel_id=1, source_target_pairs={{480,0},{496,16},{0,32},{16,48},{32,64},{48,80},{64,96},{80,112},{... | collective-permute-start | bytes 294920 | tf_op jit(solution)/shard_map/ppermute | solution.py:14
  93.3 28.4 %all-to-all-start.3 = ((bf16[8,2,96,256]{3,2,1,0:T(8,128)(2,1)}), bf16[8,2,96,256]{3,2,1,0:T(8,128)(2,1)S(1)}, u32[]{:S(2)}, u32[]{:S(2)}) async-start(bf16[8,2,96,256]{3,2,1,0:T(8,128)(2,1)} %broadcast_in_dim.23), calls=%async_computation.3 | async-start | bytes 1572864 | tf_op jit(solution)/shard_map/all_to_all | solution.py:19
  98.1 11.4 %collective-permute-start.4 = (bf16[8,96,256]{2,1,0:T(8,128)(2,1)S(1)}, bf16[8,96,256]{2,1,0:T(8,128)(2,1)S(1)}, u32[]{:S(2)}, u32[]{:S(2)}) collective-permute-start(bf16[8,96,256]{2,1,0:T(8,128)(2,1)S(1)} %all-to-all-done), channel_id=1, source_target_pairs={{0,8},{8,0},{1,9},{9,1},{2,10},{10,2},{3,11},{11,3},{4,12},{12,4},... | collective-permute-start | bytes 1179656 | tf_op jit(solution)/shard_map/ppermute | solution.py:81
  122.0 10.0 %collective-permute-start.9 = (bf16[128,2,256]{2,0,1:T(8,128)(2,1)S(1)}, bf16[128,2,256]{2,0,1:T(8,128)(2,1)S(1)}, u32[]{:S(2)}, u32[]{:S(2)}) collective-permute-start(bf16[128,2,256]{2,0,1:T(8,128)(2,1)S(1)} %fusion.6), channel_id=1, source_target_pairs={{0,32},{32,0},{1,33},{33,1},{2,34},{34,2},{3,35},{35,3},{4,36},{36... | collective-permute-start | bytes 393224 | tf_op jit(solution)/shard_map/ppermute | solution.py:124
  124.2 11.6 %collective-permute-start.8 = (f32[128,2,256]{2,0,1:T(8,128)S(1)}, f32[128,2,256]{2,0,1:T(8,128)S(1)}, u32[]{:S(2)}, u32[]{:S(2)}) collective-permute-start(f32[128,2,256]{2,0,1:T(8,128)S(1)} %convolution_bitcast_fusion.2), channel_id=1, source_target_pairs={{0,16},{16,0},{1,17},{17,1},{2,18},{18,2},{3,19},{19,3},{4,20},{20... | collective-permute-start | bytes 786440 | tf_op jit(solution)/shard_map/ppermute | solution.py:125
  126.9 8.9 %collective-permute-start.10 = (bf16[128,2,256]{2,0,1:T(8,128)(2,1)S(1)}, bf16[128,2,256]{2,0,1:T(8,128)(2,1)S(1)}, u32[]{:S(2)}, u32[]{:S(2)}) collective-permute-start(bf16[128,2,256]{2,0,1:T(8,128)(2,1)S(1)} %fusion.7), channel_id=1, source_target_pairs={{0,48},{48,0},{16,32},{32,16},{1,49},{49,1},{17,33},{33,17},{2,50}... | collective-permute-start | bytes 393224 | tf_op jit(solution)/shard_map/ppermute | solution.py:121
  (5 other events, 4.1 us)

commit v3 on v2

v3 whole, which is shorter than its diff:
```python
import jax
import jax.numpy as jnp
from jax import lax
from jax.experimental import pallas as pl
from jax.experimental.pallas import tpu as pltpu
from jax.sharding import Mesh, PartitionSpec as P


ORB = ("xl", "y")
PTS = ("z", "xh", "core")
BF = jnp.bfloat16
F32 = jnp.float32
SWAP = [(0, 1), (1, 0)]
LAST = (((1,), (1,)), ((), ()))
WHOLE = pl.BlockSpec(memory_space=pltpu.VMEM)
SCALARS = pl.BlockSpec(memory_space=pltpu.SMEM)


def from_tile(value, steps):
    return lax.ppermute(value, PTS, [((i + steps) % 32, i) for i in range(32)])


def trade(value, axis, bit, at):
    size = lax.axis_size(axis)
    got = lax.ppermute(value, axis, [(i, i ^ bit) for i in range(size)])
    upper = (lax.axis_index(axis) & bit) != 0
    return jnp.stack([jnp.where(upper, got, value), jnp.where(upper, value, got)], axis=at)


def to_all(value, axes, count):
    copies = jnp.broadcast_to(value[None], (count,) + value.shape)
    return lax.all_to_all(copies, axes, 0, 0, tiled=True)


def green_kernel(core, taus, eps_occ, eps_vir, mine, mate, up, down, out, panel, left, total, rows12):
    rows = mine.shape[0]
    nocc, cols = eps_occ.shape[1], mine.shape[1]
    panel[0:rows] = up[...]
    panel[rows : 2 * rows] = down[...]
    panel[2 * rows : 3 * rows] = up[...]

    @pl.when(core[0] == 0)
    def _():
        panel[3 * rows : 4 * rows] = mine[...]

    @pl.when(core[0] != 0)
    def _():
        panel[3 * rows : 4 * rows] = down[...]

    for t in range(2):
        for lo, hi, eps, sign in ((0, nocc, eps_occ, 1.0), (nocc, cols, eps_vir, -1.0)):
            expo = jnp.exp((sign * taus[t]) * eps[...])
            for s, slab in enumerate((mine, mate)):
                at = (2 * s + t) * rows
                left[at : at + rows, lo:hi] = (slab[:, lo:hi].astype(F32) * expo).astype(BF)
    lane = lax.broadcasted_iota(jnp.int32, (2 * rows, 4 * rows), 1)
    for q, (lo, hi) in enumerate(((0, nocc), (nocc, cols))):
        a = lax.dot_general(
            left[0 : 2 * rows, lo:hi], panel[:, lo:hi], LAST, preferred_element_type=F32
        )
        b = lax.dot_general(
            left[2 * rows : 4 * rows, lo:hi], panel[:, lo:hi], LAST, preferred_element_type=F32
        )
        total[q] = jnp.where(lane < 2 * rows, a, b)
    for j in range(16):
        rows12[j, 0:12] = total[0, 12 * j : 12 * j + 12]
        rows12[j, 12:24] = total[1, 12 * j : 12 * j + 12]
    out[...] = rows12[...].astype(BF)


def green(core, taus, eps_occ, eps_vir, mine, mate, up, down):
    rows, cols = mine.shape
    return pl.pallas_call(
        green_kernel,
        out_shape=jax.ShapeDtypeStruct((16, 24, 4 * rows), BF),
        in_specs=[SCALARS, SCALARS] + [WHOLE] * 6,
        out_specs=WHOLE,
        scratch_shapes=[
            pltpu.VMEM((4 * rows, cols), BF),
            pltpu.VMEM((4 * rows, cols), BF),
            pltpu.VMEM((2, 2 * rows, 4 * rows), F32),
            pltpu.VMEM((16, 24, 4 * rows), F32),
        ],
        compiler_params=pltpu.CompilerParams(vmem_limit_bytes=16 * 2**20),
        cost_estimate=pl.CostEstimate(
            flops=8 * rows * 4 * rows * cols, bytes_accessed=10 * rows * cols, transcendentals=4 * cols
        ),
        name="green",
    )(core, taus, eps_occ, eps_vir, mine, mate, up, down)


def product_kernel(parts, out, total):
    total[...] = parts[...].astype(F32).sum(axis=0)
    both = (total[0:12] * total[12:24]).astype(BF)
    for j in range(16):
        out[j] = both


def product(parts):
    return pl.pallas_call(
        product_kernel,
        out_shape=jax.ShapeDtypeStruct((16, 12, parts.shape[2]), BF),
        in_specs=[WHOLE],
        out_specs=WHOLE,
        scratch_shapes=[pltpu.VMEM(parts.shape[1:], F32)],
        compiler_params=pltpu.CompilerParams(vmem_limit_bytes=8 * 2**20),
        cost_estimate=pl.CostEstimate(
            flops=parts.size, bytes_accessed=4 * parts.size, transcendentals=0
        ),
        name="product",
    )(parts)


def on_device(phi_occ, phi_vir, eps_occ, eps_vir, taus, pair_mask, basis):
    core, xh = lax.axis_index("core"), lax.axis_index("xh")
    naux, rows = basis.shape[1], phi_occ.shape[0]
    first = core == 0
    mine = jnp.concatenate([phi_occ, phi_vir], axis=1)
    up = from_tile(mine, 2)
    down = from_tile(mine, -4)
    mate = lax.ppermute(mine, "core", SWAP)
    moves = [(z * 16 + o, (o // 2) * 16 + z * 2 + o % 2) for z in range(8) for o in range(16)]
    part = lax.ppermute(basis, ("z", "xl", "y"), moves)
    mask = jnp.pad(pair_mask.astype(BF), ((0, 0), (0, 120)))
    extra = jnp.concatenate([basis, jnp.broadcast_to(mask, (rows, 128))], axis=1)

    part_sums = green(
        core.reshape(1), taus, eps_occ[None], eps_vir[None], mine, mate, up, down
    )
    part_sums, extra, part = lax.optimization_barrier((part_sums, extra, part))
    sums = lax.all_to_all(part_sums, ORB, 0, 0, tiled=True)
    x_up = from_tile(extra, 2)
    x_down = from_tile(extra, -4)
    x_mate = lax.ppermute(extra, "core", SWAP)
    part = trade(part, "y", 4, 0)
    x_fourth = jnp.where(first, extra, x_down)

    def masks(slab):
        return slab[0, naux : naux + 8].astype(F32)

    m_own, m_mate, m_up, m_down = masks(extra), masks(x_mate), masks(x_up), masks(x_down)
    row_mask = jnp.stack(
        [m_own[5], m_own[0], jnp.where(first, m_mate[4], m_mate[6]), jnp.where(first, m_mate[3], m_mate[1])]
    )
    col_mask = jnp.stack(
        [m_up[2], m_down[7], jnp.where(first, m_up[3], m_up[1]), jnp.where(first, m_own[4], m_down[6])]
    )
    row_mask = jnp.repeat(row_mask, rows)
    col_mask = jnp.repeat(col_mask, rows)

    both = product(sums)
    both, part = lax.optimization_barrier((both, part))
    both = lax.all_to_all(both, ORB, 0, 0, tiled=True).reshape(2, rows, 4 * rows)
    part = trade(part, "y", 2, 1)
    by_row = (both.astype(F32) * row_mask).astype(BF)
    by_col = (both.astype(F32) * col_mask).astype(BF)

    def aux(slab):
        return slab[:, :naux]

    def rows_of(block, *panels):
        return jnp.einsum("trc,cq->trq", block, jnp.concatenate(panels), preferred_element_type=F32)

    def cols_of(block, panel):
        return jnp.einsum("trc,rq->tcq", block, panel, preferred_element_type=F32)

    r2, r3 = 2 * rows, 3 * rows
    to_up = cols_of(by_col[:, :, :rows], aux(extra)) + cols_of(by_col[:, :, r2:r3], aux(x_mate))
    last = cols_of(by_col[:, :, r3:], aux(x_mate))
    zero = jnp.zeros_like(last)
    to_down = cols_of(by_col[:, :, rows:r2], aux(extra)) + jnp.where(first, zero, last)
    to_mate = rows_of(by_row[:, :, r2:], aux(x_up), aux(x_fourth))
    own = rows_of(by_row[:, :, :r2], aux(x_up), aux(x_down)) + jnp.where(first, last, zero)
    to_up, part = lax.optimization_barrier((to_up.astype(BF), part))
    got_up = from_tile(to_up, -2)
    got_down = from_tile(to_down.astype(BF), 4)
    got_mate = lax.ppermute(to_mate, "core", SWAP)
    part = trade(part, "y", 1, 0)
    projected = (own + got_mate + got_up.astype(F32) + got_down.astype(F32)).astype(BF)

    projected, part = lax.optimization_barrier((projected, part))
    gathered = to_all(projected, "z", 8)
    part = trade(part, "xl", 1, 1)
    blocks = part.reshape(2, 8, rows, naux)
    at = xh * 2 + core

    def response(flip):
        j = at ^ flip
        chosen = lax.dynamic_slice(
            blocks, (j // 2, 0, 0, (j % 2) * (naux // 2)), (1, 8, rows, naux // 2)
        )[0]
        return jnp.einsum("zrp,ztrq->ptq", chosen, gathered, preferred_element_type=F32)

    both_way = lax.ppermute(
        response(3).astype(BF), ("xh", "core"), [(0, 3), (3, 0), (1, 2), (2, 1)]
    )
    across = lax.ppermute(response(2).astype(BF), "xh", SWAP)
    beside = lax.ppermute(response(1), "core", SWAP)
    return response(0) + beside + across.astype(F32) + both_way.astype(F32)


def solution(mesh):
    names = ("z", "xh", "core", "xl", "y")
    fine = Mesh(mesh.devices.reshape(8, 2, 2, 2, 8), names)
    placed = (P(PTS, ORB), P(PTS, ORB), P(ORB), P(ORB), P(), P(PTS, None), P(PTS, ORB))

    return jax.shard_map(
        on_device, mesh=fine, in_specs=placed, out_specs=P(PTS, None, ORB), check_vma=False
    )
```

time: 138 us -> 156 us (1.13)
  starting transfers between devices: 65.5 us -> 81.3 us
  waiting for transfers between devices: 44.6 us -> 51.8 us
  local copies, waits for them, and re-layouts: 12.2 us -> 8.05 us
  Pallas kernels: 0 us -> 3.05 us
  other arithmetic: 5.91 us -> 3.16 us
    ppermute x1 -> x5, starting transfers between devices: 2.47 us -> 18.3 us  [the longest x4 15.3 us: trade(): got = lax.ppermute(value, axis, [(i, i ^ bit) for i in range(size)])]
    all_to_all x3 -> x1, starting transfers between devices: 17 us -> 3.55 us  [to_all(): return lax.all_to_all(copies, axes, 0, 0, tiled=True)]
    all_to_all x1 -> x2, starting transfers between devices: 4.38 us -> 12.5 us  [the longest x1 7.62 us: on_device(): sums = lax.all_to_all(part_sums, ORB, 0, 0, tiled=True)]
    ppermute x1 -> x5, waiting for transfers between devices: 8.78 us -> 16.4 us  [the longest x4 16.4 us: trade(): got = lax.ppermute(value, axis, [(i, i ^ bit) for i in range(size)])]
    ppermute x4 -> x6, waiting for transfers between devices: 5.42 us -> 12.6 us  [from_tile(): return lax.ppermute(value, PTS, [((i + steps) % 32, i) for i in range(32)])]
    ppermute x4 -> x6, starting transfers between devices: 17.2 us -> 24 us  [from_tile(): return lax.ppermute(value, PTS, [((i + steps) % 32, i) for i in range(32)])]
    all_to_all x3 -> x1, waiting for transfers between devices: 17.5 us -> 12.2 us  [to_all(): return lax.all_to_all(copies, axes, 0, 0, tiled=True)]
    pallas_call x0 -> x2, Pallas kernels: none -> 3.05 us  [the longest x1 2.29 us: green(): pl.pallas_call(green_kernel, out_shape=jax.ShapeDtypeStruct((16, 24, 4 *...]
  transfers between devices with their start and end apart: 15 -> 20, of which waited for: 7 -> 10; matrix products, arithmetic and copies ran while one was open for 10% -> 5% of each run, Pallas kernels for 0% -> 1%
where the time goes in v3:
time: 156 us; the launch traced here: 155 us
  starting transfers between devices  81.3 us (52%)
  waiting for transfers between devices  51.8 us (33%)
  local copies, waits for them, and re-layouts  8.05 us (5%)
  between operations  5.71 us (4%)
  other arithmetic  3.16 us (2%)
  Pallas kernels  3.05 us (2%)
  matrix products  2.26 us (1%)
    ppermute x6, starting transfers between devices, from_tile(): return lax.ppermute(value, PTS, [((i + steps) % 32, i) for i in range(32)])  24 us
    ppermute x4, waiting for transfers between devices, trade(): got = lax.ppermute(value, axis, [(i, i ^ bit) for i in range(size)])  16.4 us
    ppermute x4, starting transfers between devices, trade(): got = lax.ppermute(value, axis, [(i, i ^ bit) for i in range(size)])  15.3 us
    ppermute x6, waiting for transfers between devices, from_tile(): return lax.ppermute(value, PTS, [((i + steps) % 32, i) for i in range(32)])  12.6 us
    all_to_all x1, waiting for transfers between devices, to_all(): return lax.all_to_all(copies, axes, 0, 0, tiled=True)  12.2 us
    ppermute x1, starting transfers between devices, on_device(): mate = lax.ppermute(mine, 'core', SWAP)  8.75 us
    all_to_all x1, starting transfers between devices, on_device(): sums = lax.all_to_all(part_sums, ORB, 0, 0, tiled=True)  7.62 us
    all_to_all x1, waiting for transfers between devices, on_device(): lax.all_to_all(both, ORB, 0, 0, tiled=True).reshape(2, rows, 4 * rows)  6.39 us
  transfers between devices with their start and end apart: 20, of which 10 were waited for; matrix products, arithmetic and copies ran while one was open for 5% of the time, Pallas kernels for 1%

profile of v3, /device:TPU:1, one launch (start us, length us, event | category | flops | bytes accessed | tf_op | source)
XLA Modules:
  0.0 155.3 jit_solution(12411571592243868152)
XLA Ops:
  1.7 8.7 %collective-permute-start = (bf16[96,1408]{1,0:T(8,128)(2,1)S(1)}, bf16[96,1408]{1,0:T(8,128)(2,1)S(1)}, u32[]{:S(2)}, u32[]{:S(2)}) collective-permute-start(bf16[96,1408]{1,0:T(8,128)(2,1)S(1)} %constant_dynamic-update-slice_fusion.mine), channel_id=1, source_target_pairs={{0,16},{16,0},{1,17},{17,1},{2,18},{18,2},{3,19},{19,3},{4,20},{20... | collective-permute-start | bytes 811016 | tf_op jit(solution)/shard_map/ppermute | solution.py:121
  10.5 7.8 %collective-permute-start.1 = (bf16[96,1408]{1,0:T(8,128)(2,1)S(1)}, bf16[96,1408]{1,0:T(8,128)(2,1)S(1)}, u32[]{:S(2)}, u32[]{:S(2)}) collective-permute-start(bf16[96,1408]{1,0:T(8,128)(2,1)S(1)} %constant_dynamic-update-slice_fusion.mine), channel_id=1, source_target_pairs={{32,0},{48,16},{64,32},{80,48},{96,64},{112,80},{128,96},{144,112}... | collective-permute-start | bytes 811016 | tf_op jit(solution)/shard_map/ppermute | solution.py:20
  21.6 2.4 %collective-permute-done.1.up = bf16[96,1408]{1,0:T(8,128)(2,1)S(1)} collective-permute-done((bf16[96,1408]{1,0:T(8,128)(2,1)S(1)}, bf16[96,1408]{1,0:T(8,128)(2,1)S(1)}, u32[]{:S(2)}, u32[]{:S(2)}) %collective-permute-start.1) | collective-permute-done | bytes 270368 | tf_op jit(solution)/shard_map/ppermute | solution.py:20
  24.1 6.1 %collective-permute-done.2.down = bf16[96,1408]{1,0:T(8,128)(2,1)S(1)} collective-permute-done((bf16[96,1408]{1,0:T(8,128)(2,1)S(1)}, bf16[96,1408]{1,0:T(8,128)(2,1)S(1)}, u32[]{:S(2)}, u32[]{:S(2)}) %collective-permute-start.2) | collective-permute-done | bytes 270368 | tf_op jit(solution)/shard_map/ppermute | solution.py:20
  35.1 3.1 %collective-permute-start.5 = (bf16[96,384]{1,0:T(8,128)(2,1)S(1)}, bf16[96,384]{1,0:T(8,128)(2,1)S(1)}, u32[]{:S(2)}, u32[]{:S(2)}) collective-permute-start(bf16[96,384]{1,0:T(8,128)(2,1)S(1)} %pad_maximum_fusion.6), channel_id=1, source_target_pairs={{0,16},{16,0},{1,17},{17,1},{2,18},{18,2},{3,19},{19,3},{4,20},{20... | collective-permute-start | bytes 221192 | tf_op jit(solution)/shard_map/ppermute | solution.py:134
  38.2 2.8 %collective-permute-start.7 = (bf16[96,384]{1,0:T(8,128)(2,1)S(1)}, bf16[96,384]{1,0:T(8,128)(2,1)S(1)}, u32[]{:S(2)}, u32[]{:S(2)}) collective-permute-start(bf16[96,384]{1,0:T(8,128)(2,1)S(1)} %pad_maximum_fusion.6), channel_id=1, source_target_pairs={{448,0},{464,16},{480,32},{496,48},{0,64},{16,80},{32,96},{48,112}... | collective-permute-start | bytes 221192 | tf_op jit(solution)/shard_map/ppermute | solution.py:20
  41.0 7.6 %all-to-all-start = ((bf16[16,24,384]{2,1,0:T(8,128)(2,1)}), bf16[16,24,384]{2,1,0:T(8,128)(2,1)S(1)}, u32[]{:S(2)}, u32[]{:S(2)}) async-start(bf16[16,24,384]{2,1,0:T(8,128)(2,1)} %green.1), calls=%async_computation | async-start | bytes 589824 | tf_op jit(solution)/shard_map/all_to_all | solution.py:131
  48.6 7.2 %collective-permute-start.4 = (bf16[96,256]{1,0:T(8,128)(2,1)S(1)}, bf16[96,256]{1,0:T(8,128)(2,1)S(1)}, u32[]{:S(2)}, u32[]{:S(2)}) collective-permute-start(bf16[96,256]{1,0:T(8,128)(2,1)S(1)} %collective-permute-done.3), channel_id=1, source_target_pairs={{0,4},{1,5},{2,6},{3,7},{4,0},{5,1},{6,2},{7,3},{8,12},{9,13},{10,... | collective-permute-start | bytes 147464 | tf_op jit(solution)/shard_map/ppermute | solution.py:25
  56.4 6.9 %collective-permute-done.4 = bf16[96,256]{1,0:T(8,128)(2,1)S(1)} collective-permute-done((bf16[96,256]{1,0:T(8,128)(2,1)S(1)}, bf16[96,256]{1,0:T(8,128)(2,1)S(1)}, u32[]{:S(2)}, u32[]{:S(2)}) %collective-permute-start.4) | collective-permute-done | bytes 49184 | tf_op jit(solution)/shard_map/ppermute | solution.py:25
  76.2 4.9 %all-to-all-start.1 = ((bf16[16,12,384]{2,1,0:T(8,128)(2,1)}), bf16[16,12,384]{2,1,0:T(8,128)(2,1)S(1)}, u32[]{:S(2)}, u32[]{:S(2)}) async-start(bf16[16,12,384]{2,1,0:T(8,128)(2,1)} %product.1), calls=%async_computation.1 | async-start | bytes 393216 | tf_op jit(solution)/shard_map/all_to_all | solution.py:153
  82.2 6.4 %all-to-all-done.1 = bf16[16,12,384]{2,1,0:T(8,128)(2,1)S(1)} async-done(((bf16[16,12,384]{2,1,0:T(8,128)(2,1)}), bf16[16,12,384]{2,1,0:T(8,128)(2,1)S(1)}, u32[]{:S(2)}, u32[]{:S(2)}) %all-to-all-start.1) | async-done | bytes 147488 | tf_op jit(solution)/shard_map/all_to_all | solution.py:153
  89.1 4.5 %collective-permute-start.8 = (f32[2,96,256]{2,1,0:T(8,128)S(1)}, f32[2,96,256]{2,1,0:T(8,128)S(1)}, u32[]{:S(2)}, u32[]{:S(2)}) collective-permute-start(f32[2,96,256]{2,1,0:T(8,128)S(1)} %fusion.21), channel_id=1, source_target_pairs={{0,16},{16,0},{1,17},{17,1},{2,18},{18,2},{3,19},{19,3},{4,20},{20... | collective-permute-start | bytes 589832 | tf_op jit(solution)/shard_map/ppermute | solution.py:177
  94.0 3.6 %collective-permute-start.12 = (bf16[2,2,96,256]{3,2,1,0:T(8,128)(2,1)S(1)}, bf16[2,2,96,256]{3,2,1,0:T(8,128)(2,1)S(1)}, u32[]{:S(2)}, u32[]{:S(2)}) collective-permute-start(bf16[2,2,96,256]{3,2,1,0:T(8,128)(2,1)S(1)} %pad_maximum_fusion.2), channel_id=1, source_target_pairs={{0,1},{1,0},{2,3},{3,2},{4,5},{5,4},{6,7},{7,6},{8,9},{9,8},{10,11... | collective-permute-start | bytes 589832 | tf_op jit(solution)/shard_map/ppermute | solution.py:25
  97.9 4.4 %collective-permute-start.11 = (bf16[2,96,256]{2,1,0:T(8,128)(2,1)S(1)}, bf16[2,96,256]{2,1,0:T(8,128)(2,1)S(1)}, u32[]{:S(2)}, u32[]{:S(2)}) collective-permute-start(bf16[2,96,256]{2,1,0:T(8,128)(2,1)S(1)} %add_convert_fusion), channel_id=1, source_target_pairs={{64,0},{80,16},{96,32},{112,48},{128,64},{144,80},{160,96},{176,11... | collective-permute-start | bytes 294920 | tf_op jit(solution)/shard_map/ppermute | solution.py:20
  102.3 5.1 %collective-permute-start.10 = (bf16[2,96,256]{2,1,0:T(8,128)(2,1)S(1)}, bf16[2,96,256]{2,1,0:T(8,128)(2,1)S(1)}, u32[]{:S(2)}, u32[]{:S(2)}) collective-permute-start(bf16[2,96,256]{2,1,0:T(8,128)(2,1)S(1)} %fusion.9), channel_id=1, source_target_pairs={{480,0},{496,16},{0,32},{16,48},{32,64},{48,80},{64,96},{80,112},{... | collective-permute-start | bytes 294920 | tf_op jit(solution)/shard_map/ppermute | solution.py:20
  107.6 4.0 %collective-permute-done.10 = bf16[2,96,256]{2,1,0:T(8,128)(2,1)S(1)} collective-permute-done((bf16[2,96,256]{2,1,0:T(8,128)(2,1)S(1)}, bf16[2,96,256]{2,1,0:T(8,128)(2,1)S(1)}, u32[]{:S(2)}, u32[]{:S(2)}) %collective-permute-start.10) | collective-permute-done | bytes 98336 | tf_op jit(solution)/shard_map/ppermute | solution.py:20
  112.8 3.5 %all-to-all-start.2 = ((bf16[8,2,96,256]{3,2,1,0:T(8,128)(2,1)}), bf16[8,2,96,256]{3,2,1,0:T(8,128)(2,1)S(1)}, u32[]{:S(2)}, u32[]{:S(2)}) async-start(bf16[8,2,96,256]{3,2,1,0:T(8,128)(2,1)} %broadcast_in_dim.35), calls=%async_computation.2 | async-start | bytes 1572864 | tf_op jit(solution)/shard_map/all_to_all | solution.py:32
  116.3 2.6 %collective-permute-start.13 = (bf16[2,2,2,96,256]{4,3,2,1,0:T(8,128)(2,1)S(1)}, bf16[2,2,2,96,256]{4,3,2,1,0:T(8,128)(2,1)S(1)}, u32[]{:S(2)}, u32[]{:S(2)}) collective-permute-start(bf16[2,2,2,96,256]{4,3,2,1,0:T(8,128)(2,1)S(1)} %pad_maximum_fusion.1), channel_id=1, source_target_pairs={{0,8},{8,0},{1,9},{9,1},{2,10},{10,2},{3,11},{11,3},{4,12},{12,4},... | collective-permute-start | bytes 1179656 | tf_op jit(solution)/shard_map/ppermute | solution.py:25
  119.1 8.4 %collective-permute-done.13 = bf16[2,2,2,96,256]{4,3,2,1,0:T(8,128)(2,1)S(1)} collective-permute-done((bf16[2,2,2,96,256]{4,3,2,1,0:T(8,128)(2,1)S(1)}, bf16[2,2,2,96,256]{4,3,2,1,0:T(8,128)(2,1)S(1)}, u32[]{:S(2)}, u32[]{:S(2)}) %collective-permute-start.13) | collective-permute-done | bytes 393248 | tf_op jit(solution)/shard_map/ppermute | solution.py:25
  127.6 12.2 %all-to-all-done.2 = bf16[8,2,96,256]{3,2,1,0:T(8,128)(2,1)S(1)} async-done(((bf16[8,2,96,256]{3,2,1,0:T(8,128)(2,1)}), bf16[8,2,96,256]{3,2,1,0:T(8,128)(2,1)S(1)}, u32[]{:S(2)}, u32[]{:S(2)}) %all-to-all-start.2) | async-done | bytes 786464 | tf_op jit(solution)/shard_map/all_to_all | solution.py:32
  140.1 2.4 %collective-permute-start.14 = (f32[128,2,256]{2,0,1:T(8,128)S(1)}, f32[128,2,256]{2,0,1:T(8,128)S(1)}, u32[]{:S(2)}, u32[]{:S(2)}) collective-permute-start(f32[128,2,256]{2,0,1:T(8,128)S(1)} %convolution_bitcast_fusion.2), channel_id=1, source_target_pairs={{0,16},{16,0},{1,17},{17,1},{2,18},{18,2},{3,19},{19,3},{4,20},{20... | collective-permute-start | bytes 786440 | tf_op jit(solution)/shard_map/ppermute | solution.py:198
  142.9 2.9 %collective-permute-start.16 = (bf16[128,2,256]{2,0,1:T(8,128)(2,1)S(1)}, bf16[128,2,256]{2,0,1:T(8,128)(2,1)S(1)}, u32[]{:S(2)}, u32[]{:S(2)}) collective-permute-start(bf16[128,2,256]{2,0,1:T(8,128)(2,1)S(1)} %fusion.7), channel_id=1, source_target_pairs={{0,48},{48,0},{16,32},{32,16},{1,49},{49,1},{17,33},{33,17},{2,50}... | collective-permute-start | bytes 393224 | tf_op jit(solution)/shard_map/ppermute | solution.py:194
  146.1 3.8 %collective-permute-start.15 = (bf16[128,2,256]{2,0,1:T(8,128)(2,1)S(1)}, bf16[128,2,256]{2,0,1:T(8,128)(2,1)S(1)}, u32[]{:S(2)}, u32[]{:S(2)}) collective-permute-start(bf16[128,2,256]{2,0,1:T(8,128)(2,1)S(1)} %fusion.6), channel_id=1, source_target_pairs={{0,32},{32,0},{1,33},{33,1},{2,34},{34,2},{3,35},{35,3},{4,36},{36... | collective-permute-start | bytes 393224 | tf_op jit(solution)/shard_map/ppermute | solution.py:197
  151.4 2.7 %collective-permute-done.15 = bf16[128,2,256]{2,0,1:T(8,128)(2,1)S(1)} collective-permute-done((bf16[128,2,256]{2,0,1:T(8,128)(2,1)S(1)}, bf16[128,2,256]{2,0,1:T(8,128)(2,1)S(1)}, u32[]{:S(2)}, u32[]{:S(2)}) %collective-permute-start.15) | collective-permute-done | bytes 131104 | tf_op jit(solution)/shard_map/ppermute | solution.py:197
  (75 shorter events, 25.5 us)
Async XLA Ops:
  0.7 19.5 %copy-start.2 = (bf16[96,256]{1,0:T(8,128)(2,1)S(1)}, bf16[96,256]{1,0:T(8,128)(2,1)}, u32[]{:S(2)}) copy-start(bf16[96,256]{1,0:T(8,128)(2,1)} %param.13) | copy-start | bytes 147460
  0.7 20.1 %copy-start.4 = (s32[1,8]{1,0:T(1,128)S(1)}, s32[1,8]{1,0:T(1,128)}, u32[]{:S(2)}) copy-start(s32[1,8]{1,0:T(1,128)} %param.12) | copy-start | bytes 100
  1.7 19.9 %collective-permute-start = (bf16[96,1408]{1,0:T(8,128)(2,1)S(1)}, bf16[96,1408]{1,0:T(8,128)(2,1)S(1)}, u32[]{:S(2)}, u32[]{:S(2)}) collective-permute-start(bf16[96,1408]{1,0:T(8,128)(2,1)S(1)} %constant_dynamic-update-slice_fusion.mine), channel_id=1, source_target_pairs={{0,16},{16,0},{1,17},{17,1},{2,18},{18,2},{3,19},{19,3},{4,20},{20... | collective-permute-start | bytes 811016 | tf_op jit(solution)/shard_map/ppermute | solution.py:121
  10.5 13.6 %collective-permute-start.1 = (bf16[96,1408]{1,0:T(8,128)(2,1)S(1)}, bf16[96,1408]{1,0:T(8,128)(2,1)S(1)}, u32[]{:S(2)}, u32[]{:S(2)}) collective-permute-start(bf16[96,1408]{1,0:T(8,128)(2,1)S(1)} %constant_dynamic-update-slice_fusion.mine), channel_id=1, source_target_pairs={{32,0},{48,16},{64,32},{80,48},{96,64},{112,80},{128,96},{144,112}... | collective-permute-start | bytes 811016 | tf_op jit(solution)/shard_map/ppermute | solution.py:20
  18.3 11.9 %collective-permute-start.2 = (bf16[96,1408]{1,0:T(8,128)(2,1)S(1)}, bf16[96,1408]{1,0:T(8,128)(2,1)S(1)}, u32[]{:S(2)}, u32[]{:S(2)}) collective-permute-start(bf16[96,1408]{1,0:T(8,128)(2,1)S(1)} %constant_dynamic-update-slice_fusion.mine), channel_id=1, source_target_pairs={{448,0},{464,16},{480,32},{496,48},{0,64},{16,80},{32,96},{48,112}... | collective-permute-start | bytes 811016 | tf_op jit(solution)/shard_map/ppermute | solution.py:20
  20.2 12.9 %collective-permute-start.3 = (bf16[96,256]{1,0:T(8,128)(2,1)S(1)}, bf16[96,256]{1,0:T(8,128)(2,1)S(1)}, u32[]{:S(2)}, u32[]{:S(2)}) collective-permute-start(bf16[96,256]{1,0:T(8,128)(2,1)S(1)} %copy-done.2), channel_id=1, source_target_pairs={{0,0},{1,1},{2,64},{3,65},{4,128},{5,129},{6,192},{7,193},{8,256},... | collective-permute-start | bytes 147464 | tf_op jit(solution)/shard_map/ppermute | solution.py:123
  20.9 0.7 copy-start.3
  30.2 0.7 copy-start.1
  33.2 36.9 %collective-permute-start.6 = (bf16[96,384]{1,0:T(8,128)(2,1)S(1)}, bf16[96,384]{1,0:T(8,128)(2,1)S(1)}, u32[]{:S(2)}, u32[]{:S(2)}) collective-permute-start(bf16[96,384]{1,0:T(8,128)(2,1)S(1)} %pad_maximum_fusion.6), channel_id=1, source_target_pairs={{32,0},{48,16},{64,32},{80,48},{96,64},{112,80},{128,96},{144,112}... | collective-permute-start | bytes 221192 | tf_op jit(solution)/shard_map/ppermute | solution.py:20
  35.1 28.3 %collective-permute-start.5 = (bf16[96,384]{1,0:T(8,128)(2,1)S(1)}, bf16[96,384]{1,0:T(8,128)(2,1)S(1)}, u32[]{:S(2)}, u32[]{:S(2)}) collective-permute-start(bf16[96,384]{1,0:T(8,128)(2,1)S(1)} %pad_maximum_fusion.6), channel_id=1, source_target_pairs={{0,16},{16,0},{1,17},{17,1},{2,18},{18,2},{3,19},{19,3},{4,20},{20... | collective-permute-start | bytes 221192 | tf_op jit(solution)/shard_map/ppermute | solution.py:134
  38.2 29.9 %collective-permute-start.7 = (bf16[96,384]{1,0:T(8,128)(2,1)S(1)}, bf16[96,384]{1,0:T(8,128)(2,1)S(1)}, u32[]{:S(2)}, u32[]{:S(2)}) collective-permute-start(bf16[96,384]{1,0:T(8,128)(2,1)S(1)} %pad_maximum_fusion.6), channel_id=1, source_target_pairs={{448,0},{464,16},{480,32},{496,48},{0,64},{16,80},{32,96},{48,112}... | collective-permute-start | bytes 221192 | tf_op jit(solution)/shard_map/ppermute | solution.py:20
  41.0 31.0 %all-to-all-start = ((bf16[16,24,384]{2,1,0:T(8,128)(2,1)}), bf16[16,24,384]{2,1,0:T(8,128)(2,1)S(1)}, u32[]{:S(2)}, u32[]{:S(2)}) async-start(bf16[16,24,384]{2,1,0:T(8,128)(2,1)} %green.1), calls=%async_computation | async-start | bytes 589824 | tf_op jit(solution)/shard_map/all_to_all | solution.py:131
  48.6 14.7 %collective-permute-start.4 = (bf16[96,256]{1,0:T(8,128)(2,1)S(1)}, bf16[96,256]{1,0:T(8,128)(2,1)S(1)}, u32[]{:S(2)}, u32[]{:S(2)}) collective-permute-start(bf16[96,256]{1,0:T(8,128)(2,1)S(1)} %collective-permute-done.3), channel_id=1, source_target_pairs={{0,4},{1,5},{2,6},{3,7},{4,0},{5,1},{6,2},{7,3},{8,12},{9,13},{10,... | collective-permute-start | bytes 147464 | tf_op jit(solution)/shard_map/ppermute | solution.py:25
  72.8 9.4 %collective-permute-start.9 = (bf16[2,96,256]{2,1,0:T(8,128)(2,1)S(1)}, bf16[2,96,256]{2,1,0:T(8,128)(2,1)S(1)}, u32[]{:S(2)}, u32[]{:S(2)}) collective-permute-start(bf16[2,96,256]{2,1,0:T(8,128)(2,1)S(1)} %pad_maximum_fusion.5), channel_id=1, source_target_pairs={{0,2},{1,3},{2,0},{3,1},{4,6},{5,7},{6,4},{7,5},{8,10},{9,11},{10,... | collective-permute-start | bytes 294920 | tf_op jit(solution)/shard_map/ppermute | solution.py:25
  76.2 12.4 %all-to-all-start.1 = ((bf16[16,12,384]{2,1,0:T(8,128)(2,1)}), bf16[16,12,384]{2,1,0:T(8,128)(2,1)S(1)}, u32[]{:S(2)}, u32[]{:S(2)}) async-start(bf16[16,12,384]{2,1,0:T(8,128)(2,1)} %product.1), calls=%async_computation.1 | async-start | bytes 393216 | tf_op jit(solution)/shard_map/all_to_all | solution.py:153
  89.1 22.6 %collective-permute-start.8 = (f32[2,96,256]{2,1,0:T(8,128)S(1)}, f32[2,96,256]{2,1,0:T(8,128)S(1)}, u32[]{:S(2)}, u32[]{:S(2)}) collective-permute-start(f32[2,96,256]{2,1,0:T(8,128)S(1)} %fusion.21), channel_id=1, source_target_pairs={{0,16},{16,0},{1,17},{17,1},{2,18},{18,2},{3,19},{19,3},{4,20},{20... | collective-permute-start | bytes 589832 | tf_op jit(solution)/shard_map/ppermute | solution.py:177
  94.0 13.5 %collective-permute-start.12 = (bf16[2,2,96,256]{3,2,1,0:T(8,128)(2,1)S(1)}, bf16[2,2,96,256]{3,2,1,0:T(8,128)(2,1)S(1)}, u32[]{:S(2)}, u32[]{:S(2)}) collective-permute-start(bf16[2,2,96,256]{3,2,1,0:T(8,128)(2,1)S(1)} %pad_maximum_fusion.2), channel_id=1, source_target_pairs={{0,1},{1,0},{2,3},{3,2},{4,5},{5,4},{6,7},{7,6},{8,9},{9,8},{10,11... | collective-permute-start | bytes 589832 | tf_op jit(solution)/shard_map/ppermute | solution.py:25
  97.9 9.7 %collective-permute-start.11 = (bf16[2,96,256]{2,1,0:T(8,128)(2,1)S(1)}, bf16[2,96,256]{2,1,0:T(8,128)(2,1)S(1)}, u32[]{:S(2)}, u32[]{:S(2)}) collective-permute-start(bf16[2,96,256]{2,1,0:T(8,128)(2,1)S(1)} %add_convert_fusion), channel_id=1, source_target_pairs={{64,0},{80,16},{96,32},{112,48},{128,64},{144,80},{160,96},{176,11... | collective-permute-start | bytes 294920 | tf_op jit(solution)/shard_map/ppermute | solution.py:20
  102.3 9.3 %collective-permute-start.10 = (bf16[2,96,256]{2,1,0:T(8,128)(2,1)S(1)}, bf16[2,96,256]{2,1,0:T(8,128)(2,1)S(1)}, u32[]{:S(2)}, u32[]{:S(2)}) collective-permute-start(bf16[2,96,256]{2,1,0:T(8,128)(2,1)S(1)} %fusion.9), channel_id=1, source_target_pairs={{480,0},{496,16},{0,32},{16,48},{32,64},{48,80},{64,96},{80,112},{... | collective-permute-start | bytes 294920 | tf_op jit(solution)/shard_map/ppermute | solution.py:20
  112.8 27.0 %all-to-all-start.2 = ((bf16[8,2,96,256]{3,2,1,0:T(8,128)(2,1)}), bf16[8,2,96,256]{3,2,1,0:T(8,128)(2,1)S(1)}, u32[]{:S(2)}, u32[]{:S(2)}) async-start(bf16[8,2,96,256]{3,2,1,0:T(8,128)(2,1)} %broadcast_in_dim.35), calls=%async_computation.2 | async-start | bytes 1572864 | tf_op jit(solution)/shard_map/all_to_all | solution.py:32
  116.3 11.1 %collective-permute-start.13 = (bf16[2,2,2,96,256]{4,3,2,1,0:T(8,128)(2,1)S(1)}, bf16[2,2,2,96,256]{4,3,2,1,0:T(8,128)(2,1)S(1)}, u32[]{:S(2)}, u32[]{:S(2)}) collective-permute-start(bf16[2,2,2,96,256]{4,3,2,1,0:T(8,128)(2,1)S(1)} %pad_maximum_fusion.1), channel_id=1, source_target_pairs={{0,8},{8,0},{1,9},{9,1},{2,10},{10,2},{3,11},{11,3},{4,12},{12,4},... | collective-permute-start | bytes 1179656 | tf_op jit(solution)/shard_map/ppermute | solution.py:25
  140.1 14.0 %collective-permute-start.14 = (f32[128,2,256]{2,0,1:T(8,128)S(1)}, f32[128,2,256]{2,0,1:T(8,128)S(1)}, u32[]{:S(2)}, u32[]{:S(2)}) collective-permute-start(f32[128,2,256]{2,0,1:T(8,128)S(1)} %convolution_bitcast_fusion.2), channel_id=1, source_target_pairs={{0,16},{16,0},{1,17},{17,1},{2,18},{18,2},{3,19},{19,3},{4,20},{20... | collective-permute-start | bytes 786440 | tf_op jit(solution)/shard_map/ppermute | solution.py:198
  142.9 8.5 %collective-permute-start.16 = (bf16[128,2,256]{2,0,1:T(8,128)(2,1)S(1)}, bf16[128,2,256]{2,0,1:T(8,128)(2,1)S(1)}, u32[]{:S(2)}, u32[]{:S(2)}) collective-permute-start(bf16[128,2,256]{2,0,1:T(8,128)(2,1)S(1)} %fusion.7), channel_id=1, source_target_pairs={{0,48},{48,0},{16,32},{32,16},{1,49},{49,1},{17,33},{33,17},{2,50}... | collective-permute-start | bytes 393224 | tf_op jit(solution)/shard_map/ppermute | solution.py:194
  146.1 8.0 %collective-permute-start.15 = (bf16[128,2,256]{2,0,1:T(8,128)(2,1)S(1)}, bf16[128,2,256]{2,0,1:T(8,128)(2,1)S(1)}, u32[]{:S(2)}, u32[]{:S(2)}) collective-permute-start(bf16[128,2,256]{2,0,1:T(8,128)(2,1)S(1)} %fusion.6), channel_id=1, source_target_pairs={{0,32},{32,0},{1,33},{33,1},{2,34},{34,2},{3,35},{35,3},{4,36},{36... | collective-permute-start | bytes 393224 | tf_op jit(solution)/shard_map/ppermute | solution.py:197
  (1 other events, 0.7 us)

commit v4 on v3

--- a/solution.py
+++ b/solution.py
@@ -20,9 +20,12 @@
     return lax.ppermute(value, PTS, [((i + steps) % 32, i) for i in range(32)])
 
 
-def trade(value, axis, bit, at):
+def trade(value, axis, bit):
     size = lax.axis_size(axis)
-    got = lax.ppermute(value, axis, [(i, i ^ bit) for i in range(size)])
+    return lax.ppermute(value, axis, [(i, i ^ bit) for i in range(size)])
+
+
+def join(value, got, axis, bit, at):
     upper = (lax.axis_index(axis) & bit) != 0
     return jnp.stack([jnp.where(upper, got, value), jnp.where(upper, value, got)], axis=at)
 
@@ -34,18 +37,18 @@
 
 def green_kernel(core, taus, eps_occ, eps_vir, mine, mate, up, down, out, panel, left, total, rows12):
     rows = mine.shape[0]
-    nocc, cols = eps_occ.shape[1], mine.shape[1]
-    panel[0:rows] = up[...]
-    panel[rows : 2 * rows] = down[...]
-    panel[2 * rows : 3 * rows] = up[...]
+    nocc, cols = eps_occ.shape[1], eps_occ.shape[1] + eps_vir.shape[1]
+    panel[0:rows] = up[:, :cols]
+    panel[rows : 2 * rows] = down[:, :cols]
+    panel[2 * rows : 3 * rows] = up[:, :cols]
 
     @pl.when(core[0] == 0)
     def _():
-        panel[3 * rows : 4 * rows] = mine[...]
+        panel[3 * rows : 4 * rows] = mine[:, :cols]
 
     @pl.when(core[0] != 0)
     def _():
-        panel[3 * rows : 4 * rows] = down[...]
+        panel[3 * rows : 4 * rows] = down[:, :cols]
 
     for t in range(2):
         for lo, hi, eps, sign in ((0, nocc, eps_occ, 1.0), (nocc, cols, eps_vir, -1.0)):
@@ -69,7 +72,7 @@
 
 
 def green(core, taus, eps_occ, eps_vir, mine, mate, up, down):
-    rows, cols = mine.shape
+    rows, cols = mine.shape[0], eps_occ.shape[1] + eps_vir.shape[1]
     return pl.pallas_call(
         green_kernel,
         out_shape=jax.ShapeDtypeStruct((16, 24, 4 * rows), BF),
@@ -115,24 +118,25 @@
     core, xh = lax.axis_index("core"), lax.axis_index("xh")
     naux, rows = basis.shape[1], phi_occ.shape[0]
     first = core == 0
-    mine = jnp.concatenate([phi_occ, phi_vir], axis=1)
+    mask = jnp.pad(pair_mask.astype(BF), ((0, 0), (0, 120)))
+    mine = jnp.concatenate(
+        [phi_occ, phi_vir, basis, jnp.broadcast_to(mask, (rows, 128))], axis=1
+    )
     up = from_tile(mine, 2)
     down = from_tile(mine, -4)
     mate = lax.ppermute(mine, "core", SWAP)
     moves = [(z * 16 + o, (o // 2) * 16 + z * 2 + o % 2) for z in range(8) for o in range(16)]
     part = lax.ppermute(basis, ("z", "xl", "y"), moves)
-    mask = jnp.pad(pair_mask.astype(BF), ((0, 0), (0, 120)))
-    extra = jnp.concatenate([basis, jnp.broadcast_to(mask, (rows, 128))], axis=1)
+    got = trade(part, "y", 4)
 
     part_sums = green(
         core.reshape(1), taus, eps_occ[None], eps_vir[None], mine, mate, up, down
     )
-    part_sums, extra, part = lax.optimization_barrier((part_sums, extra, part))
+    part_sums, part = lax.optimization_barrier((part_sums, part))
     sums = lax.all_to_all(part_sums, ORB, 0, 0, tiled=True)
-    x_up = from_tile(extra, 2)
-    x_down = from_tile(extra, -4)
-    x_mate = lax.ppermute(extra, "core", SWAP)
-    part = trade(part, "y", 4, 0)
+    part = join(part, got, "y", 4, 0)
+    got = trade(part, "y", 2)
+    extra, x_mate, x_up, x_down = (slab[:, -naux - 128 :] for slab in (mine, mate, up, down))
     x_fourth = jnp.where(first, extra, x_down)
 
     def masks(slab):
@@ -151,7 +155,8 @@
     both = product(sums)
     both, part = lax.optimization_barrier((both, part))
     both = lax.all_to_all(both, ORB, 0, 0, tiled=True).reshape(2, rows, 4 * rows)
-    part = trade(part, "y", 2, 1)
+    part = join(part, got, "y", 2, 1)
+    got = trade(part, "y", 1)
     by_row = (both.astype(F32) * row_mask).astype(BF)
     by_col = (both.astype(F32) * col_mask).astype(BF)
 
@@ -171,16 +176,16 @@
     to_down = cols_of(by_col[:, :, rows:r2], aux(extra)) + jnp.where(first, zero, last)
     to_mate = rows_of(by_row[:, :, r2:], aux(x_up), aux(x_fourth))
     own = rows_of(by_row[:, :, :r2], aux(x_up), aux(x_down)) + jnp.where(first, last, zero)
-    to_up, part = lax.optimization_barrier((to_up.astype(BF), part))
+    to_up = to_up.astype(BF)
     got_up = from_tile(to_up, -2)
     got_down = from_tile(to_down.astype(BF), 4)
     got_mate = lax.ppermute(to_mate, "core", SWAP)
-    part = trade(part, "y", 1, 0)
     projected = (own + got_mate + got_up.astype(F32) + got_down.astype(F32)).astype(BF)
 
     projected, part = lax.optimization_barrier((projected, part))
     gathered = to_all(projected, "z", 8)
-    part = trade(part, "xl", 1, 1)
+    part = join(part, got, "y", 1, 0)
+    part = join(part, trade(part, "xl", 1), "xl", 1, 1)
     blocks = part.reshape(2, 8, rows, naux)
     at = xh * 2 + core
 

time: 156 us -> 139 us (0.89)
  waiting for transfers between devices: 51.8 us -> 34.9 us
  local copies, waits for them, and re-layouts: 8.05 us -> 5.88 us
  other arithmetic: 3.16 us -> 4.83 us
    ppermute x5 -> x4, starting transfers between devices: 18.3 us -> 26.8 us  [trade(): return lax.ppermute(value, axis, [(i, i ^ bit) for i in range(size)])]
    all_to_all x1, waiting for transfers between devices: 12.2 us -> 5.5 us  [to_all(): return lax.all_to_all(copies, axes, 0, 0, tiled=True)]
    ppermute x1, starting transfers between devices: 8.75 us -> 2.86 us  [on_device(): mate = lax.ppermute(mine, 'core', SWAP)]
    ppermute x6 -> x4, waiting for transfers between devices: 12.6 us -> 7.59 us  [from_tile(): return lax.ppermute(value, PTS, [((i + steps) % 32, i) for i in range(32)])]
    ppermute x5 -> x4, waiting for transfers between devices: 16.4 us -> 12 us  [trade(): return lax.ppermute(value, axis, [(i, i ^ bit) for i in range(size)])]
    all_to_all x1, starting transfers between devices: 7.62 us -> 4.01 us  [on_device(): sums = lax.all_to_all(part_sums, ORB, 0, 0, tiled=True)]
    ppermute x6 -> x4, starting transfers between devices: 24 us -> 23.5 us  [from_tile(): return lax.ppermute(value, PTS, [((i + steps) % 32, i) for i in range(32)])]
  transfers between devices with their start and end apart: 20 -> 17, of which waited for: 10 -> 7; matrix products, arithmetic and copies ran while one was open for 5% -> 5% of each run, Pallas kernels for 1% -> 2%
where the time goes in v4:
time: 139 us; the launch traced here: 138 us
  starting transfers between devices  81.7 us (59%)
  waiting for transfers between devices  34.9 us (25%)
  local copies, waits for them, and re-layouts  5.88 us (4%)
  between operations  5.75 us (4%)
  other arithmetic  4.83 us (3%)
  Pallas kernels  3.02 us (2%)
  matrix products  2.26 us (2%)
    ppermute x4, starting transfers between devices, trade(): return lax.ppermute(value, axis, [(i, i ^ bit) for i in range(size)])  26.8 us
    ppermute x4, starting transfers between devices, from_tile(): return lax.ppermute(value, PTS, [((i + steps) % 32, i) for i in range(32)])  23.5 us
    ppermute x4, waiting for transfers between devices, trade(): return lax.ppermute(value, axis, [(i, i ^ bit) for i in range(size)])  12 us
    ppermute x4, waiting for transfers between devices, from_tile(): return lax.ppermute(value, PTS, [((i + steps) % 32, i) for i in range(32)])  7.59 us
    all_to_all x1, waiting for transfers between devices, on_device(): lax.all_to_all(both, ORB, 0, 0, tiled=True).reshape(2, rows, 4 * rows)  5.78 us
    ppermute x1, starting transfers between devices, on_device(): got_mate = lax.ppermute(to_mate, 'core', SWAP)  5.63 us
    all_to_all x1, starting transfers between devices, on_device(): lax.all_to_all(both, ORB, 0, 0, tiled=True).reshape(2, rows, 4 * rows)  5.58 us
    all_to_all x1, waiting for transfers between devices, to_all(): return lax.all_to_all(copies, axes, 0, 0, tiled=True)  5.5 us
  transfers between devices with their start and end apart: 17, of which 7 were waited for; matrix products, arithmetic and copies ran while one was open for 5% of the time, Pallas kernels for 2%

profile of v4, /device:TPU:1, one launch (start us, length us, event | category | flops | bytes accessed | tf_op | source)
XLA Modules:
  0.0 138.4 jit_solution(8288556253078104704)
XLA Ops:
  1.8 13.9 %collective-permute-start.3 = (bf16[96,1792]{1,0:T(8,128)(2,1)S(1)}, bf16[96,1792]{1,0:T(8,128)(2,1)S(1)}, u32[]{:S(2)}, u32[]{:S(2)}) collective-permute-start(bf16[96,1792]{1,0:T(8,128)(2,1)S(1)} %pad_maximum_fusion.2.mine), channel_id=1, source_target_pairs={{32,0},{48,16},{64,32},{80,48},{96,64},{112,80},{128,96},{144,112}... | collective-permute-start | bytes 1032200 | tf_op jit(solution)/shard_map/ppermute | solution.py:20
  15.7 2.9 %collective-permute-start.2 = (bf16[96,1792]{1,0:T(8,128)(2,1)S(1)}, bf16[96,1792]{1,0:T(8,128)(2,1)S(1)}, u32[]{:S(2)}, u32[]{:S(2)}) collective-permute-start(bf16[96,1792]{1,0:T(8,128)(2,1)S(1)} %pad_maximum_fusion.2.mine), channel_id=1, source_target_pairs={{0,16},{16,0},{1,17},{17,1},{2,18},{18,2},{3,19},{19,3},{4,20},{20... | collective-permute-start | bytes 1032200 | tf_op jit(solution)/shard_map/ppermute | solution.py:127
  18.6 1.9 %collective-permute-start.4 = (bf16[96,1792]{1,0:T(8,128)(2,1)S(1)}, bf16[96,1792]{1,0:T(8,128)(2,1)S(1)}, u32[]{:S(2)}, u32[]{:S(2)}) collective-permute-start(bf16[96,1792]{1,0:T(8,128)(2,1)S(1)} %pad_maximum_fusion.2.mine), channel_id=1, source_target_pairs={{448,0},{464,16},{480,32},{496,48},{0,64},{16,80},{32,96},{48,112}... | collective-permute-start | bytes 1032200 | tf_op jit(solution)/shard_map/ppermute | solution.py:20
  21.9 17.0 %collective-permute-start.1 = (bf16[96,256]{1,0:T(8,128)(2,1)S(1)}, bf16[96,256]{1,0:T(8,128)(2,1)S(1)}, u32[]{:S(2)}, u32[]{:S(2)}) collective-permute-start(bf16[96,256]{1,0:T(8,128)(2,1)S(1)} %collective-permute-done), channel_id=1, source_target_pairs={{0,4},{1,5},{2,6},{3,7},{4,0},{5,1},{6,2},{7,3},{8,12},{9,13},{10,... | collective-permute-start | bytes 147464 | tf_op jit(solution)/shard_map/ppermute | solution.py:25
  39.7 2.3 %green.1 = bf16[16,24,384]{2,1,0:T(8,128)(2,1)} custom-call(s32[1]{0:T(128)} %bitcast.core, f32[2]{0:T(128)S(1)} %copy-done.1, f32[1,128]{1,0:T(1,128)S(1)} %bitcast.114, f32[1,1280]{1,0:T(1,128)S(1)} %broadcast_in_dim.29.eps_vir, bf16[96,1792]{1,0:T(8,128)(2,1)S(1)} %pad_maximum_fusion.2.mine, bf16[96,1792]{1,0:T(8,128)(2,1)S(1)} %collective-permute-done.2.mate, ...), custom_call_target="tpu_custom_call" | custom-call | flops 415236096 | bytes 1351680 | tf_op jit(solution)/shard_map/green/pallas_call | solution.py:76
  41.9 4.0 %all-to-all-start = ((bf16[16,24,384]{2,1,0:T(8,128)(2,1)}), bf16[16,24,384]{2,1,0:T(8,128)(2,1)S(1)}, u32[]{:S(2)}, u32[]{:S(2)}) async-start(bf16[16,24,384]{2,1,0:T(8,128)(2,1)} %green.1), calls=%async_computation | async-start | bytes 589824 | tf_op jit(solution)/shard_map/all_to_all | solution.py:136
  46.7 4.2 %collective-permute-start.5 = (bf16[2,96,256]{2,1,0:T(8,128)(2,1)S(1)}, bf16[2,96,256]{2,1,0:T(8,128)(2,1)S(1)}, u32[]{:S(2)}, u32[]{:S(2)}) collective-permute-start(bf16[2,96,256]{2,1,0:T(8,128)(2,1)S(1)} %pad_maximum_fusion.6), channel_id=1, source_target_pairs={{0,2},{1,3},{2,0},{3,1},{4,6},{5,7},{6,4},{7,5},{8,10},{9,11},{10,... | collective-permute-start | bytes 294920 | tf_op jit(solution)/shard_map/ppermute | solution.py:25
  59.5 5.6 %all-to-all-start.1 = ((bf16[16,12,384]{2,1,0:T(8,128)(2,1)}), bf16[16,12,384]{2,1,0:T(8,128)(2,1)S(1)}, u32[]{:S(2)}, u32[]{:S(2)}) async-start(bf16[16,12,384]{2,1,0:T(8,128)(2,1)} %product.1), calls=%async_computation.1 | async-start | bytes 393216 | tf_op jit(solution)/shard_map/all_to_all | solution.py:157
  66.8 5.8 %all-to-all-done.1 = bf16[16,12,384]{2,1,0:T(8,128)(2,1)S(1)} async-done(((bf16[16,12,384]{2,1,0:T(8,128)(2,1)}), bf16[16,12,384]{2,1,0:T(8,128)(2,1)S(1)}, u32[]{:S(2)}, u32[]{:S(2)}) %all-to-all-start.1) | async-done | bytes 147488 | tf_op jit(solution)/shard_map/all_to_all | solution.py:157
  73.1 5.6 %collective-permute-start.7 = (f32[2,96,256]{2,1,0:T(8,128)S(1)}, f32[2,96,256]{2,1,0:T(8,128)S(1)}, u32[]{:S(2)}, u32[]{:S(2)}) collective-permute-start(f32[2,96,256]{2,1,0:T(8,128)S(1)} %fusion.21), channel_id=1, source_target_pairs={{0,16},{16,0},{1,17},{17,1},{2,18},{18,2},{3,19},{19,3},{4,20},{20... | collective-permute-start | bytes 589832 | tf_op jit(solution)/shard_map/ppermute | solution.py:182
  79.3 5.8 %collective-permute-start.9 = (bf16[2,96,256]{2,1,0:T(8,128)(2,1)S(1)}, bf16[2,96,256]{2,1,0:T(8,128)(2,1)S(1)}, u32[]{:S(2)}, u32[]{:S(2)}) collective-permute-start(bf16[2,96,256]{2,1,0:T(8,128)(2,1)S(1)} %add_convert_fusion), channel_id=1, source_target_pairs={{64,0},{80,16},{96,32},{112,48},{128,64},{144,80},{160,96},{176,11... | collective-permute-start | bytes 294920 | tf_op jit(solution)/shard_map/ppermute | solution.py:20
  85.2 1.9 %collective-permute-start.8 = (bf16[2,96,256]{2,1,0:T(8,128)(2,1)S(1)}, bf16[2,96,256]{2,1,0:T(8,128)(2,1)S(1)}, u32[]{:S(2)}, u32[]{:S(2)}) collective-permute-start(bf16[2,96,256]{2,1,0:T(8,128)(2,1)S(1)} %fusion.9), channel_id=1, source_target_pairs={{480,0},{496,16},{0,32},{16,48},{32,64},{48,80},{64,96},{80,112},{... | collective-permute-start | bytes 294920 | tf_op jit(solution)/shard_map/ppermute | solution.py:20
  87.2 7.6 %collective-permute-done.8 = bf16[2,96,256]{2,1,0:T(8,128)(2,1)S(1)} collective-permute-done((bf16[2,96,256]{2,1,0:T(8,128)(2,1)S(1)}, bf16[2,96,256]{2,1,0:T(8,128)(2,1)S(1)}, u32[]{:S(2)}, u32[]{:S(2)}) %collective-permute-start.8) | collective-permute-done | bytes 98336 | tf_op jit(solution)/shard_map/ppermute | solution.py:20
  96.0 3.5 %all-to-all-start.2 = ((bf16[8,2,96,256]{3,2,1,0:T(8,128)(2,1)}), bf16[8,2,96,256]{3,2,1,0:T(8,128)(2,1)S(1)}, u32[]{:S(2)}, u32[]{:S(2)}) async-start(bf16[8,2,96,256]{3,2,1,0:T(8,128)(2,1)} %broadcast_in_dim.35), calls=%async_computation.2 | async-start | bytes 1572864 | tf_op jit(solution)/shard_map/all_to_all | solution.py:35
  99.5 3.0 %collective-permute-start.6 = (bf16[2,2,96,256]{3,2,1,0:T(8,128)(2,1)S(1)}, bf16[2,2,96,256]{3,2,1,0:T(8,128)(2,1)S(1)}, u32[]{:S(2)}, u32[]{:S(2)}) collective-permute-start(bf16[2,2,96,256]{3,2,1,0:T(8,128)(2,1)S(1)} %pad_maximum_fusion.3), channel_id=1, source_target_pairs={{0,1},{1,0},{2,3},{3,2},{4,5},{5,4},{6,7},{7,6},{8,9},{9,8},{10,11... | collective-permute-start | bytes 589832 | tf_op jit(solution)/shard_map/ppermute | solution.py:25
  102.5 4.2 %collective-permute-done.6 = bf16[2,2,96,256]{3,2,1,0:T(8,128)(2,1)S(1)} collective-permute-done((bf16[2,2,96,256]{3,2,1,0:T(8,128)(2,1)S(1)}, bf16[2,2,96,256]{3,2,1,0:T(8,128)(2,1)S(1)}, u32[]{:S(2)}, u32[]{:S(2)}) %collective-permute-start.6) | collective-permute-done | bytes 196640 | tf_op jit(solution)/shard_map/ppermute | solution.py:25
  106.8 2.7 %collective-permute-start.10 = (bf16[2,2,2,96,256]{4,3,2,1,0:T(8,128)(2,1)S(1)}, bf16[2,2,2,96,256]{4,3,2,1,0:T(8,128)(2,1)S(1)}, u32[]{:S(2)}, u32[]{:S(2)}) collective-permute-start(bf16[2,2,2,96,256]{4,3,2,1,0:T(8,128)(2,1)S(1)} %pad_maximum_fusion.1), channel_id=1, source_target_pairs={{0,8},{8,0},{1,9},{9,1},{2,10},{10,2},{3,11},{11,3},{4,12},{12,4},... | collective-permute-start | bytes 1179656 | tf_op jit(solution)/shard_map/ppermute | solution.py:25
  109.6 7.8 %collective-permute-done.10 = bf16[2,2,2,96,256]{4,3,2,1,0:T(8,128)(2,1)S(1)} collective-permute-done((bf16[2,2,2,96,256]{4,3,2,1,0:T(8,128)(2,1)S(1)}, bf16[2,2,2,96,256]{4,3,2,1,0:T(8,128)(2,1)S(1)}, u32[]{:S(2)}, u32[]{:S(2)}) %collective-permute-start.10) | collective-permute-done | bytes 393248 | tf_op jit(solution)/shard_map/ppermute | solution.py:25
  117.5 5.5 %all-to-all-done.2 = bf16[8,2,96,256]{3,2,1,0:T(8,128)(2,1)S(1)} async-done(((bf16[8,2,96,256]{3,2,1,0:T(8,128)(2,1)}), bf16[8,2,96,256]{3,2,1,0:T(8,128)(2,1)S(1)}, u32[]{:S(2)}, u32[]{:S(2)}) %all-to-all-start.2) | async-done | bytes 786464 | tf_op jit(solution)/shard_map/all_to_all | solution.py:35
  123.3 2.4 %collective-permute-start.11 = (f32[128,2,256]{2,0,1:T(8,128)S(1)}, f32[128,2,256]{2,0,1:T(8,128)S(1)}, u32[]{:S(2)}, u32[]{:S(2)}) collective-permute-start(f32[128,2,256]{2,0,1:T(8,128)S(1)} %convolution_bitcast_fusion.2), channel_id=1, source_target_pairs={{0,16},{16,0},{1,17},{17,1},{2,18},{18,2},{3,19},{19,3},{4,20},{20... | collective-permute-start | bytes 786440 | tf_op jit(solution)/shard_map/ppermute | solution.py:203
  126.0 1.9 %collective-permute-start.13 = (bf16[128,2,256]{2,0,1:T(8,128)(2,1)S(1)}, bf16[128,2,256]{2,0,1:T(8,128)(2,1)S(1)}, u32[]{:S(2)}, u32[]{:S(2)}) collective-permute-start(bf16[128,2,256]{2,0,1:T(8,128)(2,1)S(1)} %fusion.7), channel_id=1, source_target_pairs={{0,48},{48,0},{16,32},{32,16},{1,49},{49,1},{17,33},{33,17},{2,50}... | collective-permute-start | bytes 393224 | tf_op jit(solution)/shard_map/ppermute | solution.py:199
  128.3 4.8 %collective-permute-start.12 = (bf16[128,2,256]{2,0,1:T(8,128)(2,1)S(1)}, bf16[128,2,256]{2,0,1:T(8,128)(2,1)S(1)}, u32[]{:S(2)}, u32[]{:S(2)}) collective-permute-start(bf16[128,2,256]{2,0,1:T(8,128)(2,1)S(1)} %fusion.6), channel_id=1, source_target_pairs={{0,32},{32,0},{1,33},{33,1},{2,34},{34,2},{3,35},{35,3},{4,36},{36... | collective-permute-start | bytes 393224 | tf_op jit(solution)/shard_map/ppermute | solution.py:202
  133.1 1.9 %collective-permute-done.13 = bf16[128,2,256]{2,0,1:T(8,128)(2,1)S(1)} collective-permute-done((bf16[128,2,256]{2,0,1:T(8,128)(2,1)S(1)}, bf16[128,2,256]{2,0,1:T(8,128)(2,1)S(1)}, u32[]{:S(2)}, u32[]{:S(2)}) %collective-permute-start.13) | collective-permute-done | bytes 131104 | tf_op jit(solution)/shard_map/ppermute | solution.py:199
  135.0 2.2 %collective-permute-done.12 = bf16[128,2,256]{2,0,1:T(8,128)(2,1)S(1)} collective-permute-done((bf16[128,2,256]{2,0,1:T(8,128)(2,1)S(1)}, bf16[128,2,256]{2,0,1:T(8,128)(2,1)S(1)}, u32[]{:S(2)}, u32[]{:S(2)}) %collective-permute-start.12) | collective-permute-done | bytes 131104 | tf_op jit(solution)/shard_map/ppermute | solution.py:202
  (71 shorter events, 14.4 us)
Async XLA Ops:
  0.0 0.8 copy-start.4
  0.8 19.8 %copy-start.3 = (bf16[96,256]{1,0:T(8,128)(2,1)S(1)}, bf16[96,256]{1,0:T(8,128)(2,1)}, u32[]{:S(2)}) copy-start(bf16[96,256]{1,0:T(8,128)(2,1)} %param.13) | copy-start | bytes 147460
  1.8 20.1 %copy-start.5 = (f32[1280]{0:T(1024)S(1)}, f32[1280]{0:T(1024)}, u32[]{:S(2)}) copy-start(f32[1280]{0:T(1024)} %param.10) | copy-start | bytes 15364
  1.8 37.1 %collective-permute-start.3 = (bf16[96,1792]{1,0:T(8,128)(2,1)S(1)}, bf16[96,1792]{1,0:T(8,128)(2,1)S(1)}, u32[]{:S(2)}, u32[]{:S(2)}) collective-permute-start(bf16[96,1792]{1,0:T(8,128)(2,1)S(1)} %pad_maximum_fusion.2.mine), channel_id=1, source_target_pairs={{32,0},{48,16},{64,32},{80,48},{96,64},{112,80},{128,96},{144,112}... | collective-permute-start | bytes 1032200 | tf_op jit(solution)/shard_map/ppermute | solution.py:20
  15.7 23.2 %collective-permute-start.2 = (bf16[96,1792]{1,0:T(8,128)(2,1)S(1)}, bf16[96,1792]{1,0:T(8,128)(2,1)S(1)}, u32[]{:S(2)}, u32[]{:S(2)}) collective-permute-start(bf16[96,1792]{1,0:T(8,128)(2,1)S(1)} %pad_maximum_fusion.2.mine), channel_id=1, source_target_pairs={{0,16},{16,0},{1,17},{17,1},{2,18},{18,2},{3,19},{19,3},{4,20},{20... | collective-permute-start | bytes 1032200 | tf_op jit(solution)/shard_map/ppermute | solution.py:127
  18.6 20.3 %collective-permute-start.4 = (bf16[96,1792]{1,0:T(8,128)(2,1)S(1)}, bf16[96,1792]{1,0:T(8,128)(2,1)S(1)}, u32[]{:S(2)}, u32[]{:S(2)}) collective-permute-start(bf16[96,1792]{1,0:T(8,128)(2,1)S(1)} %pad_maximum_fusion.2.mine), channel_id=1, source_target_pairs={{448,0},{464,16},{480,32},{496,48},{0,64},{16,80},{32,96},{48,112}... | collective-permute-start | bytes 1032200 | tf_op jit(solution)/shard_map/ppermute | solution.py:20
  20.5 1.4 collective-permute-start
  21.9 24.7 %collective-permute-start.1 = (bf16[96,256]{1,0:T(8,128)(2,1)S(1)}, bf16[96,256]{1,0:T(8,128)(2,1)S(1)}, u32[]{:S(2)}, u32[]{:S(2)}) collective-permute-start(bf16[96,256]{1,0:T(8,128)(2,1)S(1)} %collective-permute-done), channel_id=1, source_target_pairs={{0,4},{1,5},{2,6},{3,7},{4,0},{5,1},{6,2},{7,3},{8,12},{9,13},{10,... | collective-permute-start | bytes 147464 | tf_op jit(solution)/shard_map/ppermute | solution.py:25
  38.9 27.9 %copy-start = (bf16[96,1792]{1,0:T(8,128)(2,1)}, bf16[96,1792]{1,0:T(8,128)(2,1)S(1)}, u32[]{:S(2)}) copy-start(bf16[96,1792]{1,0:T(8,128)(2,1)S(1)} %collective-permute-done.4.down) | copy-start | bytes 1032196
  38.9 0.7 copy-start.1
  38.9 0.7 copy-start.2
  41.9 16.8 %all-to-all-start = ((bf16[16,24,384]{2,1,0:T(8,128)(2,1)}), bf16[16,24,384]{2,1,0:T(8,128)(2,1)S(1)}, u32[]{:S(2)}, u32[]{:S(2)}) async-start(bf16[16,24,384]{2,1,0:T(8,128)(2,1)} %green.1), calls=%async_computation | async-start | bytes 589824 | tf_op jit(solution)/shard_map/all_to_all | solution.py:136
  46.7 20.1 %collective-permute-start.5 = (bf16[2,96,256]{2,1,0:T(8,128)(2,1)S(1)}, bf16[2,96,256]{2,1,0:T(8,128)(2,1)S(1)}, u32[]{:S(2)}, u32[]{:S(2)}) collective-permute-start(bf16[2,96,256]{2,1,0:T(8,128)(2,1)S(1)} %pad_maximum_fusion.6), channel_id=1, source_target_pairs={{0,2},{1,3},{2,0},{3,1},{4,6},{5,7},{6,4},{7,5},{8,10},{9,11},{10,... | collective-permute-start | bytes 294920 | tf_op jit(solution)/shard_map/ppermute | solution.py:25
  59.5 13.1 %all-to-all-start.1 = ((bf16[16,12,384]{2,1,0:T(8,128)(2,1)}), bf16[16,12,384]{2,1,0:T(8,128)(2,1)S(1)}, u32[]{:S(2)}, u32[]{:S(2)}) async-start(bf16[16,12,384]{2,1,0:T(8,128)(2,1)} %product.1), calls=%async_computation.1 | async-start | bytes 393216 | tf_op jit(solution)/shard_map/all_to_all | solution.py:157
  73.1 21.7 %collective-permute-start.7 = (f32[2,96,256]{2,1,0:T(8,128)S(1)}, f32[2,96,256]{2,1,0:T(8,128)S(1)}, u32[]{:S(2)}, u32[]{:S(2)}) collective-permute-start(f32[2,96,256]{2,1,0:T(8,128)S(1)} %fusion.21), channel_id=1, source_target_pairs={{0,16},{16,0},{1,17},{17,1},{2,18},{18,2},{3,19},{19,3},{4,20},{20... | collective-permute-start | bytes 589832 | tf_op jit(solution)/shard_map/ppermute | solution.py:182
  79.3 7.9 %collective-permute-start.9 = (bf16[2,96,256]{2,1,0:T(8,128)(2,1)S(1)}, bf16[2,96,256]{2,1,0:T(8,128)(2,1)S(1)}, u32[]{:S(2)}, u32[]{:S(2)}) collective-permute-start(bf16[2,96,256]{2,1,0:T(8,128)(2,1)S(1)} %add_convert_fusion), channel_id=1, source_target_pairs={{64,0},{80,16},{96,32},{112,48},{128,64},{144,80},{160,96},{176,11... | collective-permute-start | bytes 294920 | tf_op jit(solution)/shard_map/ppermute | solution.py:20
  85.2 9.6 %collective-permute-start.8 = (bf16[2,96,256]{2,1,0:T(8,128)(2,1)S(1)}, bf16[2,96,256]{2,1,0:T(8,128)(2,1)S(1)}, u32[]{:S(2)}, u32[]{:S(2)}) collective-permute-start(bf16[2,96,256]{2,1,0:T(8,128)(2,1)S(1)} %fusion.9), channel_id=1, source_target_pairs={{480,0},{496,16},{0,32},{16,48},{32,64},{48,80},{64,96},{80,112},{... | collective-permute-start | bytes 294920 | tf_op jit(solution)/shard_map/ppermute | solution.py:20
  87.1 7.6 %slice-start = ((bf16[96,1792]{1,0:T(8,128)(2,1)}), bf16[96,256]{1,0:T(8,128)(2,1)S(1)}, s32[]{:S(2)}) async-start(bf16[96,1792]{1,0:T(8,128)(2,1)} %copy-done), calls=%async_computation.3 | async-start | bytes 98304 | tf_op jit(solution)/shard_map/slice | solution.py:164
  96.0 27.0 %all-to-all-start.2 = ((bf16[8,2,96,256]{3,2,1,0:T(8,128)(2,1)}), bf16[8,2,96,256]{3,2,1,0:T(8,128)(2,1)S(1)}, u32[]{:S(2)}, u32[]{:S(2)}) async-start(bf16[8,2,96,256]{3,2,1,0:T(8,128)(2,1)} %broadcast_in_dim.35), calls=%async_computation.2 | async-start | bytes 1572864 | tf_op jit(solution)/shard_map/all_to_all | solution.py:35
  99.5 7.2 %collective-permute-start.6 = (bf16[2,2,96,256]{3,2,1,0:T(8,128)(2,1)S(1)}, bf16[2,2,96,256]{3,2,1,0:T(8,128)(2,1)S(1)}, u32[]{:S(2)}, u32[]{:S(2)}) collective-permute-start(bf16[2,2,96,256]{3,2,1,0:T(8,128)(2,1)S(1)} %pad_maximum_fusion.3), channel_id=1, source_target_pairs={{0,1},{1,0},{2,3},{3,2},{4,5},{5,4},{6,7},{7,6},{8,9},{9,8},{10,11... | collective-permute-start | bytes 589832 | tf_op jit(solution)/shard_map/ppermute | solution.py:25
  106.8 10.6 %collective-permute-start.10 = (bf16[2,2,2,96,256]{4,3,2,1,0:T(8,128)(2,1)S(1)}, bf16[2,2,2,96,256]{4,3,2,1,0:T(8,128)(2,1)S(1)}, u32[]{:S(2)}, u32[]{:S(2)}) collective-permute-start(bf16[2,2,2,96,256]{4,3,2,1,0:T(8,128)(2,1)S(1)} %pad_maximum_fusion.1), channel_id=1, source_target_pairs={{0,8},{8,0},{1,9},{9,1},{2,10},{10,2},{3,11},{11,3},{4,12},{12,4},... | collective-permute-start | bytes 1179656 | tf_op jit(solution)/shard_map/ppermute | solution.py:25
  123.3 13.9 %collective-permute-start.11 = (f32[128,2,256]{2,0,1:T(8,128)S(1)}, f32[128,2,256]{2,0,1:T(8,128)S(1)}, u32[]{:S(2)}, u32[]{:S(2)}) collective-permute-start(f32[128,2,256]{2,0,1:T(8,128)S(1)} %convolution_bitcast_fusion.2), channel_id=1, source_target_pairs={{0,16},{16,0},{1,17},{17,1},{2,18},{18,2},{3,19},{19,3},{4,20},{20... | collective-permute-start | bytes 786440 | tf_op jit(solution)/shard_map/ppermute | solution.py:203
  126.0 9.0 %collective-permute-start.13 = (bf16[128,2,256]{2,0,1:T(8,128)(2,1)S(1)}, bf16[128,2,256]{2,0,1:T(8,128)(2,1)S(1)}, u32[]{:S(2)}, u32[]{:S(2)}) collective-permute-start(bf16[128,2,256]{2,0,1:T(8,128)(2,1)S(1)} %fusion.7), channel_id=1, source_target_pairs={{0,48},{48,0},{16,32},{32,16},{1,49},{49,1},{17,33},{33,17},{2,50}... | collective-permute-start | bytes 393224 | tf_op jit(solution)/shard_map/ppermute | solution.py:199
  128.3 8.9 %collective-permute-start.12 = (bf16[128,2,256]{2,0,1:T(8,128)(2,1)S(1)}, bf16[128,2,256]{2,0,1:T(8,128)(2,1)S(1)}, u32[]{:S(2)}, u32[]{:S(2)}) collective-permute-start(bf16[128,2,256]{2,0,1:T(8,128)(2,1)S(1)} %fusion.6), channel_id=1, source_target_pairs={{0,32},{32,0},{1,33},{33,1},{2,34},{34,2},{3,35},{35,3},{4,36},{36... | collective-permute-start | bytes 393224 | tf_op jit(solution)/shard_map/ppermute | solution.py:202

commit v5 on v4

--- a/solution.py
+++ b/solution.py
@@ -12,6 +12,7 @@
 F32 = jnp.float32
 SWAP = [(0, 1), (1, 0)]
 LAST = (((1,), (1,)), ((), ()))
+FIRST = (((0,), (0,)), ((), ()))
 WHOLE = pl.BlockSpec(memory_space=pltpu.VMEM)
 SCALARS = pl.BlockSpec(memory_space=pltpu.SMEM)
 
@@ -28,11 +29,6 @@
 def join(value, got, axis, bit, at):
     upper = (lax.axis_index(axis) & bit) != 0
     return jnp.stack([jnp.where(upper, got, value), jnp.where(upper, value, got)], axis=at)
-
-
-def to_all(value, axes, count):
-    copies = jnp.broadcast_to(value[None], (count,) + value.shape)
-    return lax.all_to_all(copies, axes, 0, 0, tiled=True)
 
 
 def green_kernel(core, taus, eps_occ, eps_vir, mine, mate, up, down, out, panel, left, total, rows12):
@@ -114,10 +110,111 @@
     )(parts)
 
 
+def project_kernel(core, parts, mine, mate, up, down, to_up, to_down, to_mate, own, chi, panel):
+    rows, naux = own.shape[1], own.shape[2]
+    lo = mine.shape[1] - naux - 128
+    mid = lo + naux
+    first = core[0] == 0
+    for j in range(16):
+        chi[12 * j : 12 * j + 12] = parts[j].astype(F32)
+    lane = lax.broadcasted_iota(jnp.int32, (1, 128), 1)
+    wide = lax.broadcasted_iota(jnp.int32, (1, 4 * rows), 1)
+    weight = jnp.where(first, 1.0, 0.0).astype(F32)
+
+    def pick(slab, slot):
+        row = slab[0:8, mid : mid + 128].astype(F32)[0:1]
+        return jnp.sum(jnp.where(lane == slot, row, 0.0), axis=1, keepdims=True)
+
+    def spread(a, b, c, d):
+        return jnp.where(
+            wide < 2 * rows, jnp.where(wide < rows, a, b), jnp.where(wide < 3 * rows, c, d)
+        )
+
+    row_mask = spread(
+        pick(mine, 5),
+        pick(mine, 0),
+        pick(mate, jnp.where(first, 4, 6)),
+        pick(mate, jnp.where(first, 3, 1)),
+    )
+    col_mask = spread(
+        pick(up, 2),
+        pick(down, 7),
+        pick(up, jnp.where(first, 3, 1)),
+        pick(mine, 4) * weight + pick(down, 6) * (1.0 - weight),
+    )
+    panel[0:rows] = up[:, lo:mid]
+    panel[rows : 2 * rows] = down[:, lo:mid]
+    panel[2 * rows : 3 * rows] = up[:, lo:mid]
+
+    @pl.when(first)
+    def _():
+        panel[3 * rows : 4 * rows] = mine[:, lo:mid]
+
+    @pl.when(core[0] != 0)
+    def _():
+        panel[3 * rows : 4 * rows] = down[:, lo:mid]
+
+    by_row = chi[...] * row_mask
+    near = jnp.where(wide < 2 * rows, by_row, 0.0).astype(BF)
+    far = jnp.where(wide < 2 * rows, 0.0, by_row).astype(BF)
+    mine_rows = jnp.dot(near, panel[...], preferred_element_type=F32)
+    mate_rows = jnp.dot(far, panel[...], preferred_element_type=F32)
+    for t in range(2):
+        by_col = (chi[t * rows : (t + 1) * rows] * col_mask).astype(BF)
+        a = lax.dot_general(by_col, mine[:, lo:mid], FIRST, preferred_element_type=F32)
+        b = lax.dot_general(by_col, mate[:, lo:mid], FIRST, preferred_element_type=F32)
+        last = b[3 * rows :]
+        to_up[t] = (a[:rows] + b[2 * rows : 3 * rows]).astype(BF)
+        to_down[t] = (a[rows : 2 * rows] + last * (1.0 - weight)).astype(BF)
+        own[t] = mine_rows[t * rows : (t + 1) * rows] + last * weight
+        to_mate[t] = mate_rows[t * rows : (t + 1) * rows]
+
+
+def project(core, parts, mine, mate, up, down, naux):
+    rows = mine.shape[0]
+    shape = (2, rows, naux)
+    return pl.pallas_call(
+        project_kernel,
+        out_shape=(
+            jax.ShapeDtypeStruct(shape, BF),
+            jax.ShapeDtypeStruct(shape, BF),
+            jax.ShapeDtypeStruct(shape, F32),
+            jax.ShapeDtypeStruct(shape, F32),
+        ),
+        in_specs=[SCALARS] + [WHOLE] * 5,
+        out_specs=(WHOLE,) * 4,
+        scratch_shapes=[pltpu.VMEM((2 * rows, 4 * rows), F32), pltpu.VMEM((4 * rows, naux), BF)],
+        compiler_params=pltpu.CompilerParams(vmem_limit_bytes=16 * 2**20),
+        cost_estimate=pl.CostEstimate(
+            flops=32 * rows * rows * naux, bytes_accessed=24 * rows * naux, transcendentals=0
+        ),
+        name="project",
+    )(core, parts, mine, mate, up, down)
+
+
+def combine_kernel(own, a, b, c, out):
+    total = (own[...] + a[...] + b[...].astype(F32) + c[...].astype(F32)).astype(BF)
+    for z in range(8):
+        out[z] = total
+
+
+def combine(own, a, b, c):
+    return pl.pallas_call(
+        combine_kernel,
+        out_shape=jax.ShapeDtypeStruct((8,) + own.shape, BF),
+        in_specs=[WHOLE] * 4,
+        out_specs=WHOLE,
+        compiler_params=pltpu.CompilerParams(vmem_limit_bytes=8 * 2**20),
+        cost_estimate=pl.CostEstimate(
+            flops=4 * own.size, bytes_accessed=28 * own.size, transcendentals=0
+        ),
+        name="combine",
+    )(own, a, b, c)
+
+
 def on_device(phi_occ, phi_vir, eps_occ, eps_vir, taus, pair_mask, basis):
     core, xh = lax.axis_index("core"), lax.axis_index("xh")
     naux, rows = basis.shape[1], phi_occ.shape[0]
-    first = core == 0
     mask = jnp.pad(pair_mask.astype(BF), ((0, 0), (0, 120)))
     mine = jnp.concatenate(
         [phi_occ, phi_vir, basis, jnp.broadcast_to(mask, (rows, 128))], axis=1
@@ -125,67 +222,34 @@
     up = from_tile(mine, 2)
     down = from_tile(mine, -4)
     mate = lax.ppermute(mine, "core", SWAP)
-    moves = [(z * 16 + o, (o // 2) * 16 + z * 2 + o % 2) for z in range(8) for o in range(16)]
-    part = lax.ppermute(basis, ("z", "xl", "y"), moves)
-    got = trade(part, "y", 4)
+    got = []
+    for m in range(4):
+        pairs = [
+            ((i // 2) * 16 + 2 * z + i % 2, z * 16 + (i ^ (2 * m)))
+            for z in range(8)
+            for i in range(16)
+        ]
+        got.append(lax.ppermute(basis, ("z", "xl", "y"), pairs))
 
     part_sums = green(
         core.reshape(1), taus, eps_occ[None], eps_vir[None], mine, mate, up, down
     )
-    part_sums, part = lax.optimization_barrier((part_sums, part))
     sums = lax.all_to_all(part_sums, ORB, 0, 0, tiled=True)
-    part = join(part, got, "y", 4, 0)
-    got = trade(part, "y", 2)
-    extra, x_mate, x_up, x_down = (slab[:, -naux - 128 :] for slab in (mine, mate, up, down))
-    x_fourth = jnp.where(first, extra, x_down)
-
-    def masks(slab):
-        return slab[0, naux : naux + 8].astype(F32)
-
-    m_own, m_mate, m_up, m_down = masks(extra), masks(x_mate), masks(x_up), masks(x_down)
-    row_mask = jnp.stack(
-        [m_own[5], m_own[0], jnp.where(first, m_mate[4], m_mate[6]), jnp.where(first, m_mate[3], m_mate[1])]
-    )
-    col_mask = jnp.stack(
-        [m_up[2], m_down[7], jnp.where(first, m_up[3], m_up[1]), jnp.where(first, m_own[4], m_down[6])]
-    )
-    row_mask = jnp.repeat(row_mask, rows)
-    col_mask = jnp.repeat(col_mask, rows)
+    y = lax.axis_index("y")
+    odd, upper = (y & 2) != 0, (y & 4) != 0
+    got = [jnp.where(odd, got[m ^ 1], got[m]) for m in range(4)]
+    part = jnp.stack([jnp.where(upper, got[m ^ 2], got[m]) for m in range(4)])
 
     both = product(sums)
-    both, part = lax.optimization_barrier((both, part))
-    both = lax.all_to_all(both, ORB, 0, 0, tiled=True).reshape(2, rows, 4 * rows)
-    part = join(part, got, "y", 2, 1)
-    got = trade(part, "y", 1)
-    by_row = (both.astype(F32) * row_mask).astype(BF)
-    by_col = (both.astype(F32) * col_mask).astype(BF)
-
-    def aux(slab):
-        return slab[:, :naux]
-
-    def rows_of(block, *panels):
-        return jnp.einsum("trc,cq->trq", block, jnp.concatenate(panels), preferred_element_type=F32)
-
-    def cols_of(block, panel):
-        return jnp.einsum("trc,rq->tcq", block, panel, preferred_element_type=F32)
-
-    r2, r3 = 2 * rows, 3 * rows
-    to_up = cols_of(by_col[:, :, :rows], aux(extra)) + cols_of(by_col[:, :, r2:r3], aux(x_mate))
-    last = cols_of(by_col[:, :, r3:], aux(x_mate))
-    zero = jnp.zeros_like(last)
-    to_down = cols_of(by_col[:, :, rows:r2], aux(extra)) + jnp.where(first, zero, last)
-    to_mate = rows_of(by_row[:, :, r2:], aux(x_up), aux(x_fourth))
-    own = rows_of(by_row[:, :, :r2], aux(x_up), aux(x_down)) + jnp.where(first, last, zero)
-    to_up = to_up.astype(BF)
+    both = lax.all_to_all(both, ORB, 0, 0, tiled=True)
+    part = join(part, trade(part, "xl", 1), "xl", 1, 0)
+    to_up, to_down, to_mate, own = project(core.reshape(1), both, mine, mate, up, down, naux)
     got_up = from_tile(to_up, -2)
-    got_down = from_tile(to_down.astype(BF), 4)
+    got_down = from_tile(to_down, 4)
     got_mate = lax.ppermute(to_mate, "core", SWAP)
-    projected = (own + got_mate + got_up.astype(F32) + got_down.astype(F32)).astype(BF)
-
-    projected, part = lax.optimization_barrier((projected, part))
-    gathered = to_all(projected, "z", 8)
-    part = join(part, got, "y", 1, 0)
-    part = join(part, trade(part, "xl", 1), "xl", 1, 1)
+    copies = combine(own, got_mate, got_up, got_down)
+    gathered = lax.all_to_all(copies, "z", 0, 0, tiled=True)
+    part = join(part, trade(part, "y", 1), "y", 1, 0)
     blocks = part.reshape(2, 8, rows, naux)
     at = xh * 2 + core
 

time: 139 us -> 142 us (1.022); the launches traced: 138 us -> 139 us
  blocking collectives: 0 us -> 28.9 us
  starting transfers between devices: 81.7 us -> 69.2 us
  between operations: 5.75 us -> 0.47 us
  local copies, waits for them, and re-layouts: 5.88 us -> 1.61 us
  other arithmetic: 4.83 us -> 1.89 us
  waiting for transfers between devices: 34.9 us -> 32.9 us
    all_to_all x0 -> x2, blocking collectives: none -> 28.9 us  [the longest x1 15.5 us: on_device(): sums = lax.all_to_all(part_sums, ORB, 0, 0, tiled=True)]
    ppermute x4 -> x2, starting transfers between devices: 26.8 us -> 6.68 us  [trade(): return lax.ppermute(value, axis, [(i, i ^ bit) for i in range(size)])]
    ppermute x1 -> x4, starting transfers between devices: 0.66 us -> 9.64 us  [on_device(): got.append(lax.ppermute(basis, ('z', 'xl', 'y'), pairs))]
    ppermute x4, starting transfers between devices: 23.5 us -> 15.2 us  [from_tile(): return lax.ppermute(value, PTS, [((i + steps) % 32, i) for i in range(32)])]
    ppermute x1, starting transfers between devices: 2.86 us -> 8.75 us  [on_device(): mate = lax.ppermute(mine, 'core', SWAP)]
    all_to_all x3 -> x1, waiting for transfers between devices: 11.3 us -> 6.25 us  [on_device(): gathered = lax.all_to_all(copies, 'z', 0, 0, tiled=True)]
    ppermute x1, starting transfers between devices: 1.92 us -> 4.89 us  [on_device(): lax.ppermute(response(3).astype(BF), ('xh', 'core'), [(0, 3), (3, 0), (1,...]
    ppermute x4, waiting for transfers between devices: 7.59 us -> 10.5 us  [from_tile(): return lax.ppermute(value, PTS, [((i + steps) % 32, i) for i in range(32)])]
  transfers between devices with their start and end apart: 17 -> 16, of which waited for: 7 -> 7; matrix products, arithmetic and copies ran while one was open for 5% -> 1% of each run, Pallas kernels for 2% -> 1%
where the time goes in v5:
time: 142 us; the launch traced here: 139 us
  starting transfers between devices  69.2 us (49%)
  waiting for transfers between devices  32.9 us (23%)
  blocking collectives  28.9 us (20%)
  Pallas kernels  3.15 us (2%)
  other arithmetic  1.89 us (1%)
  local copies, waits for them, and re-layouts  1.61 us (1%)
    all_to_all x1, blocking collectives, on_device(): sums = lax.all_to_all(part_sums, ORB, 0, 0, tiled=True)  15.5 us
    ppermute x4, starting transfers between devices, from_tile(): return lax.ppermute(value, PTS, [((i + steps) % 32, i) for i in range(32)])  15.2 us
    all_to_all x1, starting transfers between devices, on_device(): gathered = lax.all_to_all(copies, 'z', 0, 0, tiled=True)  14.7 us
    all_to_all x1, blocking collectives, on_device(): both = lax.all_to_all(both, ORB, 0, 0, tiled=True)  13.3 us
    ppermute x4, waiting for transfers between devices, from_tile(): return lax.ppermute(value, PTS, [((i + steps) % 32, i) for i in range(32)])  10.5 us
    ppermute x2, waiting for transfers between devices, trade(): return lax.ppermute(value, axis, [(i, i ^ bit) for i in range(size)])  10.2 us
    ppermute x4, starting transfers between devices, on_device(): got.append(lax.ppermute(basis, ('z', 'xl', 'y'), pairs))  9.64 us
    ppermute x1, starting transfers between devices, on_device(): mate = lax.ppermute(mine, 'core', SWAP)  8.75 us
  transfers between devices with their start and end apart: 16, of which 7 were waited for; matrix products, arithmetic and copies ran while one was open for 1% of the time, Pallas kernels for 1%

profile of v5, /device:TPU:1, one launch (start us, length us, event | category | flops | bytes accessed | tf_op | source)
XLA Modules:
  0.0 139.4 jit_solution(16124883700037480765)
XLA Ops:
  1.7 8.7 %collective-permute-start.6 = (bf16[96,1792]{1,0:T(8,128)(2,1)S(1)}, bf16[96,1792]{1,0:T(8,128)(2,1)S(1)}, u32[]{:S(2)}, u32[]{:S(2)}) collective-permute-start(bf16[96,1792]{1,0:T(8,128)(2,1)S(1)} %maximum_maximum_fusion.mine), channel_id=1, source_target_pairs={{0,16},{16,0},{1,17},{17,1},{2,18},{18,2},{3,19},{19,3},{4,20},{20... | collective-permute-start | bytes 1032200 | tf_op jit(solution)/shard_map/ppermute | solution.py:224
  10.5 7.8 %collective-permute-start.7 = (bf16[96,1792]{1,0:T(8,128)(2,1)S(1)}, bf16[96,1792]{1,0:T(8,128)(2,1)S(1)}, u32[]{:S(2)}, u32[]{:S(2)}) collective-permute-start(bf16[96,1792]{1,0:T(8,128)(2,1)S(1)} %maximum_maximum_fusion.mine), channel_id=1, source_target_pairs={{32,0},{48,16},{64,32},{80,48},{96,64},{112,80},{128,96},{144,112}... | collective-permute-start | bytes 1032200 | tf_op jit(solution)/shard_map/ppermute | solution.py:21
  18.3 1.9 %collective-permute-start.8 = (bf16[96,1792]{1,0:T(8,128)(2,1)S(1)}, bf16[96,1792]{1,0:T(8,128)(2,1)S(1)}, u32[]{:S(2)}, u32[]{:S(2)}) collective-permute-start(bf16[96,1792]{1,0:T(8,128)(2,1)S(1)} %maximum_maximum_fusion.mine), channel_id=1, source_target_pairs={{448,0},{464,16},{480,32},{496,48},{0,64},{16,80},{32,96},{48,112}... | collective-permute-start | bytes 1032200 | tf_op jit(solution)/shard_map/ppermute | solution.py:21
  20.2 5.4 %collective-permute-done.7.up = bf16[96,1792]{1,0:T(8,128)(2,1)S(1)} collective-permute-done((bf16[96,1792]{1,0:T(8,128)(2,1)S(1)}, bf16[96,1792]{1,0:T(8,128)(2,1)S(1)}, u32[]{:S(2)}, u32[]{:S(2)}) %collective-permute-start.7) | collective-permute-done | bytes 344096 | tf_op jit(solution)/shard_map/ppermute | solution.py:21
  25.7 5.0 %collective-permute-done.8.down = bf16[96,1792]{1,0:T(8,128)(2,1)S(1)} collective-permute-done((bf16[96,1792]{1,0:T(8,128)(2,1)S(1)}, bf16[96,1792]{1,0:T(8,128)(2,1)S(1)}, u32[]{:S(2)}, u32[]{:S(2)}) %collective-permute-start.8) | collective-permute-done | bytes 344096 | tf_op jit(solution)/shard_map/ppermute | solution.py:21
  31.4 1.6 %green.1 = bf16[16,24,384]{2,1,0:T(8,128)(2,1)S(1)} custom-call(s32[1]{0:T(128)} %bitcast.10.core, f32[2]{0:T(128)S(1)} %copy-done, f32[1,128]{1,0:T(1,128)S(1)} %bitcast.76, f32[1,1280]{1,0:T(1,128)S(1)} %broadcast_in_dim.14.eps_vir, bf16[96,1792]{1,0:T(8,128)(2,1)S(1)} %maximum_maximum_fusion.mine, bf16[96,1792]{1,0:T(8,128)(2,1)S(1)} %collective-permute-done.6.mate, ...), custom_call_target="tpu_custom_call" | custom-call | flops 415236096 | bytes 1351680 | tf_op jit(solution)/shard_map/green/pallas_call | solution.py:72
  32.9 15.5 %all_to_all.15.parts = bf16[16,24,384]{2,1,0:T(8,128)(2,1)S(1)} all-to-all(bf16[16,24,384]{2,1,0:T(8,128)(2,1)S(1)} %green.1), channel_id=1, replica_groups=mesh['z'=8,'xh'=2,'core'=2,'xl'=2,'y'=8] {'xl','y'}, dimensions={0} | all-to-all | bytes 589824 | tf_op jit(solution)/shard_map/all_to_all | solution.py:237
  48.5 13.3 %all_to_all.16.parts = bf16[16,12,384]{2,1,0:T(8,128)(2,1)S(1)} all-to-all(bf16[16,12,384]{2,1,0:T(8,128)(2,1)S(1)} %product.1), channel_id=1, replica_groups=mesh['z'=8,'xh'=2,'core'=2,'xl'=2,'y'=8] {'xl','y'}, dimensions={0} | all-to-all | bytes 294912 | tf_op jit(solution)/shard_map/all_to_all | solution.py:244
  62.5 4.9 %collective-permute-start.9 = (f32[2,96,256]{2,1,0:T(8,128)S(1)}, f32[2,96,256]{2,1,0:T(8,128)S(1)}, u32[]{:S(2)}, u32[]{:S(2)}) collective-permute-start(f32[2,96,256]{2,1,0:T(8,128)S(1)} %get-tuple-element.10), channel_id=1, source_target_pairs={{0,16},{16,0},{1,17},{17,1},{2,18},{18,2},{3,19},{19,3},{4,20},{20... | collective-permute-start | bytes 589832 | tf_op jit(solution)/shard_map/ppermute | solution.py:249
  67.4 1.9 %collective-permute-start.10 = (bf16[2,96,256]{2,1,0:T(8,128)(2,1)S(1)}, bf16[2,96,256]{2,1,0:T(8,128)(2,1)S(1)}, u32[]{:S(2)}, u32[]{:S(2)}) collective-permute-start(bf16[2,96,256]{2,1,0:T(8,128)(2,1)S(1)} %get-tuple-element.11), channel_id=1, source_target_pairs={{480,0},{496,16},{0,32},{16,48},{32,64},{48,80},{64,96},{80,112},{... | collective-permute-start | bytes 294920 | tf_op jit(solution)/shard_map/ppermute | solution.py:21
  69.3 3.6 %collective-permute-start.11 = (bf16[2,96,256]{2,1,0:T(8,128)(2,1)S(1)}, bf16[2,96,256]{2,1,0:T(8,128)(2,1)S(1)}, u32[]{:S(2)}, u32[]{:S(2)}) collective-permute-start(bf16[2,96,256]{2,1,0:T(8,128)(2,1)S(1)} %get-tuple-element.12), channel_id=1, source_target_pairs={{64,0},{80,16},{96,32},{112,48},{128,64},{144,80},{160,96},{176,11... | collective-permute-start | bytes 294920 | tf_op jit(solution)/shard_map/ppermute | solution.py:21
  72.9 3.5 %collective-permute-start = (bf16[96,256]{1,0:T(8,128)(2,1)S(1)}, bf16[96,256]{1,0:T(8,128)(2,1)S(1)}, u32[]{:S(2)}, u32[]{:S(2)}) collective-permute-start(bf16[96,256]{1,0:T(8,128)(2,1)S(1)} %copy-done.2), channel_id=1, source_target_pairs={{0,6},{1,7},{64,4},{65,5},{128,2},{129,3},{192,0},{193,1},{256,14}... | collective-permute-start | bytes 147464 | tf_op jit(solution)/shard_map/ppermute | solution.py:232
  76.4 2.3 %collective-permute-start.1 = (bf16[96,256]{1,0:T(8,128)(2,1)S(1)}, bf16[96,256]{1,0:T(8,128)(2,1)S(1)}, u32[]{:S(2)}, u32[]{:S(2)}) collective-permute-start(bf16[96,256]{1,0:T(8,128)(2,1)S(1)} %copy-done.2), channel_id=1, source_target_pairs={{0,4},{1,5},{64,6},{65,7},{128,0},{129,1},{192,2},{193,3},{256,12}... | collective-permute-start | bytes 147464 | tf_op jit(solution)/shard_map/ppermute | solution.py:232
  78.8 3.1 %collective-permute-start.2 = (bf16[96,256]{1,0:T(8,128)(2,1)S(1)}, bf16[96,256]{1,0:T(8,128)(2,1)S(1)}, u32[]{:S(2)}, u32[]{:S(2)}) collective-permute-start(bf16[96,256]{1,0:T(8,128)(2,1)S(1)} %copy-done.2), channel_id=1, source_target_pairs={{0,2},{1,3},{64,0},{65,1},{128,6},{129,7},{192,4},{193,5},{256,10}... | collective-permute-start | bytes 147464 | tf_op jit(solution)/shard_map/ppermute | solution.py:232
  83.6 14.7 %all-to-all-start.2 = ((bf16[8,2,96,256]{3,2,1,0:T(8,128)(2,1)}), bf16[8,2,96,256]{3,2,1,0:T(8,128)(2,1)S(1)}, u32[]{:S(2)}, u32[]{:S(2)}) async-start(bf16[8,2,96,256]{3,2,1,0:T(8,128)(2,1)} %combine.1), calls=%async_computation.2 | async-start | bytes 1572864 | tf_op jit(solution)/shard_map/all_to_all | solution.py:251
  98.4 3.7 %collective-permute-start.4 = (bf16[4,96,256]{2,1,0:T(8,128)(2,1)S(1)}, bf16[4,96,256]{2,1,0:T(8,128)(2,1)S(1)}, u32[]{:S(2)}, u32[]{:S(2)}) collective-permute-start(bf16[4,96,256]{2,1,0:T(8,128)(2,1)S(1)} %pad_maximum_fusion.1), channel_id=1, source_target_pairs={{0,8},{8,0},{1,9},{9,1},{2,10},{10,2},{3,11},{11,3},{4,12},{12,4},... | collective-permute-start | bytes 589832 | tf_op jit(solution)/shard_map/ppermute | solution.py:26
  102.1 3.3 %collective-permute-done.4 = bf16[4,96,256]{2,1,0:T(8,128)(2,1)S(1)} collective-permute-done((bf16[4,96,256]{2,1,0:T(8,128)(2,1)S(1)}, bf16[4,96,256]{2,1,0:T(8,128)(2,1)S(1)}, u32[]{:S(2)}, u32[]{:S(2)}) %collective-permute-start.4) | collective-permute-done | bytes 196640 | tf_op jit(solution)/shard_map/ppermute | solution.py:26
  105.5 3.0 %collective-permute-start.5 = (bf16[2,4,96,256]{3,2,1,0:T(8,128)(2,1)S(1)}, bf16[2,4,96,256]{3,2,1,0:T(8,128)(2,1)S(1)}, u32[]{:S(2)}, u32[]{:S(2)}) collective-permute-start(bf16[2,4,96,256]{3,2,1,0:T(8,128)(2,1)S(1)} %pad_maximum_fusion), channel_id=1, source_target_pairs={{0,1},{1,0},{2,3},{3,2},{4,5},{5,4},{6,7},{7,6},{8,9},{9,8},{10,11... | collective-permute-start | bytes 1179656 | tf_op jit(solution)/shard_map/ppermute | solution.py:26
  108.6 6.9 %collective-permute-done.5 = bf16[2,4,96,256]{3,2,1,0:T(8,128)(2,1)S(1)} collective-permute-done((bf16[2,4,96,256]{3,2,1,0:T(8,128)(2,1)S(1)}, bf16[2,4,96,256]{3,2,1,0:T(8,128)(2,1)S(1)}, u32[]{:S(2)}, u32[]{:S(2)}) %collective-permute-start.5) | collective-permute-done | bytes 393248 | tf_op jit(solution)/shard_map/ppermute | solution.py:26
  115.6 6.3 %all-to-all-done.2 = bf16[8,2,96,256]{3,2,1,0:T(8,128)(2,1)S(1)} async-done(((bf16[8,2,96,256]{3,2,1,0:T(8,128)(2,1)}), bf16[8,2,96,256]{3,2,1,0:T(8,128)(2,1)S(1)}, u32[]{:S(2)}, u32[]{:S(2)}) %all-to-all-start.2) | async-done | bytes 786464 | tf_op jit(solution)/shard_map/all_to_all | solution.py:251
  122.2 2.4 %collective-permute-start.12 = (f32[128,2,256]{2,0,1:T(8,128)S(1)}, f32[128,2,256]{2,0,1:T(8,128)S(1)}, u32[]{:S(2)}, u32[]{:S(2)}) collective-permute-start(f32[128,2,256]{2,0,1:T(8,128)S(1)} %convolution_bitcast_fusion.2), channel_id=1, source_target_pairs={{0,16},{16,0},{1,17},{17,1},{2,18},{18,2},{3,19},{19,3},{4,20},{20... | collective-permute-start | bytes 786440 | tf_op jit(solution)/shard_map/ppermute | solution.py:267
  124.9 4.9 %collective-permute-start.14 = (bf16[128,2,256]{2,0,1:T(8,128)(2,1)S(1)}, bf16[128,2,256]{2,0,1:T(8,128)(2,1)S(1)}, u32[]{:S(2)}, u32[]{:S(2)}) collective-permute-start(bf16[128,2,256]{2,0,1:T(8,128)(2,1)S(1)} %fusion.4), channel_id=1, source_target_pairs={{0,48},{48,0},{16,32},{32,16},{1,49},{49,1},{17,33},{33,17},{2,50}... | collective-permute-start | bytes 393224 | tf_op jit(solution)/shard_map/ppermute | solution.py:263
  130.2 2.0 %collective-permute-start.13 = (bf16[128,2,256]{2,0,1:T(8,128)(2,1)S(1)}, bf16[128,2,256]{2,0,1:T(8,128)(2,1)S(1)}, u32[]{:S(2)}, u32[]{:S(2)}) collective-permute-start(bf16[128,2,256]{2,0,1:T(8,128)(2,1)S(1)} %fusion.3), channel_id=1, source_target_pairs={{0,32},{32,0},{1,33},{33,1},{2,34},{34,2},{3,35},{35,3},{4,36},{36... | collective-permute-start | bytes 393224 | tf_op jit(solution)/shard_map/ppermute | solution.py:266
  133.7 4.4 %collective-permute-done.13 = bf16[128,2,256]{2,0,1:T(8,128)(2,1)S(1)} collective-permute-done((bf16[128,2,256]{2,0,1:T(8,128)(2,1)S(1)}, bf16[128,2,256]{2,0,1:T(8,128)(2,1)S(1)}, u32[]{:S(2)}, u32[]{:S(2)}) %collective-permute-start.13) | collective-permute-done | bytes 131104 | tf_op jit(solution)/shard_map/ppermute | solution.py:266
  (37 shorter events, 8.5 us)
Async XLA Ops:
  0.7 19.5 %copy-start.3 = (f32[1280]{0:T(1024)S(1)}, f32[1280]{0:T(1024)}, u32[]{:S(2)}) copy-start(f32[1280]{0:T(1024)} %param.10) | copy-start | bytes 15364
  1.7 18.5 %collective-permute-start.6 = (bf16[96,1792]{1,0:T(8,128)(2,1)S(1)}, bf16[96,1792]{1,0:T(8,128)(2,1)S(1)}, u32[]{:S(2)}, u32[]{:S(2)}) collective-permute-start(bf16[96,1792]{1,0:T(8,128)(2,1)S(1)} %maximum_maximum_fusion.mine), channel_id=1, source_target_pairs={{0,16},{16,0},{1,17},{17,1},{2,18},{18,2},{3,19},{19,3},{4,20},{20... | collective-permute-start | bytes 1032200 | tf_op jit(solution)/shard_map/ppermute | solution.py:224
  10.5 15.2 %collective-permute-start.7 = (bf16[96,1792]{1,0:T(8,128)(2,1)S(1)}, bf16[96,1792]{1,0:T(8,128)(2,1)S(1)}, u32[]{:S(2)}, u32[]{:S(2)}) collective-permute-start(bf16[96,1792]{1,0:T(8,128)(2,1)S(1)} %maximum_maximum_fusion.mine), channel_id=1, source_target_pairs={{32,0},{48,16},{64,32},{80,48},{96,64},{112,80},{128,96},{144,112}... | collective-permute-start | bytes 1032200 | tf_op jit(solution)/shard_map/ppermute | solution.py:21
  18.3 12.4 %collective-permute-start.8 = (bf16[96,1792]{1,0:T(8,128)(2,1)S(1)}, bf16[96,1792]{1,0:T(8,128)(2,1)S(1)}, u32[]{:S(2)}, u32[]{:S(2)}) collective-permute-start(bf16[96,1792]{1,0:T(8,128)(2,1)S(1)} %maximum_maximum_fusion.mine), channel_id=1, source_target_pairs={{448,0},{464,16},{480,32},{496,48},{0,64},{16,80},{32,96},{48,112}... | collective-permute-start | bytes 1032200 | tf_op jit(solution)/shard_map/ppermute | solution.py:21
  30.7 0.7 copy-start
  30.7 0.7 copy-start.1
  61.9 11.0 %copy-start.2 = (bf16[96,256]{1,0:T(8,128)(2,1)S(1)}, bf16[96,256]{1,0:T(8,128)(2,1)}, u32[]{:S(2)}) copy-start(bf16[96,256]{1,0:T(8,128)(2,1)} %param.13) | copy-start | bytes 147460
  62.5 20.1 %collective-permute-start.9 = (f32[2,96,256]{2,1,0:T(8,128)S(1)}, f32[2,96,256]{2,1,0:T(8,128)S(1)}, u32[]{:S(2)}, u32[]{:S(2)}) collective-permute-start(f32[2,96,256]{2,1,0:T(8,128)S(1)} %get-tuple-element.10), channel_id=1, source_target_pairs={{0,16},{16,0},{1,17},{17,1},{2,18},{18,2},{3,19},{19,3},{4,20},{20... | collective-permute-start | bytes 589832 | tf_op jit(solution)/shard_map/ppermute | solution.py:249
  67.4 11.4 %collective-permute-start.10 = (bf16[2,96,256]{2,1,0:T(8,128)(2,1)S(1)}, bf16[2,96,256]{2,1,0:T(8,128)(2,1)S(1)}, u32[]{:S(2)}, u32[]{:S(2)}) collective-permute-start(bf16[2,96,256]{2,1,0:T(8,128)(2,1)S(1)} %get-tuple-element.11), channel_id=1, source_target_pairs={{480,0},{496,16},{0,32},{16,48},{32,64},{48,80},{64,96},{80,112},{... | collective-permute-start | bytes 294920 | tf_op jit(solution)/shard_map/ppermute | solution.py:21
  69.3 12.6 %collective-permute-start.11 = (bf16[2,96,256]{2,1,0:T(8,128)(2,1)S(1)}, bf16[2,96,256]{2,1,0:T(8,128)(2,1)S(1)}, u32[]{:S(2)}, u32[]{:S(2)}) collective-permute-start(bf16[2,96,256]{2,1,0:T(8,128)(2,1)S(1)} %get-tuple-element.12), channel_id=1, source_target_pairs={{64,0},{80,16},{96,32},{112,48},{128,64},{144,80},{160,96},{176,11... | collective-permute-start | bytes 294920 | tf_op jit(solution)/shard_map/ppermute | solution.py:21
  72.9 25.4 %collective-permute-start = (bf16[96,256]{1,0:T(8,128)(2,1)S(1)}, bf16[96,256]{1,0:T(8,128)(2,1)S(1)}, u32[]{:S(2)}, u32[]{:S(2)}) collective-permute-start(bf16[96,256]{1,0:T(8,128)(2,1)S(1)} %copy-done.2), channel_id=1, source_target_pairs={{0,6},{1,7},{64,4},{65,5},{128,2},{129,3},{192,0},{193,1},{256,14}... | collective-permute-start | bytes 147464 | tf_op jit(solution)/shard_map/ppermute | solution.py:232
  76.4 21.8 %collective-permute-start.1 = (bf16[96,256]{1,0:T(8,128)(2,1)S(1)}, bf16[96,256]{1,0:T(8,128)(2,1)S(1)}, u32[]{:S(2)}, u32[]{:S(2)}) collective-permute-start(bf16[96,256]{1,0:T(8,128)(2,1)S(1)} %copy-done.2), channel_id=1, source_target_pairs={{0,4},{1,5},{64,6},{65,7},{128,0},{129,1},{192,2},{193,3},{256,12}... | collective-permute-start | bytes 147464 | tf_op jit(solution)/shard_map/ppermute | solution.py:232
  78.8 19.5 %collective-permute-start.2 = (bf16[96,256]{1,0:T(8,128)(2,1)S(1)}, bf16[96,256]{1,0:T(8,128)(2,1)S(1)}, u32[]{:S(2)}, u32[]{:S(2)}) collective-permute-start(bf16[96,256]{1,0:T(8,128)(2,1)S(1)} %copy-done.2), channel_id=1, source_target_pairs={{0,2},{1,3},{64,0},{65,1},{128,6},{129,7},{192,4},{193,5},{256,10}... | collective-permute-start | bytes 147464 | tf_op jit(solution)/shard_map/ppermute | solution.py:232
  81.9 16.4 %collective-permute-start.3 = (bf16[96,256]{1,0:T(8,128)(2,1)S(1)}, bf16[96,256]{1,0:T(8,128)(2,1)S(1)}, u32[]{:S(2)}, u32[]{:S(2)}) collective-permute-start(bf16[96,256]{1,0:T(8,128)(2,1)S(1)} %copy-done.2), channel_id=1, source_target_pairs={{0,0},{1,1},{64,2},{65,3},{128,4},{129,5},{192,6},{193,7},{256,8},... | collective-permute-start | bytes 147464 | tf_op jit(solution)/shard_map/ppermute | solution.py:232
  83.6 38.3 %all-to-all-start.2 = ((bf16[8,2,96,256]{3,2,1,0:T(8,128)(2,1)}), bf16[8,2,96,256]{3,2,1,0:T(8,128)(2,1)S(1)}, u32[]{:S(2)}, u32[]{:S(2)}) async-start(bf16[8,2,96,256]{3,2,1,0:T(8,128)(2,1)} %combine.1), calls=%async_computation.2 | async-start | bytes 1572864 | tf_op jit(solution)/shard_map/all_to_all | solution.py:251
  98.4 7.0 %collective-permute-start.4 = (bf16[4,96,256]{2,1,0:T(8,128)(2,1)S(1)}, bf16[4,96,256]{2,1,0:T(8,128)(2,1)S(1)}, u32[]{:S(2)}, u32[]{:S(2)}) collective-permute-start(bf16[4,96,256]{2,1,0:T(8,128)(2,1)S(1)} %pad_maximum_fusion.1), channel_id=1, source_target_pairs={{0,8},{8,0},{1,9},{9,1},{2,10},{10,2},{3,11},{11,3},{4,12},{12,4},... | collective-permute-start | bytes 589832 | tf_op jit(solution)/shard_map/ppermute | solution.py:26
  105.5 10.0 %collective-permute-start.5 = (bf16[2,4,96,256]{3,2,1,0:T(8,128)(2,1)S(1)}, bf16[2,4,96,256]{3,2,1,0:T(8,128)(2,1)S(1)}, u32[]{:S(2)}, u32[]{:S(2)}) collective-permute-start(bf16[2,4,96,256]{3,2,1,0:T(8,128)(2,1)S(1)} %pad_maximum_fusion), channel_id=1, source_target_pairs={{0,1},{1,0},{2,3},{3,2},{4,5},{5,4},{6,7},{7,6},{8,9},{9,8},{10,11... | collective-permute-start | bytes 1179656 | tf_op jit(solution)/shard_map/ppermute | solution.py:26
  122.2 15.9 %collective-permute-start.12 = (f32[128,2,256]{2,0,1:T(8,128)S(1)}, f32[128,2,256]{2,0,1:T(8,128)S(1)}, u32[]{:S(2)}, u32[]{:S(2)}) collective-permute-start(f32[128,2,256]{2,0,1:T(8,128)S(1)} %convolution_bitcast_fusion.2), channel_id=1, source_target_pairs={{0,16},{16,0},{1,17},{17,1},{2,18},{18,2},{3,19},{19,3},{4,20},{20... | collective-permute-start | bytes 786440 | tf_op jit(solution)/shard_map/ppermute | solution.py:267
  124.9 8.7 %collective-permute-start.14 = (bf16[128,2,256]{2,0,1:T(8,128)(2,1)S(1)}, bf16[128,2,256]{2,0,1:T(8,128)(2,1)S(1)}, u32[]{:S(2)}, u32[]{:S(2)}) collective-permute-start(bf16[128,2,256]{2,0,1:T(8,128)(2,1)S(1)} %fusion.4), channel_id=1, source_target_pairs={{0,48},{48,0},{16,32},{32,16},{1,49},{49,1},{17,33},{33,17},{2,50}... | collective-permute-start | bytes 393224 | tf_op jit(solution)/shard_map/ppermute | solution.py:263
  130.2 8.0 %collective-permute-start.13 = (bf16[128,2,256]{2,0,1:T(8,128)(2,1)S(1)}, bf16[128,2,256]{2,0,1:T(8,128)(2,1)S(1)}, u32[]{:S(2)}, u32[]{:S(2)}) collective-permute-start(bf16[128,2,256]{2,0,1:T(8,128)(2,1)S(1)} %fusion.3), channel_id=1, source_target_pairs={{0,32},{32,0},{1,33},{33,1},{2,34},{34,2},{3,35},{35,3},{4,36},{36... | collective-permute-start | bytes 393224 | tf_op jit(solution)/shard_map/ppermute | solution.py:266

commit v6 on v5

--- a/solution.py
+++ b/solution.py
@@ -215,6 +215,12 @@
 def on_device(phi_occ, phi_vir, eps_occ, eps_vir, taus, pair_mask, basis):
     core, xh = lax.axis_index("core"), lax.axis_index("xh")
     naux, rows = basis.shape[1], phi_occ.shape[0]
+    got = []
+    for far in (0, 4):
+        pairs = [
+            ((i // 2) * 16 + 2 * z + i % 2, z * 16 + (i ^ far)) for z in range(8) for i in range(16)
+        ]
+        got.append(lax.ppermute(basis, ("z", "xl", "y"), pairs))
     mask = jnp.pad(pair_mask.astype(BF), ((0, 0), (0, 120)))
     mine = jnp.concatenate(
         [phi_occ, phi_vir, basis, jnp.broadcast_to(mask, (rows, 128))], axis=1
@@ -222,26 +228,16 @@
     up = from_tile(mine, 2)
     down = from_tile(mine, -4)
     mate = lax.ppermute(mine, "core", SWAP)
-    got = []
-    for m in range(4):
-        pairs = [
-            ((i // 2) * 16 + 2 * z + i % 2, z * 16 + (i ^ (2 * m)))
-            for z in range(8)
-            for i in range(16)
-        ]
-        got.append(lax.ppermute(basis, ("z", "xl", "y"), pairs))
-
     part_sums = green(
         core.reshape(1), taus, eps_occ[None], eps_vir[None], mine, mate, up, down
     )
     sums = lax.all_to_all(part_sums, ORB, 0, 0, tiled=True)
-    y = lax.axis_index("y")
-    odd, upper = (y & 2) != 0, (y & 4) != 0
-    got = [jnp.where(odd, got[m ^ 1], got[m]) for m in range(4)]
-    part = jnp.stack([jnp.where(upper, got[m ^ 2], got[m]) for m in range(4)])
+    part = join(got[0], got[1], "y", 4, 0)
+    got = trade(part, "y", 2)
 
     both = product(sums)
     both = lax.all_to_all(both, ORB, 0, 0, tiled=True)
+    part = join(part, got, "y", 2, 1)
     part = join(part, trade(part, "xl", 1), "xl", 1, 0)
     to_up, to_down, to_mate, own = project(core.reshape(1), both, mine, mate, up, down, naux)
     got_up = from_tile(to_up, -2)

time: 142 us -> 129 us (0.908); the launches traced: 139 us -> 128 us
  blocking collectives: 28.9 us -> 0 us
  waiting for transfers between devices: 32.9 us -> 44.1 us
  starting transfers between devices: 69.2 us -> 73.8 us
  Pallas kernels: 3.15 us -> 4.57 us
    all_to_all x2 -> x0, blocking collectives: 28.9 us -> none  [the longest x1 15.5 us: on_device(): sums = lax.all_to_all(part_sums, ORB, 0, 0, tiled=True)]
    all_to_all x0 -> x2, starting transfers between devices: none -> 16.1 us  [the longest x1 8.99 us: on_device(): both = lax.all_to_all(both, ORB, 0, 0, tiled=True)]
    all_to_all x1, starting transfers between devices: 14.7 us -> 3.55 us  [on_device(): gathered = lax.all_to_all(copies, 'z', 0, 0, tiled=True)]
    all_to_all x0 -> x2, waiting for transfers between devices: none -> 8.5 us  [the longest x1 7.68 us: on_device(): both = lax.all_to_all(both, ORB, 0, 0, tiled=True)]
    ppermute x4, waiting for transfers between devices: 10.5 us -> 12.9 us  [from_tile(): return lax.ppermute(value, PTS, [((i + steps) % 32, i) for i in range(32)])]
    ppermute x2 -> x3, starting transfers between devices: 6.68 us -> 8.89 us  [trade(): return lax.ppermute(value, axis, [(i, i ^ bit) for i in range(size)])]
    ppermute x2 -> x3, waiting for transfers between devices: 10.2 us -> 12.3 us  [trade(): return lax.ppermute(value, axis, [(i, i ^ bit) for i in range(size)])]
    ppermute x4 -> x2, starting transfers between devices: 9.64 us -> 7.84 us  [on_device(): got.append(lax.ppermute(basis, ('z', 'xl', 'y'), pairs))]
  transfers between devices with their start and end apart: 16 -> 17, of which waited for: 7 -> 10; matrix products, arithmetic and copies ran while one was open for 1% -> 1% of each run, Pallas kernels for 1% -> 1%
where the time goes in v6:
time: 129 us; the launch traced here: 128 us
  starting transfers between devices  73.8 us (57%)
  waiting for transfers between devices  44.1 us (34%)
  Pallas kernels  4.57 us (4%)
  other arithmetic  1.9 us (1%)
  local copies, waits for them, and re-layouts  1.61 us (1%)
  matrix products  1.29 us (1%)
    ppermute x4, starting transfers between devices, from_tile(): return lax.ppermute(value, PTS, [((i + steps) % 32, i) for i in range(32)])  14.1 us
    ppermute x4, waiting for transfers between devices, from_tile(): return lax.ppermute(value, PTS, [((i + steps) % 32, i) for i in range(32)])  12.9 us
    ppermute x3, waiting for transfers between devices, trade(): return lax.ppermute(value, axis, [(i, i ^ bit) for i in range(size)])  12.3 us
    all_to_all x1, starting transfers between devices, on_device(): both = lax.all_to_all(both, ORB, 0, 0, tiled=True)  8.99 us
    ppermute x3, starting transfers between devices, trade(): return lax.ppermute(value, axis, [(i, i ^ bit) for i in range(size)])  8.89 us
    ppermute x1, starting transfers between devices, on_device(): mate = lax.ppermute(mine, 'core', SWAP)  8.75 us
    ppermute x2, starting transfers between devices, on_device(): got.append(lax.ppermute(basis, ('z', 'xl', 'y'), pairs))  7.84 us
    all_to_all x1, waiting for transfers between devices, on_device(): both = lax.all_to_all(both, ORB, 0, 0, tiled=True)  7.68 us
  transfers between devices with their start and end apart: 17, of which 10 were waited for; matrix products, arithmetic and copies ran while one was open for 1% of the time, Pallas kernels for 1%

profile of v6, /device:TPU:1, one launch (start us, length us, event | category | flops | bytes accessed | tf_op | source)
XLA Modules:
  0.0 127.8 jit_solution(12745120914471640544)
XLA Ops:
  1.7 8.7 %collective-permute-start.5 = (bf16[96,1792]{1,0:T(8,128)(2,1)S(1)}, bf16[96,1792]{1,0:T(8,128)(2,1)S(1)}, u32[]{:S(2)}, u32[]{:S(2)}) collective-permute-start(bf16[96,1792]{1,0:T(8,128)(2,1)S(1)} %maximum_maximum_fusion.mine), channel_id=1, source_target_pairs={{0,16},{16,0},{1,17},{17,1},{2,18},{18,2},{3,19},{19,3},{4,20},{20... | collective-permute-start | bytes 1032200 | tf_op jit(solution)/shard_map/ppermute | solution.py:230
  10.5 7.8 %collective-permute-start.6 = (bf16[96,1792]{1,0:T(8,128)(2,1)S(1)}, bf16[96,1792]{1,0:T(8,128)(2,1)S(1)}, u32[]{:S(2)}, u32[]{:S(2)}) collective-permute-start(bf16[96,1792]{1,0:T(8,128)(2,1)S(1)} %maximum_maximum_fusion.mine), channel_id=1, source_target_pairs={{32,0},{48,16},{64,32},{80,48},{96,64},{112,80},{128,96},{144,112}... | collective-permute-start | bytes 1032200 | tf_op jit(solution)/shard_map/ppermute | solution.py:21
  18.3 1.9 %collective-permute-start.7 = (bf16[96,1792]{1,0:T(8,128)(2,1)S(1)}, bf16[96,1792]{1,0:T(8,128)(2,1)S(1)}, u32[]{:S(2)}, u32[]{:S(2)}) collective-permute-start(bf16[96,1792]{1,0:T(8,128)(2,1)S(1)} %maximum_maximum_fusion.mine), channel_id=1, source_target_pairs={{448,0},{464,16},{480,32},{496,48},{0,64},{16,80},{32,96},{48,112}... | collective-permute-start | bytes 1032200 | tf_op jit(solution)/shard_map/ppermute | solution.py:21
  20.2 5.4 %collective-permute-done.6.up = bf16[96,1792]{1,0:T(8,128)(2,1)S(1)} collective-permute-done((bf16[96,1792]{1,0:T(8,128)(2,1)S(1)}, bf16[96,1792]{1,0:T(8,128)(2,1)S(1)}, u32[]{:S(2)}, u32[]{:S(2)}) %collective-permute-start.6) | collective-permute-done | bytes 344096 | tf_op jit(solution)/shard_map/ppermute | solution.py:21
  25.7 5.0 %collective-permute-done.7.down = bf16[96,1792]{1,0:T(8,128)(2,1)S(1)} collective-permute-done((bf16[96,1792]{1,0:T(8,128)(2,1)S(1)}, bf16[96,1792]{1,0:T(8,128)(2,1)S(1)}, u32[]{:S(2)}, u32[]{:S(2)}) %collective-permute-start.7) | collective-permute-done | bytes 344096 | tf_op jit(solution)/shard_map/ppermute | solution.py:21
  31.4 2.3 %green.1 = bf16[16,24,384]{2,1,0:T(8,128)(2,1)} custom-call(s32[1]{0:T(128)} %bitcast.11.core, f32[2]{0:T(128)S(1)} %copy-done, f32[1,128]{1,0:T(1,128)S(1)} %bitcast.78, f32[1,1280]{1,0:T(1,128)S(1)} %broadcast_in_dim.14.eps_vir, bf16[96,1792]{1,0:T(8,128)(2,1)S(1)} %maximum_maximum_fusion.mine, bf16[96,1792]{1,0:T(8,128)(2,1)S(1)} %collective-permute-done.5.mate, ...), custom_call_target="tpu_custom_call" | custom-call | flops 415236096 | bytes 1351680 | tf_op jit(solution)/shard_map/green/pallas_call | solution.py:72
  33.7 7.1 %all-to-all-start = ((bf16[16,24,384]{2,1,0:T(8,128)(2,1)}), bf16[16,24,384]{2,1,0:T(8,128)(2,1)S(1)}, u32[]{:S(2)}, u32[]{:S(2)}) async-start(bf16[16,24,384]{2,1,0:T(8,128)(2,1)} %green.1), calls=%async_computation | async-start | bytes 589824 | tf_op jit(solution)/shard_map/all_to_all | solution.py:234
  40.8 7.2 %collective-permute-start = (bf16[96,256]{1,0:T(8,128)(2,1)S(1)}, bf16[96,256]{1,0:T(8,128)(2,1)S(1)}, u32[]{:S(2)}, u32[]{:S(2)}) collective-permute-start(bf16[96,256]{1,0:T(8,128)(2,1)S(1)} %copy-done.2), channel_id=1, source_target_pairs={{0,4},{1,5},{64,6},{65,7},{128,0},{129,1},{192,2},{193,3},{256,12}... | collective-permute-start | bytes 147464 | tf_op jit(solution)/shard_map/ppermute | solution.py:223
  50.2 9.0 %all-to-all-start.1 = ((bf16[16,12,384]{2,1,0:T(8,128)(2,1)}), bf16[16,12,384]{2,1,0:T(8,128)(2,1)S(1)}, u32[]{:S(2)}, u32[]{:S(2)}) async-start(bf16[16,12,384]{2,1,0:T(8,128)(2,1)} %product.1), calls=%async_computation.1 | async-start | bytes 393216 | tf_op jit(solution)/shard_map/all_to_all | solution.py:239
  59.2 7.7 %all-to-all-done.1.parts = bf16[16,12,384]{2,1,0:T(8,128)(2,1)S(1)} async-done(((bf16[16,12,384]{2,1,0:T(8,128)(2,1)}), bf16[16,12,384]{2,1,0:T(8,128)(2,1)S(1)}, u32[]{:S(2)}, u32[]{:S(2)}) %all-to-all-start.1) | async-done | bytes 147488 | tf_op jit(solution)/shard_map/all_to_all | solution.py:239
  67.5 5.5 %collective-permute-start.8 = (f32[2,96,256]{2,1,0:T(8,128)S(1)}, f32[2,96,256]{2,1,0:T(8,128)S(1)}, u32[]{:S(2)}, u32[]{:S(2)}) collective-permute-start(f32[2,96,256]{2,1,0:T(8,128)S(1)} %get-tuple-element.10), channel_id=1, source_target_pairs={{0,16},{16,0},{1,17},{17,1},{2,18},{18,2},{3,19},{19,3},{4,20},{20... | collective-permute-start | bytes 589832 | tf_op jit(solution)/shard_map/ppermute | solution.py:245
  74.9 2.5 %collective-permute-start.10 = (bf16[2,96,256]{2,1,0:T(8,128)(2,1)S(1)}, bf16[2,96,256]{2,1,0:T(8,128)(2,1)S(1)}, u32[]{:S(2)}, u32[]{:S(2)}) collective-permute-start(bf16[2,96,256]{2,1,0:T(8,128)(2,1)S(1)} %get-tuple-element.12), channel_id=1, source_target_pairs={{64,0},{80,16},{96,32},{112,48},{128,64},{144,80},{160,96},{176,11... | collective-permute-start | bytes 294920 | tf_op jit(solution)/shard_map/ppermute | solution.py:21
  77.5 3.0 %collective-permute-start.2 = (bf16[2,96,256]{2,1,0:T(8,128)(2,1)S(1)}, bf16[2,96,256]{2,1,0:T(8,128)(2,1)S(1)}, u32[]{:S(2)}, u32[]{:S(2)}) collective-permute-start(bf16[2,96,256]{2,1,0:T(8,128)(2,1)S(1)} %pad_maximum_fusion.2), channel_id=1, source_target_pairs={{0,2},{1,3},{2,0},{3,1},{4,6},{5,7},{6,4},{7,5},{8,10},{9,11},{10,... | collective-permute-start | bytes 294920 | tf_op jit(solution)/shard_map/ppermute | solution.py:26
  80.5 2.4 %collective-permute-done.9.b = bf16[2,96,256]{2,1,0:T(8,128)(2,1)S(1)} collective-permute-done((bf16[2,96,256]{2,1,0:T(8,128)(2,1)S(1)}, bf16[2,96,256]{2,1,0:T(8,128)(2,1)S(1)}, u32[]{:S(2)}, u32[]{:S(2)}) %collective-permute-start.9) | collective-permute-done | bytes 98336 | tf_op jit(solution)/shard_map/ppermute | solution.py:21
  83.8 3.5 %all-to-all-start.2 = ((bf16[8,2,96,256]{3,2,1,0:T(8,128)(2,1)}), bf16[8,2,96,256]{3,2,1,0:T(8,128)(2,1)S(1)}, u32[]{:S(2)}, u32[]{:S(2)}) async-start(bf16[8,2,96,256]{3,2,1,0:T(8,128)(2,1)} %combine.1), calls=%async_computation.2 | async-start | bytes 1572864 | tf_op jit(solution)/shard_map/all_to_all | solution.py:247
  87.4 2.7 %collective-permute-start.3 = (bf16[2,2,96,256]{3,2,1,0:T(8,128)(2,1)S(1)}, bf16[2,2,96,256]{3,2,1,0:T(8,128)(2,1)S(1)}, u32[]{:S(2)}, u32[]{:S(2)}) collective-permute-start(bf16[2,2,96,256]{3,2,1,0:T(8,128)(2,1)S(1)} %pad_maximum_fusion.1), channel_id=1, source_target_pairs={{0,8},{8,0},{1,9},{9,1},{2,10},{10,2},{3,11},{11,3},{4,12},{12,4},... | collective-permute-start | bytes 589832 | tf_op jit(solution)/shard_map/ppermute | solution.py:26
  90.2 4.8 %collective-permute-done.3 = bf16[2,2,96,256]{3,2,1,0:T(8,128)(2,1)S(1)} collective-permute-done((bf16[2,2,96,256]{3,2,1,0:T(8,128)(2,1)S(1)}, bf16[2,2,96,256]{3,2,1,0:T(8,128)(2,1)S(1)}, u32[]{:S(2)}, u32[]{:S(2)}) %collective-permute-start.3) | collective-permute-done | bytes 196640 | tf_op jit(solution)/shard_map/ppermute | solution.py:26
  95.0 3.2 %collective-permute-start.4 = (bf16[2,2,2,96,256]{4,3,2,1,0:T(8,128)(2,1)S(1)}, bf16[2,2,2,96,256]{4,3,2,1,0:T(8,128)(2,1)S(1)}, u32[]{:S(2)}, u32[]{:S(2)}) collective-permute-start(bf16[2,2,2,96,256]{4,3,2,1,0:T(8,128)(2,1)S(1)} %pad_maximum_fusion), channel_id=1, source_target_pairs={{0,1},{1,0},{2,3},{3,2},{4,5},{5,4},{6,7},{7,6},{8,9},{9,8},{10,11... | collective-permute-start | bytes 1179656 | tf_op jit(solution)/shard_map/ppermute | solution.py:26
  98.4 7.5 %collective-permute-done.4 = bf16[2,2,2,96,256]{4,3,2,1,0:T(8,128)(2,1)S(1)} collective-permute-done((bf16[2,2,2,96,256]{4,3,2,1,0:T(8,128)(2,1)S(1)}, bf16[2,2,2,96,256]{4,3,2,1,0:T(8,128)(2,1)S(1)}, u32[]{:S(2)}, u32[]{:S(2)}) %collective-permute-start.4) | collective-permute-done | bytes 393248 | tf_op jit(solution)/shard_map/ppermute | solution.py:26
  105.9 4.9 %all-to-all-done.2 = bf16[8,2,96,256]{3,2,1,0:T(8,128)(2,1)S(1)} async-done(((bf16[8,2,96,256]{3,2,1,0:T(8,128)(2,1)}), bf16[8,2,96,256]{3,2,1,0:T(8,128)(2,1)S(1)}, u32[]{:S(2)}, u32[]{:S(2)}) %all-to-all-start.2) | async-done | bytes 786464 | tf_op jit(solution)/shard_map/all_to_all | solution.py:247
  111.2 2.4 %collective-permute-start.11 = (f32[128,2,256]{2,0,1:T(8,128)S(1)}, f32[128,2,256]{2,0,1:T(8,128)S(1)}, u32[]{:S(2)}, u32[]{:S(2)}) collective-permute-start(f32[128,2,256]{2,0,1:T(8,128)S(1)} %convolution_bitcast_fusion.2), channel_id=1, source_target_pairs={{0,16},{16,0},{1,17},{17,1},{2,18},{18,2},{3,19},{19,3},{4,20},{20... | collective-permute-start | bytes 786440 | tf_op jit(solution)/shard_map/ppermute | solution.py:263
  113.9 4.3 %collective-permute-start.13 = (bf16[128,2,256]{2,0,1:T(8,128)(2,1)S(1)}, bf16[128,2,256]{2,0,1:T(8,128)(2,1)S(1)}, u32[]{:S(2)}, u32[]{:S(2)}) collective-permute-start(bf16[128,2,256]{2,0,1:T(8,128)(2,1)S(1)} %fusion.4), channel_id=1, source_target_pairs={{0,48},{48,0},{16,32},{32,16},{1,49},{49,1},{17,33},{33,17},{2,50}... | collective-permute-start | bytes 393224 | tf_op jit(solution)/shard_map/ppermute | solution.py:259
  118.6 2.4 %collective-permute-start.12 = (bf16[128,2,256]{2,0,1:T(8,128)(2,1)S(1)}, bf16[128,2,256]{2,0,1:T(8,128)(2,1)S(1)}, u32[]{:S(2)}, u32[]{:S(2)}) collective-permute-start(bf16[128,2,256]{2,0,1:T(8,128)(2,1)S(1)} %fusion.3), channel_id=1, source_target_pairs={{0,32},{32,0},{1,33},{33,1},{2,34},{34,2},{3,35},{35,3},{4,36},{36... | collective-permute-start | bytes 393224 | tf_op jit(solution)/shard_map/ppermute | solution.py:262
  122.4 4.1 %collective-permute-done.12 = bf16[128,2,256]{2,0,1:T(8,128)(2,1)S(1)} collective-permute-done((bf16[128,2,256]{2,0,1:T(8,128)(2,1)S(1)}, bf16[128,2,256]{2,0,1:T(8,128)(2,1)S(1)}, u32[]{:S(2)}, u32[]{:S(2)}) %collective-permute-start.12) | collective-permute-done | bytes 131104 | tf_op jit(solution)/shard_map/ppermute | solution.py:262
  (39 shorter events, 12.0 us)
Async XLA Ops:
  0.7 19.5 %copy-start.3 = (f32[1280]{0:T(1024)S(1)}, f32[1280]{0:T(1024)}, u32[]{:S(2)}) copy-start(f32[1280]{0:T(1024)} %param.10) | copy-start | bytes 15364
  1.7 18.5 %collective-permute-start.5 = (bf16[96,1792]{1,0:T(8,128)(2,1)S(1)}, bf16[96,1792]{1,0:T(8,128)(2,1)S(1)}, u32[]{:S(2)}, u32[]{:S(2)}) collective-permute-start(bf16[96,1792]{1,0:T(8,128)(2,1)S(1)} %maximum_maximum_fusion.mine), channel_id=1, source_target_pairs={{0,16},{16,0},{1,17},{17,1},{2,18},{18,2},{3,19},{19,3},{4,20},{20... | collective-permute-start | bytes 1032200 | tf_op jit(solution)/shard_map/ppermute | solution.py:230
  10.5 15.2 %collective-permute-start.6 = (bf16[96,1792]{1,0:T(8,128)(2,1)S(1)}, bf16[96,1792]{1,0:T(8,128)(2,1)S(1)}, u32[]{:S(2)}, u32[]{:S(2)}) collective-permute-start(bf16[96,1792]{1,0:T(8,128)(2,1)S(1)} %maximum_maximum_fusion.mine), channel_id=1, source_target_pairs={{32,0},{48,16},{64,32},{80,48},{96,64},{112,80},{128,96},{144,112}... | collective-permute-start | bytes 1032200 | tf_op jit(solution)/shard_map/ppermute | solution.py:21
  18.3 12.4 %collective-permute-start.7 = (bf16[96,1792]{1,0:T(8,128)(2,1)S(1)}, bf16[96,1792]{1,0:T(8,128)(2,1)S(1)}, u32[]{:S(2)}, u32[]{:S(2)}) collective-permute-start(bf16[96,1792]{1,0:T(8,128)(2,1)S(1)} %maximum_maximum_fusion.mine), channel_id=1, source_target_pairs={{448,0},{464,16},{480,32},{496,48},{0,64},{16,80},{32,96},{48,112}... | collective-permute-start | bytes 1032200 | tf_op jit(solution)/shard_map/ppermute | solution.py:21
  30.7 0.7 copy-start
  30.7 0.7 copy-start.1
  33.7 7.1 %copy-start.2 = (bf16[96,256]{1,0:T(8,128)(2,1)S(1)}, bf16[96,256]{1,0:T(8,128)(2,1)}, u32[]{:S(2)}) copy-start(bf16[96,256]{1,0:T(8,128)(2,1)} %param.13) | copy-start | bytes 147460
  33.7 15.8 %all-to-all-start = ((bf16[16,24,384]{2,1,0:T(8,128)(2,1)}), bf16[16,24,384]{2,1,0:T(8,128)(2,1)S(1)}, u32[]{:S(2)}, u32[]{:S(2)}) async-start(bf16[16,24,384]{2,1,0:T(8,128)(2,1)} %green.1), calls=%async_computation | async-start | bytes 589824 | tf_op jit(solution)/shard_map/all_to_all | solution.py:234
  40.8 18.4 %collective-permute-start = (bf16[96,256]{1,0:T(8,128)(2,1)S(1)}, bf16[96,256]{1,0:T(8,128)(2,1)S(1)}, u32[]{:S(2)}, u32[]{:S(2)}) collective-permute-start(bf16[96,256]{1,0:T(8,128)(2,1)S(1)} %copy-done.2), channel_id=1, source_target_pairs={{0,4},{1,5},{64,6},{65,7},{128,0},{129,1},{192,2},{193,3},{256,12}... | collective-permute-start | bytes 147464 | tf_op jit(solution)/shard_map/ppermute | solution.py:223
  47.9 11.3 %collective-permute-start.1 = (bf16[96,256]{1,0:T(8,128)(2,1)S(1)}, bf16[96,256]{1,0:T(8,128)(2,1)S(1)}, u32[]{:S(2)}, u32[]{:S(2)}) collective-permute-start(bf16[96,256]{1,0:T(8,128)(2,1)S(1)} %copy-done.2), channel_id=1, source_target_pairs={{0,0},{1,1},{64,2},{65,3},{128,4},{129,5},{192,6},{193,7},{256,8},... | collective-permute-start | bytes 147464 | tf_op jit(solution)/shard_map/ppermute | solution.py:223
  50.2 16.7 %all-to-all-start.1 = ((bf16[16,12,384]{2,1,0:T(8,128)(2,1)}), bf16[16,12,384]{2,1,0:T(8,128)(2,1)S(1)}, u32[]{:S(2)}, u32[]{:S(2)}) async-start(bf16[16,12,384]{2,1,0:T(8,128)(2,1)} %product.1), calls=%async_computation.1 | async-start | bytes 393216 | tf_op jit(solution)/shard_map/all_to_all | solution.py:239
  67.5 15.4 %collective-permute-start.8 = (f32[2,96,256]{2,1,0:T(8,128)S(1)}, f32[2,96,256]{2,1,0:T(8,128)S(1)}, u32[]{:S(2)}, u32[]{:S(2)}) collective-permute-start(f32[2,96,256]{2,1,0:T(8,128)S(1)} %get-tuple-element.10), channel_id=1, source_target_pairs={{0,16},{16,0},{1,17},{17,1},{2,18},{18,2},{3,19},{19,3},{4,20},{20... | collective-permute-start | bytes 589832 | tf_op jit(solution)/shard_map/ppermute | solution.py:245
  73.0 9.8 %collective-permute-start.9 = (bf16[2,96,256]{2,1,0:T(8,128)(2,1)S(1)}, bf16[2,96,256]{2,1,0:T(8,128)(2,1)S(1)}, u32[]{:S(2)}, u32[]{:S(2)}) collective-permute-start(bf16[2,96,256]{2,1,0:T(8,128)(2,1)S(1)} %get-tuple-element.11), channel_id=1, source_target_pairs={{480,0},{496,16},{0,32},{16,48},{32,64},{48,80},{64,96},{80,112},{... | collective-permute-start | bytes 294920 | tf_op jit(solution)/shard_map/ppermute | solution.py:21
  74.9 7.9 %collective-permute-start.10 = (bf16[2,96,256]{2,1,0:T(8,128)(2,1)S(1)}, bf16[2,96,256]{2,1,0:T(8,128)(2,1)S(1)}, u32[]{:S(2)}, u32[]{:S(2)}) collective-permute-start(bf16[2,96,256]{2,1,0:T(8,128)(2,1)S(1)} %get-tuple-element.12), channel_id=1, source_target_pairs={{64,0},{80,16},{96,32},{112,48},{128,64},{144,80},{160,96},{176,11... | collective-permute-start | bytes 294920 | tf_op jit(solution)/shard_map/ppermute | solution.py:21
  77.5 9.9 %collective-permute-start.2 = (bf16[2,96,256]{2,1,0:T(8,128)(2,1)S(1)}, bf16[2,96,256]{2,1,0:T(8,128)(2,1)S(1)}, u32[]{:S(2)}, u32[]{:S(2)}) collective-permute-start(bf16[2,96,256]{2,1,0:T(8,128)(2,1)S(1)} %pad_maximum_fusion.2), channel_id=1, source_target_pairs={{0,2},{1,3},{2,0},{3,1},{4,6},{5,7},{6,4},{7,5},{8,10},{9,11},{10,... | collective-permute-start | bytes 294920 | tf_op jit(solution)/shard_map/ppermute | solution.py:26
  83.8 27.0 %all-to-all-start.2 = ((bf16[8,2,96,256]{3,2,1,0:T(8,128)(2,1)}), bf16[8,2,96,256]{3,2,1,0:T(8,128)(2,1)S(1)}, u32[]{:S(2)}, u32[]{:S(2)}) async-start(bf16[8,2,96,256]{3,2,1,0:T(8,128)(2,1)} %combine.1), calls=%async_computation.2 | async-start | bytes 1572864 | tf_op jit(solution)/shard_map/all_to_all | solution.py:247
  87.4 7.5 %collective-permute-start.3 = (bf16[2,2,96,256]{3,2,1,0:T(8,128)(2,1)S(1)}, bf16[2,2,96,256]{3,2,1,0:T(8,128)(2,1)S(1)}, u32[]{:S(2)}, u32[]{:S(2)}) collective-permute-start(bf16[2,2,96,256]{3,2,1,0:T(8,128)(2,1)S(1)} %pad_maximum_fusion.1), channel_id=1, source_target_pairs={{0,8},{8,0},{1,9},{9,1},{2,10},{10,2},{3,11},{11,3},{4,12},{12,4},... | collective-permute-start | bytes 589832 | tf_op jit(solution)/shard_map/ppermute | solution.py:26
  95.0 10.8 %collective-permute-start.4 = (bf16[2,2,2,96,256]{4,3,2,1,0:T(8,128)(2,1)S(1)}, bf16[2,2,2,96,256]{4,3,2,1,0:T(8,128)(2,1)S(1)}, u32[]{:S(2)}, u32[]{:S(2)}) collective-permute-start(bf16[2,2,2,96,256]{4,3,2,1,0:T(8,128)(2,1)S(1)} %pad_maximum_fusion), channel_id=1, source_target_pairs={{0,1},{1,0},{2,3},{3,2},{4,5},{5,4},{6,7},{7,6},{8,9},{9,8},{10,11... | collective-permute-start | bytes 1179656 | tf_op jit(solution)/shard_map/ppermute | solution.py:26
  111.2 15.4 %collective-permute-start.11 = (f32[128,2,256]{2,0,1:T(8,128)S(1)}, f32[128,2,256]{2,0,1:T(8,128)S(1)}, u32[]{:S(2)}, u32[]{:S(2)}) collective-permute-start(f32[128,2,256]{2,0,1:T(8,128)S(1)} %convolution_bitcast_fusion.2), channel_id=1, source_target_pairs={{0,16},{16,0},{1,17},{17,1},{2,18},{18,2},{3,19},{19,3},{4,20},{20... | collective-permute-start | bytes 786440 | tf_op jit(solution)/shard_map/ppermute | solution.py:263
  113.9 8.5 %collective-permute-start.13 = (bf16[128,2,256]{2,0,1:T(8,128)(2,1)S(1)}, bf16[128,2,256]{2,0,1:T(8,128)(2,1)S(1)}, u32[]{:S(2)}, u32[]{:S(2)}) collective-permute-start(bf16[128,2,256]{2,0,1:T(8,128)(2,1)S(1)} %fusion.4), channel_id=1, source_target_pairs={{0,48},{48,0},{16,32},{32,16},{1,49},{49,1},{17,33},{33,17},{2,50}... | collective-permute-start | bytes 393224 | tf_op jit(solution)/shard_map/ppermute | solution.py:259
  118.6 8.0 %collective-permute-start.12 = (bf16[128,2,256]{2,0,1:T(8,128)(2,1)S(1)}, bf16[128,2,256]{2,0,1:T(8,128)(2,1)S(1)}, u32[]{:S(2)}, u32[]{:S(2)}) collective-permute-start(bf16[128,2,256]{2,0,1:T(8,128)(2,1)S(1)} %fusion.3), channel_id=1, source_target_pairs={{0,32},{32,0},{1,33},{33,1},{2,34},{34,2},{3,35},{35,3},{4,36},{36... | collective-permute-start | bytes 393224 | tf_op jit(solution)/shard_map/ppermute | solution.py:262

commit v7 on v5

--- a/solution.py
+++ b/solution.py
@@ -31,9 +31,9 @@
     return jnp.stack([jnp.where(upper, got, value), jnp.where(upper, value, got)], axis=at)
 
 
-def green_kernel(core, taus, eps_occ, eps_vir, mine, mate, up, down, out, panel, left, total, rows12):
+def green_kernel(core, expo_occ, expo_vir, mine, mate, up, down, out, panel, left, total, rows12):
     rows = mine.shape[0]
-    nocc, cols = eps_occ.shape[1], eps_occ.shape[1] + eps_vir.shape[1]
+    nocc, cols = expo_occ.shape[1], expo_occ.shape[1] + expo_vir.shape[1]
     panel[0:rows] = up[:, :cols]
     panel[rows : 2 * rows] = down[:, :cols]
     panel[2 * rows : 3 * rows] = up[:, :cols]
@@ -47,11 +47,11 @@
         panel[3 * rows : 4 * rows] = down[:, :cols]
 
     for t in range(2):
-        for lo, hi, eps, sign in ((0, nocc, eps_occ, 1.0), (nocc, cols, eps_vir, -1.0)):
-            expo = jnp.exp((sign * taus[t]) * eps[...])
+        for lo, hi, expo in ((0, nocc, expo_occ), (nocc, cols, expo_vir)):
             for s, slab in enumerate((mine, mate)):
                 at = (2 * s + t) * rows
-                left[at : at + rows, lo:hi] = (slab[:, lo:hi].astype(F32) * expo).astype(BF)
+                value = slab[:, lo:hi].astype(F32) * expo[t : t + 1]
+                left[at : at + rows, lo:hi] = value.astype(BF)
     lane = lax.broadcasted_iota(jnp.int32, (2 * rows, 4 * rows), 1)
     for q, (lo, hi) in enumerate(((0, nocc), (nocc, cols))):
         a = lax.dot_general(
@@ -67,12 +67,12 @@
     out[...] = rows12[...].astype(BF)
 
 
-def green(core, taus, eps_occ, eps_vir, mine, mate, up, down):
-    rows, cols = mine.shape[0], eps_occ.shape[1] + eps_vir.shape[1]
+def green(core, expo_occ, expo_vir, mine, mate, up, down):
+    rows, cols = mine.shape[0], expo_occ.shape[1] + expo_vir.shape[1]
     return pl.pallas_call(
         green_kernel,
         out_shape=jax.ShapeDtypeStruct((16, 24, 4 * rows), BF),
-        in_specs=[SCALARS, SCALARS] + [WHOLE] * 6,
+        in_specs=[SCALARS] + [WHOLE] * 6,
         out_specs=WHOLE,
         scratch_shapes=[
             pltpu.VMEM((4 * rows, cols), BF),
@@ -82,10 +82,10 @@
         ],
         compiler_params=pltpu.CompilerParams(vmem_limit_bytes=16 * 2**20),
         cost_estimate=pl.CostEstimate(
-            flops=8 * rows * 4 * rows * cols, bytes_accessed=10 * rows * cols, transcendentals=4 * cols
+            flops=8 * rows * 4 * rows * cols, bytes_accessed=10 * rows * cols, transcendentals=0
         ),
         name="green",
-    )(core, taus, eps_occ, eps_vir, mine, mate, up, down)
+    )(core, expo_occ, expo_vir, mine, mate, up, down)
 
 
 def product_kernel(parts, out, total):
@@ -222,26 +222,20 @@
     up = from_tile(mine, 2)
     down = from_tile(mine, -4)
     mate = lax.ppermute(mine, "core", SWAP)
+    expo_occ = jnp.exp(taus[:, None] * eps_occ[None, :])
+    expo_vir = jnp.exp(-taus[:, None] * eps_vir[None, :])
+    part_sums = green(core.reshape(1), expo_occ, expo_vir, mine, mate, up, down)
     got = []
-    for m in range(4):
+    for far in (0, 4):
         pairs = [
-            ((i // 2) * 16 + 2 * z + i % 2, z * 16 + (i ^ (2 * m)))
-            for z in range(8)
-            for i in range(16)
+            ((i // 2) * 16 + 2 * z + i % 2, z * 16 + (i ^ far)) for z in range(8) for i in range(16)
         ]
         got.append(lax.ppermute(basis, ("z", "xl", "y"), pairs))
-
-    part_sums = green(
-        core.reshape(1), taus, eps_occ[None], eps_vir[None], mine, mate, up, down
-    )
     sums = lax.all_to_all(part_sums, ORB, 0, 0, tiled=True)
-    y = lax.axis_index("y")
-    odd, upper = (y & 2) != 0, (y & 4) != 0
-    got = [jnp.where(odd, got[m ^ 1], got[m]) for m in range(4)]
-    part = jnp.stack([jnp.where(upper, got[m ^ 2], got[m]) for m in range(4)])
-
     both = product(sums)
     both = lax.all_to_all(both, ORB, 0, 0, tiled=True)
+    part = join(got[0], got[1], "y", 4, 0)
+    part = join(part, trade(part, "y", 2), "y", 2, 1)
     part = join(part, trade(part, "xl", 1), "xl", 1, 0)
     to_up, to_down, to_mate, own = project(core.reshape(1), both, mine, mate, up, down, naux)
     got_up = from_tile(to_up, -2)

time: 142 us -> 127 us (0.89); the launches traced: 139 us -> 127 us
  blocking collectives: 28.9 us -> 0 us
  waiting for transfers between devices: 32.9 us -> 43.3 us
  starting transfers between devices: 69.2 us -> 73.8 us
    all_to_all x2 -> x0, blocking collectives: 28.9 us -> none  [the longest x1 15.5 us: on_device(): sums = lax.all_to_all(part_sums, ORB, 0, 0, tiled=True)]
    all_to_all x0 -> x2, starting transfers between devices: none -> 16.1 us  [the longest x1 8.99 us: on_device(): both = lax.all_to_all(both, ORB, 0, 0, tiled=True)]
    all_to_all x1, starting transfers between devices: 14.7 us -> 3.55 us  [on_device(): gathered = lax.all_to_all(copies, 'z', 0, 0, tiled=True)]
    all_to_all x0 -> x2, waiting for transfers between devices: none -> 8.5 us  [the longest x1 7.68 us: on_device(): both = lax.all_to_all(both, ORB, 0, 0, tiled=True)]
    ppermute x2 -> x3, starting transfers between devices: 6.68 us -> 8.92 us  [trade(): return lax.ppermute(value, axis, [(i, i ^ bit) for i in range(size)])]
    ppermute x2 -> x3, waiting for transfers between devices: 10.2 us -> 12.3 us  [trade(): return lax.ppermute(value, axis, [(i, i ^ bit) for i in range(size)])]
    ppermute x4 -> x2, starting transfers between devices: 9.64 us -> 7.84 us  [on_device(): got.append(lax.ppermute(basis, ('z', 'xl', 'y'), pairs))]
    ppermute x4, waiting for transfers between devices: 10.5 us -> 12 us  [from_tile(): return lax.ppermute(value, PTS, [((i + steps) % 32, i) for i in range(32)])]
  transfers between devices with their start and end apart: 16 -> 17, of which waited for: 7 -> 10; matrix products, arithmetic and copies ran while one was open for 1% -> 1% of each run, Pallas kernels for 1% -> 1%
where the time goes in v7:
time: 127 us
  starting transfers between devices  73.8 us (58%)
  waiting for transfers between devices  43.3 us (34%)
  Pallas kernels  4.02 us (3%)
  other arithmetic  2.05 us (2%)
  local copies, waits for them, and re-layouts  1.58 us (1%)
  matrix products  1.29 us (1%)
    ppermute x4, starting transfers between devices, from_tile(): return lax.ppermute(value, PTS, [((i + steps) % 32, i) for i in range(32)])  14.1 us
    ppermute x3, waiting for transfers between devices, trade(): return lax.ppermute(value, axis, [(i, i ^ bit) for i in range(size)])  12.3 us
    ppermute x4, waiting for transfers between devices, from_tile(): return lax.ppermute(value, PTS, [((i + steps) % 32, i) for i in range(32)])  12 us
    all_to_all x1, starting transfers between devices, on_device(): both = lax.all_to_all(both, ORB, 0, 0, tiled=True)  8.99 us
    ppermute x3, starting transfers between devices, trade(): return lax.ppermute(value, axis, [(i, i ^ bit) for i in range(size)])  8.92 us
    ppermute x1, starting transfers between devices, on_device(): mate = lax.ppermute(mine, 'core', SWAP)  8.75 us
    ppermute x2, starting transfers between devices, on_device(): got.append(lax.ppermute(basis, ('z', 'xl', 'y'), pairs))  7.84 us
    all_to_all x1, waiting for transfers between devices, on_device(): both = lax.all_to_all(both, ORB, 0, 0, tiled=True)  7.68 us
  transfers between devices with their start and end apart: 17, of which 10 were waited for; matrix products, arithmetic and copies ran while one was open for 1% of the time, Pallas kernels for 1%

profile of v7, /device:TPU:1, one launch (start us, length us, event | category | flops | bytes accessed | tf_op | source)
XLA Modules:
  0.0 126.6 jit_solution(6041405366038212345)
XLA Ops:
  1.7 8.7 %collective-permute-start.5 = (bf16[96,1792]{1,0:T(8,128)(2,1)S(1)}, bf16[96,1792]{1,0:T(8,128)(2,1)S(1)}, u32[]{:S(2)}, u32[]{:S(2)}) collective-permute-start(bf16[96,1792]{1,0:T(8,128)(2,1)S(1)} %maximum_maximum_fusion.mine), channel_id=1, source_target_pairs={{0,16},{16,0},{1,17},{17,1},{2,18},{18,2},{3,19},{19,3},{4,20},{20... | collective-permute-start | bytes 1032200 | tf_op jit(solution)/shard_map/ppermute | solution.py:224
  10.5 7.8 %collective-permute-start.6 = (bf16[96,1792]{1,0:T(8,128)(2,1)S(1)}, bf16[96,1792]{1,0:T(8,128)(2,1)S(1)}, u32[]{:S(2)}, u32[]{:S(2)}) collective-permute-start(bf16[96,1792]{1,0:T(8,128)(2,1)S(1)} %maximum_maximum_fusion.mine), channel_id=1, source_target_pairs={{32,0},{48,16},{64,32},{80,48},{96,64},{112,80},{128,96},{144,112}... | collective-permute-start | bytes 1032200 | tf_op jit(solution)/shard_map/ppermute | solution.py:21
  18.3 1.9 %collective-permute-start.7 = (bf16[96,1792]{1,0:T(8,128)(2,1)S(1)}, bf16[96,1792]{1,0:T(8,128)(2,1)S(1)}, u32[]{:S(2)}, u32[]{:S(2)}) collective-permute-start(bf16[96,1792]{1,0:T(8,128)(2,1)S(1)} %maximum_maximum_fusion.mine), channel_id=1, source_target_pairs={{448,0},{464,16},{480,32},{496,48},{0,64},{16,80},{32,96},{48,112}... | collective-permute-start | bytes 1032200 | tf_op jit(solution)/shard_map/ppermute | solution.py:21
  21.1 4.6 %collective-permute-done.6.up = bf16[96,1792]{1,0:T(8,128)(2,1)S(1)} collective-permute-done((bf16[96,1792]{1,0:T(8,128)(2,1)S(1)}, bf16[96,1792]{1,0:T(8,128)(2,1)S(1)}, u32[]{:S(2)}, u32[]{:S(2)}) %collective-permute-start.6) | collective-permute-done | bytes 344096 | tf_op jit(solution)/shard_map/ppermute | solution.py:21
  25.7 5.0 %collective-permute-done.7.down = bf16[96,1792]{1,0:T(8,128)(2,1)S(1)} collective-permute-done((bf16[96,1792]{1,0:T(8,128)(2,1)S(1)}, bf16[96,1792]{1,0:T(8,128)(2,1)S(1)}, u32[]{:S(2)}, u32[]{:S(2)}) %collective-permute-start.7) | collective-permute-done | bytes 344096 | tf_op jit(solution)/shard_map/ppermute | solution.py:21
  32.5 7.1 %all-to-all-start = ((bf16[16,24,384]{2,1,0:T(8,128)(2,1)}), bf16[16,24,384]{2,1,0:T(8,128)(2,1)S(1)}, u32[]{:S(2)}, u32[]{:S(2)}) async-start(bf16[16,24,384]{2,1,0:T(8,128)(2,1)} %green.1), calls=%async_computation | async-start | bytes 589824 | tf_op jit(solution)/shard_map/all_to_all | solution.py:234
  39.6 7.2 %collective-permute-start = (bf16[96,256]{1,0:T(8,128)(2,1)S(1)}, bf16[96,256]{1,0:T(8,128)(2,1)S(1)}, u32[]{:S(2)}, u32[]{:S(2)}) collective-permute-start(bf16[96,256]{1,0:T(8,128)(2,1)S(1)} %copy-done), channel_id=1, source_target_pairs={{0,4},{1,5},{64,6},{65,7},{128,0},{129,1},{192,2},{193,3},{256,12}... | collective-permute-start | bytes 147464 | tf_op jit(solution)/shard_map/ppermute | solution.py:233
  49.0 9.0 %all-to-all-start.1 = ((bf16[16,12,384]{2,1,0:T(8,128)(2,1)}), bf16[16,12,384]{2,1,0:T(8,128)(2,1)S(1)}, u32[]{:S(2)}, u32[]{:S(2)}) async-start(bf16[16,12,384]{2,1,0:T(8,128)(2,1)} %product.1), calls=%async_computation.1 | async-start | bytes 393216 | tf_op jit(solution)/shard_map/all_to_all | solution.py:236
  58.0 7.7 %all-to-all-done.1.parts = bf16[16,12,384]{2,1,0:T(8,128)(2,1)S(1)} async-done(((bf16[16,12,384]{2,1,0:T(8,128)(2,1)}), bf16[16,12,384]{2,1,0:T(8,128)(2,1)S(1)}, u32[]{:S(2)}, u32[]{:S(2)}) %all-to-all-start.1) | async-done | bytes 147488 | tf_op jit(solution)/shard_map/all_to_all | solution.py:236
  66.3 5.5 %collective-permute-start.8 = (f32[2,96,256]{2,1,0:T(8,128)S(1)}, f32[2,96,256]{2,1,0:T(8,128)S(1)}, u32[]{:S(2)}, u32[]{:S(2)}) collective-permute-start(f32[2,96,256]{2,1,0:T(8,128)S(1)} %get-tuple-element.10), channel_id=1, source_target_pairs={{0,16},{16,0},{1,17},{17,1},{2,18},{18,2},{3,19},{19,3},{4,20},{20... | collective-permute-start | bytes 589832 | tf_op jit(solution)/shard_map/ppermute | solution.py:243
  71.8 1.9 %collective-permute-start.9 = (bf16[2,96,256]{2,1,0:T(8,128)(2,1)S(1)}, bf16[2,96,256]{2,1,0:T(8,128)(2,1)S(1)}, u32[]{:S(2)}, u32[]{:S(2)}) collective-permute-start(bf16[2,96,256]{2,1,0:T(8,128)(2,1)S(1)} %get-tuple-element.11), channel_id=1, source_target_pairs={{480,0},{496,16},{0,32},{16,48},{32,64},{48,80},{64,96},{80,112},{... | collective-permute-start | bytes 294920 | tf_op jit(solution)/shard_map/ppermute | solution.py:21
  73.7 2.5 %collective-permute-start.10 = (bf16[2,96,256]{2,1,0:T(8,128)(2,1)S(1)}, bf16[2,96,256]{2,1,0:T(8,128)(2,1)S(1)}, u32[]{:S(2)}, u32[]{:S(2)}) collective-permute-start(bf16[2,96,256]{2,1,0:T(8,128)(2,1)S(1)} %get-tuple-element.12), channel_id=1, source_target_pairs={{64,0},{80,16},{96,32},{112,48},{128,64},{144,80},{160,96},{176,11... | collective-permute-start | bytes 294920 | tf_op jit(solution)/shard_map/ppermute | solution.py:21
  76.3 3.0 %collective-permute-start.2 = (bf16[2,96,256]{2,1,0:T(8,128)(2,1)S(1)}, bf16[2,96,256]{2,1,0:T(8,128)(2,1)S(1)}, u32[]{:S(2)}, u32[]{:S(2)}) collective-permute-start(bf16[2,96,256]{2,1,0:T(8,128)(2,1)S(1)} %pad_maximum_fusion.2), channel_id=1, source_target_pairs={{0,2},{1,3},{2,0},{3,1},{4,6},{5,7},{6,4},{7,5},{8,10},{9,11},{10,... | collective-permute-start | bytes 294920 | tf_op jit(solution)/shard_map/ppermute | solution.py:26
  79.3 2.4 %collective-permute-done.9.b = bf16[2,96,256]{2,1,0:T(8,128)(2,1)S(1)} collective-permute-done((bf16[2,96,256]{2,1,0:T(8,128)(2,1)S(1)}, bf16[2,96,256]{2,1,0:T(8,128)(2,1)S(1)}, u32[]{:S(2)}, u32[]{:S(2)}) %collective-permute-start.9) | collective-permute-done | bytes 98336 | tf_op jit(solution)/shard_map/ppermute | solution.py:21
  82.6 3.5 %all-to-all-start.2 = ((bf16[8,2,96,256]{3,2,1,0:T(8,128)(2,1)}), bf16[8,2,96,256]{3,2,1,0:T(8,128)(2,1)S(1)}, u32[]{:S(2)}, u32[]{:S(2)}) async-start(bf16[8,2,96,256]{3,2,1,0:T(8,128)(2,1)} %combine.1), calls=%async_computation.2 | async-start | bytes 1572864 | tf_op jit(solution)/shard_map/all_to_all | solution.py:245
  86.2 2.7 %collective-permute-start.3 = (bf16[2,2,96,256]{3,2,1,0:T(8,128)(2,1)S(1)}, bf16[2,2,96,256]{3,2,1,0:T(8,128)(2,1)S(1)}, u32[]{:S(2)}, u32[]{:S(2)}) collective-permute-start(bf16[2,2,96,256]{3,2,1,0:T(8,128)(2,1)S(1)} %pad_maximum_fusion.1), channel_id=1, source_target_pairs={{0,8},{8,0},{1,9},{9,1},{2,10},{10,2},{3,11},{11,3},{4,12},{12,4},... | collective-permute-start | bytes 589832 | tf_op jit(solution)/shard_map/ppermute | solution.py:26
  88.9 4.8 %collective-permute-done.3 = bf16[2,2,96,256]{3,2,1,0:T(8,128)(2,1)S(1)} collective-permute-done((bf16[2,2,96,256]{3,2,1,0:T(8,128)(2,1)S(1)}, bf16[2,2,96,256]{3,2,1,0:T(8,128)(2,1)S(1)}, u32[]{:S(2)}, u32[]{:S(2)}) %collective-permute-start.3) | collective-permute-done | bytes 196640 | tf_op jit(solution)/shard_map/ppermute | solution.py:26
  93.8 3.2 %collective-permute-start.4 = (bf16[2,2,2,96,256]{4,3,2,1,0:T(8,128)(2,1)S(1)}, bf16[2,2,2,96,256]{4,3,2,1,0:T(8,128)(2,1)S(1)}, u32[]{:S(2)}, u32[]{:S(2)}) collective-permute-start(bf16[2,2,2,96,256]{4,3,2,1,0:T(8,128)(2,1)S(1)} %pad_maximum_fusion), channel_id=1, source_target_pairs={{0,1},{1,0},{2,3},{3,2},{4,5},{5,4},{6,7},{7,6},{8,9},{9,8},{10,11... | collective-permute-start | bytes 1179656 | tf_op jit(solution)/shard_map/ppermute | solution.py:26
  97.2 7.5 %collective-permute-done.4 = bf16[2,2,2,96,256]{4,3,2,1,0:T(8,128)(2,1)S(1)} collective-permute-done((bf16[2,2,2,96,256]{4,3,2,1,0:T(8,128)(2,1)S(1)}, bf16[2,2,2,96,256]{4,3,2,1,0:T(8,128)(2,1)S(1)}, u32[]{:S(2)}, u32[]{:S(2)}) %collective-permute-start.4) | collective-permute-done | bytes 393248 | tf_op jit(solution)/shard_map/ppermute | solution.py:26
  104.7 4.9 %all-to-all-done.2 = bf16[8,2,96,256]{3,2,1,0:T(8,128)(2,1)S(1)} async-done(((bf16[8,2,96,256]{3,2,1,0:T(8,128)(2,1)}), bf16[8,2,96,256]{3,2,1,0:T(8,128)(2,1)S(1)}, u32[]{:S(2)}, u32[]{:S(2)}) %all-to-all-start.2) | async-done | bytes 786464 | tf_op jit(solution)/shard_map/all_to_all | solution.py:245
  110.0 2.4 %collective-permute-start.11 = (f32[128,2,256]{2,0,1:T(8,128)S(1)}, f32[128,2,256]{2,0,1:T(8,128)S(1)}, u32[]{:S(2)}, u32[]{:S(2)}) collective-permute-start(f32[128,2,256]{2,0,1:T(8,128)S(1)} %convolution_bitcast_fusion.2), channel_id=1, source_target_pairs={{0,16},{16,0},{1,17},{17,1},{2,18},{18,2},{3,19},{19,3},{4,20},{20... | collective-permute-start | bytes 786440 | tf_op jit(solution)/shard_map/ppermute | solution.py:261
  112.7 4.3 %collective-permute-start.13 = (bf16[128,2,256]{2,0,1:T(8,128)(2,1)S(1)}, bf16[128,2,256]{2,0,1:T(8,128)(2,1)S(1)}, u32[]{:S(2)}, u32[]{:S(2)}) collective-permute-start(bf16[128,2,256]{2,0,1:T(8,128)(2,1)S(1)} %fusion.4), channel_id=1, source_target_pairs={{0,48},{48,0},{16,32},{32,16},{1,49},{49,1},{17,33},{33,17},{2,50}... | collective-permute-start | bytes 393224 | tf_op jit(solution)/shard_map/ppermute | solution.py:257
  117.4 2.4 %collective-permute-start.12 = (bf16[128,2,256]{2,0,1:T(8,128)(2,1)S(1)}, bf16[128,2,256]{2,0,1:T(8,128)(2,1)S(1)}, u32[]{:S(2)}, u32[]{:S(2)}) collective-permute-start(bf16[128,2,256]{2,0,1:T(8,128)(2,1)S(1)} %fusion.3), channel_id=1, source_target_pairs={{0,32},{32,0},{1,33},{33,1},{2,34},{34,2},{3,35},{35,3},{4,36},{36... | collective-permute-start | bytes 393224 | tf_op jit(solution)/shard_map/ppermute | solution.py:260
  121.2 4.1 %collective-permute-done.12 = bf16[128,2,256]{2,0,1:T(8,128)(2,1)S(1)} collective-permute-done((bf16[128,2,256]{2,0,1:T(8,128)(2,1)S(1)}, bf16[128,2,256]{2,0,1:T(8,128)(2,1)S(1)}, u32[]{:S(2)}, u32[]{:S(2)}) %collective-permute-start.12) | collective-permute-done | bytes 131104 | tf_op jit(solution)/shard_map/ppermute | solution.py:260
  (41 shorter events, 11.9 us)
Async XLA Ops:
  0.7 19.5 %copy-start.3 = (f32[2]{0:T(128)S(1)}, f32[2]{0:T(128)}, u32[]{:S(2)}) copy-start(f32[2]{0:T(128)} %param.11) | copy-start | bytes 28
  1.7 19.2 %copy-start.1 = (f32[1280]{0:T(1024)S(1)}, f32[1280]{0:T(1024)}, u32[]{:S(2)}) copy-start(f32[1280]{0:T(1024)} %param.10) | copy-start | bytes 15364
  1.7 19.3 %collective-permute-start.5 = (bf16[96,1792]{1,0:T(8,128)(2,1)S(1)}, bf16[96,1792]{1,0:T(8,128)(2,1)S(1)}, u32[]{:S(2)}, u32[]{:S(2)}) collective-permute-start(bf16[96,1792]{1,0:T(8,128)(2,1)S(1)} %maximum_maximum_fusion.mine), channel_id=1, source_target_pairs={{0,16},{16,0},{1,17},{17,1},{2,18},{18,2},{3,19},{19,3},{4,20},{20... | collective-permute-start | bytes 1032200 | tf_op jit(solution)/shard_map/ppermute | solution.py:224
  10.5 15.2 %collective-permute-start.6 = (bf16[96,1792]{1,0:T(8,128)(2,1)S(1)}, bf16[96,1792]{1,0:T(8,128)(2,1)S(1)}, u32[]{:S(2)}, u32[]{:S(2)}) collective-permute-start(bf16[96,1792]{1,0:T(8,128)(2,1)S(1)} %maximum_maximum_fusion.mine), channel_id=1, source_target_pairs={{32,0},{48,16},{64,32},{80,48},{96,64},{112,80},{128,96},{144,112}... | collective-permute-start | bytes 1032200 | tf_op jit(solution)/shard_map/ppermute | solution.py:21
  18.3 12.4 %collective-permute-start.7 = (bf16[96,1792]{1,0:T(8,128)(2,1)S(1)}, bf16[96,1792]{1,0:T(8,128)(2,1)S(1)}, u32[]{:S(2)}, u32[]{:S(2)}) collective-permute-start(bf16[96,1792]{1,0:T(8,128)(2,1)S(1)} %maximum_maximum_fusion.mine), channel_id=1, source_target_pairs={{448,0},{464,16},{480,32},{496,48},{0,64},{16,80},{32,96},{48,112}... | collective-permute-start | bytes 1032200 | tf_op jit(solution)/shard_map/ppermute | solution.py:21
  20.2 0.7 copy-start.2
  32.5 7.1 %copy-start = (bf16[96,256]{1,0:T(8,128)(2,1)S(1)}, bf16[96,256]{1,0:T(8,128)(2,1)}, u32[]{:S(2)}) copy-start(bf16[96,256]{1,0:T(8,128)(2,1)} %param.13) | copy-start | bytes 147460
  32.5 15.8 %all-to-all-start = ((bf16[16,24,384]{2,1,0:T(8,128)(2,1)}), bf16[16,24,384]{2,1,0:T(8,128)(2,1)S(1)}, u32[]{:S(2)}, u32[]{:S(2)}) async-start(bf16[16,24,384]{2,1,0:T(8,128)(2,1)} %green.1), calls=%async_computation | async-start | bytes 589824 | tf_op jit(solution)/shard_map/all_to_all | solution.py:234
  39.6 18.4 %collective-permute-start = (bf16[96,256]{1,0:T(8,128)(2,1)S(1)}, bf16[96,256]{1,0:T(8,128)(2,1)S(1)}, u32[]{:S(2)}, u32[]{:S(2)}) collective-permute-start(bf16[96,256]{1,0:T(8,128)(2,1)S(1)} %copy-done), channel_id=1, source_target_pairs={{0,4},{1,5},{64,6},{65,7},{128,0},{129,1},{192,2},{193,3},{256,12}... | collective-permute-start | bytes 147464 | tf_op jit(solution)/shard_map/ppermute | solution.py:233
  46.7 11.3 %collective-permute-start.1 = (bf16[96,256]{1,0:T(8,128)(2,1)S(1)}, bf16[96,256]{1,0:T(8,128)(2,1)S(1)}, u32[]{:S(2)}, u32[]{:S(2)}) collective-permute-start(bf16[96,256]{1,0:T(8,128)(2,1)S(1)} %copy-done), channel_id=1, source_target_pairs={{0,0},{1,1},{64,2},{65,3},{128,4},{129,5},{192,6},{193,7},{256,8},... | collective-permute-start | bytes 147464 | tf_op jit(solution)/shard_map/ppermute | solution.py:233
  49.0 16.7 %all-to-all-start.1 = ((bf16[16,12,384]{2,1,0:T(8,128)(2,1)}), bf16[16,12,384]{2,1,0:T(8,128)(2,1)S(1)}, u32[]{:S(2)}, u32[]{:S(2)}) async-start(bf16[16,12,384]{2,1,0:T(8,128)(2,1)} %product.1), calls=%async_computation.1 | async-start | bytes 393216 | tf_op jit(solution)/shard_map/all_to_all | solution.py:236
  66.3 15.4 %collective-permute-start.8 = (f32[2,96,256]{2,1,0:T(8,128)S(1)}, f32[2,96,256]{2,1,0:T(8,128)S(1)}, u32[]{:S(2)}, u32[]{:S(2)}) collective-permute-start(f32[2,96,256]{2,1,0:T(8,128)S(1)} %get-tuple-element.10), channel_id=1, source_target_pairs={{0,16},{16,0},{1,17},{17,1},{2,18},{18,2},{3,19},{19,3},{4,20},{20... | collective-permute-start | bytes 589832 | tf_op jit(solution)/shard_map/ppermute | solution.py:243
  71.8 9.8 %collective-permute-start.9 = (bf16[2,96,256]{2,1,0:T(8,128)(2,1)S(1)}, bf16[2,96,256]{2,1,0:T(8,128)(2,1)S(1)}, u32[]{:S(2)}, u32[]{:S(2)}) collective-permute-start(bf16[2,96,256]{2,1,0:T(8,128)(2,1)S(1)} %get-tuple-element.11), channel_id=1, source_target_pairs={{480,0},{496,16},{0,32},{16,48},{32,64},{48,80},{64,96},{80,112},{... | collective-permute-start | bytes 294920 | tf_op jit(solution)/shard_map/ppermute | solution.py:21
  73.7 7.9 %collective-permute-start.10 = (bf16[2,96,256]{2,1,0:T(8,128)(2,1)S(1)}, bf16[2,96,256]{2,1,0:T(8,128)(2,1)S(1)}, u32[]{:S(2)}, u32[]{:S(2)}) collective-permute-start(bf16[2,96,256]{2,1,0:T(8,128)(2,1)S(1)} %get-tuple-element.12), channel_id=1, source_target_pairs={{64,0},{80,16},{96,32},{112,48},{128,64},{144,80},{160,96},{176,11... | collective-permute-start | bytes 294920 | tf_op jit(solution)/shard_map/ppermute | solution.py:21
  76.3 9.9 %collective-permute-start.2 = (bf16[2,96,256]{2,1,0:T(8,128)(2,1)S(1)}, bf16[2,96,256]{2,1,0:T(8,128)(2,1)S(1)}, u32[]{:S(2)}, u32[]{:S(2)}) collective-permute-start(bf16[2,96,256]{2,1,0:T(8,128)(2,1)S(1)} %pad_maximum_fusion.2), channel_id=1, source_target_pairs={{0,2},{1,3},{2,0},{3,1},{4,6},{5,7},{6,4},{7,5},{8,10},{9,11},{10,... | collective-permute-start | bytes 294920 | tf_op jit(solution)/shard_map/ppermute | solution.py:26
  82.6 27.0 %all-to-all-start.2 = ((bf16[8,2,96,256]{3,2,1,0:T(8,128)(2,1)}), bf16[8,2,96,256]{3,2,1,0:T(8,128)(2,1)S(1)}, u32[]{:S(2)}, u32[]{:S(2)}) async-start(bf16[8,2,96,256]{3,2,1,0:T(8,128)(2,1)} %combine.1), calls=%async_computation.2 | async-start | bytes 1572864 | tf_op jit(solution)/shard_map/all_to_all | solution.py:245
  86.2 7.5 %collective-permute-start.3 = (bf16[2,2,96,256]{3,2,1,0:T(8,128)(2,1)S(1)}, bf16[2,2,96,256]{3,2,1,0:T(8,128)(2,1)S(1)}, u32[]{:S(2)}, u32[]{:S(2)}) collective-permute-start(bf16[2,2,96,256]{3,2,1,0:T(8,128)(2,1)S(1)} %pad_maximum_fusion.1), channel_id=1, source_target_pairs={{0,8},{8,0},{1,9},{9,1},{2,10},{10,2},{3,11},{11,3},{4,12},{12,4},... | collective-permute-start | bytes 589832 | tf_op jit(solution)/shard_map/ppermute | solution.py:26
  93.8 10.8 %collective-permute-start.4 = (bf16[2,2,2,96,256]{4,3,2,1,0:T(8,128)(2,1)S(1)}, bf16[2,2,2,96,256]{4,3,2,1,0:T(8,128)(2,1)S(1)}, u32[]{:S(2)}, u32[]{:S(2)}) collective-permute-start(bf16[2,2,2,96,256]{4,3,2,1,0:T(8,128)(2,1)S(1)} %pad_maximum_fusion), channel_id=1, source_target_pairs={{0,1},{1,0},{2,3},{3,2},{4,5},{5,4},{6,7},{7,6},{8,9},{9,8},{10,11... | collective-permute-start | bytes 1179656 | tf_op jit(solution)/shard_map/ppermute | solution.py:26
  110.0 15.4 %collective-permute-start.11 = (f32[128,2,256]{2,0,1:T(8,128)S(1)}, f32[128,2,256]{2,0,1:T(8,128)S(1)}, u32[]{:S(2)}, u32[]{:S(2)}) collective-permute-start(f32[128,2,256]{2,0,1:T(8,128)S(1)} %convolution_bitcast_fusion.2), channel_id=1, source_target_pairs={{0,16},{16,0},{1,17},{17,1},{2,18},{18,2},{3,19},{19,3},{4,20},{20... | collective-permute-start | bytes 786440 | tf_op jit(solution)/shard_map/ppermute | solution.py:261
  112.7 8.5 %collective-permute-start.13 = (bf16[128,2,256]{2,0,1:T(8,128)(2,1)S(1)}, bf16[128,2,256]{2,0,1:T(8,128)(2,1)S(1)}, u32[]{:S(2)}, u32[]{:S(2)}) collective-permute-start(bf16[128,2,256]{2,0,1:T(8,128)(2,1)S(1)} %fusion.4), channel_id=1, source_target_pairs={{0,48},{48,0},{16,32},{32,16},{1,49},{49,1},{17,33},{33,17},{2,50}... | collective-permute-start | bytes 393224 | tf_op jit(solution)/shard_map/ppermute | solution.py:257
  117.4 8.0 %collective-permute-start.12 = (bf16[128,2,256]{2,0,1:T(8,128)(2,1)S(1)}, bf16[128,2,256]{2,0,1:T(8,128)(2,1)S(1)}, u32[]{:S(2)}, u32[]{:S(2)}) collective-permute-start(bf16[128,2,256]{2,0,1:T(8,128)(2,1)S(1)} %fusion.3), channel_id=1, source_target_pairs={{0,32},{32,0},{1,33},{33,1},{2,34},{34,2},{3,35},{35,3},{4,36},{36... | collective-permute-start | bytes 393224 | tf_op jit(solution)/shard_map/ppermute | solution.py:260

commit v8 on v7

--- a/solution.py
+++ b/solution.py
@@ -212,6 +212,26 @@
     )(own, a, b, c)
 
 
+def finish_kernel(own, beside, across, diag, out):
+    for t in range(2):
+        out[:, t, :] = own[t] + beside[t] + across[t].astype(F32) + diag[t].astype(F32)
+
+
+def finish(own, beside, across, diag):
+    times, count, naux = own.shape
+    return pl.pallas_call(
+        finish_kernel,
+        out_shape=jax.ShapeDtypeStruct((count, times, naux), F32),
+        in_specs=[WHOLE] * 4,
+        out_specs=WHOLE,
+        compiler_params=pltpu.CompilerParams(vmem_limit_bytes=8 * 2**20),
+        cost_estimate=pl.CostEstimate(
+            flops=4 * own.size, bytes_accessed=16 * own.size, transcendentals=0
+        ),
+        name="finish",
+    )(own, beside, across, diag)
+
+
 def on_device(phi_occ, phi_vir, eps_occ, eps_vir, taus, pair_mask, basis):
     core, xh = lax.axis_index("core"), lax.axis_index("xh")
     naux, rows = basis.shape[1], phi_occ.shape[0]
@@ -234,17 +254,24 @@
     sums = lax.all_to_all(part_sums, ORB, 0, 0, tiled=True)
     both = product(sums)
     both = lax.all_to_all(both, ORB, 0, 0, tiled=True)
-    part = join(got[0], got[1], "y", 4, 0)
-    part = join(part, trade(part, "y", 2), "y", 2, 1)
-    part = join(part, trade(part, "xl", 1), "xl", 1, 0)
     to_up, to_down, to_mate, own = project(core.reshape(1), both, mine, mate, up, down, naux)
     got_up = from_tile(to_up, -2)
     got_down = from_tile(to_down, 4)
     got_mate = lax.ppermute(to_mate, "core", SWAP)
     copies = combine(own, got_mate, got_up, got_down)
     gathered = lax.all_to_all(copies, "z", 0, 0, tiled=True)
-    part = join(part, trade(part, "y", 1), "y", 1, 0)
-    blocks = part.reshape(2, 8, rows, naux)
+    part = join(got[0], got[1], "y", 4, 0)
+    part = join(part, trade(part, "y", 2), "y", 2, 1)
+    others = [part]
+    for flip in (9, 8, 1):
+        others.append(lax.ppermute(part, ORB, [(i, i ^ flip) for i in range(16)]))
+    _, both, across_xl, across_y = others
+    odd, right = (lax.axis_index("y") & 1) != 0, lax.axis_index("xl") != 0
+    a = [jnp.where(odd, across_y, part), jnp.where(odd, part, across_y)]
+    b = [jnp.where(odd, both, across_xl), jnp.where(odd, across_xl, both)]
+    blocks = jnp.stack(
+        [jnp.stack([jnp.where(right, b[h], a[h]), jnp.where(right, a[h], b[h])]) for h in range(2)]
+    ).reshape(2, 8, rows, naux)
     at = xh * 2 + core
 
     def response(flip):
@@ -252,14 +279,14 @@
         chosen = lax.dynamic_slice(
             blocks, (j // 2, 0, 0, (j % 2) * (naux // 2)), (1, 8, rows, naux // 2)
         )[0]
-        return jnp.einsum("zrp,ztrq->ptq", chosen, gathered, preferred_element_type=F32)
+        return jnp.einsum("zrp,ztrq->tpq", chosen, gathered, preferred_element_type=F32)
 
     both_way = lax.ppermute(
         response(3).astype(BF), ("xh", "core"), [(0, 3), (3, 0), (1, 2), (2, 1)]
     )
     across = lax.ppermute(response(2).astype(BF), "xh", SWAP)
     beside = lax.ppermute(response(1), "core", SWAP)
-    return response(0) + beside + across.astype(F32) + both_way.astype(F32)
+    return finish(response(0), beside, across, both_way)
 
 
 def solution(mesh):

time: 127 us -> 132 us (1.039)
  blocking collectives: 0 us -> 28.8 us
  waiting for transfers between devices: 43.3 us -> 24.4 us
  starting transfers between devices: 73.8 us -> 70.3 us
    all_to_all x0 -> x2, blocking collectives: none -> 28.8 us  [the longest x1 15.5 us: on_device(): sums = lax.all_to_all(part_sums, ORB, 0, 0, tiled=True)]
    all_to_all x2 -> x0, starting transfers between devices: 16.1 us -> none  [the longest x1 8.99 us: on_device(): both = lax.all_to_all(both, ORB, 0, 0, tiled=True)]
    ppermute x0 -> x3, starting transfers between devices: none -> 11.6 us  [on_device(): others.append(lax.ppermute(part, ORB, [(i, i ^ flip) for i in range(16)]))]
    ppermute x3 -> x1, waiting for transfers between devices: 12.3 us -> 2.03 us  [trade(): return lax.ppermute(value, axis, [(i, i ^ bit) for i in range(size)])]
    all_to_all x2 -> x0, waiting for transfers between devices: 8.5 us -> none  [the longest x1 7.68 us: on_device(): both = lax.all_to_all(both, ORB, 0, 0, tiled=True)]
    ppermute x0 -> x3, waiting for transfers between devices: none -> 6.07 us  [on_device(): others.append(lax.ppermute(part, ORB, [(i, i ^ flip) for i in range(16)]))]
    all_to_all x1, starting transfers between devices: 3.55 us -> 8.79 us  [on_device(): gathered = lax.all_to_all(copies, 'z', 0, 0, tiled=True)]
    all_to_all x1, waiting for transfers between devices: 4.95 us -> 0.01 us  [on_device(): gathered = lax.all_to_all(copies, 'z', 0, 0, tiled=True)]
  transfers between devices with their start and end apart: 17 -> 16, of which waited for: 10 -> 8; matrix products, arithmetic and copies ran while one was open for 1% -> 1% of each run, Pallas kernels for 1% -> 1%
where the time goes in v8:
time: 132 us; the launch traced here: 131 us
  starting transfers between devices  70.3 us (53%)
  blocking collectives  28.8 us (22%)
  waiting for transfers between devices  24.4 us (18%)
  Pallas kernels  3.41 us (3%)
  other arithmetic  2.07 us (2%)
  matrix products  1.34 us (1%)
    all_to_all x1, blocking collectives, on_device(): sums = lax.all_to_all(part_sums, ORB, 0, 0, tiled=True)  15.5 us
    ppermute x4, starting transfers between devices, from_tile(): return lax.ppermute(value, PTS, [((i + steps) % 32, i) for i in range(32)])  15.2 us
    all_to_all x1, blocking collectives, on_device(): both = lax.all_to_all(both, ORB, 0, 0, tiled=True)  13.3 us
    ppermute x3, starting transfers between devices, on_device(): others.append(lax.ppermute(part, ORB, [(i, i ^ flip) for i in range(16)]))  11.6 us
    ppermute x4, waiting for transfers between devices, from_tile(): return lax.ppermute(value, PTS, [((i + steps) % 32, i) for i in range(32)])  9.73 us
    all_to_all x1, starting transfers between devices, on_device(): gathered = lax.all_to_all(copies, 'z', 0, 0, tiled=True)  8.79 us
    ppermute x1, starting transfers between devices, on_device(): mate = lax.ppermute(mine, 'core', SWAP)  8.75 us
    ppermute x1, starting transfers between devices, on_device(): across = lax.ppermute(response(2).astype(BF), 'xh', SWAP)  6.8 us
  transfers between devices with their start and end apart: 16, of which 8 were waited for; matrix products, arithmetic and copies ran while one was open for 1% of the time, Pallas kernels for 1%

profile of v8, /device:TPU:1, one launch (start us, length us, event | category | flops | bytes accessed | tf_op | source)
XLA Modules:
  0.0 131.5 jit_solution(556588495644040571)
XLA Ops:
  1.7 8.7 %collective-permute-start = (bf16[96,1792]{1,0:T(8,128)(2,1)S(1)}, bf16[96,1792]{1,0:T(8,128)(2,1)S(1)}, u32[]{:S(2)}, u32[]{:S(2)}) collective-permute-start(bf16[96,1792]{1,0:T(8,128)(2,1)S(1)} %maximum_maximum_fusion.mine), channel_id=1, source_target_pairs={{0,16},{16,0},{1,17},{17,1},{2,18},{18,2},{3,19},{19,3},{4,20},{20... | collective-permute-start | bytes 1032200 | tf_op jit(solution)/shard_map/ppermute | solution.py:244
  10.5 7.8 %collective-permute-start.1 = (bf16[96,1792]{1,0:T(8,128)(2,1)S(1)}, bf16[96,1792]{1,0:T(8,128)(2,1)S(1)}, u32[]{:S(2)}, u32[]{:S(2)}) collective-permute-start(bf16[96,1792]{1,0:T(8,128)(2,1)S(1)} %maximum_maximum_fusion.mine), channel_id=1, source_target_pairs={{32,0},{48,16},{64,32},{80,48},{96,64},{112,80},{128,96},{144,112}... | collective-permute-start | bytes 1032200 | tf_op jit(solution)/shard_map/ppermute | solution.py:21
  18.3 1.9 %collective-permute-start.2 = (bf16[96,1792]{1,0:T(8,128)(2,1)S(1)}, bf16[96,1792]{1,0:T(8,128)(2,1)S(1)}, u32[]{:S(2)}, u32[]{:S(2)}) collective-permute-start(bf16[96,1792]{1,0:T(8,128)(2,1)S(1)} %maximum_maximum_fusion.mine), channel_id=1, source_target_pairs={{448,0},{464,16},{480,32},{496,48},{0,64},{16,80},{32,96},{48,112}... | collective-permute-start | bytes 1032200 | tf_op jit(solution)/shard_map/ppermute | solution.py:21
  21.1 4.6 %collective-permute-done.1.up = bf16[96,1792]{1,0:T(8,128)(2,1)S(1)} collective-permute-done((bf16[96,1792]{1,0:T(8,128)(2,1)S(1)}, bf16[96,1792]{1,0:T(8,128)(2,1)S(1)}, u32[]{:S(2)}, u32[]{:S(2)}) %collective-permute-start.1) | collective-permute-done | bytes 344096 | tf_op jit(solution)/shard_map/ppermute | solution.py:21
  25.7 5.0 %collective-permute-done.2.down = bf16[96,1792]{1,0:T(8,128)(2,1)S(1)} collective-permute-done((bf16[96,1792]{1,0:T(8,128)(2,1)S(1)}, bf16[96,1792]{1,0:T(8,128)(2,1)S(1)}, u32[]{:S(2)}, u32[]{:S(2)}) %collective-permute-start.2) | collective-permute-done | bytes 344096 | tf_op jit(solution)/shard_map/ppermute | solution.py:21
  31.7 15.5 %all_to_all.15.parts = bf16[16,24,384]{2,1,0:T(8,128)(2,1)S(1)} all-to-all(bf16[16,24,384]{2,1,0:T(8,128)(2,1)S(1)} %green.1), channel_id=1, replica_groups=mesh['z'=8,'xh'=2,'core'=2,'xl'=2,'y'=8] {'xl','y'}, dimensions={0} | all-to-all | bytes 589824 | tf_op jit(solution)/shard_map/all_to_all | solution.py:254
  47.3 13.3 %all_to_all.16.parts = bf16[16,12,384]{2,1,0:T(8,128)(2,1)S(1)} all-to-all(bf16[16,12,384]{2,1,0:T(8,128)(2,1)S(1)} %product.1), channel_id=1, replica_groups=mesh['z'=8,'xh'=2,'core'=2,'xl'=2,'y'=8] {'xl','y'}, dimensions={0} | all-to-all | bytes 294912 | tf_op jit(solution)/shard_map/all_to_all | solution.py:256
  61.2 4.9 %collective-permute-start.3 = (f32[2,96,256]{2,1,0:T(8,128)S(1)}, f32[2,96,256]{2,1,0:T(8,128)S(1)}, u32[]{:S(2)}, u32[]{:S(2)}) collective-permute-start(f32[2,96,256]{2,1,0:T(8,128)S(1)} %get-tuple-element.10), channel_id=1, source_target_pairs={{0,16},{16,0},{1,17},{17,1},{2,18},{18,2},{3,19},{19,3},{4,20},{20... | collective-permute-start | bytes 589832 | tf_op jit(solution)/shard_map/ppermute | solution.py:260
  66.2 1.9 %collective-permute-start.4 = (bf16[2,96,256]{2,1,0:T(8,128)(2,1)S(1)}, bf16[2,96,256]{2,1,0:T(8,128)(2,1)S(1)}, u32[]{:S(2)}, u32[]{:S(2)}) collective-permute-start(bf16[2,96,256]{2,1,0:T(8,128)(2,1)S(1)} %get-tuple-element.11), channel_id=1, source_target_pairs={{480,0},{496,16},{0,32},{16,48},{32,64},{48,80},{64,96},{80,112},{... | collective-permute-start | bytes 294920 | tf_op jit(solution)/shard_map/ppermute | solution.py:21
  68.1 3.6 %collective-permute-start.5 = (bf16[2,96,256]{2,1,0:T(8,128)(2,1)S(1)}, bf16[2,96,256]{2,1,0:T(8,128)(2,1)S(1)}, u32[]{:S(2)}, u32[]{:S(2)}) collective-permute-start(bf16[2,96,256]{2,1,0:T(8,128)(2,1)S(1)} %get-tuple-element.12), channel_id=1, source_target_pairs={{64,0},{80,16},{96,32},{112,48},{128,64},{144,80},{160,96},{176,11... | collective-permute-start | bytes 294920 | tf_op jit(solution)/shard_map/ppermute | solution.py:21
  71.7 3.6 %collective-permute-start.6 = (bf16[96,256]{1,0:T(8,128)(2,1)S(1)}, bf16[96,256]{1,0:T(8,128)(2,1)S(1)}, u32[]{:S(2)}, u32[]{:S(2)}) collective-permute-start(bf16[96,256]{1,0:T(8,128)(2,1)S(1)} %copy-done), channel_id=1, source_target_pairs={{0,4},{1,5},{64,6},{65,7},{128,0},{129,1},{192,2},{193,3},{256,12}... | collective-permute-start | bytes 147464 | tf_op jit(solution)/shard_map/ppermute | solution.py:253
  77.0 8.8 %all-to-all-start.2 = ((bf16[8,2,96,256]{3,2,1,0:T(8,128)(2,1)}), bf16[8,2,96,256]{3,2,1,0:T(8,128)(2,1)S(1)}, u32[]{:S(2)}, u32[]{:S(2)}) async-start(bf16[8,2,96,256]{3,2,1,0:T(8,128)(2,1)} %combine.1), calls=%async_computation.2 | async-start | bytes 1572864 | tf_op jit(solution)/shard_map/all_to_all | solution.py:262
  85.8 4.2 %collective-permute-start.8 = (bf16[2,96,256]{2,1,0:T(8,128)(2,1)S(1)}, bf16[2,96,256]{2,1,0:T(8,128)(2,1)S(1)}, u32[]{:S(2)}, u32[]{:S(2)}) collective-permute-start(bf16[2,96,256]{2,1,0:T(8,128)(2,1)S(1)} %pad_maximum_fusion.3), channel_id=1, source_target_pairs={{0,2},{1,3},{2,0},{3,1},{4,6},{5,7},{6,4},{7,5},{8,10},{9,11},{10,... | collective-permute-start | bytes 294920 | tf_op jit(solution)/shard_map/ppermute | solution.py:26
  90.1 2.0 %collective-permute-done.8 = bf16[2,96,256]{2,1,0:T(8,128)(2,1)S(1)} collective-permute-done((bf16[2,96,256]{2,1,0:T(8,128)(2,1)S(1)}, bf16[2,96,256]{2,1,0:T(8,128)(2,1)S(1)}, u32[]{:S(2)}, u32[]{:S(2)}) %collective-permute-start.8) | collective-permute-done | bytes 98336 | tf_op jit(solution)/shard_map/ppermute | solution.py:26
  92.1 6.6 %collective-permute-start.10 = (bf16[2,2,96,256]{3,2,1,0:T(8,128)(2,1)S(1)}, bf16[2,2,96,256]{3,2,1,0:T(8,128)(2,1)S(1)}, u32[]{:S(2)}, u32[]{:S(2)}) collective-permute-start(bf16[2,2,96,256]{3,2,1,0:T(8,128)(2,1)S(1)} %pad_maximum_fusion.2), channel_id=1, source_target_pairs={{0,8},{1,9},{2,10},{3,11},{4,12},{5,13},{6,14},{7,15},{8,0},{9,1},... | collective-permute-start | bytes 589832 | tf_op jit(solution)/shard_map/ppermute | solution.py:267
  98.7 1.9 %collective-permute-start.9 = (bf16[2,2,96,256]{3,2,1,0:T(8,128)(2,1)S(1)}, bf16[2,2,96,256]{3,2,1,0:T(8,128)(2,1)S(1)}, u32[]{:S(2)}, u32[]{:S(2)}) collective-permute-start(bf16[2,2,96,256]{3,2,1,0:T(8,128)(2,1)S(1)} %pad_maximum_fusion.2), channel_id=1, source_target_pairs={{0,9},{1,8},{2,11},{3,10},{4,13},{5,12},{6,15},{7,14},{8,1},{9,0},... | collective-permute-start | bytes 589832 | tf_op jit(solution)/shard_map/ppermute | solution.py:267
  100.7 3.1 %collective-permute-start.11 = (bf16[2,2,96,256]{3,2,1,0:T(8,128)(2,1)S(1)}, bf16[2,2,96,256]{3,2,1,0:T(8,128)(2,1)S(1)}, u32[]{:S(2)}, u32[]{:S(2)}) collective-permute-start(bf16[2,2,96,256]{3,2,1,0:T(8,128)(2,1)S(1)} %pad_maximum_fusion.2), channel_id=1, source_target_pairs={{0,1},{1,0},{2,3},{3,2},{4,5},{5,4},{6,7},{7,6},{8,9},{9,8},{10,11... | collective-permute-start | bytes 589832 | tf_op jit(solution)/shard_map/ppermute | solution.py:267
  103.9 2.7 %collective-permute-done.9 = bf16[2,2,96,256]{3,2,1,0:T(8,128)(2,1)S(1)} collective-permute-done((bf16[2,2,96,256]{3,2,1,0:T(8,128)(2,1)S(1)}, bf16[2,2,96,256]{3,2,1,0:T(8,128)(2,1)S(1)}, u32[]{:S(2)}, u32[]{:S(2)}) %collective-permute-start.9) | collective-permute-done | bytes 196640 | tf_op jit(solution)/shard_map/ppermute | solution.py:267
  106.6 3.4 %collective-permute-done.11 = bf16[2,2,96,256]{3,2,1,0:T(8,128)(2,1)S(1)} collective-permute-done((bf16[2,2,96,256]{3,2,1,0:T(8,128)(2,1)S(1)}, bf16[2,2,96,256]{3,2,1,0:T(8,128)(2,1)S(1)}, u32[]{:S(2)}, u32[]{:S(2)}) %collective-permute-start.11) | collective-permute-done | bytes 196640 | tf_op jit(solution)/shard_map/ppermute | solution.py:267
  110.5 3.9 %collective-permute-start.12 = (f32[2,128,256]{2,1,0:T(8,128)S(1)}, f32[2,128,256]{2,1,0:T(8,128)S(1)}, u32[]{:S(2)}, u32[]{:S(2)}) collective-permute-start(f32[2,128,256]{2,1,0:T(8,128)S(1)} %convolution_bitcast_fusion.2), channel_id=1, source_target_pairs={{0,16},{16,0},{1,17},{17,1},{2,18},{18,2},{3,19},{19,3},{4,20},{20... | collective-permute-start | bytes 786440 | tf_op jit(solution)/shard_map/ppermute | solution.py:288
  114.7 6.8 %collective-permute-start.13 = (bf16[2,128,256]{2,1,0:T(8,128)(2,1)S(1)}, bf16[2,128,256]{2,1,0:T(8,128)(2,1)S(1)}, u32[]{:S(2)}, u32[]{:S(2)}) collective-permute-start(bf16[2,128,256]{2,1,0:T(8,128)(2,1)S(1)} %fusion.3), channel_id=1, source_target_pairs={{0,32},{32,0},{1,33},{33,1},{2,34},{34,2},{3,35},{35,3},{4,36},{36... | collective-permute-start | bytes 393224 | tf_op jit(solution)/shard_map/ppermute | solution.py:287
  121.9 1.9 %collective-permute-start.14 = (bf16[2,128,256]{2,1,0:T(8,128)(2,1)S(1)}, bf16[2,128,256]{2,1,0:T(8,128)(2,1)S(1)}, u32[]{:S(2)}, u32[]{:S(2)}) collective-permute-start(bf16[2,128,256]{2,1,0:T(8,128)(2,1)S(1)} %fusion.2), channel_id=1, source_target_pairs={{0,48},{48,0},{16,32},{32,16},{1,49},{49,1},{17,33},{33,17},{2,50}... | collective-permute-start | bytes 393224 | tf_op jit(solution)/shard_map/ppermute | solution.py:284
  124.1 1.2 collective-permute-done.13.across
  125.3 5.3 %collective-permute-done.14.diag = bf16[2,128,256]{2,1,0:T(8,128)(2,1)S(1)} collective-permute-done((bf16[2,128,256]{2,1,0:T(8,128)(2,1)S(1)}, bf16[2,128,256]{2,1,0:T(8,128)(2,1)S(1)}, u32[]{:S(2)}, u32[]{:S(2)}) %collective-permute-start.14) | collective-permute-done | bytes 131104 | tf_op jit(solution)/shard_map/ppermute | solution.py:284
  (40 shorter events, 8.2 us)
Async XLA Ops:
  0.7 19.5 %copy-start.3 = (f32[2]{0:T(128)S(1)}, f32[2]{0:T(128)}, u32[]{:S(2)}) copy-start(f32[2]{0:T(128)} %param.11) | copy-start | bytes 28
  1.7 19.2 %copy-start.1 = (f32[1280]{0:T(1024)S(1)}, f32[1280]{0:T(1024)}, u32[]{:S(2)}) copy-start(f32[1280]{0:T(1024)} %param.10) | copy-start | bytes 15364
  1.7 19.3 %collective-permute-start = (bf16[96,1792]{1,0:T(8,128)(2,1)S(1)}, bf16[96,1792]{1,0:T(8,128)(2,1)S(1)}, u32[]{:S(2)}, u32[]{:S(2)}) collective-permute-start(bf16[96,1792]{1,0:T(8,128)(2,1)S(1)} %maximum_maximum_fusion.mine), channel_id=1, source_target_pairs={{0,16},{16,0},{1,17},{17,1},{2,18},{18,2},{3,19},{19,3},{4,20},{20... | collective-permute-start | bytes 1032200 | tf_op jit(solution)/shard_map/ppermute | solution.py:244
  10.5 15.2 %collective-permute-start.1 = (bf16[96,1792]{1,0:T(8,128)(2,1)S(1)}, bf16[96,1792]{1,0:T(8,128)(2,1)S(1)}, u32[]{:S(2)}, u32[]{:S(2)}) collective-permute-start(bf16[96,1792]{1,0:T(8,128)(2,1)S(1)} %maximum_maximum_fusion.mine), channel_id=1, source_target_pairs={{32,0},{48,16},{64,32},{80,48},{96,64},{112,80},{128,96},{144,112}... | collective-permute-start | bytes 1032200 | tf_op jit(solution)/shard_map/ppermute | solution.py:21
  18.3 12.4 %collective-permute-start.2 = (bf16[96,1792]{1,0:T(8,128)(2,1)S(1)}, bf16[96,1792]{1,0:T(8,128)(2,1)S(1)}, u32[]{:S(2)}, u32[]{:S(2)}) collective-permute-start(bf16[96,1792]{1,0:T(8,128)(2,1)S(1)} %maximum_maximum_fusion.mine), channel_id=1, source_target_pairs={{448,0},{464,16},{480,32},{496,48},{0,64},{16,80},{32,96},{48,112}... | collective-permute-start | bytes 1032200 | tf_op jit(solution)/shard_map/ppermute | solution.py:21
  20.2 0.7 copy-start.2
  60.7 11.0 %copy-start = (bf16[96,256]{1,0:T(8,128)(2,1)S(1)}, bf16[96,256]{1,0:T(8,128)(2,1)}, u32[]{:S(2)}) copy-start(bf16[96,256]{1,0:T(8,128)(2,1)} %param.13) | copy-start | bytes 147460
  61.2 14.8 %collective-permute-start.3 = (f32[2,96,256]{2,1,0:T(8,128)S(1)}, f32[2,96,256]{2,1,0:T(8,128)S(1)}, u32[]{:S(2)}, u32[]{:S(2)}) collective-permute-start(f32[2,96,256]{2,1,0:T(8,128)S(1)} %get-tuple-element.10), channel_id=1, source_target_pairs={{0,16},{16,0},{1,17},{17,1},{2,18},{18,2},{3,19},{19,3},{4,20},{20... | collective-permute-start | bytes 589832 | tf_op jit(solution)/shard_map/ppermute | solution.py:260
  66.2 9.8 %collective-permute-start.4 = (bf16[2,96,256]{2,1,0:T(8,128)(2,1)S(1)}, bf16[2,96,256]{2,1,0:T(8,128)(2,1)S(1)}, u32[]{:S(2)}, u32[]{:S(2)}) collective-permute-start(bf16[2,96,256]{2,1,0:T(8,128)(2,1)S(1)} %get-tuple-element.11), channel_id=1, source_target_pairs={{480,0},{496,16},{0,32},{16,48},{32,64},{48,80},{64,96},{80,112},{... | collective-permute-start | bytes 294920 | tf_op jit(solution)/shard_map/ppermute | solution.py:21
  68.1 7.9 %collective-permute-start.5 = (bf16[2,96,256]{2,1,0:T(8,128)(2,1)S(1)}, bf16[2,96,256]{2,1,0:T(8,128)(2,1)S(1)}, u32[]{:S(2)}, u32[]{:S(2)}) collective-permute-start(bf16[2,96,256]{2,1,0:T(8,128)(2,1)S(1)} %get-tuple-element.12), channel_id=1, source_target_pairs={{64,0},{80,16},{96,32},{112,48},{128,64},{144,80},{160,96},{176,11... | collective-permute-start | bytes 294920 | tf_op jit(solution)/shard_map/ppermute | solution.py:21
  71.7 14.1 %collective-permute-start.6 = (bf16[96,256]{1,0:T(8,128)(2,1)S(1)}, bf16[96,256]{1,0:T(8,128)(2,1)S(1)}, u32[]{:S(2)}, u32[]{:S(2)}) collective-permute-start(bf16[96,256]{1,0:T(8,128)(2,1)S(1)} %copy-done), channel_id=1, source_target_pairs={{0,4},{1,5},{64,6},{65,7},{128,0},{129,1},{192,2},{193,3},{256,12}... | collective-permute-start | bytes 147464 | tf_op jit(solution)/shard_map/ppermute | solution.py:253
  75.3 10.5 %collective-permute-start.7 = (bf16[96,256]{1,0:T(8,128)(2,1)S(1)}, bf16[96,256]{1,0:T(8,128)(2,1)S(1)}, u32[]{:S(2)}, u32[]{:S(2)}) collective-permute-start(bf16[96,256]{1,0:T(8,128)(2,1)S(1)} %copy-done), channel_id=1, source_target_pairs={{0,0},{1,1},{64,2},{65,3},{128,4},{129,5},{192,6},{193,7},{256,8},... | collective-permute-start | bytes 147464 | tf_op jit(solution)/shard_map/ppermute | solution.py:253
  77.0 33.2 %all-to-all-start.2 = ((bf16[8,2,96,256]{3,2,1,0:T(8,128)(2,1)}), bf16[8,2,96,256]{3,2,1,0:T(8,128)(2,1)S(1)}, u32[]{:S(2)}, u32[]{:S(2)}) async-start(bf16[8,2,96,256]{3,2,1,0:T(8,128)(2,1)} %combine.1), calls=%async_computation.2 | async-start | bytes 1572864 | tf_op jit(solution)/shard_map/all_to_all | solution.py:262
  85.8 6.3 %collective-permute-start.8 = (bf16[2,96,256]{2,1,0:T(8,128)(2,1)S(1)}, bf16[2,96,256]{2,1,0:T(8,128)(2,1)S(1)}, u32[]{:S(2)}, u32[]{:S(2)}) collective-permute-start(bf16[2,96,256]{2,1,0:T(8,128)(2,1)S(1)} %pad_maximum_fusion.3), channel_id=1, source_target_pairs={{0,2},{1,3},{2,0},{3,1},{4,6},{5,7},{6,4},{7,5},{8,10},{9,11},{10,... | collective-permute-start | bytes 294920 | tf_op jit(solution)/shard_map/ppermute | solution.py:26
  92.1 11.8 %collective-permute-start.10 = (bf16[2,2,96,256]{3,2,1,0:T(8,128)(2,1)S(1)}, bf16[2,2,96,256]{3,2,1,0:T(8,128)(2,1)S(1)}, u32[]{:S(2)}, u32[]{:S(2)}) collective-permute-start(bf16[2,2,96,256]{3,2,1,0:T(8,128)(2,1)S(1)} %pad_maximum_fusion.2), channel_id=1, source_target_pairs={{0,8},{1,9},{2,10},{3,11},{4,12},{5,13},{6,14},{7,15},{8,0},{9,1},... | collective-permute-start | bytes 589832 | tf_op jit(solution)/shard_map/ppermute | solution.py:267
  98.7 7.8 %collective-permute-start.9 = (bf16[2,2,96,256]{3,2,1,0:T(8,128)(2,1)S(1)}, bf16[2,2,96,256]{3,2,1,0:T(8,128)(2,1)S(1)}, u32[]{:S(2)}, u32[]{:S(2)}) collective-permute-start(bf16[2,2,96,256]{3,2,1,0:T(8,128)(2,1)S(1)} %pad_maximum_fusion.2), channel_id=1, source_target_pairs={{0,9},{1,8},{2,11},{3,10},{4,13},{5,12},{6,15},{7,14},{8,1},{9,0},... | collective-permute-start | bytes 589832 | tf_op jit(solution)/shard_map/ppermute | solution.py:267
  100.7 9.3 %collective-permute-start.11 = (bf16[2,2,96,256]{3,2,1,0:T(8,128)(2,1)S(1)}, bf16[2,2,96,256]{3,2,1,0:T(8,128)(2,1)S(1)}, u32[]{:S(2)}, u32[]{:S(2)}) collective-permute-start(bf16[2,2,96,256]{3,2,1,0:T(8,128)(2,1)S(1)} %pad_maximum_fusion.2), channel_id=1, source_target_pairs={{0,1},{1,0},{2,3},{3,2},{4,5},{5,4},{6,7},{7,6},{8,9},{9,8},{10,11... | collective-permute-start | bytes 589832 | tf_op jit(solution)/shard_map/ppermute | solution.py:267
  110.5 20.2 %collective-permute-start.12 = (f32[2,128,256]{2,1,0:T(8,128)S(1)}, f32[2,128,256]{2,1,0:T(8,128)S(1)}, u32[]{:S(2)}, u32[]{:S(2)}) collective-permute-start(f32[2,128,256]{2,1,0:T(8,128)S(1)} %convolution_bitcast_fusion.2), channel_id=1, source_target_pairs={{0,16},{16,0},{1,17},{17,1},{2,18},{18,2},{3,19},{19,3},{4,20},{20... | collective-permute-start | bytes 786440 | tf_op jit(solution)/shard_map/ppermute | solution.py:288
  114.7 10.6 %collective-permute-start.13 = (bf16[2,128,256]{2,1,0:T(8,128)(2,1)S(1)}, bf16[2,128,256]{2,1,0:T(8,128)(2,1)S(1)}, u32[]{:S(2)}, u32[]{:S(2)}) collective-permute-start(bf16[2,128,256]{2,1,0:T(8,128)(2,1)S(1)} %fusion.3), channel_id=1, source_target_pairs={{0,32},{32,0},{1,33},{33,1},{2,34},{34,2},{3,35},{35,3},{4,36},{36... | collective-permute-start | bytes 393224 | tf_op jit(solution)/shard_map/ppermute | solution.py:287
  121.9 8.8 %collective-permute-start.14 = (bf16[2,128,256]{2,1,0:T(8,128)(2,1)S(1)}, bf16[2,128,256]{2,1,0:T(8,128)(2,1)S(1)}, u32[]{:S(2)}, u32[]{:S(2)}) collective-permute-start(bf16[2,128,256]{2,1,0:T(8,128)(2,1)S(1)} %fusion.2), channel_id=1, source_target_pairs={{0,48},{48,0},{16,32},{32,16},{1,49},{49,1},{17,33},{33,17},{2,50}... | collective-permute-start | bytes 393224 | tf_op jit(solution)/shard_map/ppermute | solution.py:284

commit v9 on v8

--- a/solution.py
+++ b/solution.py
@@ -235,33 +235,31 @@
 def on_device(phi_occ, phi_vir, eps_occ, eps_vir, taus, pair_mask, basis):
     core, xh = lax.axis_index("core"), lax.axis_index("xh")
     naux, rows = basis.shape[1], phi_occ.shape[0]
-    mask = jnp.pad(pair_mask.astype(BF), ((0, 0), (0, 120)))
-    mine = jnp.concatenate(
-        [phi_occ, phi_vir, basis, jnp.broadcast_to(mask, (rows, 128))], axis=1
-    )
+    mask = jnp.broadcast_to(jnp.pad(pair_mask, ((0, 0), (0, 120))), (rows, 128))
+    mine = jnp.concatenate([phi_occ, phi_vir, basis, mask.astype(BF)], axis=1)
     up = from_tile(mine, 2)
     down = from_tile(mine, -4)
     mate = lax.ppermute(mine, "core", SWAP)
-    expo_occ = jnp.exp(taus[:, None] * eps_occ[None, :])
-    expo_vir = jnp.exp(-taus[:, None] * eps_vir[None, :])
-    part_sums = green(core.reshape(1), expo_occ, expo_vir, mine, mate, up, down)
     got = []
     for far in (0, 4):
         pairs = [
             ((i // 2) * 16 + 2 * z + i % 2, z * 16 + (i ^ far)) for z in range(8) for i in range(16)
         ]
         got.append(lax.ppermute(basis, ("z", "xl", "y"), pairs))
+    expo_occ = jnp.exp(taus[:, None] * eps_occ[None, :])
+    expo_vir = jnp.exp(-taus[:, None] * eps_vir[None, :])
+    part_sums = green(core.reshape(1), expo_occ, expo_vir, mine, mate, up, down)
     sums = lax.all_to_all(part_sums, ORB, 0, 0, tiled=True)
     both = product(sums)
     both = lax.all_to_all(both, ORB, 0, 0, tiled=True)
+    part = join(got[0], got[1], "y", 4, 0)
+    part = join(part, trade(part, "y", 2), "y", 2, 1)
     to_up, to_down, to_mate, own = project(core.reshape(1), both, mine, mate, up, down, naux)
     got_up = from_tile(to_up, -2)
     got_down = from_tile(to_down, 4)
     got_mate = lax.ppermute(to_mate, "core", SWAP)
     copies = combine(own, got_mate, got_up, got_down)
     gathered = lax.all_to_all(copies, "z", 0, 0, tiled=True)
-    part = join(got[0], got[1], "y", 4, 0)
-    part = join(part, trade(part, "y", 2), "y", 2, 1)
     others = [part]
     for flip in (9, 8, 1):
         others.append(lax.ppermute(part, ORB, [(i, i ^ flip) for i in range(16)]))

time: 132 us -> 132 us (level)
  no operation moved by 1% of the time
where the time goes in v9:
time: 132 us; the launch traced here: 131 us
  starting transfers between devices  70.3 us (53%)
  blocking collectives  28.8 us (22%)
  waiting for transfers between devices  24.4 us (18%)
  Pallas kernels  3.41 us (3%)
  other arithmetic  2.07 us (2%)
  matrix products  1.34 us (1%)
    all_to_all x1, blocking collectives, on_device(): sums = lax.all_to_all(part_sums, ORB, 0, 0, tiled=True)  15.5 us
    ppermute x4, starting transfers between devices, from_tile(): return lax.ppermute(value, PTS, [((i + steps) % 32, i) for i in range(32)])  15.2 us
    all_to_all x1, blocking collectives, on_device(): both = lax.all_to_all(both, ORB, 0, 0, tiled=True)  13.3 us
    ppermute x3, starting transfers between devices, on_device(): others.append(lax.ppermute(part, ORB, [(i, i ^ flip) for i in range(16)]))  11.6 us
    ppermute x4, waiting for transfers between devices, from_tile(): return lax.ppermute(value, PTS, [((i + steps) % 32, i) for i in range(32)])  9.73 us
    all_to_all x1, starting transfers between devices, on_device(): gathered = lax.all_to_all(copies, 'z', 0, 0, tiled=True)  8.79 us
    ppermute x1, starting transfers between devices, on_device(): mate = lax.ppermute(mine, 'core', SWAP)  8.75 us
    ppermute x1, starting transfers between devices, on_device(): across = lax.ppermute(response(2).astype(BF), 'xh', SWAP)  6.8 us
  transfers between devices with their start and end apart: 16, of which 8 were waited for; matrix products, arithmetic and copies ran while one was open for 1% of the time, Pallas kernels for 1%

profile of v9, /device:TPU:1, one launch (start us, length us, event | category | flops | bytes accessed | tf_op | source)
XLA Modules:
  0.0 131.5 jit_solution(556588495644040571)
XLA Ops:
  1.7 8.7 %collective-permute-start = (bf16[96,1792]{1,0:T(8,128)(2,1)S(1)}, bf16[96,1792]{1,0:T(8,128)(2,1)S(1)}, u32[]{:S(2)}, u32[]{:S(2)}) collective-permute-start(bf16[96,1792]{1,0:T(8,128)(2,1)S(1)} %maximum_maximum_fusion.mine), channel_id=1, source_target_pairs={{0,16},{16,0},{1,17},{17,1},{2,18},{18,2},{3,19},{19,3},{4,20},{20... | collective-permute-start | bytes 1032200 | tf_op jit(solution)/shard_map/ppermute | solution.py:242
  10.5 7.8 %collective-permute-start.1 = (bf16[96,1792]{1,0:T(8,128)(2,1)S(1)}, bf16[96,1792]{1,0:T(8,128)(2,1)S(1)}, u32[]{:S(2)}, u32[]{:S(2)}) collective-permute-start(bf16[96,1792]{1,0:T(8,128)(2,1)S(1)} %maximum_maximum_fusion.mine), channel_id=1, source_target_pairs={{32,0},{48,16},{64,32},{80,48},{96,64},{112,80},{128,96},{144,112}... | collective-permute-start | bytes 1032200 | tf_op jit(solution)/shard_map/ppermute | solution.py:21
  18.3 1.9 %collective-permute-start.2 = (bf16[96,1792]{1,0:T(8,128)(2,1)S(1)}, bf16[96,1792]{1,0:T(8,128)(2,1)S(1)}, u32[]{:S(2)}, u32[]{:S(2)}) collective-permute-start(bf16[96,1792]{1,0:T(8,128)(2,1)S(1)} %maximum_maximum_fusion.mine), channel_id=1, source_target_pairs={{448,0},{464,16},{480,32},{496,48},{0,64},{16,80},{32,96},{48,112}... | collective-permute-start | bytes 1032200 | tf_op jit(solution)/shard_map/ppermute | solution.py:21
  21.1 4.6 %collective-permute-done.1.up = bf16[96,1792]{1,0:T(8,128)(2,1)S(1)} collective-permute-done((bf16[96,1792]{1,0:T(8,128)(2,1)S(1)}, bf16[96,1792]{1,0:T(8,128)(2,1)S(1)}, u32[]{:S(2)}, u32[]{:S(2)}) %collective-permute-start.1) | collective-permute-done | bytes 344096 | tf_op jit(solution)/shard_map/ppermute | solution.py:21
  25.7 5.0 %collective-permute-done.2.down = bf16[96,1792]{1,0:T(8,128)(2,1)S(1)} collective-permute-done((bf16[96,1792]{1,0:T(8,128)(2,1)S(1)}, bf16[96,1792]{1,0:T(8,128)(2,1)S(1)}, u32[]{:S(2)}, u32[]{:S(2)}) %collective-permute-start.2) | collective-permute-done | bytes 344096 | tf_op jit(solution)/shard_map/ppermute | solution.py:21
  31.7 15.5 %all_to_all.15.parts = bf16[16,24,384]{2,1,0:T(8,128)(2,1)S(1)} all-to-all(bf16[16,24,384]{2,1,0:T(8,128)(2,1)S(1)} %green.1), channel_id=1, replica_groups=mesh['z'=8,'xh'=2,'core'=2,'xl'=2,'y'=8] {'xl','y'}, dimensions={0} | all-to-all | bytes 589824 | tf_op jit(solution)/shard_map/all_to_all | solution.py:252
  47.3 13.3 %all_to_all.16.parts = bf16[16,12,384]{2,1,0:T(8,128)(2,1)S(1)} all-to-all(bf16[16,12,384]{2,1,0:T(8,128)(2,1)S(1)} %product.1), channel_id=1, replica_groups=mesh['z'=8,'xh'=2,'core'=2,'xl'=2,'y'=8] {'xl','y'}, dimensions={0} | all-to-all | bytes 294912 | tf_op jit(solution)/shard_map/all_to_all | solution.py:254
  61.2 4.9 %collective-permute-start.3 = (f32[2,96,256]{2,1,0:T(8,128)S(1)}, f32[2,96,256]{2,1,0:T(8,128)S(1)}, u32[]{:S(2)}, u32[]{:S(2)}) collective-permute-start(f32[2,96,256]{2,1,0:T(8,128)S(1)} %get-tuple-element.10), channel_id=1, source_target_pairs={{0,16},{16,0},{1,17},{17,1},{2,18},{18,2},{3,19},{19,3},{4,20},{20... | collective-permute-start | bytes 589832 | tf_op jit(solution)/shard_map/ppermute | solution.py:260
  66.2 1.9 %collective-permute-start.4 = (bf16[2,96,256]{2,1,0:T(8,128)(2,1)S(1)}, bf16[2,96,256]{2,1,0:T(8,128)(2,1)S(1)}, u32[]{:S(2)}, u32[]{:S(2)}) collective-permute-start(bf16[2,96,256]{2,1,0:T(8,128)(2,1)S(1)} %get-tuple-element.11), channel_id=1, source_target_pairs={{480,0},{496,16},{0,32},{16,48},{32,64},{48,80},{64,96},{80,112},{... | collective-permute-start | bytes 294920 | tf_op jit(solution)/shard_map/ppermute | solution.py:21
  68.1 3.6 %collective-permute-start.5 = (bf16[2,96,256]{2,1,0:T(8,128)(2,1)S(1)}, bf16[2,96,256]{2,1,0:T(8,128)(2,1)S(1)}, u32[]{:S(2)}, u32[]{:S(2)}) collective-permute-start(bf16[2,96,256]{2,1,0:T(8,128)(2,1)S(1)} %get-tuple-element.12), channel_id=1, source_target_pairs={{64,0},{80,16},{96,32},{112,48},{128,64},{144,80},{160,96},{176,11... | collective-permute-start | bytes 294920 | tf_op jit(solution)/shard_map/ppermute | solution.py:21
  71.7 3.6 %collective-permute-start.6 = (bf16[96,256]{1,0:T(8,128)(2,1)S(1)}, bf16[96,256]{1,0:T(8,128)(2,1)S(1)}, u32[]{:S(2)}, u32[]{:S(2)}) collective-permute-start(bf16[96,256]{1,0:T(8,128)(2,1)S(1)} %copy-done), channel_id=1, source_target_pairs={{0,4},{1,5},{64,6},{65,7},{128,0},{129,1},{192,2},{193,3},{256,12}... | collective-permute-start | bytes 147464 | tf_op jit(solution)/shard_map/ppermute | solution.py:248
  77.0 8.8 %all-to-all-start.2 = ((bf16[8,2,96,256]{3,2,1,0:T(8,128)(2,1)}), bf16[8,2,96,256]{3,2,1,0:T(8,128)(2,1)S(1)}, u32[]{:S(2)}, u32[]{:S(2)}) async-start(bf16[8,2,96,256]{3,2,1,0:T(8,128)(2,1)} %combine.1), calls=%async_computation.2 | async-start | bytes 1572864 | tf_op jit(solution)/shard_map/all_to_all | solution.py:262
  85.8 4.2 %collective-permute-start.8 = (bf16[2,96,256]{2,1,0:T(8,128)(2,1)S(1)}, bf16[2,96,256]{2,1,0:T(8,128)(2,1)S(1)}, u32[]{:S(2)}, u32[]{:S(2)}) collective-permute-start(bf16[2,96,256]{2,1,0:T(8,128)(2,1)S(1)} %pad_maximum_fusion.3), channel_id=1, source_target_pairs={{0,2},{1,3},{2,0},{3,1},{4,6},{5,7},{6,4},{7,5},{8,10},{9,11},{10,... | collective-permute-start | bytes 294920 | tf_op jit(solution)/shard_map/ppermute | solution.py:26
  90.1 2.0 %collective-permute-done.8 = bf16[2,96,256]{2,1,0:T(8,128)(2,1)S(1)} collective-permute-done((bf16[2,96,256]{2,1,0:T(8,128)(2,1)S(1)}, bf16[2,96,256]{2,1,0:T(8,128)(2,1)S(1)}, u32[]{:S(2)}, u32[]{:S(2)}) %collective-permute-start.8) | collective-permute-done | bytes 98336 | tf_op jit(solution)/shard_map/ppermute | solution.py:26
  92.1 6.6 %collective-permute-start.10 = (bf16[2,2,96,256]{3,2,1,0:T(8,128)(2,1)S(1)}, bf16[2,2,96,256]{3,2,1,0:T(8,128)(2,1)S(1)}, u32[]{:S(2)}, u32[]{:S(2)}) collective-permute-start(bf16[2,2,96,256]{3,2,1,0:T(8,128)(2,1)S(1)} %pad_maximum_fusion.2), channel_id=1, source_target_pairs={{0,8},{1,9},{2,10},{3,11},{4,12},{5,13},{6,14},{7,15},{8,0},{9,1},... | collective-permute-start | bytes 589832 | tf_op jit(solution)/shard_map/ppermute | solution.py:265
  98.7 1.9 %collective-permute-start.9 = (bf16[2,2,96,256]{3,2,1,0:T(8,128)(2,1)S(1)}, bf16[2,2,96,256]{3,2,1,0:T(8,128)(2,1)S(1)}, u32[]{:S(2)}, u32[]{:S(2)}) collective-permute-start(bf16[2,2,96,256]{3,2,1,0:T(8,128)(2,1)S(1)} %pad_maximum_fusion.2), channel_id=1, source_target_pairs={{0,9},{1,8},{2,11},{3,10},{4,13},{5,12},{6,15},{7,14},{8,1},{9,0},... | collective-permute-start | bytes 589832 | tf_op jit(solution)/shard_map/ppermute | solution.py:265
  100.7 3.1 %collective-permute-start.11 = (bf16[2,2,96,256]{3,2,1,0:T(8,128)(2,1)S(1)}, bf16[2,2,96,256]{3,2,1,0:T(8,128)(2,1)S(1)}, u32[]{:S(2)}, u32[]{:S(2)}) collective-permute-start(bf16[2,2,96,256]{3,2,1,0:T(8,128)(2,1)S(1)} %pad_maximum_fusion.2), channel_id=1, source_target_pairs={{0,1},{1,0},{2,3},{3,2},{4,5},{5,4},{6,7},{7,6},{8,9},{9,8},{10,11... | collective-permute-start | bytes 589832 | tf_op jit(solution)/shard_map/ppermute | solution.py:265
  103.9 2.7 %collective-permute-done.9 = bf16[2,2,96,256]{3,2,1,0:T(8,128)(2,1)S(1)} collective-permute-done((bf16[2,2,96,256]{3,2,1,0:T(8,128)(2,1)S(1)}, bf16[2,2,96,256]{3,2,1,0:T(8,128)(2,1)S(1)}, u32[]{:S(2)}, u32[]{:S(2)}) %collective-permute-start.9) | collective-permute-done | bytes 196640 | tf_op jit(solution)/shard_map/ppermute | solution.py:265
  106.6 3.4 %collective-permute-done.11 = bf16[2,2,96,256]{3,2,1,0:T(8,128)(2,1)S(1)} collective-permute-done((bf16[2,2,96,256]{3,2,1,0:T(8,128)(2,1)S(1)}, bf16[2,2,96,256]{3,2,1,0:T(8,128)(2,1)S(1)}, u32[]{:S(2)}, u32[]{:S(2)}) %collective-permute-start.11) | collective-permute-done | bytes 196640 | tf_op jit(solution)/shard_map/ppermute | solution.py:265
  110.5 3.9 %collective-permute-start.12 = (f32[2,128,256]{2,1,0:T(8,128)S(1)}, f32[2,128,256]{2,1,0:T(8,128)S(1)}, u32[]{:S(2)}, u32[]{:S(2)}) collective-permute-start(f32[2,128,256]{2,1,0:T(8,128)S(1)} %convolution_bitcast_fusion.2), channel_id=1, source_target_pairs={{0,16},{16,0},{1,17},{17,1},{2,18},{18,2},{3,19},{19,3},{4,20},{20... | collective-permute-start | bytes 786440 | tf_op jit(solution)/shard_map/ppermute | solution.py:286
  114.7 6.8 %collective-permute-start.13 = (bf16[2,128,256]{2,1,0:T(8,128)(2,1)S(1)}, bf16[2,128,256]{2,1,0:T(8,128)(2,1)S(1)}, u32[]{:S(2)}, u32[]{:S(2)}) collective-permute-start(bf16[2,128,256]{2,1,0:T(8,128)(2,1)S(1)} %fusion.3), channel_id=1, source_target_pairs={{0,32},{32,0},{1,33},{33,1},{2,34},{34,2},{3,35},{35,3},{4,36},{36... | collective-permute-start | bytes 393224 | tf_op jit(solution)/shard_map/ppermute | solution.py:285
  121.9 1.9 %collective-permute-start.14 = (bf16[2,128,256]{2,1,0:T(8,128)(2,1)S(1)}, bf16[2,128,256]{2,1,0:T(8,128)(2,1)S(1)}, u32[]{:S(2)}, u32[]{:S(2)}) collective-permute-start(bf16[2,128,256]{2,1,0:T(8,128)(2,1)S(1)} %fusion.2), channel_id=1, source_target_pairs={{0,48},{48,0},{16,32},{32,16},{1,49},{49,1},{17,33},{33,17},{2,50}... | collective-permute-start | bytes 393224 | tf_op jit(solution)/shard_map/ppermute | solution.py:282
  124.1 1.2 collective-permute-done.13.across
  125.3 5.3 %collective-permute-done.14.diag = bf16[2,128,256]{2,1,0:T(8,128)(2,1)S(1)} collective-permute-done((bf16[2,128,256]{2,1,0:T(8,128)(2,1)S(1)}, bf16[2,128,256]{2,1,0:T(8,128)(2,1)S(1)}, u32[]{:S(2)}, u32[]{:S(2)}) %collective-permute-start.14) | collective-permute-done | bytes 131104 | tf_op jit(solution)/shard_map/ppermute | solution.py:282
  (40 shorter events, 8.2 us)
Async XLA Ops:
  0.7 19.5 %copy-start.3 = (f32[2]{0:T(128)S(1)}, f32[2]{0:T(128)}, u32[]{:S(2)}) copy-start(f32[2]{0:T(128)} %param.11) | copy-start | bytes 28
  1.7 19.2 %copy-start.1 = (f32[1280]{0:T(1024)S(1)}, f32[1280]{0:T(1024)}, u32[]{:S(2)}) copy-start(f32[1280]{0:T(1024)} %param.10) | copy-start | bytes 15364
  1.7 19.3 %collective-permute-start = (bf16[96,1792]{1,0:T(8,128)(2,1)S(1)}, bf16[96,1792]{1,0:T(8,128)(2,1)S(1)}, u32[]{:S(2)}, u32[]{:S(2)}) collective-permute-start(bf16[96,1792]{1,0:T(8,128)(2,1)S(1)} %maximum_maximum_fusion.mine), channel_id=1, source_target_pairs={{0,16},{16,0},{1,17},{17,1},{2,18},{18,2},{3,19},{19,3},{4,20},{20... | collective-permute-start | bytes 1032200 | tf_op jit(solution)/shard_map/ppermute | solution.py:242
  10.5 15.2 %collective-permute-start.1 = (bf16[96,1792]{1,0:T(8,128)(2,1)S(1)}, bf16[96,1792]{1,0:T(8,128)(2,1)S(1)}, u32[]{:S(2)}, u32[]{:S(2)}) collective-permute-start(bf16[96,1792]{1,0:T(8,128)(2,1)S(1)} %maximum_maximum_fusion.mine), channel_id=1, source_target_pairs={{32,0},{48,16},{64,32},{80,48},{96,64},{112,80},{128,96},{144,112}... | collective-permute-start | bytes 1032200 | tf_op jit(solution)/shard_map/ppermute | solution.py:21
  18.3 12.4 %collective-permute-start.2 = (bf16[96,1792]{1,0:T(8,128)(2,1)S(1)}, bf16[96,1792]{1,0:T(8,128)(2,1)S(1)}, u32[]{:S(2)}, u32[]{:S(2)}) collective-permute-start(bf16[96,1792]{1,0:T(8,128)(2,1)S(1)} %maximum_maximum_fusion.mine), channel_id=1, source_target_pairs={{448,0},{464,16},{480,32},{496,48},{0,64},{16,80},{32,96},{48,112}... | collective-permute-start | bytes 1032200 | tf_op jit(solution)/shard_map/ppermute | solution.py:21
  20.2 0.7 copy-start.2
  60.7 11.0 %copy-start = (bf16[96,256]{1,0:T(8,128)(2,1)S(1)}, bf16[96,256]{1,0:T(8,128)(2,1)}, u32[]{:S(2)}) copy-start(bf16[96,256]{1,0:T(8,128)(2,1)} %param.13) | copy-start | bytes 147460
  61.2 14.8 %collective-permute-start.3 = (f32[2,96,256]{2,1,0:T(8,128)S(1)}, f32[2,96,256]{2,1,0:T(8,128)S(1)}, u32[]{:S(2)}, u32[]{:S(2)}) collective-permute-start(f32[2,96,256]{2,1,0:T(8,128)S(1)} %get-tuple-element.10), channel_id=1, source_target_pairs={{0,16},{16,0},{1,17},{17,1},{2,18},{18,2},{3,19},{19,3},{4,20},{20... | collective-permute-start | bytes 589832 | tf_op jit(solution)/shard_map/ppermute | solution.py:260
  66.2 9.8 %collective-permute-start.4 = (bf16[2,96,256]{2,1,0:T(8,128)(2,1)S(1)}, bf16[2,96,256]{2,1,0:T(8,128)(2,1)S(1)}, u32[]{:S(2)}, u32[]{:S(2)}) collective-permute-start(bf16[2,96,256]{2,1,0:T(8,128)(2,1)S(1)} %get-tuple-element.11), channel_id=1, source_target_pairs={{480,0},{496,16},{0,32},{16,48},{32,64},{48,80},{64,96},{80,112},{... | collective-permute-start | bytes 294920 | tf_op jit(solution)/shard_map/ppermute | solution.py:21
  68.1 7.9 %collective-permute-start.5 = (bf16[2,96,256]{2,1,0:T(8,128)(2,1)S(1)}, bf16[2,96,256]{2,1,0:T(8,128)(2,1)S(1)}, u32[]{:S(2)}, u32[]{:S(2)}) collective-permute-start(bf16[2,96,256]{2,1,0:T(8,128)(2,1)S(1)} %get-tuple-element.12), channel_id=1, source_target_pairs={{64,0},{80,16},{96,32},{112,48},{128,64},{144,80},{160,96},{176,11... | collective-permute-start | bytes 294920 | tf_op jit(solution)/shard_map/ppermute | solution.py:21
  71.7 14.1 %collective-permute-start.6 = (bf16[96,256]{1,0:T(8,128)(2,1)S(1)}, bf16[96,256]{1,0:T(8,128)(2,1)S(1)}, u32[]{:S(2)}, u32[]{:S(2)}) collective-permute-start(bf16[96,256]{1,0:T(8,128)(2,1)S(1)} %copy-done), channel_id=1, source_target_pairs={{0,4},{1,5},{64,6},{65,7},{128,0},{129,1},{192,2},{193,3},{256,12}... | collective-permute-start | bytes 147464 | tf_op jit(solution)/shard_map/ppermute | solution.py:248
  75.3 10.5 %collective-permute-start.7 = (bf16[96,256]{1,0:T(8,128)(2,1)S(1)}, bf16[96,256]{1,0:T(8,128)(2,1)S(1)}, u32[]{:S(2)}, u32[]{:S(2)}) collective-permute-start(bf16[96,256]{1,0:T(8,128)(2,1)S(1)} %copy-done), channel_id=1, source_target_pairs={{0,0},{1,1},{64,2},{65,3},{128,4},{129,5},{192,6},{193,7},{256,8},... | collective-permute-start | bytes 147464 | tf_op jit(solution)/shard_map/ppermute | solution.py:248
  77.0 33.2 %all-to-all-start.2 = ((bf16[8,2,96,256]{3,2,1,0:T(8,128)(2,1)}), bf16[8,2,96,256]{3,2,1,0:T(8,128)(2,1)S(1)}, u32[]{:S(2)}, u32[]{:S(2)}) async-start(bf16[8,2,96,256]{3,2,1,0:T(8,128)(2,1)} %combine.1), calls=%async_computation.2 | async-start | bytes 1572864 | tf_op jit(solution)/shard_map/all_to_all | solution.py:262
  85.8 6.3 %collective-permute-start.8 = (bf16[2,96,256]{2,1,0:T(8,128)(2,1)S(1)}, bf16[2,96,256]{2,1,0:T(8,128)(2,1)S(1)}, u32[]{:S(2)}, u32[]{:S(2)}) collective-permute-start(bf16[2,96,256]{2,1,0:T(8,128)(2,1)S(1)} %pad_maximum_fusion.3), channel_id=1, source_target_pairs={{0,2},{1,3},{2,0},{3,1},{4,6},{5,7},{6,4},{7,5},{8,10},{9,11},{10,... | collective-permute-start | bytes 294920 | tf_op jit(solution)/shard_map/ppermute | solution.py:26
  92.1 11.8 %collective-permute-start.10 = (bf16[2,2,96,256]{3,2,1,0:T(8,128)(2,1)S(1)}, bf16[2,2,96,256]{3,2,1,0:T(8,128)(2,1)S(1)}, u32[]{:S(2)}, u32[]{:S(2)}) collective-permute-start(bf16[2,2,96,256]{3,2,1,0:T(8,128)(2,1)S(1)} %pad_maximum_fusion.2), channel_id=1, source_target_pairs={{0,8},{1,9},{2,10},{3,11},{4,12},{5,13},{6,14},{7,15},{8,0},{9,1},... | collective-permute-start | bytes 589832 | tf_op jit(solution)/shard_map/ppermute | solution.py:265
  98.7 7.8 %collective-permute-start.9 = (bf16[2,2,96,256]{3,2,1,0:T(8,128)(2,1)S(1)}, bf16[2,2,96,256]{3,2,1,0:T(8,128)(2,1)S(1)}, u32[]{:S(2)}, u32[]{:S(2)}) collective-permute-start(bf16[2,2,96,256]{3,2,1,0:T(8,128)(2,1)S(1)} %pad_maximum_fusion.2), channel_id=1, source_target_pairs={{0,9},{1,8},{2,11},{3,10},{4,13},{5,12},{6,15},{7,14},{8,1},{9,0},... | collective-permute-start | bytes 589832 | tf_op jit(solution)/shard_map/ppermute | solution.py:265
  100.7 9.3 %collective-permute-start.11 = (bf16[2,2,96,256]{3,2,1,0:T(8,128)(2,1)S(1)}, bf16[2,2,96,256]{3,2,1,0:T(8,128)(2,1)S(1)}, u32[]{:S(2)}, u32[]{:S(2)}) collective-permute-start(bf16[2,2,96,256]{3,2,1,0:T(8,128)(2,1)S(1)} %pad_maximum_fusion.2), channel_id=1, source_target_pairs={{0,1},{1,0},{2,3},{3,2},{4,5},{5,4},{6,7},{7,6},{8,9},{9,8},{10,11... | collective-permute-start | bytes 589832 | tf_op jit(solution)/shard_map/ppermute | solution.py:265
  110.5 20.2 %collective-permute-start.12 = (f32[2,128,256]{2,1,0:T(8,128)S(1)}, f32[2,128,256]{2,1,0:T(8,128)S(1)}, u32[]{:S(2)}, u32[]{:S(2)}) collective-permute-start(f32[2,128,256]{2,1,0:T(8,128)S(1)} %convolution_bitcast_fusion.2), channel_id=1, source_target_pairs={{0,16},{16,0},{1,17},{17,1},{2,18},{18,2},{3,19},{19,3},{4,20},{20... | collective-permute-start | bytes 786440 | tf_op jit(solution)/shard_map/ppermute | solution.py:286
  114.7 10.6 %collective-permute-start.13 = (bf16[2,128,256]{2,1,0:T(8,128)(2,1)S(1)}, bf16[2,128,256]{2,1,0:T(8,128)(2,1)S(1)}, u32[]{:S(2)}, u32[]{:S(2)}) collective-permute-start(bf16[2,128,256]{2,1,0:T(8,128)(2,1)S(1)} %fusion.3), channel_id=1, source_target_pairs={{0,32},{32,0},{1,33},{33,1},{2,34},{34,2},{3,35},{35,3},{4,36},{36... | collective-permute-start | bytes 393224 | tf_op jit(solution)/shard_map/ppermute | solution.py:285
  121.9 8.8 %collective-permute-start.14 = (bf16[2,128,256]{2,1,0:T(8,128)(2,1)S(1)}, bf16[2,128,256]{2,1,0:T(8,128)(2,1)S(1)}, u32[]{:S(2)}, u32[]{:S(2)}) collective-permute-start(bf16[2,128,256]{2,1,0:T(8,128)(2,1)S(1)} %fusion.2), channel_id=1, source_target_pairs={{0,48},{48,0},{16,32},{32,16},{1,49},{49,1},{17,33},{33,17},{2,50}... | collective-permute-start | bytes 393224 | tf_op jit(solution)/shard_map/ppermute | solution.py:282

commit v10 on v9

--- a/solution.py
+++ b/solution.py
@@ -240,20 +240,16 @@
     up = from_tile(mine, 2)
     down = from_tile(mine, -4)
     mate = lax.ppermute(mine, "core", SWAP)
-    got = []
-    for far in (0, 4):
-        pairs = [
-            ((i // 2) * 16 + 2 * z + i % 2, z * 16 + (i ^ far)) for z in range(8) for i in range(16)
-        ]
-        got.append(lax.ppermute(basis, ("z", "xl", "y"), pairs))
+    pairs = [((i // 2) * 16 + 2 * z + i % 2, z * 16 + i) for z in range(8) for i in range(16)]
+    part = lax.ppermute(basis, ("z", "xl", "y"), pairs)
     expo_occ = jnp.exp(taus[:, None] * eps_occ[None, :])
     expo_vir = jnp.exp(-taus[:, None] * eps_vir[None, :])
     part_sums = green(core.reshape(1), expo_occ, expo_vir, mine, mate, up, down)
     sums = lax.all_to_all(part_sums, ORB, 0, 0, tiled=True)
     both = product(sums)
     both = lax.all_to_all(both, ORB, 0, 0, tiled=True)
-    part = join(got[0], got[1], "y", 4, 0)
-    part = join(part, trade(part, "y", 2), "y", 2, 1)
+    part = join(part, trade(part, "y", 2), "y", 2, 0)
+    part = join(part, trade(part, "y", 4), "y", 4, 0)
     to_up, to_down, to_mate, own = project(core.reshape(1), both, mine, mate, up, down, naux)
     got_up = from_tile(to_up, -2)
     got_down = from_tile(to_down, 4)

time: 132 us -> 136 us (1.030)
  waiting for transfers between devices: 24.4 us -> 26.5 us
  starting transfers between devices: 70.3 us -> 72.1 us
    ppermute x1 -> x2, starting transfers between devices: 4.22 us -> 14.4 us  [trade(): return lax.ppermute(value, axis, [(i, i ^ bit) for i in range(size)])]
    ppermute x2 -> x1, starting transfers between devices: 4.24 us -> 0.66 us  [on_device(): part = lax.ppermute(basis, ('z', 'xl', 'y'), pairs)]
    ppermute x1 -> x2, waiting for transfers between devices: 2.03 us -> 5.4 us  [trade(): return lax.ppermute(value, axis, [(i, i ^ bit) for i in range(size)])]
    ppermute x3, starting transfers between devices: 11.6 us -> 8.37 us  [on_device(): others.append(lax.ppermute(part, ORB, [(i, i ^ flip) for i in range(16)]))]
    all_to_all x1, starting transfers between devices: 8.79 us -> 6.99 us  [on_device(): gathered = lax.all_to_all(copies, 'z', 0, 0, tiled=True)]
  transfers between devices with their start and end apart: 16 -> 16, of which waited for: 8 -> 7; matrix products, arithmetic and copies ran while one was open for 1% -> 1% of each run, Pallas kernels for 1% -> 1%
where the time goes in v10:
time: 136 us; the launch traced here: 135 us
  starting transfers between devices  72.1 us (53%)
  blocking collectives  28.8 us (21%)
  waiting for transfers between devices  26.5 us (19%)
  Pallas kernels  3.41 us (3%)
  other arithmetic  2.07 us (2%)
    all_to_all x1, blocking collectives, on_device(): sums = lax.all_to_all(part_sums, ORB, 0, 0, tiled=True)  15.5 us
    ppermute x4, starting transfers between devices, from_tile(): return lax.ppermute(value, PTS, [((i + steps) % 32, i) for i in range(32)])  15.2 us
    ppermute x2, starting transfers between devices, trade(): return lax.ppermute(value, axis, [(i, i ^ bit) for i in range(size)])  14.4 us
    all_to_all x1, blocking collectives, on_device(): both = lax.all_to_all(both, ORB, 0, 0, tiled=True)  13.3 us
    ppermute x4, waiting for transfers between devices, from_tile(): return lax.ppermute(value, PTS, [((i + steps) % 32, i) for i in range(32)])  9.65 us
    ppermute x1, starting transfers between devices, on_device(): mate = lax.ppermute(mine, 'core', SWAP)  8.75 us
    ppermute x3, starting transfers between devices, on_device(): others.append(lax.ppermute(part, ORB, [(i, i ^ flip) for i in range(16)]))  8.37 us
    all_to_all x1, starting transfers between devices, on_device(): gathered = lax.all_to_all(copies, 'z', 0, 0, tiled=True)  6.99 us
  transfers between devices with their start and end apart: 16, of which 7 were waited for; matrix products, arithmetic and copies ran while one was open for 1% of the time, Pallas kernels for 1%

profile of v10, /device:TPU:1, one launch (start us, length us, event | category | flops | bytes accessed | tf_op | source)
XLA Modules:
  0.0 135.5 jit_solution(1640870949628381431)
XLA Ops:
  0.7 1.0 maximum_maximum_fusion.mine
  1.7 8.7 %collective-permute-start = (bf16[96,1792]{1,0:T(8,128)(2,1)S(1)}, bf16[96,1792]{1,0:T(8,128)(2,1)S(1)}, u32[]{:S(2)}, u32[]{:S(2)}) collective-permute-start(bf16[96,1792]{1,0:T(8,128)(2,1)S(1)} %maximum_maximum_fusion.mine), channel_id=1, source_target_pairs={{0,16},{16,0},{1,17},{17,1},{2,18},{18,2},{3,19},{19,3},{4,20},{20... | collective-permute-start | bytes 1032200 | tf_op jit(solution)/shard_map/ppermute | solution.py:242
  10.5 7.8 %collective-permute-start.1 = (bf16[96,1792]{1,0:T(8,128)(2,1)S(1)}, bf16[96,1792]{1,0:T(8,128)(2,1)S(1)}, u32[]{:S(2)}, u32[]{:S(2)}) collective-permute-start(bf16[96,1792]{1,0:T(8,128)(2,1)S(1)} %maximum_maximum_fusion.mine), channel_id=1, source_target_pairs={{32,0},{48,16},{64,32},{80,48},{96,64},{112,80},{128,96},{144,112}... | collective-permute-start | bytes 1032200 | tf_op jit(solution)/shard_map/ppermute | solution.py:21
  18.3 1.9 %collective-permute-start.2 = (bf16[96,1792]{1,0:T(8,128)(2,1)S(1)}, bf16[96,1792]{1,0:T(8,128)(2,1)S(1)}, u32[]{:S(2)}, u32[]{:S(2)}) collective-permute-start(bf16[96,1792]{1,0:T(8,128)(2,1)S(1)} %maximum_maximum_fusion.mine), channel_id=1, source_target_pairs={{448,0},{464,16},{480,32},{496,48},{0,64},{16,80},{32,96},{48,112}... | collective-permute-start | bytes 1032200 | tf_op jit(solution)/shard_map/ppermute | solution.py:21
  21.1 4.6 %collective-permute-done.1.up = bf16[96,1792]{1,0:T(8,128)(2,1)S(1)} collective-permute-done((bf16[96,1792]{1,0:T(8,128)(2,1)S(1)}, bf16[96,1792]{1,0:T(8,128)(2,1)S(1)}, u32[]{:S(2)}, u32[]{:S(2)}) %collective-permute-start.1) | collective-permute-done | bytes 344096 | tf_op jit(solution)/shard_map/ppermute | solution.py:21
  25.7 5.0 %collective-permute-done.2.down = bf16[96,1792]{1,0:T(8,128)(2,1)S(1)} collective-permute-done((bf16[96,1792]{1,0:T(8,128)(2,1)S(1)}, bf16[96,1792]{1,0:T(8,128)(2,1)S(1)}, u32[]{:S(2)}, u32[]{:S(2)}) %collective-permute-start.2) | collective-permute-done | bytes 344096 | tf_op jit(solution)/shard_map/ppermute | solution.py:21
  31.7 15.5 %all_to_all.15.parts = bf16[16,24,384]{2,1,0:T(8,128)(2,1)S(1)} all-to-all(bf16[16,24,384]{2,1,0:T(8,128)(2,1)S(1)} %green.1), channel_id=1, replica_groups=mesh['z'=8,'xh'=2,'core'=2,'xl'=2,'y'=8] {'xl','y'}, dimensions={0} | all-to-all | bytes 589824 | tf_op jit(solution)/shard_map/all_to_all | solution.py:248
  47.3 13.3 %all_to_all.16.parts = bf16[16,12,384]{2,1,0:T(8,128)(2,1)S(1)} all-to-all(bf16[16,12,384]{2,1,0:T(8,128)(2,1)S(1)} %product.1), channel_id=1, replica_groups=mesh['z'=8,'xh'=2,'core'=2,'xl'=2,'y'=8] {'xl','y'}, dimensions={0} | all-to-all | bytes 294912 | tf_op jit(solution)/shard_map/all_to_all | solution.py:250
  61.2 4.9 %collective-permute-start.3 = (f32[2,96,256]{2,1,0:T(8,128)S(1)}, f32[2,96,256]{2,1,0:T(8,128)S(1)}, u32[]{:S(2)}, u32[]{:S(2)}) collective-permute-start(f32[2,96,256]{2,1,0:T(8,128)S(1)} %get-tuple-element.10), channel_id=1, source_target_pairs={{0,16},{16,0},{1,17},{17,1},{2,18},{18,2},{3,19},{19,3},{4,20},{20... | collective-permute-start | bytes 589832 | tf_op jit(solution)/shard_map/ppermute | solution.py:256
  66.2 1.9 %collective-permute-start.4 = (bf16[2,96,256]{2,1,0:T(8,128)(2,1)S(1)}, bf16[2,96,256]{2,1,0:T(8,128)(2,1)S(1)}, u32[]{:S(2)}, u32[]{:S(2)}) collective-permute-start(bf16[2,96,256]{2,1,0:T(8,128)(2,1)S(1)} %get-tuple-element.11), channel_id=1, source_target_pairs={{480,0},{496,16},{0,32},{16,48},{32,64},{48,80},{64,96},{80,112},{... | collective-permute-start | bytes 294920 | tf_op jit(solution)/shard_map/ppermute | solution.py:21
  68.1 3.6 %collective-permute-start.5 = (bf16[2,96,256]{2,1,0:T(8,128)(2,1)S(1)}, bf16[2,96,256]{2,1,0:T(8,128)(2,1)S(1)}, u32[]{:S(2)}, u32[]{:S(2)}) collective-permute-start(bf16[2,96,256]{2,1,0:T(8,128)(2,1)S(1)} %get-tuple-element.12), channel_id=1, source_target_pairs={{64,0},{80,16},{96,32},{112,48},{128,64},{144,80},{160,96},{176,11... | collective-permute-start | bytes 294920 | tf_op jit(solution)/shard_map/ppermute | solution.py:21
  72.4 9.4 %collective-permute-start.7 = (bf16[96,256]{1,0:T(8,128)(2,1)S(1)}, bf16[96,256]{1,0:T(8,128)(2,1)S(1)}, u32[]{:S(2)}, u32[]{:S(2)}) collective-permute-start(bf16[96,256]{1,0:T(8,128)(2,1)S(1)} %collective-permute-done.6), channel_id=1, source_target_pairs={{0,2},{1,3},{2,0},{3,1},{4,6},{5,7},{6,4},{7,5},{8,10},{9,11},{10,... | collective-permute-start | bytes 147464 | tf_op jit(solution)/shard_map/ppermute | solution.py:26
  82.7 7.0 %all-to-all-start.2 = ((bf16[8,2,96,256]{3,2,1,0:T(8,128)(2,1)}), bf16[8,2,96,256]{3,2,1,0:T(8,128)(2,1)S(1)}, u32[]{:S(2)}, u32[]{:S(2)}) async-start(bf16[8,2,96,256]{3,2,1,0:T(8,128)(2,1)} %combine.1), calls=%async_computation.2 | async-start | bytes 1572864 | tf_op jit(solution)/shard_map/all_to_all | solution.py:258
  89.7 5.0 %collective-permute-start.8 = (bf16[2,96,256]{2,1,0:T(8,128)(2,1)S(1)}, bf16[2,96,256]{2,1,0:T(8,128)(2,1)S(1)}, u32[]{:S(2)}, u32[]{:S(2)}) collective-permute-start(bf16[2,96,256]{2,1,0:T(8,128)(2,1)S(1)} %pad_maximum_fusion.3), channel_id=1, source_target_pairs={{0,4},{1,5},{2,6},{3,7},{4,0},{5,1},{6,2},{7,3},{8,12},{9,13},{10,... | collective-permute-start | bytes 294920 | tf_op jit(solution)/shard_map/ppermute | solution.py:26
  94.8 5.4 %collective-permute-done.8 = bf16[2,96,256]{2,1,0:T(8,128)(2,1)S(1)} collective-permute-done((bf16[2,96,256]{2,1,0:T(8,128)(2,1)S(1)}, bf16[2,96,256]{2,1,0:T(8,128)(2,1)S(1)}, u32[]{:S(2)}, u32[]{:S(2)}) %collective-permute-start.8) | collective-permute-done | bytes 98336 | tf_op jit(solution)/shard_map/ppermute | solution.py:26
  100.2 1.9 %collective-permute-start.10 = (bf16[2,2,96,256]{3,2,1,0:T(8,128)(2,1)S(1)}, bf16[2,2,96,256]{3,2,1,0:T(8,128)(2,1)S(1)}, u32[]{:S(2)}, u32[]{:S(2)}) collective-permute-start(bf16[2,2,96,256]{3,2,1,0:T(8,128)(2,1)S(1)} %pad_maximum_fusion.2), channel_id=1, source_target_pairs={{0,8},{1,9},{2,10},{3,11},{4,12},{5,13},{6,14},{7,15},{8,0},{9,1},... | collective-permute-start | bytes 589832 | tf_op jit(solution)/shard_map/ppermute | solution.py:261
  102.2 2.6 %collective-permute-start.9 = (bf16[2,2,96,256]{3,2,1,0:T(8,128)(2,1)S(1)}, bf16[2,2,96,256]{3,2,1,0:T(8,128)(2,1)S(1)}, u32[]{:S(2)}, u32[]{:S(2)}) collective-permute-start(bf16[2,2,96,256]{3,2,1,0:T(8,128)(2,1)S(1)} %pad_maximum_fusion.2), channel_id=1, source_target_pairs={{0,9},{1,8},{2,11},{3,10},{4,13},{5,12},{6,15},{7,14},{8,1},{9,0},... | collective-permute-start | bytes 589832 | tf_op jit(solution)/shard_map/ppermute | solution.py:261
  104.7 3.9 %collective-permute-start.11 = (bf16[2,2,96,256]{3,2,1,0:T(8,128)(2,1)S(1)}, bf16[2,2,96,256]{3,2,1,0:T(8,128)(2,1)S(1)}, u32[]{:S(2)}, u32[]{:S(2)}) collective-permute-start(bf16[2,2,96,256]{3,2,1,0:T(8,128)(2,1)S(1)} %pad_maximum_fusion.2), channel_id=1, source_target_pairs={{0,1},{1,0},{2,3},{3,2},{4,5},{5,4},{6,7},{7,6},{8,9},{9,8},{10,11... | collective-permute-start | bytes 589832 | tf_op jit(solution)/shard_map/ppermute | solution.py:261
  109.6 4.1 %collective-permute-done.11 = bf16[2,2,96,256]{3,2,1,0:T(8,128)(2,1)S(1)} collective-permute-done((bf16[2,2,96,256]{3,2,1,0:T(8,128)(2,1)S(1)}, bf16[2,2,96,256]{3,2,1,0:T(8,128)(2,1)S(1)}, u32[]{:S(2)}, u32[]{:S(2)}) %collective-permute-start.11) | collective-permute-done | bytes 196640 | tf_op jit(solution)/shard_map/ppermute | solution.py:261
  114.2 5.0 %collective-permute-start.12 = (f32[2,128,256]{2,1,0:T(8,128)S(1)}, f32[2,128,256]{2,1,0:T(8,128)S(1)}, u32[]{:S(2)}, u32[]{:S(2)}) collective-permute-start(f32[2,128,256]{2,1,0:T(8,128)S(1)} %convolution_bitcast_fusion.2), channel_id=1, source_target_pairs={{0,16},{16,0},{1,17},{17,1},{2,18},{18,2},{3,19},{19,3},{4,20},{20... | collective-permute-start | bytes 786440 | tf_op jit(solution)/shard_map/ppermute | solution.py:282
  119.5 6.0 %collective-permute-start.13 = (bf16[2,128,256]{2,1,0:T(8,128)(2,1)S(1)}, bf16[2,128,256]{2,1,0:T(8,128)(2,1)S(1)}, u32[]{:S(2)}, u32[]{:S(2)}) collective-permute-start(bf16[2,128,256]{2,1,0:T(8,128)(2,1)S(1)} %fusion.3), channel_id=1, source_target_pairs={{0,32},{32,0},{1,33},{33,1},{2,34},{34,2},{3,35},{35,3},{4,36},{36... | collective-permute-start | bytes 393224 | tf_op jit(solution)/shard_map/ppermute | solution.py:281
  125.9 1.9 %collective-permute-start.14 = (bf16[2,128,256]{2,1,0:T(8,128)(2,1)S(1)}, bf16[2,128,256]{2,1,0:T(8,128)(2,1)S(1)}, u32[]{:S(2)}, u32[]{:S(2)}) collective-permute-start(bf16[2,128,256]{2,1,0:T(8,128)(2,1)S(1)} %fusion.2), channel_id=1, source_target_pairs={{0,48},{48,0},{16,32},{32,16},{1,49},{49,1},{17,33},{33,17},{2,50}... | collective-permute-start | bytes 393224 | tf_op jit(solution)/shard_map/ppermute | solution.py:278
  128.1 1.2 collective-permute-done.13.across
  129.4 5.3 %collective-permute-done.14.diag = bf16[2,128,256]{2,1,0:T(8,128)(2,1)S(1)} collective-permute-done((bf16[2,128,256]{2,1,0:T(8,128)(2,1)S(1)}, bf16[2,128,256]{2,1,0:T(8,128)(2,1)S(1)}, u32[]{:S(2)}, u32[]{:S(2)}) %collective-permute-start.14) | collective-permute-done | bytes 131104 | tf_op jit(solution)/shard_map/ppermute | solution.py:278
  (40 shorter events, 7.9 us)
Async XLA Ops:
  0.7 19.5 %copy-start.3 = (f32[2]{0:T(128)S(1)}, f32[2]{0:T(128)}, u32[]{:S(2)}) copy-start(f32[2]{0:T(128)} %param.11) | copy-start | bytes 28
  1.7 19.2 %copy-start.1 = (f32[1280]{0:T(1024)S(1)}, f32[1280]{0:T(1024)}, u32[]{:S(2)}) copy-start(f32[1280]{0:T(1024)} %param.10) | copy-start | bytes 15364
  1.7 19.3 %collective-permute-start = (bf16[96,1792]{1,0:T(8,128)(2,1)S(1)}, bf16[96,1792]{1,0:T(8,128)(2,1)S(1)}, u32[]{:S(2)}, u32[]{:S(2)}) collective-permute-start(bf16[96,1792]{1,0:T(8,128)(2,1)S(1)} %maximum_maximum_fusion.mine), channel_id=1, source_target_pairs={{0,16},{16,0},{1,17},{17,1},{2,18},{18,2},{3,19},{19,3},{4,20},{20... | collective-permute-start | bytes 1032200 | tf_op jit(solution)/shard_map/ppermute | solution.py:242
  10.5 15.2 %collective-permute-start.1 = (bf16[96,1792]{1,0:T(8,128)(2,1)S(1)}, bf16[96,1792]{1,0:T(8,128)(2,1)S(1)}, u32[]{:S(2)}, u32[]{:S(2)}) collective-permute-start(bf16[96,1792]{1,0:T(8,128)(2,1)S(1)} %maximum_maximum_fusion.mine), channel_id=1, source_target_pairs={{32,0},{48,16},{64,32},{80,48},{96,64},{112,80},{128,96},{144,112}... | collective-permute-start | bytes 1032200 | tf_op jit(solution)/shard_map/ppermute | solution.py:21
  18.3 12.4 %collective-permute-start.2 = (bf16[96,1792]{1,0:T(8,128)(2,1)S(1)}, bf16[96,1792]{1,0:T(8,128)(2,1)S(1)}, u32[]{:S(2)}, u32[]{:S(2)}) collective-permute-start(bf16[96,1792]{1,0:T(8,128)(2,1)S(1)} %maximum_maximum_fusion.mine), channel_id=1, source_target_pairs={{448,0},{464,16},{480,32},{496,48},{0,64},{16,80},{32,96},{48,112}... | collective-permute-start | bytes 1032200 | tf_op jit(solution)/shard_map/ppermute | solution.py:21
  20.2 0.7 copy-start.2
  60.7 11.0 %copy-start = (bf16[96,256]{1,0:T(8,128)(2,1)S(1)}, bf16[96,256]{1,0:T(8,128)(2,1)}, u32[]{:S(2)}) copy-start(bf16[96,256]{1,0:T(8,128)(2,1)} %param.13) | copy-start | bytes 147460
  61.2 20.5 %collective-permute-start.3 = (f32[2,96,256]{2,1,0:T(8,128)S(1)}, f32[2,96,256]{2,1,0:T(8,128)S(1)}, u32[]{:S(2)}, u32[]{:S(2)}) collective-permute-start(f32[2,96,256]{2,1,0:T(8,128)S(1)} %get-tuple-element.10), channel_id=1, source_target_pairs={{0,16},{16,0},{1,17},{17,1},{2,18},{18,2},{3,19},{19,3},{4,20},{20... | collective-permute-start | bytes 589832 | tf_op jit(solution)/shard_map/ppermute | solution.py:256
  66.2 15.6 %collective-permute-start.4 = (bf16[2,96,256]{2,1,0:T(8,128)(2,1)S(1)}, bf16[2,96,256]{2,1,0:T(8,128)(2,1)S(1)}, u32[]{:S(2)}, u32[]{:S(2)}) collective-permute-start(bf16[2,96,256]{2,1,0:T(8,128)(2,1)S(1)} %get-tuple-element.11), channel_id=1, source_target_pairs={{480,0},{496,16},{0,32},{16,48},{32,64},{48,80},{64,96},{80,112},{... | collective-permute-start | bytes 294920 | tf_op jit(solution)/shard_map/ppermute | solution.py:21
  68.1 13.6 %collective-permute-start.5 = (bf16[2,96,256]{2,1,0:T(8,128)(2,1)S(1)}, bf16[2,96,256]{2,1,0:T(8,128)(2,1)S(1)}, u32[]{:S(2)}, u32[]{:S(2)}) collective-permute-start(bf16[2,96,256]{2,1,0:T(8,128)(2,1)S(1)} %get-tuple-element.12), channel_id=1, source_target_pairs={{64,0},{80,16},{96,32},{112,48},{128,64},{144,80},{160,96},{176,11... | collective-permute-start | bytes 294920 | tf_op jit(solution)/shard_map/ppermute | solution.py:21
  71.7 0.7 collective-permute-start.6
  72.4 17.3 %collective-permute-start.7 = (bf16[96,256]{1,0:T(8,128)(2,1)S(1)}, bf16[96,256]{1,0:T(8,128)(2,1)S(1)}, u32[]{:S(2)}, u32[]{:S(2)}) collective-permute-start(bf16[96,256]{1,0:T(8,128)(2,1)S(1)} %collective-permute-done.6), channel_id=1, source_target_pairs={{0,2},{1,3},{2,0},{3,1},{4,6},{5,7},{6,4},{7,5},{8,10},{9,11},{10,... | collective-permute-start | bytes 147464 | tf_op jit(solution)/shard_map/ppermute | solution.py:26
  82.7 31.2 %all-to-all-start.2 = ((bf16[8,2,96,256]{3,2,1,0:T(8,128)(2,1)}), bf16[8,2,96,256]{3,2,1,0:T(8,128)(2,1)S(1)}, u32[]{:S(2)}, u32[]{:S(2)}) async-start(bf16[8,2,96,256]{3,2,1,0:T(8,128)(2,1)} %combine.1), calls=%async_computation.2 | async-start | bytes 1572864 | tf_op jit(solution)/shard_map/all_to_all | solution.py:258
  89.7 10.4 %collective-permute-start.8 = (bf16[2,96,256]{2,1,0:T(8,128)(2,1)S(1)}, bf16[2,96,256]{2,1,0:T(8,128)(2,1)S(1)}, u32[]{:S(2)}, u32[]{:S(2)}) collective-permute-start(bf16[2,96,256]{2,1,0:T(8,128)(2,1)S(1)} %pad_maximum_fusion.3), channel_id=1, source_target_pairs={{0,4},{1,5},{2,6},{3,7},{4,0},{5,1},{6,2},{7,3},{8,12},{9,13},{10,... | collective-permute-start | bytes 294920 | tf_op jit(solution)/shard_map/ppermute | solution.py:26
  100.2 8.5 %collective-permute-start.10 = (bf16[2,2,96,256]{3,2,1,0:T(8,128)(2,1)S(1)}, bf16[2,2,96,256]{3,2,1,0:T(8,128)(2,1)S(1)}, u32[]{:S(2)}, u32[]{:S(2)}) collective-permute-start(bf16[2,2,96,256]{3,2,1,0:T(8,128)(2,1)S(1)} %pad_maximum_fusion.2), channel_id=1, source_target_pairs={{0,8},{1,9},{2,10},{3,11},{4,12},{5,13},{6,14},{7,15},{8,0},{9,1},... | collective-permute-start | bytes 589832 | tf_op jit(solution)/shard_map/ppermute | solution.py:261
  102.2 7.4 %collective-permute-start.9 = (bf16[2,2,96,256]{3,2,1,0:T(8,128)(2,1)S(1)}, bf16[2,2,96,256]{3,2,1,0:T(8,128)(2,1)S(1)}, u32[]{:S(2)}, u32[]{:S(2)}) collective-permute-start(bf16[2,2,96,256]{3,2,1,0:T(8,128)(2,1)S(1)} %pad_maximum_fusion.2), channel_id=1, source_target_pairs={{0,9},{1,8},{2,11},{3,10},{4,13},{5,12},{6,15},{7,14},{8,1},{9,0},... | collective-permute-start | bytes 589832 | tf_op jit(solution)/shard_map/ppermute | solution.py:261
  104.7 9.0 %collective-permute-start.11 = (bf16[2,2,96,256]{3,2,1,0:T(8,128)(2,1)S(1)}, bf16[2,2,96,256]{3,2,1,0:T(8,128)(2,1)S(1)}, u32[]{:S(2)}, u32[]{:S(2)}) collective-permute-start(bf16[2,2,96,256]{3,2,1,0:T(8,128)(2,1)S(1)} %pad_maximum_fusion.2), channel_id=1, source_target_pairs={{0,1},{1,0},{2,3},{3,2},{4,5},{5,4},{6,7},{7,6},{8,9},{9,8},{10,11... | collective-permute-start | bytes 589832 | tf_op jit(solution)/shard_map/ppermute | solution.py:261
  114.2 20.5 %collective-permute-start.12 = (f32[2,128,256]{2,1,0:T(8,128)S(1)}, f32[2,128,256]{2,1,0:T(8,128)S(1)}, u32[]{:S(2)}, u32[]{:S(2)}) collective-permute-start(f32[2,128,256]{2,1,0:T(8,128)S(1)} %convolution_bitcast_fusion.2), channel_id=1, source_target_pairs={{0,16},{16,0},{1,17},{17,1},{2,18},{18,2},{3,19},{19,3},{4,20},{20... | collective-permute-start | bytes 786440 | tf_op jit(solution)/shard_map/ppermute | solution.py:282
  119.5 9.8 %collective-permute-start.13 = (bf16[2,128,256]{2,1,0:T(8,128)(2,1)S(1)}, bf16[2,128,256]{2,1,0:T(8,128)(2,1)S(1)}, u32[]{:S(2)}, u32[]{:S(2)}) collective-permute-start(bf16[2,128,256]{2,1,0:T(8,128)(2,1)S(1)} %fusion.3), channel_id=1, source_target_pairs={{0,32},{32,0},{1,33},{33,1},{2,34},{34,2},{3,35},{35,3},{4,36},{36... | collective-permute-start | bytes 393224 | tf_op jit(solution)/shard_map/ppermute | solution.py:281
  125.9 8.8 %collective-permute-start.14 = (bf16[2,128,256]{2,1,0:T(8,128)(2,1)S(1)}, bf16[2,128,256]{2,1,0:T(8,128)(2,1)S(1)}, u32[]{:S(2)}, u32[]{:S(2)}) collective-permute-start(bf16[2,128,256]{2,1,0:T(8,128)(2,1)S(1)} %fusion.2), channel_id=1, source_target_pairs={{0,48},{48,0},{16,32},{32,16},{1,49},{49,1},{17,33},{33,17},{2,50}... | collective-permute-start | bytes 393224 | tf_op jit(solution)/shard_map/ppermute | solution.py:278

commit v11 on v10

--- a/solution.py
+++ b/solution.py
@@ -212,24 +212,24 @@
     )(own, a, b, c)
 
 
-def finish_kernel(own, beside, across, diag, out):
+def finish_kernel(x_hi, own, beside, across, out):
     for t in range(2):
-        out[:, t, :] = own[t] + beside[t] + across[t].astype(F32) + diag[t].astype(F32)
-
-
-def finish(own, beside, across, diag):
+        out[:, t, :] = own[t] + beside[x_hi[0], t] + across[t].astype(F32)
+
+
+def finish(x_hi, own, beside, across):
     times, count, naux = own.shape
     return pl.pallas_call(
         finish_kernel,
         out_shape=jax.ShapeDtypeStruct((count, times, naux), F32),
-        in_specs=[WHOLE] * 4,
+        in_specs=[SCALARS] + [WHOLE] * 3,
         out_specs=WHOLE,
         compiler_params=pltpu.CompilerParams(vmem_limit_bytes=8 * 2**20),
         cost_estimate=pl.CostEstimate(
             flops=4 * own.size, bytes_accessed=16 * own.size, transcendentals=0
         ),
         name="finish",
-    )(own, beside, across, diag)
+    )(x_hi, own, beside, across)
 
 
 def on_device(phi_occ, phi_vir, eps_occ, eps_vir, taus, pair_mask, basis):
@@ -266,21 +266,22 @@
     blocks = jnp.stack(
         [jnp.stack([jnp.where(right, b[h], a[h]), jnp.where(right, a[h], b[h])]) for h in range(2)]
     ).reshape(2, 8, rows, naux)
-    at = xh * 2 + core
-
-    def response(flip):
-        j = at ^ flip
-        chosen = lax.dynamic_slice(
-            blocks, (j // 2, 0, 0, (j % 2) * (naux // 2)), (1, 8, rows, naux // 2)
-        )[0]
-        return jnp.einsum("zrp,ztrq->tpq", chosen, gathered, preferred_element_type=F32)
-
-    both_way = lax.ppermute(
-        response(3).astype(BF), ("xh", "core"), [(0, 3), (3, 0), (1, 2), (2, 1)]
-    )
-    across = lax.ppermute(response(2).astype(BF), "xh", SWAP)
-    beside = lax.ppermute(response(1), "core", SWAP)
-    return finish(response(0), beside, across, both_way)
+
+    def chosen(half, part_of):
+        start = (half, 0, 0, part_of * (naux // 2))
+        return lax.dynamic_slice(blocks, start, (1, 8, rows, naux // 2))[0]
+
+    def response(cols):
+        return jnp.einsum("zrp,ztrq->tpq", cols, gathered, preferred_element_type=F32)
+
+    start = (0, 0, 0, (1 - core) * (naux // 2))
+    others = lax.dynamic_slice(blocks, start, (2, 8, rows, naux // 2))
+    pair = jnp.einsum("hzrp,ztrq->htpq", others, gathered, preferred_element_type=F32)
+    beside = lax.ppermute(pair, "core", SWAP)
+    mine_here, mine_there = response(chosen(xh, core)), response(chosen(1 - xh, core))
+    there = lax.dynamic_index_in_dim(beside, 1 - xh, 0, keepdims=False)
+    across = lax.ppermute((mine_there + there).astype(BF), "xh", SWAP)
+    return finish(xh.reshape(1), mine_here, beside, across)
 
 
 def solution(mesh):

time: 136 us -> 132 us (0.971)
  starting transfers between devices: 72.1 us -> 70.2 us
  waiting for transfers between devices: 26.5 us -> 24.8 us
    ppermute x3 -> x2, starting transfers between devices: 12.9 us -> 11 us  [the longest x1 5.98 us: on_device(): across = lax.ppermute((mine_there + there).astype(BF), 'xh', SWAP)]
    ppermute x3 -> x2, waiting for transfers between devices: 6.53 us -> 4.65 us  [the longest x1 3.14 us: on_device(): across = lax.ppermute((mine_there + there).astype(BF), 'xh', SWAP)]
  transfers between devices with their start and end apart: 16 -> 15, of which waited for: 7 -> 7; matrix products, arithmetic and copies ran while one was open for 1% -> 1% of each run, Pallas kernels for 1% -> 1%
where the time goes in v11:
time: 132 us; the launch traced here: 131 us
  starting transfers between devices  70.2 us (53%)
  blocking collectives  28.8 us (22%)
  waiting for transfers between devices  24.8 us (19%)
  Pallas kernels  3.41 us (3%)
  other arithmetic  2.07 us (2%)
    all_to_all x1, blocking collectives, on_device(): sums = lax.all_to_all(part_sums, ORB, 0, 0, tiled=True)  15.5 us
    ppermute x4, starting transfers between devices, from_tile(): return lax.ppermute(value, PTS, [((i + steps) % 32, i) for i in range(32)])  15.2 us
    ppermute x2, starting transfers between devices, trade(): return lax.ppermute(value, axis, [(i, i ^ bit) for i in range(size)])  14.4 us
    all_to_all x1, blocking collectives, on_device(): both = lax.all_to_all(both, ORB, 0, 0, tiled=True)  13.3 us
    ppermute x4, waiting for transfers between devices, from_tile(): return lax.ppermute(value, PTS, [((i + steps) % 32, i) for i in range(32)])  9.65 us
    ppermute x1, starting transfers between devices, on_device(): mate = lax.ppermute(mine, 'core', SWAP)  8.75 us
    ppermute x3, starting transfers between devices, on_device(): others.append(lax.ppermute(part, ORB, [(i, i ^ flip) for i in range(16)]))  8.37 us
    all_to_all x1, starting transfers between devices, on_device(): gathered = lax.all_to_all(copies, 'z', 0, 0, tiled=True)  6.99 us
  transfers between devices with their start and end apart: 15, of which 7 were waited for; matrix products, arithmetic and copies ran while one was open for 1% of the time, Pallas kernels for 1%

profile of v11, /device:TPU:1, one launch (start us, length us, event | category | flops | bytes accessed | tf_op | source)
XLA Modules:
  0.0 131.4 jit_solution(14648768725472558209)
XLA Ops:
  0.7 1.0 maximum_maximum_fusion.mine
  1.7 8.7 %collective-permute-start = (bf16[96,1792]{1,0:T(8,128)(2,1)S(1)}, bf16[96,1792]{1,0:T(8,128)(2,1)S(1)}, u32[]{:S(2)}, u32[]{:S(2)}) collective-permute-start(bf16[96,1792]{1,0:T(8,128)(2,1)S(1)} %maximum_maximum_fusion.mine), channel_id=1, source_target_pairs={{0,16},{16,0},{1,17},{17,1},{2,18},{18,2},{3,19},{19,3},{4,20},{20... | collective-permute-start | bytes 1032200 | tf_op jit(solution)/shard_map/ppermute | solution.py:242
  10.5 7.8 %collective-permute-start.1 = (bf16[96,1792]{1,0:T(8,128)(2,1)S(1)}, bf16[96,1792]{1,0:T(8,128)(2,1)S(1)}, u32[]{:S(2)}, u32[]{:S(2)}) collective-permute-start(bf16[96,1792]{1,0:T(8,128)(2,1)S(1)} %maximum_maximum_fusion.mine), channel_id=1, source_target_pairs={{32,0},{48,16},{64,32},{80,48},{96,64},{112,80},{128,96},{144,112}... | collective-permute-start | bytes 1032200 | tf_op jit(solution)/shard_map/ppermute | solution.py:21
  18.3 1.9 %collective-permute-start.2 = (bf16[96,1792]{1,0:T(8,128)(2,1)S(1)}, bf16[96,1792]{1,0:T(8,128)(2,1)S(1)}, u32[]{:S(2)}, u32[]{:S(2)}) collective-permute-start(bf16[96,1792]{1,0:T(8,128)(2,1)S(1)} %maximum_maximum_fusion.mine), channel_id=1, source_target_pairs={{448,0},{464,16},{480,32},{496,48},{0,64},{16,80},{32,96},{48,112}... | collective-permute-start | bytes 1032200 | tf_op jit(solution)/shard_map/ppermute | solution.py:21
  21.1 4.6 %collective-permute-done.1.up = bf16[96,1792]{1,0:T(8,128)(2,1)S(1)} collective-permute-done((bf16[96,1792]{1,0:T(8,128)(2,1)S(1)}, bf16[96,1792]{1,0:T(8,128)(2,1)S(1)}, u32[]{:S(2)}, u32[]{:S(2)}) %collective-permute-start.1) | collective-permute-done | bytes 344096 | tf_op jit(solution)/shard_map/ppermute | solution.py:21
  25.7 5.0 %collective-permute-done.2.down = bf16[96,1792]{1,0:T(8,128)(2,1)S(1)} collective-permute-done((bf16[96,1792]{1,0:T(8,128)(2,1)S(1)}, bf16[96,1792]{1,0:T(8,128)(2,1)S(1)}, u32[]{:S(2)}, u32[]{:S(2)}) %collective-permute-start.2) | collective-permute-done | bytes 344096 | tf_op jit(solution)/shard_map/ppermute | solution.py:21
  30.7 1.0 green.1
  31.7 15.5 %all_to_all.15.parts = bf16[16,24,384]{2,1,0:T(8,128)(2,1)S(1)} all-to-all(bf16[16,24,384]{2,1,0:T(8,128)(2,1)S(1)} %green.1), channel_id=1, replica_groups=mesh['z'=8,'xh'=2,'core'=2,'xl'=2,'y'=8] {'xl','y'}, dimensions={0} | all-to-all | bytes 589824 | tf_op jit(solution)/shard_map/all_to_all | solution.py:248
  47.3 13.3 %all_to_all.16.parts = bf16[16,12,384]{2,1,0:T(8,128)(2,1)S(1)} all-to-all(bf16[16,12,384]{2,1,0:T(8,128)(2,1)S(1)} %product.1), channel_id=1, replica_groups=mesh['z'=8,'xh'=2,'core'=2,'xl'=2,'y'=8] {'xl','y'}, dimensions={0} | all-to-all | bytes 294912 | tf_op jit(solution)/shard_map/all_to_all | solution.py:250
  61.2 4.9 %collective-permute-start.3 = (f32[2,96,256]{2,1,0:T(8,128)S(1)}, f32[2,96,256]{2,1,0:T(8,128)S(1)}, u32[]{:S(2)}, u32[]{:S(2)}) collective-permute-start(f32[2,96,256]{2,1,0:T(8,128)S(1)} %get-tuple-element.10), channel_id=1, source_target_pairs={{0,16},{16,0},{1,17},{17,1},{2,18},{18,2},{3,19},{19,3},{4,20},{20... | collective-permute-start | bytes 589832 | tf_op jit(solution)/shard_map/ppermute | solution.py:256
  66.2 1.9 %collective-permute-start.4 = (bf16[2,96,256]{2,1,0:T(8,128)(2,1)S(1)}, bf16[2,96,256]{2,1,0:T(8,128)(2,1)S(1)}, u32[]{:S(2)}, u32[]{:S(2)}) collective-permute-start(bf16[2,96,256]{2,1,0:T(8,128)(2,1)S(1)} %get-tuple-element.11), channel_id=1, source_target_pairs={{480,0},{496,16},{0,32},{16,48},{32,64},{48,80},{64,96},{80,112},{... | collective-permute-start | bytes 294920 | tf_op jit(solution)/shard_map/ppermute | solution.py:21
  68.1 3.6 %collective-permute-start.5 = (bf16[2,96,256]{2,1,0:T(8,128)(2,1)S(1)}, bf16[2,96,256]{2,1,0:T(8,128)(2,1)S(1)}, u32[]{:S(2)}, u32[]{:S(2)}) collective-permute-start(bf16[2,96,256]{2,1,0:T(8,128)(2,1)S(1)} %get-tuple-element.12), channel_id=1, source_target_pairs={{64,0},{80,16},{96,32},{112,48},{128,64},{144,80},{160,96},{176,11... | collective-permute-start | bytes 294920 | tf_op jit(solution)/shard_map/ppermute | solution.py:21
  72.4 9.4 %collective-permute-start.7 = (bf16[96,256]{1,0:T(8,128)(2,1)S(1)}, bf16[96,256]{1,0:T(8,128)(2,1)S(1)}, u32[]{:S(2)}, u32[]{:S(2)}) collective-permute-start(bf16[96,256]{1,0:T(8,128)(2,1)S(1)} %collective-permute-done.6), channel_id=1, source_target_pairs={{0,2},{1,3},{2,0},{3,1},{4,6},{5,7},{6,4},{7,5},{8,10},{9,11},{10,... | collective-permute-start | bytes 147464 | tf_op jit(solution)/shard_map/ppermute | solution.py:26
  82.7 7.0 %all-to-all-start.2 = ((bf16[8,2,96,256]{3,2,1,0:T(8,128)(2,1)}), bf16[8,2,96,256]{3,2,1,0:T(8,128)(2,1)S(1)}, u32[]{:S(2)}, u32[]{:S(2)}) async-start(bf16[8,2,96,256]{3,2,1,0:T(8,128)(2,1)} %combine.1), calls=%async_computation.2 | async-start | bytes 1572864 | tf_op jit(solution)/shard_map/all_to_all | solution.py:258
  89.8 5.0 %collective-permute-start.8 = (bf16[2,96,256]{2,1,0:T(8,128)(2,1)S(1)}, bf16[2,96,256]{2,1,0:T(8,128)(2,1)S(1)}, u32[]{:S(2)}, u32[]{:S(2)}) collective-permute-start(bf16[2,96,256]{2,1,0:T(8,128)(2,1)S(1)} %pad_maximum_fusion.3), channel_id=1, source_target_pairs={{0,4},{1,5},{2,6},{3,7},{4,0},{5,1},{6,2},{7,3},{8,12},{9,13},{10,... | collective-permute-start | bytes 294920 | tf_op jit(solution)/shard_map/ppermute | solution.py:26
  94.8 5.4 %collective-permute-done.8 = bf16[2,96,256]{2,1,0:T(8,128)(2,1)S(1)} collective-permute-done((bf16[2,96,256]{2,1,0:T(8,128)(2,1)S(1)}, bf16[2,96,256]{2,1,0:T(8,128)(2,1)S(1)}, u32[]{:S(2)}, u32[]{:S(2)}) %collective-permute-start.8) | collective-permute-done | bytes 98336 | tf_op jit(solution)/shard_map/ppermute | solution.py:26
  100.2 1.9 %collective-permute-start.10 = (bf16[2,2,96,256]{3,2,1,0:T(8,128)(2,1)S(1)}, bf16[2,2,96,256]{3,2,1,0:T(8,128)(2,1)S(1)}, u32[]{:S(2)}, u32[]{:S(2)}) collective-permute-start(bf16[2,2,96,256]{3,2,1,0:T(8,128)(2,1)S(1)} %pad_maximum_fusion.2), channel_id=1, source_target_pairs={{0,8},{1,9},{2,10},{3,11},{4,12},{5,13},{6,14},{7,15},{8,0},{9,1},... | collective-permute-start | bytes 589832 | tf_op jit(solution)/shard_map/ppermute | solution.py:261
  102.2 2.6 %collective-permute-start.9 = (bf16[2,2,96,256]{3,2,1,0:T(8,128)(2,1)S(1)}, bf16[2,2,96,256]{3,2,1,0:T(8,128)(2,1)S(1)}, u32[]{:S(2)}, u32[]{:S(2)}) collective-permute-start(bf16[2,2,96,256]{3,2,1,0:T(8,128)(2,1)S(1)} %pad_maximum_fusion.2), channel_id=1, source_target_pairs={{0,9},{1,8},{2,11},{3,10},{4,13},{5,12},{6,15},{7,14},{8,1},{9,0},... | collective-permute-start | bytes 589832 | tf_op jit(solution)/shard_map/ppermute | solution.py:261
  104.7 3.9 %collective-permute-start.11 = (bf16[2,2,96,256]{3,2,1,0:T(8,128)(2,1)S(1)}, bf16[2,2,96,256]{3,2,1,0:T(8,128)(2,1)S(1)}, u32[]{:S(2)}, u32[]{:S(2)}) collective-permute-start(bf16[2,2,96,256]{3,2,1,0:T(8,128)(2,1)S(1)} %pad_maximum_fusion.2), channel_id=1, source_target_pairs={{0,1},{1,0},{2,3},{3,2},{4,5},{5,4},{6,7},{7,6},{8,9},{9,8},{10,11... | collective-permute-start | bytes 589832 | tf_op jit(solution)/shard_map/ppermute | solution.py:261
  109.6 4.1 %collective-permute-done.11 = bf16[2,2,96,256]{3,2,1,0:T(8,128)(2,1)S(1)} collective-permute-done((bf16[2,2,96,256]{3,2,1,0:T(8,128)(2,1)S(1)}, bf16[2,2,96,256]{3,2,1,0:T(8,128)(2,1)S(1)}, u32[]{:S(2)}, u32[]{:S(2)}) %collective-permute-start.11) | collective-permute-done | bytes 196640 | tf_op jit(solution)/shard_map/ppermute | solution.py:261
  114.3 5.0 %collective-permute-start.12 = (f32[2,2,128,256]{3,2,1,0:T(8,128)S(1)}, f32[2,2,128,256]{3,2,1,0:T(8,128)S(1)}, u32[]{:S(2)}, u32[]{:S(2)}) collective-permute-start(f32[2,2,128,256]{3,2,1,0:T(8,128)S(1)} %convolution_bitcast_fusion), channel_id=1, source_target_pairs={{0,16},{16,0},{1,17},{17,1},{2,18},{18,2},{3,19},{19,3},{4,20},{20... | collective-permute-start | bytes 1572872 | tf_op jit(solution)/shard_map/ppermute | solution.py:280
  119.3 1.5 %collective-permute-done.12.beside = f32[2,2,128,256]{3,2,1,0:T(8,128)S(1)} collective-permute-done((f32[2,2,128,256]{3,2,1,0:T(8,128)S(1)}, f32[2,2,128,256]{3,2,1,0:T(8,128)S(1)}, u32[]{:S(2)}, u32[]{:S(2)}) %collective-permute-start.12) | collective-permute-done | bytes 524320 | tf_op jit(solution)/shard_map/ppermute | solution.py:280
  121.2 6.0 %collective-permute-start.13 = (bf16[2,128,256]{2,1,0:T(8,128)(2,1)S(1)}, bf16[2,128,256]{2,1,0:T(8,128)(2,1)S(1)}, u32[]{:S(2)}, u32[]{:S(2)}) collective-permute-start(bf16[2,128,256]{2,1,0:T(8,128)(2,1)S(1)} %fusion.1), channel_id=1, source_target_pairs={{0,32},{32,0},{1,33},{33,1},{2,34},{34,2},{3,35},{35,3},{4,36},{36... | collective-permute-start | bytes 393224 | tf_op jit(solution)/shard_map/ppermute | solution.py:283
  127.5 3.1 %collective-permute-done.13.across = bf16[2,128,256]{2,1,0:T(8,128)(2,1)S(1)} collective-permute-done((bf16[2,128,256]{2,1,0:T(8,128)(2,1)S(1)}, bf16[2,128,256]{2,1,0:T(8,128)(2,1)S(1)}, u32[]{:S(2)}, u32[]{:S(2)}) %collective-permute-start.13) | collective-permute-done | bytes 131104 | tf_op jit(solution)/shard_map/ppermute | solution.py:283
  (37 shorter events, 6.8 us)
Async XLA Ops:
  0.7 19.5 %copy-start.3 = (f32[2]{0:T(128)S(1)}, f32[2]{0:T(128)}, u32[]{:S(2)}) copy-start(f32[2]{0:T(128)} %param.11) | copy-start | bytes 28
  1.7 19.2 %copy-start.1 = (f32[1280]{0:T(1024)S(1)}, f32[1280]{0:T(1024)}, u32[]{:S(2)}) copy-start(f32[1280]{0:T(1024)} %param.10) | copy-start | bytes 15364
  1.7 19.3 %collective-permute-start = (bf16[96,1792]{1,0:T(8,128)(2,1)S(1)}, bf16[96,1792]{1,0:T(8,128)(2,1)S(1)}, u32[]{:S(2)}, u32[]{:S(2)}) collective-permute-start(bf16[96,1792]{1,0:T(8,128)(2,1)S(1)} %maximum_maximum_fusion.mine), channel_id=1, source_target_pairs={{0,16},{16,0},{1,17},{17,1},{2,18},{18,2},{3,19},{19,3},{4,20},{20... | collective-permute-start | bytes 1032200 | tf_op jit(solution)/shard_map/ppermute | solution.py:242
  10.5 15.2 %collective-permute-start.1 = (bf16[96,1792]{1,0:T(8,128)(2,1)S(1)}, bf16[96,1792]{1,0:T(8,128)(2,1)S(1)}, u32[]{:S(2)}, u32[]{:S(2)}) collective-permute-start(bf16[96,1792]{1,0:T(8,128)(2,1)S(1)} %maximum_maximum_fusion.mine), channel_id=1, source_target_pairs={{32,0},{48,16},{64,32},{80,48},{96,64},{112,80},{128,96},{144,112}... | collective-permute-start | bytes 1032200 | tf_op jit(solution)/shard_map/ppermute | solution.py:21
  18.3 12.4 %collective-permute-start.2 = (bf16[96,1792]{1,0:T(8,128)(2,1)S(1)}, bf16[96,1792]{1,0:T(8,128)(2,1)S(1)}, u32[]{:S(2)}, u32[]{:S(2)}) collective-permute-start(bf16[96,1792]{1,0:T(8,128)(2,1)S(1)} %maximum_maximum_fusion.mine), channel_id=1, source_target_pairs={{448,0},{464,16},{480,32},{496,48},{0,64},{16,80},{32,96},{48,112}... | collective-permute-start | bytes 1032200 | tf_op jit(solution)/shard_map/ppermute | solution.py:21
  20.2 0.7 copy-start.2
  60.7 11.0 %copy-start = (bf16[96,256]{1,0:T(8,128)(2,1)S(1)}, bf16[96,256]{1,0:T(8,128)(2,1)}, u32[]{:S(2)}) copy-start(bf16[96,256]{1,0:T(8,128)(2,1)} %param.13) | copy-start | bytes 147460
  61.2 20.5 %collective-permute-start.3 = (f32[2,96,256]{2,1,0:T(8,128)S(1)}, f32[2,96,256]{2,1,0:T(8,128)S(1)}, u32[]{:S(2)}, u32[]{:S(2)}) collective-permute-start(f32[2,96,256]{2,1,0:T(8,128)S(1)} %get-tuple-element.10), channel_id=1, source_target_pairs={{0,16},{16,0},{1,17},{17,1},{2,18},{18,2},{3,19},{19,3},{4,20},{20... | collective-permute-start | bytes 589832 | tf_op jit(solution)/shard_map/ppermute | solution.py:256
  66.2 15.6 %collective-permute-start.4 = (bf16[2,96,256]{2,1,0:T(8,128)(2,1)S(1)}, bf16[2,96,256]{2,1,0:T(8,128)(2,1)S(1)}, u32[]{:S(2)}, u32[]{:S(2)}) collective-permute-start(bf16[2,96,256]{2,1,0:T(8,128)(2,1)S(1)} %get-tuple-element.11), channel_id=1, source_target_pairs={{480,0},{496,16},{0,32},{16,48},{32,64},{48,80},{64,96},{80,112},{... | collective-permute-start | bytes 294920 | tf_op jit(solution)/shard_map/ppermute | solution.py:21
  68.1 13.6 %collective-permute-start.5 = (bf16[2,96,256]{2,1,0:T(8,128)(2,1)S(1)}, bf16[2,96,256]{2,1,0:T(8,128)(2,1)S(1)}, u32[]{:S(2)}, u32[]{:S(2)}) collective-permute-start(bf16[2,96,256]{2,1,0:T(8,128)(2,1)S(1)} %get-tuple-element.12), channel_id=1, source_target_pairs={{64,0},{80,16},{96,32},{112,48},{128,64},{144,80},{160,96},{176,11... | collective-permute-start | bytes 294920 | tf_op jit(solution)/shard_map/ppermute | solution.py:21
  71.7 0.7 collective-permute-start.6
  72.4 17.3 %collective-permute-start.7 = (bf16[96,256]{1,0:T(8,128)(2,1)S(1)}, bf16[96,256]{1,0:T(8,128)(2,1)S(1)}, u32[]{:S(2)}, u32[]{:S(2)}) collective-permute-start(bf16[96,256]{1,0:T(8,128)(2,1)S(1)} %collective-permute-done.6), channel_id=1, source_target_pairs={{0,2},{1,3},{2,0},{3,1},{4,6},{5,7},{6,4},{7,5},{8,10},{9,11},{10,... | collective-permute-start | bytes 147464 | tf_op jit(solution)/shard_map/ppermute | solution.py:26
  82.7 31.2 %all-to-all-start.2 = ((bf16[8,2,96,256]{3,2,1,0:T(8,128)(2,1)}), bf16[8,2,96,256]{3,2,1,0:T(8,128)(2,1)S(1)}, u32[]{:S(2)}, u32[]{:S(2)}) async-start(bf16[8,2,96,256]{3,2,1,0:T(8,128)(2,1)} %combine.1), calls=%async_computation.2 | async-start | bytes 1572864 | tf_op jit(solution)/shard_map/all_to_all | solution.py:258
  89.8 10.4 %collective-permute-start.8 = (bf16[2,96,256]{2,1,0:T(8,128)(2,1)S(1)}, bf16[2,96,256]{2,1,0:T(8,128)(2,1)S(1)}, u32[]{:S(2)}, u32[]{:S(2)}) collective-permute-start(bf16[2,96,256]{2,1,0:T(8,128)(2,1)S(1)} %pad_maximum_fusion.3), channel_id=1, source_target_pairs={{0,4},{1,5},{2,6},{3,7},{4,0},{5,1},{6,2},{7,3},{8,12},{9,13},{10,... | collective-permute-start | bytes 294920 | tf_op jit(solution)/shard_map/ppermute | solution.py:26
  100.2 8.4 %collective-permute-start.10 = (bf16[2,2,96,256]{3,2,1,0:T(8,128)(2,1)S(1)}, bf16[2,2,96,256]{3,2,1,0:T(8,128)(2,1)S(1)}, u32[]{:S(2)}, u32[]{:S(2)}) collective-permute-start(bf16[2,2,96,256]{3,2,1,0:T(8,128)(2,1)S(1)} %pad_maximum_fusion.2), channel_id=1, source_target_pairs={{0,8},{1,9},{2,10},{3,11},{4,12},{5,13},{6,14},{7,15},{8,0},{9,1},... | collective-permute-start | bytes 589832 | tf_op jit(solution)/shard_map/ppermute | solution.py:261
  102.2 7.4 %collective-permute-start.9 = (bf16[2,2,96,256]{3,2,1,0:T(8,128)(2,1)S(1)}, bf16[2,2,96,256]{3,2,1,0:T(8,128)(2,1)S(1)}, u32[]{:S(2)}, u32[]{:S(2)}) collective-permute-start(bf16[2,2,96,256]{3,2,1,0:T(8,128)(2,1)S(1)} %pad_maximum_fusion.2), channel_id=1, source_target_pairs={{0,9},{1,8},{2,11},{3,10},{4,13},{5,12},{6,15},{7,14},{8,1},{9,0},... | collective-permute-start | bytes 589832 | tf_op jit(solution)/shard_map/ppermute | solution.py:261
  104.7 9.0 %collective-permute-start.11 = (bf16[2,2,96,256]{3,2,1,0:T(8,128)(2,1)S(1)}, bf16[2,2,96,256]{3,2,1,0:T(8,128)(2,1)S(1)}, u32[]{:S(2)}, u32[]{:S(2)}) collective-permute-start(bf16[2,2,96,256]{3,2,1,0:T(8,128)(2,1)S(1)} %pad_maximum_fusion.2), channel_id=1, source_target_pairs={{0,1},{1,0},{2,3},{3,2},{4,5},{5,4},{6,7},{7,6},{8,9},{9,8},{10,11... | collective-permute-start | bytes 589832 | tf_op jit(solution)/shard_map/ppermute | solution.py:261
  114.3 6.5 %collective-permute-start.12 = (f32[2,2,128,256]{3,2,1,0:T(8,128)S(1)}, f32[2,2,128,256]{3,2,1,0:T(8,128)S(1)}, u32[]{:S(2)}, u32[]{:S(2)}) collective-permute-start(f32[2,2,128,256]{3,2,1,0:T(8,128)S(1)} %convolution_bitcast_fusion), channel_id=1, source_target_pairs={{0,16},{16,0},{1,17},{17,1},{2,18},{18,2},{3,19},{19,3},{4,20},{20... | collective-permute-start | bytes 1572872 | tf_op jit(solution)/shard_map/ppermute | solution.py:280
  121.2 9.5 %collective-permute-start.13 = (bf16[2,128,256]{2,1,0:T(8,128)(2,1)S(1)}, bf16[2,128,256]{2,1,0:T(8,128)(2,1)S(1)}, u32[]{:S(2)}, u32[]{:S(2)}) collective-permute-start(bf16[2,128,256]{2,1,0:T(8,128)(2,1)S(1)} %fusion.1), channel_id=1, source_target_pairs={{0,32},{32,0},{1,33},{33,1},{2,34},{34,2},{3,35},{35,3},{4,36},{36... | collective-permute-start | bytes 393224 | tf_op jit(solution)/shard_map/ppermute | solution.py:283

commit v12 on v11

--- a/solution.py
+++ b/solution.py
@@ -52,15 +52,15 @@
                 at = (2 * s + t) * rows
                 value = slab[:, lo:hi].astype(F32) * expo[t : t + 1]
                 left[at : at + rows, lo:hi] = value.astype(BF)
-    lane = lax.broadcasted_iota(jnp.int32, (2 * rows, 4 * rows), 1)
     for q, (lo, hi) in enumerate(((0, nocc), (nocc, cols))):
-        a = lax.dot_general(
-            left[0 : 2 * rows, lo:hi], panel[:, lo:hi], LAST, preferred_element_type=F32
-        )
-        b = lax.dot_general(
-            left[2 * rows : 4 * rows, lo:hi], panel[:, lo:hi], LAST, preferred_element_type=F32
-        )
-        total[q] = jnp.where(lane < 2 * rows, a, b)
+        for s in range(2):
+            at = 2 * s * rows
+            total[q, :, at : at + 2 * rows] = lax.dot_general(
+                left[at : at + 2 * rows, lo:hi],
+                panel[at : at + 2 * rows, lo:hi],
+                LAST,
+                preferred_element_type=F32,
+            )
     for j in range(16):
         rows12[j, 0:12] = total[0, 12 * j : 12 * j + 12]
         rows12[j, 12:24] = total[1, 12 * j : 12 * j + 12]
@@ -212,24 +212,24 @@
     )(own, a, b, c)
 
 
-def finish_kernel(x_hi, own, beside, across, out):
+def finish_kernel(own, here, across, out):
     for t in range(2):
-        out[:, t, :] = own[t] + beside[x_hi[0], t] + across[t].astype(F32)
-
-
-def finish(x_hi, own, beside, across):
+        out[:, t, :] = own[t] + here[t] + across[t].astype(F32)
+
+
+def finish(own, here, across):
     times, count, naux = own.shape
     return pl.pallas_call(
         finish_kernel,
         out_shape=jax.ShapeDtypeStruct((count, times, naux), F32),
-        in_specs=[SCALARS] + [WHOLE] * 3,
+        in_specs=[WHOLE] * 3,
         out_specs=WHOLE,
         compiler_params=pltpu.CompilerParams(vmem_limit_bytes=8 * 2**20),
         cost_estimate=pl.CostEstimate(
             flops=4 * own.size, bytes_accessed=16 * own.size, transcendentals=0
         ),
         name="finish",
-    )(x_hi, own, beside, across)
+    )(own, here, across)
 
 
 def on_device(phi_occ, phi_vir, eps_occ, eps_vir, taus, pair_mask, basis):
@@ -248,14 +248,15 @@
     sums = lax.all_to_all(part_sums, ORB, 0, 0, tiled=True)
     both = product(sums)
     both = lax.all_to_all(both, ORB, 0, 0, tiled=True)
-    part = join(part, trade(part, "y", 2), "y", 2, 0)
-    part = join(part, trade(part, "y", 4), "y", 4, 0)
+    got = trade(part, "y", 2)
     to_up, to_down, to_mate, own = project(core.reshape(1), both, mine, mate, up, down, naux)
     got_up = from_tile(to_up, -2)
     got_down = from_tile(to_down, 4)
     got_mate = lax.ppermute(to_mate, "core", SWAP)
     copies = combine(own, got_mate, got_up, got_down)
     gathered = lax.all_to_all(copies, "z", 0, 0, tiled=True)
+    part = join(part, got, "y", 2, 0)
+    part = join(part, trade(part, "y", 4), "y", 4, 0)
     others = [part]
     for flip in (9, 8, 1):
         others.append(lax.ppermute(part, ORB, [(i, i ^ flip) for i in range(16)]))
@@ -274,14 +275,12 @@
     def response(cols):
         return jnp.einsum("zrp,ztrq->tpq", cols, gathered, preferred_element_type=F32)
 
-    start = (0, 0, 0, (1 - core) * (naux // 2))
-    others = lax.dynamic_slice(blocks, start, (2, 8, rows, naux // 2))
-    pair = jnp.einsum("hzrp,ztrq->htpq", others, gathered, preferred_element_type=F32)
-    beside = lax.ppermute(pair, "core", SWAP)
-    mine_here, mine_there = response(chosen(xh, core)), response(chosen(1 - xh, core))
-    there = lax.dynamic_index_in_dim(beside, 1 - xh, 0, keepdims=False)
-    across = lax.ppermute((mine_there + there).astype(BF), "xh", SWAP)
-    return finish(xh.reshape(1), mine_here, beside, across)
+    there = lax.ppermute(response(chosen(1 - xh, 1 - core)).astype(BF), "core", SWAP)
+    total = response(chosen(1 - xh, core)) + there.astype(F32)
+    across = lax.ppermute(total.astype(BF), "xh", SWAP)
+    here = lax.ppermute(response(chosen(xh, 1 - core)), "core", SWAP)
+    own = response(chosen(xh, core))
+    return finish(own, here, across)
 
 
 def solution(mesh):

time: 132 us -> 133 us (level)
  starting transfers between devices: 70.2 us -> 72.2 us
  waiting for transfers between devices: 24.8 us -> 23.2 us
    ppermute x2 -> x3, starting transfers between devices: 11 us -> 12.9 us  [the longest x1 5.97 us: on_device(): across = lax.ppermute(total.astype(BF), 'xh', SWAP)]
    ppermute x2 -> x3, waiting for transfers between devices: 4.65 us -> 3.03 us  [the longest x1 3.03 us: on_device(): across = lax.ppermute(total.astype(BF), 'xh', SWAP)]
  transfers between devices with their start and end apart: 15 -> 16, of which waited for: 7 -> 6; matrix products, arithmetic and copies ran while one was open for 1% -> 1% of each run, Pallas kernels for 1% -> 1%
where the time goes in v12:
time: 133 us; the launch traced here: 132 us
  starting transfers between devices  72.2 us (54%)
  blocking collectives  28.8 us (22%)
  waiting for transfers between devices  23.2 us (17%)
  Pallas kernels  3.11 us (2%)
  other arithmetic  2.07 us (2%)
    all_to_all x1, blocking collectives, on_device(): sums = lax.all_to_all(part_sums, ORB, 0, 0, tiled=True)  15.5 us
    ppermute x4, starting transfers between devices, from_tile(): return lax.ppermute(value, PTS, [((i + steps) % 32, i) for i in range(32)])  15.2 us
    ppermute x2, starting transfers between devices, trade(): return lax.ppermute(value, axis, [(i, i ^ bit) for i in range(size)])  14.4 us
    all_to_all x1, blocking collectives, on_device(): both = lax.all_to_all(both, ORB, 0, 0, tiled=True)  13.4 us
    ppermute x4, waiting for transfers between devices, from_tile(): return lax.ppermute(value, PTS, [((i + steps) % 32, i) for i in range(32)])  9.65 us
    ppermute x1, starting transfers between devices, on_device(): mate = lax.ppermute(mine, 'core', SWAP)  8.75 us
    ppermute x3, starting transfers between devices, on_device(): others.append(lax.ppermute(part, ORB, [(i, i ^ flip) for i in range(16)]))  8.37 us
    all_to_all x1, starting transfers between devices, on_device(): gathered = lax.all_to_all(copies, 'z', 0, 0, tiled=True)  6.99 us
  transfers between devices with their start and end apart: 16, of which 6 were waited for; matrix products, arithmetic and copies ran while one was open for 1% of the time, Pallas kernels for 1%

profile of v12, /device:TPU:1, one launch (start us, length us, event | category | flops | bytes accessed | tf_op | source)
XLA Modules:
  0.0 131.7 jit_solution(6035103395664668125)
XLA Ops:
  0.7 1.0 maximum_maximum_fusion.mine
  1.7 8.7 %collective-permute-start = (bf16[96,1792]{1,0:T(8,128)(2,1)S(1)}, bf16[96,1792]{1,0:T(8,128)(2,1)S(1)}, u32[]{:S(2)}, u32[]{:S(2)}) collective-permute-start(bf16[96,1792]{1,0:T(8,128)(2,1)S(1)} %maximum_maximum_fusion.mine), channel_id=1, source_target_pairs={{0,16},{16,0},{1,17},{17,1},{2,18},{18,2},{3,19},{19,3},{4,20},{20... | collective-permute-start | bytes 1032200 | tf_op jit(solution)/shard_map/ppermute | solution.py:242
  10.5 7.8 %collective-permute-start.1 = (bf16[96,1792]{1,0:T(8,128)(2,1)S(1)}, bf16[96,1792]{1,0:T(8,128)(2,1)S(1)}, u32[]{:S(2)}, u32[]{:S(2)}) collective-permute-start(bf16[96,1792]{1,0:T(8,128)(2,1)S(1)} %maximum_maximum_fusion.mine), channel_id=1, source_target_pairs={{32,0},{48,16},{64,32},{80,48},{96,64},{112,80},{128,96},{144,112}... | collective-permute-start | bytes 1032200 | tf_op jit(solution)/shard_map/ppermute | solution.py:21
  18.3 1.9 %collective-permute-start.2 = (bf16[96,1792]{1,0:T(8,128)(2,1)S(1)}, bf16[96,1792]{1,0:T(8,128)(2,1)S(1)}, u32[]{:S(2)}, u32[]{:S(2)}) collective-permute-start(bf16[96,1792]{1,0:T(8,128)(2,1)S(1)} %maximum_maximum_fusion.mine), channel_id=1, source_target_pairs={{448,0},{464,16},{480,32},{496,48},{0,64},{16,80},{32,96},{48,112}... | collective-permute-start | bytes 1032200 | tf_op jit(solution)/shard_map/ppermute | solution.py:21
  21.1 4.6 %collective-permute-done.1.up = bf16[96,1792]{1,0:T(8,128)(2,1)S(1)} collective-permute-done((bf16[96,1792]{1,0:T(8,128)(2,1)S(1)}, bf16[96,1792]{1,0:T(8,128)(2,1)S(1)}, u32[]{:S(2)}, u32[]{:S(2)}) %collective-permute-start.1) | collective-permute-done | bytes 344096 | tf_op jit(solution)/shard_map/ppermute | solution.py:21
  25.7 5.0 %collective-permute-done.2.down = bf16[96,1792]{1,0:T(8,128)(2,1)S(1)} collective-permute-done((bf16[96,1792]{1,0:T(8,128)(2,1)S(1)}, bf16[96,1792]{1,0:T(8,128)(2,1)S(1)}, u32[]{:S(2)}, u32[]{:S(2)}) %collective-permute-start.2) | collective-permute-done | bytes 344096 | tf_op jit(solution)/shard_map/ppermute | solution.py:21
  31.4 15.5 %all_to_all.15.parts = bf16[16,24,384]{2,1,0:T(8,128)(2,1)S(1)} all-to-all(bf16[16,24,384]{2,1,0:T(8,128)(2,1)S(1)} %green.1), channel_id=1, replica_groups=mesh['z'=8,'xh'=2,'core'=2,'xl'=2,'y'=8] {'xl','y'}, dimensions={0} | all-to-all | bytes 589824 | tf_op jit(solution)/shard_map/all_to_all | solution.py:248
  47.0 13.4 %all_to_all.16.parts = bf16[16,12,384]{2,1,0:T(8,128)(2,1)S(1)} all-to-all(bf16[16,12,384]{2,1,0:T(8,128)(2,1)S(1)} %product.1), channel_id=1, replica_groups=mesh['z'=8,'xh'=2,'core'=2,'xl'=2,'y'=8] {'xl','y'}, dimensions={0} | all-to-all | bytes 294912 | tf_op jit(solution)/shard_map/all_to_all | solution.py:250
  61.0 4.9 %collective-permute-start.3 = (f32[2,96,256]{2,1,0:T(8,128)S(1)}, f32[2,96,256]{2,1,0:T(8,128)S(1)}, u32[]{:S(2)}, u32[]{:S(2)}) collective-permute-start(f32[2,96,256]{2,1,0:T(8,128)S(1)} %get-tuple-element.10), channel_id=1, source_target_pairs={{0,16},{16,0},{1,17},{17,1},{2,18},{18,2},{3,19},{19,3},{4,20},{20... | collective-permute-start | bytes 589832 | tf_op jit(solution)/shard_map/ppermute | solution.py:255
  65.9 1.9 %collective-permute-start.4 = (bf16[2,96,256]{2,1,0:T(8,128)(2,1)S(1)}, bf16[2,96,256]{2,1,0:T(8,128)(2,1)S(1)}, u32[]{:S(2)}, u32[]{:S(2)}) collective-permute-start(bf16[2,96,256]{2,1,0:T(8,128)(2,1)S(1)} %get-tuple-element.11), channel_id=1, source_target_pairs={{480,0},{496,16},{0,32},{16,48},{32,64},{48,80},{64,96},{80,112},{... | collective-permute-start | bytes 294920 | tf_op jit(solution)/shard_map/ppermute | solution.py:21
  67.8 3.6 %collective-permute-start.5 = (bf16[2,96,256]{2,1,0:T(8,128)(2,1)S(1)}, bf16[2,96,256]{2,1,0:T(8,128)(2,1)S(1)}, u32[]{:S(2)}, u32[]{:S(2)}) collective-permute-start(bf16[2,96,256]{2,1,0:T(8,128)(2,1)S(1)} %get-tuple-element.12), channel_id=1, source_target_pairs={{64,0},{80,16},{96,32},{112,48},{128,64},{144,80},{160,96},{176,11... | collective-permute-start | bytes 294920 | tf_op jit(solution)/shard_map/ppermute | solution.py:21
  72.1 9.3 %collective-permute-start.7 = (bf16[96,256]{1,0:T(8,128)(2,1)S(1)}, bf16[96,256]{1,0:T(8,128)(2,1)S(1)}, u32[]{:S(2)}, u32[]{:S(2)}) collective-permute-start(bf16[96,256]{1,0:T(8,128)(2,1)S(1)} %collective-permute-done.6), channel_id=1, source_target_pairs={{0,2},{1,3},{2,0},{3,1},{4,6},{5,7},{6,4},{7,5},{8,10},{9,11},{10,... | collective-permute-start | bytes 147464 | tf_op jit(solution)/shard_map/ppermute | solution.py:26
  81.5 0.9 combine.1
  82.4 7.0 %all-to-all-start.2 = ((bf16[8,2,96,256]{3,2,1,0:T(8,128)(2,1)}), bf16[8,2,96,256]{3,2,1,0:T(8,128)(2,1)S(1)}, u32[]{:S(2)}, u32[]{:S(2)}) async-start(bf16[8,2,96,256]{3,2,1,0:T(8,128)(2,1)} %combine.1), calls=%async_computation.2 | async-start | bytes 1572864 | tf_op jit(solution)/shard_map/all_to_all | solution.py:257
  89.5 5.0 %collective-permute-start.8 = (bf16[2,96,256]{2,1,0:T(8,128)(2,1)S(1)}, bf16[2,96,256]{2,1,0:T(8,128)(2,1)S(1)}, u32[]{:S(2)}, u32[]{:S(2)}) collective-permute-start(bf16[2,96,256]{2,1,0:T(8,128)(2,1)S(1)} %pad_maximum_fusion.3), channel_id=1, source_target_pairs={{0,4},{1,5},{2,6},{3,7},{4,0},{5,1},{6,2},{7,3},{8,12},{9,13},{10,... | collective-permute-start | bytes 294920 | tf_op jit(solution)/shard_map/ppermute | solution.py:26
  94.5 5.4 %collective-permute-done.8 = bf16[2,96,256]{2,1,0:T(8,128)(2,1)S(1)} collective-permute-done((bf16[2,96,256]{2,1,0:T(8,128)(2,1)S(1)}, bf16[2,96,256]{2,1,0:T(8,128)(2,1)S(1)}, u32[]{:S(2)}, u32[]{:S(2)}) %collective-permute-start.8) | collective-permute-done | bytes 98336 | tf_op jit(solution)/shard_map/ppermute | solution.py:26
  99.9 1.9 %collective-permute-start.10 = (bf16[2,2,96,256]{3,2,1,0:T(8,128)(2,1)S(1)}, bf16[2,2,96,256]{3,2,1,0:T(8,128)(2,1)S(1)}, u32[]{:S(2)}, u32[]{:S(2)}) collective-permute-start(bf16[2,2,96,256]{3,2,1,0:T(8,128)(2,1)S(1)} %pad_maximum_fusion.2), channel_id=1, source_target_pairs={{0,8},{1,9},{2,10},{3,11},{4,12},{5,13},{6,14},{7,15},{8,0},{9,1},... | collective-permute-start | bytes 589832 | tf_op jit(solution)/shard_map/ppermute | solution.py:262
  101.9 2.6 %collective-permute-start.9 = (bf16[2,2,96,256]{3,2,1,0:T(8,128)(2,1)S(1)}, bf16[2,2,96,256]{3,2,1,0:T(8,128)(2,1)S(1)}, u32[]{:S(2)}, u32[]{:S(2)}) collective-permute-start(bf16[2,2,96,256]{3,2,1,0:T(8,128)(2,1)S(1)} %pad_maximum_fusion.2), channel_id=1, source_target_pairs={{0,9},{1,8},{2,11},{3,10},{4,13},{5,12},{6,15},{7,14},{8,1},{9,0},... | collective-permute-start | bytes 589832 | tf_op jit(solution)/shard_map/ppermute | solution.py:262
  104.4 3.9 %collective-permute-start.11 = (bf16[2,2,96,256]{3,2,1,0:T(8,128)(2,1)S(1)}, bf16[2,2,96,256]{3,2,1,0:T(8,128)(2,1)S(1)}, u32[]{:S(2)}, u32[]{:S(2)}) collective-permute-start(bf16[2,2,96,256]{3,2,1,0:T(8,128)(2,1)S(1)} %pad_maximum_fusion.2), channel_id=1, source_target_pairs={{0,1},{1,0},{2,3},{3,2},{4,5},{5,4},{6,7},{7,6},{8,9},{9,8},{10,11... | collective-permute-start | bytes 589832 | tf_op jit(solution)/shard_map/ppermute | solution.py:262
  109.3 4.1 %collective-permute-done.11 = bf16[2,2,96,256]{3,2,1,0:T(8,128)(2,1)S(1)} collective-permute-done((bf16[2,2,96,256]{3,2,1,0:T(8,128)(2,1)S(1)}, bf16[2,2,96,256]{3,2,1,0:T(8,128)(2,1)S(1)}, u32[]{:S(2)}, u32[]{:S(2)}) %collective-permute-start.11) | collective-permute-done | bytes 196640 | tf_op jit(solution)/shard_map/ppermute | solution.py:262
  113.9 5.0 %collective-permute-start.13 = (bf16[2,128,256]{2,1,0:T(8,128)(2,1)S(1)}, bf16[2,128,256]{2,1,0:T(8,128)(2,1)S(1)}, u32[]{:S(2)}, u32[]{:S(2)}) collective-permute-start(bf16[2,128,256]{2,1,0:T(8,128)(2,1)S(1)} %fusion.3), channel_id=1, source_target_pairs={{0,16},{16,0},{1,17},{17,1},{2,18},{18,2},{3,19},{19,3},{4,20},{20... | collective-permute-start | bytes 393224 | tf_op jit(solution)/shard_map/ppermute | solution.py:278
  119.2 1.9 %collective-permute-start.12 = (f32[2,128,256]{2,1,0:T(8,128)S(1)}, f32[2,128,256]{2,1,0:T(8,128)S(1)}, u32[]{:S(2)}, u32[]{:S(2)}) collective-permute-start(f32[2,128,256]{2,1,0:T(8,128)S(1)} %convolution_bitcast_fusion.2), channel_id=1, source_target_pairs={{0,16},{16,0},{1,17},{17,1},{2,18},{18,2},{3,19},{19,3},{4,20},{20... | collective-permute-start | bytes 786440 | tf_op jit(solution)/shard_map/ppermute | solution.py:281
  121.5 6.0 %collective-permute-start.14 = (bf16[2,128,256]{2,1,0:T(8,128)(2,1)S(1)}, bf16[2,128,256]{2,1,0:T(8,128)(2,1)S(1)}, u32[]{:S(2)}, u32[]{:S(2)}) collective-permute-start(bf16[2,128,256]{2,1,0:T(8,128)(2,1)S(1)} %fusion.1), channel_id=1, source_target_pairs={{0,32},{32,0},{1,33},{33,1},{2,34},{34,2},{3,35},{35,3},{4,36},{36... | collective-permute-start | bytes 393224 | tf_op jit(solution)/shard_map/ppermute | solution.py:280
  127.9 3.0 %collective-permute-done.14.across = bf16[2,128,256]{2,1,0:T(8,128)(2,1)S(1)} collective-permute-done((bf16[2,128,256]{2,1,0:T(8,128)(2,1)S(1)}, bf16[2,128,256]{2,1,0:T(8,128)(2,1)S(1)}, u32[]{:S(2)}, u32[]{:S(2)}) %collective-permute-start.14) | collective-permute-done | bytes 131104 | tf_op jit(solution)/shard_map/ppermute | solution.py:280
  (40 shorter events, 6.8 us)
Async XLA Ops:
  0.7 19.5 %copy-start.3 = (f32[2]{0:T(128)S(1)}, f32[2]{0:T(128)}, u32[]{:S(2)}) copy-start(f32[2]{0:T(128)} %param.11) | copy-start | bytes 28
  1.7 19.2 %copy-start.1 = (f32[1280]{0:T(1024)S(1)}, f32[1280]{0:T(1024)}, u32[]{:S(2)}) copy-start(f32[1280]{0:T(1024)} %param.10) | copy-start | bytes 15364
  1.7 19.3 %collective-permute-start = (bf16[96,1792]{1,0:T(8,128)(2,1)S(1)}, bf16[96,1792]{1,0:T(8,128)(2,1)S(1)}, u32[]{:S(2)}, u32[]{:S(2)}) collective-permute-start(bf16[96,1792]{1,0:T(8,128)(2,1)S(1)} %maximum_maximum_fusion.mine), channel_id=1, source_target_pairs={{0,16},{16,0},{1,17},{17,1},{2,18},{18,2},{3,19},{19,3},{4,20},{20... | collective-permute-start | bytes 1032200 | tf_op jit(solution)/shard_map/ppermute | solution.py:242
  10.5 15.2 %collective-permute-start.1 = (bf16[96,1792]{1,0:T(8,128)(2,1)S(1)}, bf16[96,1792]{1,0:T(8,128)(2,1)S(1)}, u32[]{:S(2)}, u32[]{:S(2)}) collective-permute-start(bf16[96,1792]{1,0:T(8,128)(2,1)S(1)} %maximum_maximum_fusion.mine), channel_id=1, source_target_pairs={{32,0},{48,16},{64,32},{80,48},{96,64},{112,80},{128,96},{144,112}... | collective-permute-start | bytes 1032200 | tf_op jit(solution)/shard_map/ppermute | solution.py:21
  18.3 12.4 %collective-permute-start.2 = (bf16[96,1792]{1,0:T(8,128)(2,1)S(1)}, bf16[96,1792]{1,0:T(8,128)(2,1)S(1)}, u32[]{:S(2)}, u32[]{:S(2)}) collective-permute-start(bf16[96,1792]{1,0:T(8,128)(2,1)S(1)} %maximum_maximum_fusion.mine), channel_id=1, source_target_pairs={{448,0},{464,16},{480,32},{496,48},{0,64},{16,80},{32,96},{48,112}... | collective-permute-start | bytes 1032200 | tf_op jit(solution)/shard_map/ppermute | solution.py:21
  20.2 0.7 copy-start.2
  60.4 11.0 %copy-start = (bf16[96,256]{1,0:T(8,128)(2,1)S(1)}, bf16[96,256]{1,0:T(8,128)(2,1)}, u32[]{:S(2)}) copy-start(bf16[96,256]{1,0:T(8,128)(2,1)} %param.13) | copy-start | bytes 147460
  61.0 20.5 %collective-permute-start.3 = (f32[2,96,256]{2,1,0:T(8,128)S(1)}, f32[2,96,256]{2,1,0:T(8,128)S(1)}, u32[]{:S(2)}, u32[]{:S(2)}) collective-permute-start(f32[2,96,256]{2,1,0:T(8,128)S(1)} %get-tuple-element.10), channel_id=1, source_target_pairs={{0,16},{16,0},{1,17},{17,1},{2,18},{18,2},{3,19},{19,3},{4,20},{20... | collective-permute-start | bytes 589832 | tf_op jit(solution)/shard_map/ppermute | solution.py:255
  65.9 15.5 %collective-permute-start.4 = (bf16[2,96,256]{2,1,0:T(8,128)(2,1)S(1)}, bf16[2,96,256]{2,1,0:T(8,128)(2,1)S(1)}, u32[]{:S(2)}, u32[]{:S(2)}) collective-permute-start(bf16[2,96,256]{2,1,0:T(8,128)(2,1)S(1)} %get-tuple-element.11), channel_id=1, source_target_pairs={{480,0},{496,16},{0,32},{16,48},{32,64},{48,80},{64,96},{80,112},{... | collective-permute-start | bytes 294920 | tf_op jit(solution)/shard_map/ppermute | solution.py:21
  67.8 13.6 %collective-permute-start.5 = (bf16[2,96,256]{2,1,0:T(8,128)(2,1)S(1)}, bf16[2,96,256]{2,1,0:T(8,128)(2,1)S(1)}, u32[]{:S(2)}, u32[]{:S(2)}) collective-permute-start(bf16[2,96,256]{2,1,0:T(8,128)(2,1)S(1)} %get-tuple-element.12), channel_id=1, source_target_pairs={{64,0},{80,16},{96,32},{112,48},{128,64},{144,80},{160,96},{176,11... | collective-permute-start | bytes 294920 | tf_op jit(solution)/shard_map/ppermute | solution.py:21
  71.4 0.7 collective-permute-start.6
  72.1 17.3 %collective-permute-start.7 = (bf16[96,256]{1,0:T(8,128)(2,1)S(1)}, bf16[96,256]{1,0:T(8,128)(2,1)S(1)}, u32[]{:S(2)}, u32[]{:S(2)}) collective-permute-start(bf16[96,256]{1,0:T(8,128)(2,1)S(1)} %collective-permute-done.6), channel_id=1, source_target_pairs={{0,2},{1,3},{2,0},{3,1},{4,6},{5,7},{6,4},{7,5},{8,10},{9,11},{10,... | collective-permute-start | bytes 147464 | tf_op jit(solution)/shard_map/ppermute | solution.py:26
  82.4 31.1 %all-to-all-start.2 = ((bf16[8,2,96,256]{3,2,1,0:T(8,128)(2,1)}), bf16[8,2,96,256]{3,2,1,0:T(8,128)(2,1)S(1)}, u32[]{:S(2)}, u32[]{:S(2)}) async-start(bf16[8,2,96,256]{3,2,1,0:T(8,128)(2,1)} %combine.1), calls=%async_computation.2 | async-start | bytes 1572864 | tf_op jit(solution)/shard_map/all_to_all | solution.py:257
  89.5 10.4 %collective-permute-start.8 = (bf16[2,96,256]{2,1,0:T(8,128)(2,1)S(1)}, bf16[2,96,256]{2,1,0:T(8,128)(2,1)S(1)}, u32[]{:S(2)}, u32[]{:S(2)}) collective-permute-start(bf16[2,96,256]{2,1,0:T(8,128)(2,1)S(1)} %pad_maximum_fusion.3), channel_id=1, source_target_pairs={{0,4},{1,5},{2,6},{3,7},{4,0},{5,1},{6,2},{7,3},{8,12},{9,13},{10,... | collective-permute-start | bytes 294920 | tf_op jit(solution)/shard_map/ppermute | solution.py:26
  99.9 8.4 %collective-permute-start.10 = (bf16[2,2,96,256]{3,2,1,0:T(8,128)(2,1)S(1)}, bf16[2,2,96,256]{3,2,1,0:T(8,128)(2,1)S(1)}, u32[]{:S(2)}, u32[]{:S(2)}) collective-permute-start(bf16[2,2,96,256]{3,2,1,0:T(8,128)(2,1)S(1)} %pad_maximum_fusion.2), channel_id=1, source_target_pairs={{0,8},{1,9},{2,10},{3,11},{4,12},{5,13},{6,14},{7,15},{8,0},{9,1},... | collective-permute-start | bytes 589832 | tf_op jit(solution)/shard_map/ppermute | solution.py:262
  101.9 7.4 %collective-permute-start.9 = (bf16[2,2,96,256]{3,2,1,0:T(8,128)(2,1)S(1)}, bf16[2,2,96,256]{3,2,1,0:T(8,128)(2,1)S(1)}, u32[]{:S(2)}, u32[]{:S(2)}) collective-permute-start(bf16[2,2,96,256]{3,2,1,0:T(8,128)(2,1)S(1)} %pad_maximum_fusion.2), channel_id=1, source_target_pairs={{0,9},{1,8},{2,11},{3,10},{4,13},{5,12},{6,15},{7,14},{8,1},{9,0},... | collective-permute-start | bytes 589832 | tf_op jit(solution)/shard_map/ppermute | solution.py:262
  104.4 9.0 %collective-permute-start.11 = (bf16[2,2,96,256]{3,2,1,0:T(8,128)(2,1)S(1)}, bf16[2,2,96,256]{3,2,1,0:T(8,128)(2,1)S(1)}, u32[]{:S(2)}, u32[]{:S(2)}) collective-permute-start(bf16[2,2,96,256]{3,2,1,0:T(8,128)(2,1)S(1)} %pad_maximum_fusion.2), channel_id=1, source_target_pairs={{0,1},{1,0},{2,3},{3,2},{4,5},{5,4},{6,7},{7,6},{8,9},{9,8},{10,11... | collective-permute-start | bytes 589832 | tf_op jit(solution)/shard_map/ppermute | solution.py:262
  113.9 7.3 %collective-permute-start.13 = (bf16[2,128,256]{2,1,0:T(8,128)(2,1)S(1)}, bf16[2,128,256]{2,1,0:T(8,128)(2,1)S(1)}, u32[]{:S(2)}, u32[]{:S(2)}) collective-permute-start(bf16[2,128,256]{2,1,0:T(8,128)(2,1)S(1)} %fusion.3), channel_id=1, source_target_pairs={{0,16},{16,0},{1,17},{17,1},{2,18},{18,2},{3,19},{19,3},{4,20},{20... | collective-permute-start | bytes 393224 | tf_op jit(solution)/shard_map/ppermute | solution.py:278
  119.2 8.6 %collective-permute-start.12 = (f32[2,128,256]{2,1,0:T(8,128)S(1)}, f32[2,128,256]{2,1,0:T(8,128)S(1)}, u32[]{:S(2)}, u32[]{:S(2)}) collective-permute-start(f32[2,128,256]{2,1,0:T(8,128)S(1)} %convolution_bitcast_fusion.2), channel_id=1, source_target_pairs={{0,16},{16,0},{1,17},{17,1},{2,18},{18,2},{3,19},{19,3},{4,20},{20... | collective-permute-start | bytes 786440 | tf_op jit(solution)/shard_map/ppermute | solution.py:281
  121.5 9.4 %collective-permute-start.14 = (bf16[2,128,256]{2,1,0:T(8,128)(2,1)S(1)}, bf16[2,128,256]{2,1,0:T(8,128)(2,1)S(1)}, u32[]{:S(2)}, u32[]{:S(2)}) collective-permute-start(bf16[2,128,256]{2,1,0:T(8,128)(2,1)S(1)} %fusion.1), channel_id=1, source_target_pairs={{0,32},{32,0},{1,33},{33,1},{2,34},{34,2},{3,35},{35,3},{4,36},{36... | collective-permute-start | bytes 393224 | tf_op jit(solution)/shard_map/ppermute | solution.py:280
